TPU v7x, 32 devices: a whole 2x2x4 slice. The times are simulated.
32 devices in a mesh: seq: 4 (over y, x), fsdp: 8 (over z, core).
Axes of the slice: x: 2, y: 2, z: 4, core: 2. Of those that a mesh axis runs over, the one named last changes fastest.
Arguments:
- inputs: bfloat16 [8, 1024, 2048], P('fsdp', 'seq'), may hold values from -6 to 6
- out_grad: bfloat16 [8, 1024, 2048], P('fsdp', 'seq'), may hold values from -6 to 6
- doc_ids: int32 [8, 1024], P('fsdp'), may hold values from 0 to 7, never falling along the last dimension, each value on 1 to 512 neighbouring positions
- routes: int32 [8, 1024, 8], P('fsdp', 'seq'), may hold values from 0 to 15, all different within a row; in each aligned block of 256 rows (0 to 255, 256 to 511, ..., all dimensions but the last counted through in order) at most 136 rows name the same one
- w_query: bfloat16 [2048, 2048], P(('seq', 'fsdp')), may hold values from -0.125 to 0.125
- w_key: bfloat16 [2048, 2048], P(('seq', 'fsdp')), may hold values from -0.125 to 0.125
- w_value: bfloat16 [2048, 2048], P(('seq', 'fsdp')), may hold values from -0.125 to 0.125
- w_output: bfloat16 [2048, 2048], P(('seq', 'fsdp')), may hold values from -1 to 1
- w_router: bfloat16 [2048, 16], P(('seq', 'fsdp')), may hold values from -0.0625 to 0.0625
- attn_gain: bfloat16 [2048], P(('seq', 'fsdp')), may hold values from 0.099609375 to 1.8984375
- ffn_gain: bfloat16 [2048], P(('seq', 'fsdp')), may hold values from 0.099609375 to 1.8984375
- query_gain: bfloat16 [2048], P(('seq', 'fsdp')), may hold values from 0.099609375 to 1.8984375
- key_gain: bfloat16 [2048], P(('seq', 'fsdp')), may hold values from 0.099609375 to 1.8984375
- w_gate: bfloat16 [16, 2048, 1024], P('fsdp', 'seq'), may hold values from -0.125 to 0.125
- w_up: bfloat16 [16, 2048, 1024], P('fsdp', 'seq'), may hold values from -0.125 to 0.125
- w_down: bfloat16 [16, 1024, 2048], P('fsdp', 'seq'), may hold values from -1 to 1
Outputs:
- output: bfloat16 [8, 1024, 2048], P('fsdp', 'seq')
- input_grad: float32 [8, 1024, 2048], P('fsdp', 'seq')
- g_query: float32 [2048, 2048], P(('seq', 'fsdp'))
- g_key: float32 [2048, 2048], P(('seq', 'fsdp'))
- g_value: float32 [2048, 2048], P(('seq', 'fsdp'))
- g_output: float32 [2048, 2048], P(('seq', 'fsdp'))
- g_router: float32 [2048, 16], P(('seq', 'fsdp'))
- g_attn_gain: float32 [2048], P(('seq', 'fsdp'))
- g_ffn_gain: float32 [2048], P(('seq', 'fsdp'))
- g_query_gain: float32 [2048], P(('seq', 'fsdp'))
- g_key_gain: float32 [2048], P(('seq', 'fsdp'))
- g_gate: float32 [16, 2048, 1024], P('fsdp', 'seq')
- g_up: float32 [16, 2048, 1024], P('fsdp', 'seq')
- g_down: float32 [16, 1024, 2048], P('fsdp', 'seq')
Inputs may be any that keep to these rules, and one draw needn't show every extreme that they name: `doc_ids`: document numbers never fall along a sequence; a document has 1 to 512 tokens, and one of them exactly that many. `routes`: each token names 8 different experts. Within the 256 tokens of one device (aligned blocks), no expert is named by more than 136 tokens, a bound that some block reaches.
All inputs are finite; a program needn't handle non-finite values.
Results may differ from a plain program's by a relative error of at most 0.017.
Values may be sent and summed in bfloat16 or wider, within the bound.
A program may use at most 320 MiB of HBM per device.

v0:
```python
from functools import partial

import jax
import jax.numpy as jnp
from jax import lax
from jax.sharding import PartitionSpec as P

HEADS = 16
CAP = 136


EPSILON = 1e-05
ROPE_BASE = 10000.0
MASKED_OUT = -1e30
PRECISE = lax.Precision.HIGHEST


def rms_scale(vector, gain_row):
    return (
        vector * lax.rsqrt(jnp.mean(vector * vector, axis=-1, keepdims=True) + EPSILON) * gain_row
    )


def rope_tables(positions, head_dim):
    half_dim = head_dim // 2
    inverse = ROPE_BASE ** (-(jnp.arange(half_dim, dtype=jnp.float32) * 2.0 / head_dim))
    angles = positions.astype(jnp.float32)[:, None] * inverse[None, :]
    angles = jnp.concatenate([angles, angles], axis=-1)
    return (jnp.cos(angles), jnp.sin(angles))


def rotate_heads(vector, cos_table, sin_table):
    rows_here = vector.shape[0]
    split = vector.reshape(rows_here, HEADS, -1)
    half_dim = split.shape[2] // 2
    turned = jnp.concatenate([-split[..., half_dim:], split[..., :half_dim]], axis=-1)
    return (split * cos_table[:, None, :] + turned * sin_table[:, None, :]).reshape(rows_here, -1)


def query_path(raw_rows, gain_row, cos_table, sin_table):
    return rotate_heads(rms_scale(raw_rows, gain_row), cos_table, sin_table)


def silu_value(vector):
    return vector / (1.0 + jnp.exp(-vector))


def allowed_pairs(doc_row, row_start, row_end):
    query_pos = row_start + jnp.arange(row_end - row_start)
    key_pos = jnp.arange(row_end)
    same_doc = doc_row[row_start:row_end, None] == doc_row[None, :row_end]
    return same_doc & (key_pos[None, :] <= query_pos[:, None])


def block_scores(queries, keys, doc_row, row_start, row_end):
    scale_by = queries.shape[2] ** (-0.5)
    raw_scores = (
        jnp.einsum(
            "qhd,khd->hqk",
            queries[row_start:row_end],
            keys[:row_end],
            preferred_element_type=jnp.float32,
        )
        * scale_by
    )
    return jnp.where(allowed_pairs(doc_row, row_start, row_end)[None], raw_scores, MASKED_OUT)


def attend(queries, keys, values, doc_row):
    seq_len = queries.shape[0]
    row_block = min(512, seq_len)
    results = []
    log_sums = []
    for row_start in range(0, seq_len, row_block):
        row_end = row_start + row_block
        scores = block_scores(queries, keys, doc_row, row_start, row_end)
        largest = jnp.max(scores, axis=-1, keepdims=True)
        weights = jnp.exp(scores - largest)
        totals = jnp.sum(weights, axis=-1, keepdims=True)
        probs_low = (weights / totals).astype(jnp.bfloat16)
        results.append(
            jnp.einsum(
                "hqk,khd->qhd", probs_low, values[:row_end], preferred_element_type=jnp.float32
            )
        )
        log_sums.append((largest + jnp.log(totals))[:, :, 0])
    return (jnp.concatenate(results, axis=0), jnp.concatenate(log_sums, axis=1))


def attend_back(queries, keys, values, grad_heads, doc_row, log_sums):
    seq_len, heads_here, head_dim = queries.shape
    row_block = min(512, seq_len)
    scale_by = head_dim ** (-0.5)
    grad_keys = jnp.zeros((seq_len, heads_here, head_dim), jnp.float32)
    grad_values = jnp.zeros((seq_len, heads_here, head_dim), jnp.float32)
    grad_queries = []
    for row_start in range(0, seq_len, row_block):
        row_end = row_start + row_block
        scores = block_scores(queries, keys, doc_row, row_start, row_end)
        probs = jnp.exp(scores - log_sums[:, row_start:row_end, None])
        grad_probs = jnp.einsum(
            "qhd,khd->hqk",
            grad_heads[row_start:row_end],
            values[:row_end],
            preferred_element_type=jnp.float32,
        )
        centre = jnp.sum(probs * grad_probs, axis=-1, keepdims=True)
        grad_scores = (probs * (grad_probs - centre)).astype(jnp.bfloat16)
        grad_queries.append(
            jnp.einsum(
                "hqk,khd->qhd", grad_scores, keys[:row_end], preferred_element_type=jnp.float32
            )
            * scale_by
        )
        grad_keys = grad_keys.at[:row_end].add(
            jnp.einsum(
                "hqk,qhd->khd",
                grad_scores,
                queries[row_start:row_end],
                preferred_element_type=jnp.float32,
            )
            * scale_by
        )
        grad_values = grad_values.at[:row_end].add(
            jnp.einsum(
                "hqk,qhd->khd",
                probs.astype(jnp.bfloat16),
                grad_heads[row_start:row_end],
                preferred_element_type=jnp.float32,
            )
        )
    return (jnp.concatenate(grad_queries, axis=0), grad_keys, grad_values)


def slot_tables(route_rows, experts, capacity):
    tok_rows, top_k = route_rows.shape
    assign = route_rows.reshape(-1)
    onehot = (assign[:, None] == jnp.arange(experts, dtype=jnp.int32)[None, :]).astype(jnp.int32)
    earlier = jnp.cumsum(onehot, axis=0) - onehot
    slot_pos = jnp.sum(earlier * onehot, axis=1)
    places = assign * capacity + slot_pos
    count_all = tok_rows * top_k
    owners = (
        jnp.full((experts * capacity,), count_all, jnp.int32)
        .at[places]
        .set(jnp.arange(count_all, dtype=jnp.int32))
    )
    return (places, owners)


def expert_forward(expert_in, expert_gate, expert_up, expert_down):
    gate_h = jnp.einsum("erd,edh->erh", expert_in, expert_gate, preferred_element_type=jnp.float32)
    up_h = jnp.einsum("erd,edh->erh", expert_in, expert_up, preferred_element_type=jnp.float32)
    silu_gate = silu_value(gate_h)
    act_low = (silu_gate * up_h).astype(jnp.bfloat16)
    expert_out = jnp.einsum(
        "erh,ehd->erd", act_low, expert_down, preferred_element_type=jnp.float32
    ).astype(jnp.bfloat16)
    return (gate_h, up_h, silu_gate, act_low, expert_out)


def expert_backward(expert_in, grad_out, kept, expert_gate, expert_up, expert_down):
    gate_h, up_h, silu_gate, act_low = kept
    grad_act = jnp.einsum("erd,ehd->erh", grad_out, expert_down, preferred_element_type=jnp.float32)
    down_local = jnp.einsum("erh,erd->ehd", act_low, grad_out, preferred_element_type=jnp.float32)
    sigmoid_gate = 1.0 / (1.0 + jnp.exp(-gate_h))
    grad_gate = (grad_act * up_h * sigmoid_gate * (1.0 + gate_h * (1.0 - sigmoid_gate))).astype(
        jnp.bfloat16
    )
    grad_up = (grad_act * silu_gate).astype(jnp.bfloat16)
    grad_in = jnp.einsum("erh,edh->erd", grad_gate, expert_gate, preferred_element_type=jnp.float32)
    grad_in = grad_in + jnp.einsum(
        "erh,edh->erd", grad_up, expert_up, preferred_element_type=jnp.float32
    )
    gate_local = jnp.einsum(
        "erd,erh->edh", expert_in, grad_gate, preferred_element_type=jnp.float32
    )
    up_local = jnp.einsum("erd,erh->edh", expert_in, grad_up, preferred_element_type=jnp.float32)
    return (grad_in.astype(jnp.bfloat16), gate_local, up_local, down_local)


def on_device(
    inputs,
    out_grad,
    doc_ids,
    routes,
    w_query,
    w_key,
    w_value,
    w_output,
    w_router,
    attn_gain,
    ffn_gain,
    query_gain,
    key_gain,
    w_gate,
    w_up,
    w_down,
):
    tok_rows = inputs.shape[1]
    model_width = inputs.shape[2]
    seq_count = lax.axis_size("seq")
    shard_count = lax.axis_size("fsdp")
    heads_here = HEADS // seq_count
    head_dim = model_width // HEADS
    local_experts = w_gate.shape[0]
    experts = local_experts * shard_count
    top_k = routes.shape[2]
    capacity = CAP
    full_weights = (
        lax.all_gather(w_query, ("seq", "fsdp"), axis=0, tiled=True),
        lax.all_gather(w_key, ("seq", "fsdp"), axis=0, tiled=True),
        lax.all_gather(w_value, ("seq", "fsdp"), axis=0, tiled=True),
        lax.all_gather(w_output, ("seq", "fsdp"), axis=0, tiled=True),
        lax.all_gather(w_router, ("seq", "fsdp"), axis=0, tiled=True),
        lax.all_gather(attn_gain, ("seq", "fsdp"), axis=0, tiled=True),
        lax.all_gather(ffn_gain, ("seq", "fsdp"), axis=0, tiled=True),
        lax.all_gather(query_gain, ("seq", "fsdp"), axis=0, tiled=True),
        lax.all_gather(key_gain, ("seq", "fsdp"), axis=0, tiled=True),
    )
    w_q, w_k, w_v, w_o, w_r, gain_a, gain_f, gain_q, gain_k = full_weights
    expert_gate, expert_up, expert_down = (
        lax.all_gather(w_gate, "seq", axis=1, tiled=True),
        lax.all_gather(w_up, "seq", axis=1, tiled=True),
        lax.all_gather(w_down, "seq", axis=1, tiled=True),
    )
    rows_in = inputs[0].astype(jnp.float32)
    grad_rows = out_grad[0].astype(jnp.float32)
    doc_row = doc_ids[0]
    route_rows = routes[0]
    h1_rows, norm_one_pull = jax.vjp(rms_scale, rows_in, gain_a.astype(jnp.float32))
    h1_low = h1_rows.astype(jnp.bfloat16)
    q_raw = jnp.dot(h1_low, w_q, preferred_element_type=jnp.float32)
    k_raw = jnp.dot(h1_low, w_k, preferred_element_type=jnp.float32)
    v_low = jnp.dot(h1_low, w_v, preferred_element_type=jnp.float32).astype(jnp.bfloat16)
    positions = lax.axis_index("seq") * tok_rows + jnp.arange(tok_rows, dtype=jnp.int32)
    cos_table, sin_table = rope_tables(positions, head_dim)
    path_fn = partial(query_path, cos_table=cos_table, sin_table=sin_table)
    q_rot, query_pull = jax.vjp(path_fn, q_raw, gain_q.astype(jnp.float32))
    k_rot, key_pull = jax.vjp(path_fn, k_raw, gain_k.astype(jnp.float32))
    q_heads, k_heads, v_heads = (
        lax.all_to_all(q_rot.astype(jnp.bfloat16), "seq", split_axis=1, concat_axis=0, tiled=True),
        lax.all_to_all(k_rot.astype(jnp.bfloat16), "seq", split_axis=1, concat_axis=0, tiled=True),
        lax.all_to_all(v_low, "seq", split_axis=1, concat_axis=0, tiled=True),
    )
    seq_len = q_heads.shape[0]
    queries = q_heads.reshape(seq_len, heads_here, head_dim)
    keys = k_heads.reshape(seq_len, heads_here, head_dim)
    values = v_heads.reshape(seq_len, heads_here, head_dim)
    heads_out, log_sums = attend(queries, keys, values, doc_row)
    attended = lax.all_to_all(
        heads_out.reshape(seq_len, heads_here * head_dim).astype(jnp.bfloat16),
        "seq",
        split_axis=0,
        concat_axis=1,
        tiled=True,
    )
    x_mid = rows_in + jnp.dot(attended, w_o, preferred_element_type=jnp.float32)
    h2_rows, norm_two_pull = jax.vjp(rms_scale, x_mid, gain_f.astype(jnp.float32))
    h2_low = h2_rows.astype(jnp.bfloat16)
    logits = jnp.dot(h2_low, w_r, preferred_element_type=jnp.float32)
    shifted = jnp.exp(logits - jnp.max(logits, axis=-1, keepdims=True))
    gate_probs = shifted / jnp.sum(shifted, axis=-1, keepdims=True)
    gates = jnp.take_along_axis(gate_probs, route_rows, axis=1)
    places, owners = slot_tables(route_rows, experts, capacity)
    token_of = owners // top_k
    padded = jnp.concatenate([h2_low, jnp.zeros((1, model_width), jnp.bfloat16)], axis=0)
    send_rows = jnp.take(padded, token_of, axis=0).reshape(experts, capacity, model_width)
    gate_pad = jnp.concatenate([gates.reshape(-1), jnp.zeros((1,), jnp.float32)], axis=0)
    grad_pad = jnp.concatenate([grad_rows, jnp.zeros((1, model_width), jnp.float32)], axis=0)
    grad_send = (
        (jnp.take(gate_pad, owners, axis=0)[:, None] * jnp.take(grad_pad, token_of, axis=0))
        .astype(jnp.bfloat16)
        .reshape(experts, capacity, model_width)
    )
    expert_in = lax.all_to_all(send_rows, "fsdp", split_axis=0, concat_axis=1, tiled=True)
    gate_h, up_h, silu_gate, act_low, expert_out = expert_forward(
        expert_in, expert_gate, expert_up, expert_down
    )
    returned = lax.all_to_all(expert_out, "fsdp", split_axis=1, concat_axis=0, tiled=True)
    grad_out = lax.all_to_all(grad_send, "fsdp", split_axis=0, concat_axis=1, tiled=True)
    grad_in_low, gate_local, up_local, down_local = expert_backward(
        expert_in, grad_out, (gate_h, up_h, silu_gate, act_low), expert_gate, expert_up, expert_down
    )
    grad_back = lax.all_to_all(grad_in_low, "fsdp", split_axis=1, concat_axis=0, tiled=True)
    returned = returned.reshape(experts * capacity, model_width)
    grad_back = grad_back.reshape(experts * capacity, model_width)
    chosen = jnp.take(returned, places, axis=0).reshape(tok_rows, top_k, model_width)
    result = x_mid + jnp.einsum(
        "tk,tkd->td", gates, chosen, precision=PRECISE, preferred_element_type=jnp.float32
    )
    grad_chosen = jnp.take(grad_back, places, axis=0).reshape(tok_rows, top_k, model_width)
    g_gate, g_up, g_down = (
        lax.psum_scatter(
            gate_local.astype(jnp.bfloat16), "seq", scatter_dimension=1, tiled=True
        ).astype(jnp.float32),
        lax.psum_scatter(
            up_local.astype(jnp.bfloat16), "seq", scatter_dimension=1, tiled=True
        ).astype(jnp.float32),
        lax.psum_scatter(
            down_local.astype(jnp.bfloat16), "seq", scatter_dimension=1, tiled=True
        ).astype(jnp.float32),
    )
    dgate = jnp.einsum(
        "tkd,td->tk", chosen, grad_rows, precision=PRECISE, preferred_element_type=jnp.float32
    )
    route_onehot = (
        route_rows[:, :, None] == jnp.arange(experts, dtype=jnp.int32)[None, None, :]
    ).astype(jnp.float32)
    grad_prob = jnp.einsum("tk,tke->te", dgate, route_onehot, precision=PRECISE)
    grad_logits = gate_probs * (grad_prob - jnp.sum(gate_probs * grad_prob, axis=-1, keepdims=True))
    router_float = w_r.astype(jnp.float32)
    grad_h2 = jnp.sum(grad_chosen.astype(jnp.float32), axis=1) + jnp.dot(
        grad_logits, router_float.T, precision=PRECISE
    )
    router_local = jnp.dot(h2_low.astype(jnp.float32).T, grad_logits, precision=PRECISE)
    grad_mid_norm, ffn_gain_local = norm_two_pull(grad_h2)
    grad_mid = grad_rows + grad_mid_norm
    grad_attn = grad_mid.astype(jnp.bfloat16)
    output_local = jnp.einsum("tc,td->cd", attended, grad_attn, preferred_element_type=jnp.float32)
    grad_attended = jnp.einsum(
        "td,cd->tc", grad_attn, w_o, preferred_element_type=jnp.float32
    ).astype(jnp.bfloat16)
    grad_heads = lax.all_to_all(
        grad_attended, "seq", split_axis=1, concat_axis=0, tiled=True
    ).reshape(seq_len, heads_here, head_dim)
    dq_heads, dk_heads, dv_heads = attend_back(queries, keys, values, grad_heads, doc_row, log_sums)
    flat_width = heads_here * head_dim
    dq_rot, dk_rot, dv_low = (
        lax.all_to_all(
            dq_heads.reshape(seq_len, flat_width).astype(jnp.bfloat16),
            "seq",
            split_axis=0,
            concat_axis=1,
            tiled=True,
        ),
        lax.all_to_all(
            dk_heads.reshape(seq_len, flat_width).astype(jnp.bfloat16),
            "seq",
            split_axis=0,
            concat_axis=1,
            tiled=True,
        ),
        lax.all_to_all(
            dv_heads.reshape(seq_len, flat_width).astype(jnp.bfloat16),
            "seq",
            split_axis=0,
            concat_axis=1,
            tiled=True,
        ),
    )
    dq_raw, query_gain_local = query_pull(dq_rot.astype(jnp.float32))
    dk_raw, key_gain_local = key_pull(dk_rot.astype(jnp.float32))
    dq_low = dq_raw.astype(jnp.bfloat16)
    dk_low = dk_raw.astype(jnp.bfloat16)
    query_local = jnp.einsum("tc,td->cd", h1_low, dq_low, preferred_element_type=jnp.float32)
    key_local = jnp.einsum("tc,td->cd", h1_low, dk_low, preferred_element_type=jnp.float32)
    value_local = jnp.einsum("tc,td->cd", h1_low, dv_low, preferred_element_type=jnp.float32)
    grad_h1 = jnp.einsum("td,cd->tc", dq_low, w_q, preferred_element_type=jnp.float32)
    grad_h1 = grad_h1 + jnp.einsum("td,cd->tc", dk_low, w_k, preferred_element_type=jnp.float32)
    grad_h1 = grad_h1 + jnp.einsum("td,cd->tc", dv_low, w_v, preferred_element_type=jnp.float32)
    grad_in_norm, attn_gain_local = norm_one_pull(grad_h1)
    input_grad = grad_mid + grad_in_norm
    summed = (
        lax.psum_scatter(query_local, ("seq", "fsdp"), scatter_dimension=0, tiled=True),
        lax.psum_scatter(key_local, ("seq", "fsdp"), scatter_dimension=0, tiled=True),
        lax.psum_scatter(value_local, ("seq", "fsdp"), scatter_dimension=0, tiled=True),
        lax.psum_scatter(output_local, ("seq", "fsdp"), scatter_dimension=0, tiled=True),
        lax.psum_scatter(router_local, ("seq", "fsdp"), scatter_dimension=0, tiled=True),
        lax.psum_scatter(attn_gain_local, ("seq", "fsdp"), scatter_dimension=0, tiled=True),
        lax.psum_scatter(ffn_gain_local, ("seq", "fsdp"), scatter_dimension=0, tiled=True),
        lax.psum_scatter(query_gain_local, ("seq", "fsdp"), scatter_dimension=0, tiled=True),
        lax.psum_scatter(key_gain_local, ("seq", "fsdp"), scatter_dimension=0, tiled=True),
    )
    return (
        result.astype(jnp.bfloat16)[None],
        input_grad[None],
        summed[0],
        summed[1],
        summed[2],
        summed[3],
        summed[4],
        summed[5],
        summed[6],
        summed[7],
        summed[8],
        g_gate,
        g_up,
        g_down,
    )


def solution(mesh):
    in_specs = (
        P("fsdp", "seq", None),
        P("fsdp", "seq", None),
        P("fsdp", None),
        P("fsdp", "seq", None),
        P(("seq", "fsdp"), None),
        P(("seq", "fsdp"), None),
        P(("seq", "fsdp"), None),
        P(("seq", "fsdp"), None),
        P(("seq", "fsdp"), None),
        P(("seq", "fsdp")),
        P(("seq", "fsdp")),
        P(("seq", "fsdp")),
        P(("seq", "fsdp")),
        P("fsdp", "seq", None),
        P("fsdp", "seq", None),
        P("fsdp", "seq", None),
    )
    out_specs = (
        P("fsdp", "seq", None),
        P("fsdp", "seq", None),
        P(("seq", "fsdp"), None),
        P(("seq", "fsdp"), None),
        P(("seq", "fsdp"), None),
        P(("seq", "fsdp"), None),
        P(("seq", "fsdp"), None),
        P(("seq", "fsdp")),
        P(("seq", "fsdp")),
        P(("seq", "fsdp")),
        P(("seq", "fsdp")),
        P("fsdp", "seq", None),
        P("fsdp", "seq", None),
        P("fsdp", "seq", None),
    )
    return jax.shard_map(
        on_device, mesh=mesh, in_specs=in_specs, out_specs=out_specs, check_vma=False
    )
```

profile of v0, /device:TPU:0, one launch (start us, length us, event | category | flops | bytes accessed | tf_op | source)
XLA Modules:
  0.0 2339.6 jit_solution(15474286081735777571)
XLA Ops:
  12.6 42.7 %all-reduce.17 = (bf16[2048]{0:T(1024)(128)(2,1)S(1)}, bf16[2048]{0:T(1024)(128)(2,1)S(1)}, bf16[2048]{0:T(1024)(128)(2,1)S(1)}, bf16[2048]{0:T(1024)(128)(2,1)}) all-reduce(bf16[2048]{0:T(1024)(128)(2,1)S(1)} %dynamic-update-slice.10, bf16[2048]{0:T(1024)(128)(2,1)S(1)} %dynamic-update-slice.11, ...), channel_id=1, replica_groups=mesh['seq'=4,'fsdp'=8] {'seq','fsdp'}, use_global_device_ids=true, to_apply=%add.8 | all-reduce | flops 8192 | bytes 32768
  57.4 34.2 %all-gather.9.cloned.1.call-done = bf16[2048,2048]{1,0:T(8,128)(2,1)} async-done(((bf16[64,2048]{1,0:T(8,128)(2,1)}), bf16[2048,2048]{1,0:T(8,128)(2,1)}) %all-gather.9.cloned.1.call-update) | async-done | bytes 8388624 | tf_op jit(solution)/shard_map/all_gather | solution.py:213
  102.9 73.9 %all-gather.11.cloned.1.call-done = bf16[2048,2048]{1,0:T(8,128)(2,1)} async-done(((bf16[64,2048]{1,0:T(8,128)(2,1)}), bf16[2048,2048]{1,0:T(8,128)(2,1)}) %all-gather.11.cloned.1.call-update) | async-done | bytes 8388624 | tf_op jit(solution)/shard_map/all_gather | solution.py:211
  185.0 70.8 %all-gather.13.cloned.1.call-done = bf16[2048,2048]{1,0:T(8,128)(2,1)} async-done(((bf16[64,2048]{1,0:T(8,128)(2,1)}), bf16[2048,2048]{1,0:T(8,128)(2,1)}) %all-gather.13.cloned.1.call-update) | async-done | bytes 8388624 | tf_op jit(solution)/shard_map/all_gather | solution.py:212
  282.8 13.0 all-to-all-done.2
  341.6 8.1 scatter_custom_fusion
  366.0 9.7 gather_fusion
  375.6 8.6 broadcast_select_fusion
  390.0 194.4 %all-to-all-done.4 = bf16[16,136,2048]{2,1,0:T(8,128)(2,1)} async-done(((bf16[16,136,2048]{2,1,0:T(8,128)(2,1)}), bf16[16,136,2048]{2,1,0:T(8,128)(2,1)}, u32[]{:S(2)}, u32[]{:S(2)}) %all-to-all-start.4) | async-done | bytes 8912928 | tf_op jit(solution)/shard_map/all_to_all | solution.py:276
  584.4 8.8 copy.103
  593.2 16.3 fusion.119
  609.5 18.8 multiply_convert_fusion.3
  628.3 13.7 convolution_convert_fusion
  641.9 26.4 %copy.104 = bf16[2,1088,2048]{2,0,1:T(2,128)(2,1)} copy(bf16[2,1088,2048]{2,1,0:T(8,128)(2,1)S(1)} %convolution_convert_fusion) | data formatting | bytes 17825792 | tf_op jit(solution)/shard_map/convert_element_type | solution.py:158
  673.7 224.5 %all-gather = bf16[32,64,16]{1,2,0:T(8,128)(2,1)S(1)} all-gather(bf16[1,64,16]{1,2,0:T(8,128)(2,1)S(1)} %bitcast.349), channel_id=1, replica_groups=mesh['seq'=4,'fsdp'=8] {'seq','fsdp'}, dimensions={0}, use_global_device_ids=true | all-gather | bytes 67584 | tf_op jit(solution)/shard_map/all_gather | solution.py:215
  898.9 11.2 gather_fusion.2
  910.7 11.1 copy.105
  921.9 21.1 gather_fusion.4
  943.0 8.9 fusion.58
  953.1 17.2 gather_fusion.3
  970.9 11.7 gather_fusion.1
  982.8 9.8 multiply_convert_fusion
  999.9 203.7 %all-to-all-done.6 = bf16[16,136,2048]{2,1,0:T(8,128)(2,1)} async-done(((bf16[16,136,2048]{2,1,0:T(8,128)(2,1)}), bf16[16,136,2048]{2,1,0:T(8,128)(2,1)}, u32[]{:S(2)}, u32[]{:S(2)}) %all-to-all-start.6) | async-done | bytes 8912928 | tf_op jit(solution)/shard_map/all_to_all | solution.py:281
  1203.6 8.9 copy.106
  1212.4 17.6 convolution_convert_fusion.1
  1230.1 21.6 multiply_convert_fusion.1
  1251.7 18.1 convolution_convert_fusion.2
  1269.8 17.7 fusion.120
  1287.5 18.7 add_convert_fusion
  1306.1 17.3 copy.107
  1328.5 18.0 convolution_convert_fusion.3
  1347.5 10.7 fusion.3
  1358.2 165.3 %all-to-all-done.7 = bf16[2,1088,2048]{2,0,1:T(2,128)(2,1)} async-done(((bf16[2,1088,2048]{2,0,1:T(2,128)(2,1)}), bf16[2,1088,2048]{2,0,1:T(2,128)(2,1)}, u32[]{:S(2)}, u32[]{:S(2)}) %all-to-all-start.7) | async-done | bytes 8912928 | tf_op jit(solution)/shard_map/all_to_all | solution.py:285
  1523.6 11.2 copy.108
  1534.8 21.2 gather_fusion.5
  1556.0 13.5 convert_reduce_fusion
  1577.3 8.1 fusion.71
  1597.9 24.5 %all-to-all-done.8 = bf16[256,4,512]{2,0,1:T(8,128)(2,1)S(1)} async-done(((bf16[256,4,512]{2,0,1:T(8,128)(2,1)}), bf16[256,4,512]{2,0,1:T(8,128)(2,1)S(1)}, u32[]{:S(2)}, u32[]{:S(2)}) %all-to-all-start.8) | async-done | bytes 1048608 | tf_op jit(solution)/shard_map/all_to_all | solution.py:324
  1634.9 27.2 %all_to_all.182 = bf16[4,256,512]{1,2,0:T(8,128)(2,1)S(1)} all-to-all(bf16[4,256,512]{1,2,0:T(8,128)(2,1)S(1)} %copy.129), channel_id=1, replica_groups=mesh['seq'=4,'fsdp'=8] {'seq'}, dimensions={0} | all-to-all | bytes 2097152 | tf_op jit(solution)/shard_map/all_to_all | solution.py:344
  1663.1 8.3 fusion.65
  1702.9 16.1 all-to-all-done.9
  1728.5 19.1 all-to-all-done.10
  1763.2 8.2 fusion.101
  1777.6 8.2 fusion.103
  1816.0 39.5 %all-reduce.16 = (f32[2048]{0:T(1024)S(1)}, f32[2048]{0:T(1024)S(1)}, f32[2048]{0:T(1024)S(1)}, f32[2048]{0:T(1024)S(1)}) all-reduce(f32[2048]{0:T(1024)S(1)} %get-tuple-element.85, f32[2048]{0:T(1024)S(1)} %get-tuple-element.83, f32[2048]{0:T(1024)S(1)} %get-tuple-element.81, ...), channel_id=7, replica_groups=mesh['seq'=4,'fsdp'=8] {'seq','fsdp'}, use_global_device_ids=true, to_apply=%region_28.30.clone | all-reduce | flops 8192 | bytes 65536
  1861.3 97.3 %reduce-scatter.15.cloned.1.call-done = f32[64,2048]{1,0:T(8,128)} async-done(((f32[2048,2048]{1,0:T(8,128)}), f32[64,2048]{1,0:T(8,128)}) %reduce-scatter.15.cloned.1.call-update) | async-done | bytes 524304 | tf_op jit(solution)/shard_map/reduce_scatter | solution.py:367
  1958.6 187.1 %reduce-scatter.13.cloned.1.call-done = f32[64,2048]{1,0:T(8,128)} async-done(((f32[2048,2048]{1,0:T(8,128)}), f32[64,2048]{1,0:T(8,128)}) %reduce-scatter.13.cloned.1.call-update) | async-done | bytes 524304 | tf_op jit(solution)/shard_map/reduce_scatter | solution.py:366
  2145.7 187.1 %reduce-scatter.11.cloned.1.call-done = f32[64,2048]{1,0:T(8,128)} async-done(((f32[2048,2048]{1,0:T(8,128)}), f32[64,2048]{1,0:T(8,128)}) %reduce-scatter.11.cloned.1.call-update) | async-done | bytes 524304 | tf_op jit(solution)/shard_map/reduce_scatter | solution.py:365
  (466 shorter events, 274.6 us)
Async XLA Ops:
  7.2 84.4 %all-gather.9.cloned.1.call-start = ((), (), s32[]{:S(2)}) async-start(), calls=%async_computation.20 | async-start | bytes 8650752 | tf_op jit(solution)/shard_map/all_gather | solution.py:213
  7.9 168.8 %all-gather.11.cloned.1.call-start = ((), (), s32[]{:S(2)}) async-start(), calls=%async_computation.21 | async-start | bytes 8650752 | tf_op jit(solution)/shard_map/all_gather | solution.py:211
  8.7 247.1 %all-gather.13.cloned.1.call-start = ((), (), s32[]{:S(2)}) async-start(), calls=%async_computation.22 | async-start | bytes 8650752 | tf_op jit(solution)/shard_map/all_gather | solution.py:212
  9.4 340.5 %all-gather.15.cloned.1.call-start = ((), (), s32[]{:S(2)}) async-start(), calls=%async_computation.23 | async-start | bytes 8650752 | tf_op jit(solution)/shard_map/all_gather | solution.py:214
  10.0 583.2 %all-gather.17.cloned.1.call-start = ((), (), s32[]{:S(2)}) async-start(), calls=%async_computation.24 | async-start | bytes 10485760 | tf_op jit(solution)/shard_map/all_gather | solution.py:223
  10.6 45.3 %copy-start.81 = (s32[1,256,8]{1,2,0:T(8,128)S(1)}, s32[1,256,8]{1,2,0:T(8,128)}, u32[]{:S(2)}) copy-start(s32[1,256,8]{1,2,0:T(8,128)} %param.33) | copy-start | bytes 24580
  10.6 598.9 %all-gather.19.cloned.1.call-start = ((), (), s32[]{:S(2)}) async-start(), calls=%async_computation.25 | async-start | bytes 10485760 | tf_op jit(solution)/shard_map/all_gather | solution.py:224
  11.6 85.8 %copy-start.85 = (f32[256]{0:T(256)}, f32[256]{0:T(256)S(1)}, u32[]{:S(2)}) copy-start(f32[256]{0:T(256)S(1)} %fusion.95) | copy-start | bytes 3076
  55.3 200.5 %copy-start.61 = (f32[2048]{0:T(1024)}, f32[2048]{0:T(1024)S(1)}, u32[]{:S(2)}) copy-start(f32[2048]{0:T(1024)S(1)} %convert_element_type.183) | copy-start | bytes 24580
  55.3 211.5 %copy-start.67 = (f32[2048]{0:T(1024)}, f32[2048]{0:T(1024)S(1)}, u32[]{:S(2)}) copy-start(f32[2048]{0:T(1024)S(1)} %convert_element_type.186) | copy-start | bytes 24580
  56.0 220.2 %copy-start.50 = (s32[1,256,8]{2,1,0:T(8,128)}, s32[1,256,8]{2,1,0:T(8,128)S(1)}, u32[]{:S(2)}) copy-start(s32[1,256,8]{2,1,0:T(8,128)S(1)} %copy.97) | copy-start | bytes 24580
  57.4 207.9 %copy-start.55 = (f32[256,128]{1,0:T(8,128)}, f32[256,128]{1,0:T(8,128)S(1)}, u32[]{:S(2)}) copy-start(f32[256,128]{1,0:T(8,128)S(1)} %get-tuple-element.124) | copy-start | bytes 393220
  57.4 209.2 %copy-start.57 = (f32[256,128]{1,0:T(8,128)}, f32[256,128]{1,0:T(8,128)S(1)}, u32[]{:S(2)}) copy-start(f32[256,128]{1,0:T(8,128)S(1)} %get-tuple-element.123) | copy-start | bytes 393220
  98.4 174.1 %all-to-all-start = ((bf16[256,4,512]{2,0,1:T(8,128)(2,1)}), bf16[256,4,512]{2,0,1:T(8,128)(2,1)}, u32[]{:S(2)}, u32[]{:S(2)}) async-start(bf16[256,4,512]{2,0,1:T(8,128)(2,1)} %bitcast.300), calls=%async_computation | async-start | bytes 2097152 | tf_op jit(solution)/shard_map/all_to_all | solution.py:244
  182.6 84.1 %copy-start.10 = (f32[256,2048]{1,0:T(8,128)}, f32[256,2048]{1,0:T(8,128)S(1)}, u32[]{:S(2)}) copy-start(f32[256,2048]{1,0:T(8,128)S(1)} %get-tuple-element.130) | copy-start | bytes 6291460
  272.5 23.3 all-to-all-start.2
  281.7 59.9 %copy-start.75 = (s32[2048]{0:T(1024)}, s32[2048]{0:T(1024)S(1)}, u32[]{:S(2)}) copy-start(s32[2048]{0:T(1024)S(1)} %fusion.77) | copy-start | bytes 24580
  295.8 16.9 all-to-all-start.1
  337.8 19.3 all-to-all-start.3
  341.3 22.0 copy-start.73
  349.8 25.8 %copy-start.87 = (pred[16,136]{1,0:T(8,128)(4,1)}, pred[16,136]{1,0:T(8,128)(4,1)S(1)}, u32[]{:S(2)}) copy-start(pred[16,136]{1,0:T(8,128)(4,1)S(1)} %broadcast_in_dim.151) | copy-start | bytes 6532
  384.2 200.1 %all-to-all-start.4 = ((bf16[16,136,2048]{2,1,0:T(8,128)(2,1)}), bf16[16,136,2048]{2,1,0:T(8,128)(2,1)}, u32[]{:S(2)}, u32[]{:S(2)}) async-start(bf16[16,136,2048]{2,1,0:T(8,128)(2,1)} %broadcast_select_fusion), calls=%async_computation.4 | async-start | bytes 17825792 | tf_op jit(solution)/shard_map/all_to_all | solution.py:276
  389.2 239.0 %all-gather.21.cloned.1.call-start = ((), (), s32[]{:S(2)}) async-start(), calls=%async_computation.26 | async-start | bytes 10485760 | tf_op jit(solution)/shard_map/all_gather | solution.py:225
  668.3 230.1 %copy-start.32 = (bf16[1,256,2048]{2,1,0:T(8,128)(2,1)S(1)}, bf16[1,256,2048]{2,1,0:T(8,128)(2,1)}, u32[]{:S(2)}) copy-start(bf16[1,256,2048]{2,1,0:T(8,128)(2,1)} %param.31) | copy-start | bytes 3145732
  668.3 242.4 %all-to-all-start.5 = ((bf16[2,1088,2048]{2,0,1:T(2,128)(2,1)}), bf16[2,1088,2048]{2,0,1:T(2,128)(2,1)}, u32[]{:S(2)}, u32[]{:S(2)}) async-start(bf16[2,1088,2048]{2,0,1:T(2,128)(2,1)} %copy.104), calls=%async_computation.5 | async-start | bytes 17825792 | tf_op jit(solution)/shard_map/all_to_all | solution.py:280
  910.2 32.7 %copy-start.108 = (pred[2048]{0:T(1024)(128)(4,1)}, pred[2048]{0:T(1024)(128)(4,1)S(1)}, u32[]{:S(2)}) copy-start(pred[2048]{0:T(1024)(128)(4,1)S(1)} %compare_and_fusion.1) | copy-start | bytes 6148
  921.9 21.1 copy-start.33
  953.0 44.5 %copy-start.63 = (f32[256,1,16]{0,2,1:T(8,128)}, f32[256,1,16]{0,2,1:T(8,128)S(1)}, u32[]{:S(2)}) copy-start(f32[256,1,16]{0,2,1:T(8,128)S(1)} %copy.136) | copy-start | bytes 49156
  953.1 44.5 %copy-start = (f32[256,16]{0,1:T(8,128)}, f32[256,16]{0,1:T(8,128)S(1)}, u32[]{:S(2)}) copy-start(f32[256,16]{0,1:T(8,128)S(1)} %get-tuple-element.96) | copy-start | bytes 49156
  953.1 44.5 %copy-start.102 = (f32[256]{0:T(256)}, f32[256]{0:T(256)S(1)}, u32[]{:S(2)}) copy-start(f32[256]{0:T(256)S(1)} %get-tuple-element.95) | copy-start | bytes 3076
  992.5 211.0 %all-to-all-start.6 = ((bf16[16,136,2048]{2,1,0:T(8,128)(2,1)}), bf16[16,136,2048]{2,1,0:T(8,128)(2,1)}, u32[]{:S(2)}, u32[]{:S(2)}) async-start(bf16[16,136,2048]{2,1,0:T(8,128)(2,1)} %multiply_convert_fusion), calls=%async_computation.6 | async-start | bytes 17825792 | tf_op jit(solution)/shard_map/all_to_all | solution.py:281
  997.5 788.4 %reduce-scatter.25.cloned.1.call-start = ((), (), s32[]{:S(2)}) async-start(), calls=%async_computation.34 | async-start | bytes 1081344
  999.8 787.5 %reduce-scatter.23.cloned.1.call-start = ((), (), s32[]{:S(2)}) async-start(), calls=%async_computation.33 | async-start | bytes 10485760 | tf_op jit(solution)/shard_map/reduce_scatter | solution.py:300
  1230.0 561.5 %reduce-scatter.21.cloned.1.call-start = ((), (), s32[]{:S(2)}) async-start(), calls=%async_computation.32 | async-start | bytes 10485760 | tf_op jit(solution)/shard_map/reduce_scatter | solution.py:297
  1323.4 200.2 %all-to-all-start.7 = ((bf16[2,1088,2048]{2,0,1:T(2,128)(2,1)}), bf16[2,1088,2048]{2,0,1:T(2,128)(2,1)}, u32[]{:S(2)}, u32[]{:S(2)}) async-start(bf16[2,1088,2048]{2,0,1:T(2,128)(2,1)} %copy.107), calls=%async_computation.7 | async-start | bytes 17825792 | tf_op jit(solution)/shard_map/all_to_all | solution.py:285
  1328.5 467.2 %reduce-scatter.19.cloned.1.call-start = ((), (), s32[]{:S(2)}) async-start(), calls=%async_computation.31 | async-start | bytes 10485760 | tf_op jit(solution)/shard_map/reduce_scatter | solution.py:294
  1346.6 514.8 %reduce-scatter.17.cloned.1.call-start = ((), (), s32[]{:S(2)}) async-start(), calls=%async_computation.30 | async-start | bytes 17301504 | tf_op jit(solution)/shard_map/reduce_scatter | solution.py:368
  1594.3 28.2 %all-to-all-start.8 = ((bf16[256,4,512]{2,0,1:T(8,128)(2,1)}), bf16[256,4,512]{2,0,1:T(8,128)(2,1)S(1)}, u32[]{:S(2)}, u32[]{:S(2)}) async-start(bf16[256,4,512]{2,0,1:T(8,128)(2,1)} %bitcast.297), calls=%async_computation.8 | async-start | bytes 2097152 | tf_op jit(solution)/shard_map/all_to_all | solution.py:324
  1597.8 360.8 %reduce-scatter.15.cloned.1.call-start = ((), (), s32[]{:S(2)}) async-start(), calls=%async_computation.29 | async-start | bytes 17301504 | tf_op jit(solution)/shard_map/reduce_scatter | solution.py:367
  1633.4 29.6 %copy-start.7 = (bf16[1,256,2048]{2,1,0:T(8,128)(2,1)S(1)}, bf16[1,256,2048]{2,1,0:T(8,128)(2,1)}, u32[]{:S(2)}) copy-start(bf16[1,256,2048]{2,1,0:T(8,128)(2,1)} %param.30) | copy-start | bytes 3145732
  1633.4 29.6 %copy-start.62 = (f32[2048]{0:T(1024)S(1)}, f32[2048]{0:T(1024)}, u32[]{:S(2)}) copy-start(f32[2048]{0:T(1024)} %copy-done.61) | copy-start | bytes 24580
  1633.4 29.6 %copy-start.86 = (f32[256]{0:T(256)S(1)}, f32[256]{0:T(256)}, u32[]{:S(2)}) copy-start(f32[256]{0:T(256)} %copy-done.85) | copy-start | bytes 3076
  1691.7 27.3 %all-to-all-start.9 = ((bf16[4,256,512]{1,2,0:T(8,128)(2,1)}), bf16[4,256,512]{1,2,0:T(8,128)(2,1)}, u32[]{:S(2)}, u32[]{:S(2)}) async-start(bf16[4,256,512]{1,2,0:T(8,128)(2,1)} %copy.117), calls=%async_computation.9 | async-start | bytes 2097152 | tf_op jit(solution)/shard_map/all_to_all | solution.py:330
  1719.0 28.6 %all-to-all-start.10 = ((bf16[4,256,512]{1,2,0:T(8,128)(2,1)}), bf16[4,256,512]{1,2,0:T(8,128)(2,1)}, u32[]{:S(2)}, u32[]{:S(2)}) async-start(bf16[4,256,512]{1,2,0:T(8,128)(2,1)} %copy.123), calls=%async_computation.10 | async-start | bytes 2097152 | tf_op jit(solution)/shard_map/all_to_all | solution.py:337
  1723.3 422.4 %reduce-scatter.13.cloned.1.call-start = ((), (), s32[]{:S(2)}) async-start(), calls=%async_computation.28 | async-start | bytes 17301504 | tf_op jit(solution)/shard_map/reduce_scatter | solution.py:366
  1771.5 561.4 %reduce-scatter.11.cloned.1.call-start = ((), (), s32[]{:S(2)}) async-start(), calls=%async_computation.27 | async-start | bytes 17301504 | tf_op jit(solution)/shard_map/reduce_scatter | solution.py:365
  1811.9 46.0 %copy-start.105 = (f32[256]{0:T(256)S(1)}, f32[256]{0:T(256)}, u32[]{:S(2)}) copy-start(f32[256]{0:T(256)} %copy-done.104) | copy-start | bytes 3076
  1811.9 46.0 %copy-start.16 = (f32[256,2048]{1,0:T(8,128)S(1)}, f32[256,2048]{1,0:T(8,128)}, u32[]{:S(2)}) copy-start(f32[256,2048]{1,0:T(8,128)} %copy-done.14) | copy-start | bytes 6291460
  (102 other events, 501.3 us)
Sparse Core Ops, SparseCore 0:
  11.0 80.5 all-gather.8
  94.6 82.1 all-gather.10
  179.8 75.9 all-gather.12
  258.6 80.9 all-gather.14
  341.3 86.4 all-gather.16
  429.5 87.5 all-gather.18
  519.0 87.5 all-gather.20
  1000.6 168.6 reduce-scatter.24
  1230.1 84.4 reduce-scatter.22
  1317.6 86.4 reduce-scatter.20
  1407.4 86.3 reduce-scatter.18
  1585.6 184.6 reduce-scatter.16
  1773.2 185.3 reduce-scatter.14
  1961.3 184.3 reduce-scatter.12
  2148.4 184.3 reduce-scatter.10
where the time goes:
time: 2350 us; the launch traced here: 2340 us
  waiting for transfers between devices  1300 us (55%)
  blocking collectives  334 us (14%)
  matrix products  294 us (13%)
  local copies, waits for them, and re-layouts  257 us (11%)
  other arithmetic  90.4 us (4%)
  starting transfers between devices  48.7 us (2%)
    all_gather x1, blocking collectives, on_device(): lax.all_gather(w_router, ('seq', 'fsdp'), axis=0, tiled=True)  224 us
    all_to_all x1, waiting for transfers between devices, on_device(): lax.all_to_all(grad_send, 'fsdp', split_axis=0, concat_axis=1, tiled=True)  204 us
    all_to_all x1, waiting for transfers between devices, on_device(): lax.all_to_all(send_rows, 'fsdp', split_axis=0, concat_axis=1, tiled=True)  194 us
    reduce_scatter x1, waiting for transfers between devices, on_device(): lax.psum_scatter(query_local, ('seq', 'fsdp'), scatter_dimension=0, tiled...  187 us
    reduce_scatter x1, waiting for transfers between devices, on_device(): lax.psum_scatter(key_local, ('seq', 'fsdp'), scatter_dimension=0, tiled=T...  187 us
    all_to_all x1, waiting for transfers between devices, on_device(): lax.all_to_all(grad_in_low, 'fsdp', split_axis=1, concat_axis=0, tiled=True)  165 us
    reduce_scatter x1, waiting for transfers between devices, on_device(): lax.psum_scatter(value_local, ('seq', 'fsdp'), scatter_dimension=0, tiled...  97.3 us
    unnamed x2, blocking collectives  82.2 us
  transfers between devices with their start and end apart: 26, of which 15 were waited for; matrix products, arithmetic and copies ran while one was open for 21% of the time, Pallas kernels for 0%

commit v1 on v0

v1 whole, which is shorter than its diff:
```python
from functools import partial

import jax
import jax.numpy as jnp
from jax import lax
from jax.experimental import pallas as pl
from jax.experimental.pallas import tpu as pltpu
from jax.sharding import PartitionSpec as P

CAP = 136
HEAD = 128
EPSILON = 1e-05
ROPE_BASE = 10000.0
MASKED_OUT = -1e30
ANY = pl.ANY
MESH = pl.DeviceIdType.MESH
DMA = pltpu.SemaphoreType.DMA
BF = jnp.bfloat16
F32 = jnp.float32


def remote(src, dst, send, recv, **where):
    return pltpu.make_async_remote_copy(
        src_ref=src, dst_ref=dst, send_sem=send, recv_sem=recv, device_id=where, device_id_type=MESH
    )


def greet(count, places, seq_count=1):
    i, p, sib = places
    barrier = pltpu.get_barrier_semaphore()
    pl.semaphore_signal(barrier, inc=1, device_id={"fsdp": sib}, device_id_type=MESH)
    here = lax.axis_index("seq")
    for d in range(1, seq_count):
        peer = lax.rem(here + d, seq_count)
        pl.semaphore_signal(barrier, inc=1, device_id={"seq": peer}, device_id_type=MESH)

    @pl.when(p > 0)
    def _():
        pl.semaphore_signal(barrier, inc=1, device_id={"fsdp": i - 2}, device_id_type=MESH)

    @pl.when(p < count - 1)
    def _():
        pl.semaphore_signal(barrier, inc=1, device_id={"fsdp": i + 2}, device_id_type=MESH)

    last = count - 1
    pl.semaphore_wait(barrier, seq_count + (p + last) // count + (last - p + last) // count)


def slot_of(ref, axis, index):
    return ref.at[index] if axis == 0 else ref.at[:, index]


class LineGather:
    def __init__(self, count, places, refs, axes, send_r, send_l, send_s, recv):
        self.count, self.places = count, places
        self.refs, self.axes = refs, axes
        self.sems = (send_r, send_l, send_s, recv)

    def copy(self, a, slot, kind, t, device):
        send = self.sems[kind].at[a, t]
        ref = slot_of(self.refs[a], self.axes[a], slot)
        return remote(ref, ref, send, self.sems[3].at[a, slot], fsdp=device)

    def first(self, a):
        i, p, sib = self.places

        @pl.when(p < self.count - 1)
        def _():
            self.copy(a, i, 0, 0, i + 2).start()

        @pl.when(p > 0)
        def _():
            self.copy(a, i, 1, 0, i - 2).start()

        self.copy(a, i, 2, 0, sib).start()

    def forward(self, t):
        i, p, sib = self.places
        count = self.count
        for a in range(len(self.refs)):

            @pl.when(p - t >= 0)
            def _():
                slot = i - 2 * t
                self.copy(a, slot, 0, t, sib).wait_recv()

                @pl.when(p < count - 1)
                def _():
                    self.copy(a, slot, 0, t, i + 2).start()

                self.copy(a, slot, 2, t, sib).start()

            @pl.when(p + t < count)
            def _():
                slot = i + 2 * t
                self.copy(a, slot, 1, t, sib).wait_recv()

                @pl.when(p > 0)
                def _():
                    self.copy(a, slot, 1, t, i - 2).start()

                self.copy(a, slot, 2, count + t, sib).start()

    def finish(self):
        i, p, sib = self.places
        count = self.count
        for a in range(len(self.refs)):
            for q in range(count):
                self.copy(a, 2 * q + lax.rem(sib, 2), 2, 0, sib).wait_recv()
            self.copy(a, i, 2, 0, sib).wait_send()

            @pl.when(p < count - 1)
            def _():
                self.copy(a, i, 0, 0, i + 2).wait_send()

            @pl.when(p > 0)
            def _():
                self.copy(a, i, 1, 0, i - 2).wait_send()

            for t in range(1, count):

                @pl.when(p - t >= 0)
                def _():
                    slot = i - 2 * t

                    @pl.when(p < count - 1)
                    def _():
                        self.copy(a, slot, 0, t, i + 2).wait_send()

                    self.copy(a, slot, 2, t, sib).wait_send()

                @pl.when(p + t < count)
                def _():
                    slot = i + 2 * t

                    @pl.when(p > 0)
                    def _():
                        self.copy(a, slot, 1, t, i - 2).wait_send()

                    self.copy(a, slot, 2, count + t, sib).wait_send()


def line_sems(arrays, count):
    return [DMA((arrays, count)), DMA((arrays, count)), DMA((arrays, 2 * count)), DMA((arrays, 2 * count))]


def where_am_i():
    i = lax.axis_index("fsdp")
    p = i // 2
    c = i % 2
    return i, p, 2 * p + 1 - c


def gather_kernel(count, x_ref, o_ref, hold, send_r, send_l, send_s, recv, local):
    places = where_am_i()
    i = places[0]
    take = pltpu.make_async_copy(x_ref, hold, local.at[0])
    take.start()
    greet(count, places)
    take.wait()
    put = pltpu.make_async_copy(hold, o_ref.at[i], local.at[1])
    put.start()
    put.wait()
    line = LineGather(count, places, [o_ref], [0], send_r, send_l, send_s, recv)
    line.first(0)
    for t in range(1, count):
        line.forward(t)
    line.finish()


def line_gather(block, shards, collective):
    count = shards // 2
    return pl.pallas_call(
        partial(gather_kernel, count),
        out_shape=jax.ShapeDtypeStruct((shards,) + block.shape, block.dtype),
        in_specs=[pl.BlockSpec(memory_space=ANY)],
        out_specs=pl.BlockSpec(memory_space=ANY),
        scratch_shapes=[pltpu.VMEM(block.shape, block.dtype)] + line_sems(1, count) + [DMA((2,))],
        compiler_params=pltpu.CompilerParams(collective_id=collective, has_side_effects=True),
        name="line_gather",
    )(block)


def start_kernel(count, seq_count, *refs):
    wq, wk, wv, wo, small, gains, routes = refs[:7]
    outs = refs[7:14]
    holds = refs[14:21]
    send_x, recv_x, local, send_r, send_l, send_s, recv = refs[21:]
    places = where_am_i()
    i = places[0]
    here = lax.axis_index("seq")
    width = wq.shape[1] // seq_count

    def columns(ref, peer):
        return ref.at[:, pl.ds(pl.multiple_of(peer * width, width), width)]

    own = [columns(wq, here), columns(wk, here), columns(wv, here), wo, small, gains, routes]
    for a in range(7):
        pltpu.make_async_copy(own[a], holds[a], local.at[a]).start()
    greet(count, places, seq_count)

    def piece(a, d):
        peer = lax.rem(here + d, seq_count)
        src = small if a == 4 else columns((wq, wk, wv)[a], peer)
        slot = 3 if a == 4 else a
        return remote(
            src, outs[a].at[here, i], send_x.at[slot, d - 1], recv_x.at[slot, d - 1], seq=peer
        )

    def arrived(a, d):
        origin = lax.rem(here + seq_count - d, seq_count)
        slot = 3 if a == 4 else a
        return remote(
            outs[a].at[origin, i],
            outs[a].at[origin, i],
            send_x.at[slot, d - 1],
            recv_x.at[slot, d - 1],
            seq=origin,
        )

    for a in (4, 0, 1, 2):
        for d in range(1, seq_count):
            piece(a, d).start()
    axes = [1, 1, 1, 0, 1, 0, 0]
    for a in (3, 5, 6, 4, 0, 1, 2):
        pltpu.make_async_copy(own[a], holds[a], local.at[a]).wait()
        target = outs[a].at[here, i] if axes[a] == 1 else outs[a].at[i]
        pltpu.make_async_copy(holds[a], target, local.at[a]).start()
    line = LineGather(count, places, outs, axes, send_r, send_l, send_s, recv)
    for a in (5, 6, 4, 0, 1, 2, 3):
        target = outs[a].at[here, i] if axes[a] == 1 else outs[a].at[i]
        pltpu.make_async_copy(holds[a], target, local.at[a]).wait()
        if axes[a] == 1:
            for d in range(1, seq_count):
                arrived(a, d).wait_recv()
        line.first(a)
    for t in range(1, count):
        line.forward(t)
    line.finish()
    for a in (4, 0, 1, 2):
        for d in range(1, seq_count):
            piece(a, d).wait_send()


def gather_start(arrays, seq_count, shards, collective):
    count = shards // 2
    wq, wk, wv, wo, small, gains, routes = arrays
    rows, model_width = wq.shape
    width = model_width // seq_count
    sheet = jax.ShapeDtypeStruct((seq_count, shards, rows, width), BF)
    shapes = [
        sheet,
        sheet,
        sheet,
        jax.ShapeDtypeStruct((shards,) + wo.shape, BF),
        jax.ShapeDtypeStruct((seq_count, shards) + small.shape, BF),
        jax.ShapeDtypeStruct((shards,) + gains.shape, BF),
        jax.ShapeDtypeStruct((shards,) + routes.shape, jnp.int32),
    ]
    holds = [pltpu.VMEM((rows, width), BF)] * 3 + [
        pltpu.VMEM(wo.shape, BF),
        pltpu.VMEM(small.shape, BF),
        pltpu.VMEM(gains.shape, BF),
        pltpu.VMEM(routes.shape, jnp.int32),
    ]
    return pl.pallas_call(
        partial(start_kernel, count, seq_count),
        out_shape=shapes,
        in_specs=[pl.BlockSpec(memory_space=ANY)] * 7,
        out_specs=[pl.BlockSpec(memory_space=ANY)] * 7,
        scratch_shapes=holds
        + [DMA((4, seq_count - 1)), DMA((4, seq_count - 1)), DMA((7,))]
        + line_sems(7, count),
        compiler_params=pltpu.CompilerParams(collective_id=collective, has_side_effects=True),
        name="gather_start",
    )(*arrays)


class LineScatter:
    def __init__(self, count, places, sources, axes, bufs, sems):
        self.count, self.places = count, places
        self.sources, self.axes = sources, axes
        self.own, self.sib, self.in_r, self.in_l = bufs
        self.sems = sems

    def load(self, a, q):
        i = self.places[0]
        src = slot_of(self.sources[a], self.axes[a], 2 * q + lax.rem(i, 2))
        return pltpu.make_async_copy(src, self.own[a].at[q], self.sems[6].at[a, q])

    def to_sib(self, a, q):
        sib = self.places[2]
        src = slot_of(self.sources[a], self.axes[a], 2 * q + lax.rem(sib, 2))
        return remote(src, self.sib[a].at[q], self.sems[2].at[a, q], self.sems[5].at[a, q], fsdp=sib)

    def right(self, a, q):
        i = self.places[0]
        return remote(
            self.own[a].at[q], self.in_r[a].at[q], self.sems[0].at[a, q], self.sems[3].at[a, q], fsdp=i + 2
        )

    def left(self, a, q):
        i = self.places[0]
        return remote(
            self.own[a].at[q], self.in_l[a].at[q], self.sems[1].at[a, q], self.sems[4].at[a, q], fsdp=i - 2
        )

    def order(self):
        order, low, high = [], 0, self.count - 1
        while low <= high:
            order.append(high)
            if low < high:
                order.append(low)
            low, high = low + 1, high - 1
        return order

    def begin_loads(self):
        for q in self.order():
            for a in range(len(self.sources)):
                self.load(a, q).start()

    def begin(self):
        for q in self.order():
            for a in range(len(self.sources)):
                self.to_sib(a, q).start()

    def add(self, a, q, others):
        own = self.own[a]
        lead = own.shape[1:-2]
        rows, width = own.shape[-2:]
        step = rows
        while step * width > 65536 and step % 16 == 0:
            step //= 2

        def strip(index):
            total = own[index].astype(F32) + self.sib[a][index].astype(F32)
            for other in others:
                total += other[a][index].astype(F32)
            own[index] = total.astype(own.dtype)

        def rows_of(prefix):
            if step == rows:
                strip(prefix)
                return

            @pl.loop(0, rows // step)
            def _(k):
                strip(prefix + (pl.ds(pl.multiple_of(k * step, step), step),))

        if lead:
            for b in range(lead[0]):
                rows_of((q, b))
        else:
            rows_of((q,))

    def ready(self, a, q):
        self.load(a, q).wait()
        self.to_sib(a, q).wait_recv()

    def run(self, after):
        i, p, sib = self.places
        count = self.count
        arrays = range(len(self.sources))
        for j in range(count - 1):
            q = count - 1 - j

            @pl.when(q > p)
            def _():
                for a in arrays:
                    self.ready(a, q)

                    @pl.when(p > 0)
                    def _():
                        self.right(a, q).wait_recv()
                        self.add(a, q, [self.in_r])

                    @pl.when(p == 0)
                    def _():
                        self.add(a, q, [])

                    self.right(a, q).start()

            @pl.when(j < p)
            def _():
                for a in arrays:
                    self.ready(a, j)

                    @pl.when(p < count - 1)
                    def _():
                        self.left(a, j).wait_recv()
                        self.add(a, j, [self.in_l])

                    @pl.when(p == count - 1)
                    def _():
                        self.add(a, j, [])

                    self.left(a, j).start()

        for q in range(count):

            @pl.when(q == p)
            def _():
                for a in arrays:
                    self.ready(a, q)
                    if q > 0:
                        self.right(a, q).wait_recv()
                    if q < count - 1:
                        self.left(a, q).wait_recv()
                    sides = ([self.in_r] if q > 0 else []) + ([self.in_l] if q < count - 1 else [])
                    self.add(a, q, sides)
                    after(a, q)

    def finish(self):
        i, p, sib = self.places
        for a in range(len(self.sources)):
            for q in range(self.count):
                self.to_sib(a, q).wait_send()

                @pl.when(q > p)
                def _():
                    self.right(a, q).wait_send()

                @pl.when(q < p)
                def _():
                    self.left(a, q).wait_send()


def scatter_kernel(count, x_ref, o_ref, own, sibling, in_r, in_l, s0, s1, s2, r0, r1, r2, local):
    places = where_am_i()
    line = LineScatter(
        count, places, [x_ref], [0], ([own], [sibling], [in_r], [in_l]), (s0, s1, s2, r0, r1, r2, local)
    )
    line.begin_loads()
    greet(count, places)
    line.begin()

    def after(a, q):
        out = pltpu.make_async_copy(own.at[q], o_ref, local.at[0, q])
        out.start()
        out.wait()

    line.run(after)
    line.finish()


def line_scatter(blocks, shards, collective):
    count = shards // 2
    block = blocks.shape[1:]
    return pl.pallas_call(
        partial(scatter_kernel, count),
        out_shape=jax.ShapeDtypeStruct(block, blocks.dtype),
        in_specs=[pl.BlockSpec(memory_space=ANY)],
        out_specs=pl.BlockSpec(memory_space=ANY),
        scratch_shapes=[pltpu.VMEM((count,) + block, blocks.dtype)] * 4 + [DMA((1, count))] * 7,
        compiler_params=pltpu.CompilerParams(
            collective_id=collective, has_side_effects=True, vmem_limit_bytes=48 << 20
        ),
        name="line_scatter",
    )(blocks)


def end_kernel(count, seq_count, *refs):
    sources = refs[:6]
    outs = refs[6:12]
    bufs = tuple(refs[12 + 6 * k : 18 + 6 * k] for k in range(4))
    landing = refs[36]
    sems = refs[37:44]
    send_x, recv_x, local = refs[44:]
    places = where_am_i()
    here = lax.axis_index("seq")
    width = sources[0].shape[3]
    line = LineScatter(count, places, sources, [1, 1, 1, 0, 1, 0], bufs, sems)
    line.begin_loads()
    greet(count, places, seq_count)
    line.begin()
    own = bufs[0]

    def at_home(a, block):
        if a == 4:
            return landing.at[block]
        start = pl.multiple_of(block * width, width)
        return outs[a].at[:, pl.ds(start, width)]

    def piece(a, q, d):
        peer = lax.rem(here + d, seq_count)
        slot = 3 if a == 4 else a
        return remote(
            own[a].at[q, peer], at_home(a, here), send_x.at[slot, d - 1], recv_x.at[slot, d - 1], seq=peer
        )

    def arrived(a, d):
        origin = lax.rem(here + seq_count - d, seq_count)
        slot = 3 if a == 4 else a
        return remote(
            at_home(a, origin), at_home(a, origin), send_x.at[slot, d - 1], recv_x.at[slot, d - 1], seq=origin
        )

    def after(a, q):
        if a in (3, 5):
            pltpu.make_async_copy(own[a].at[q], outs[a], local.at[a]).start()
        else:
            for d in range(1, seq_count):
                piece(a, q, d).start()
            pltpu.make_async_copy(own[a].at[q, here], at_home(a, here), local.at[a]).start()

    line.run(after)
    for q in range(count):

        @pl.when(q == places[1])
        def _():
            for a in range(6):
                if a in (3, 5):
                    pltpu.make_async_copy(own[a].at[q], outs[a], local.at[a]).wait()
                else:
                    pltpu.make_async_copy(own[a].at[q, here], at_home(a, here), local.at[a]).wait()
                    for d in range(1, seq_count):
                        piece(a, q, d).wait_send()
                        arrived(a, d).wait_recv()

    total = landing[0]
    for block in range(1, seq_count):
        total += landing[block]
    landing[0] = total
    last = pltpu.make_async_copy(landing.at[0], outs[4], local.at[4])
    last.start()
    last.wait()
    line.finish()


def scatter_end(arrays, seq_count, shards, collective):
    count = shards // 2
    gq, gk, gv, go, small, gains = arrays
    rows, width = gq.shape[2:]
    home = jax.ShapeDtypeStruct((rows, width * seq_count), BF)
    shapes = [
        home,
        home,
        home,
        jax.ShapeDtypeStruct(go.shape[1:], BF),
        jax.ShapeDtypeStruct(small.shape[2:], F32),
        jax.ShapeDtypeStruct(gains.shape[1:], F32),
    ]
    blocks = []
    for a in range(6):
        shape = arrays[a].shape
        block = (shape[0],) + shape[2:] if a in (0, 1, 2, 4) else shape[1:]
        blocks.append(pltpu.VMEM((count,) + block, arrays[a].dtype))
    return pl.pallas_call(
        partial(end_kernel, count, seq_count),
        out_shape=shapes,
        in_specs=[pl.BlockSpec(memory_space=ANY)] * 6,
        out_specs=[pl.BlockSpec(memory_space=ANY)] * 6,
        scratch_shapes=blocks * 4
        + [pltpu.VMEM((seq_count,) + small.shape[2:], F32)]
        + [DMA((6, count))] * 7
        + [DMA((4, seq_count - 1)), DMA((4, seq_count - 1)), DMA((6,))],
        compiler_params=pltpu.CompilerParams(
            collective_id=collective, has_side_effects=True, vmem_limit_bytes=56 << 20
        ),
        name="scatter_end",
    )(*arrays)


def greet_seq(seq_count):
    here = lax.axis_index("seq")
    barrier = pltpu.get_barrier_semaphore()
    for d in range(1, seq_count):
        peer = lax.rem(here + d, seq_count)
        pl.semaphore_signal(barrier, inc=1, device_id={"seq": peer}, device_id_type=MESH)
    pl.semaphore_wait(barrier, seq_count - 1)
    return here


def seq_scatter_kernel(seq_count, x_ref, o_ref, own, inbox, send, recv, local):
    take = pltpu.make_async_copy(x_ref.at[lax.axis_index("seq")], own, local)
    take.start()
    here = greet_seq(seq_count)
    copies = []
    for d in range(1, seq_count):
        peer = lax.rem(here + d, seq_count)
        copies.append(
            remote(x_ref.at[peer], inbox.at[d - 1], send.at[d - 1], recv.at[d - 1], seq=peer)
        )
    for copy in copies:
        copy.start()
    take.wait()
    for copy in copies:
        copy.wait_recv()
    rows = own.shape[0]
    step = min(32, rows)

    @pl.loop(0, rows // step)
    def _(k):
        strip = pl.ds(pl.multiple_of(k * step, step), step)
        total = own[strip, :].astype(F32)
        for d in range(seq_count - 1):
            total += inbox[d, strip, :].astype(F32)
        o_ref[strip, :] = total

    for copy in copies:
        copy.wait_send()


def seq_scatter(blocks, collective):
    seq_count = blocks.shape[0]
    block = blocks.shape[1:]
    return pl.pallas_call(
        partial(seq_scatter_kernel, seq_count),
        out_shape=jax.ShapeDtypeStruct(block, F32),
        in_specs=[pl.BlockSpec(memory_space=ANY)],
        out_specs=pl.BlockSpec(memory_space=pltpu.VMEM),
        scratch_shapes=[
            pltpu.VMEM(block, blocks.dtype),
            pltpu.VMEM((seq_count - 1,) + block, blocks.dtype),
            DMA((seq_count - 1,)),
            DMA((seq_count - 1,)),
            DMA,
        ],
        compiler_params=pltpu.CompilerParams(
            collective_id=collective, has_side_effects=True, vmem_limit_bytes=32 << 20
        ),
        name="seq_scatter",
    )(blocks)


def seq_sum_kernel(seq_count, x_ref, o_ref, inbox, send, recv):
    here = greet_seq(seq_count)
    copies = []
    for d in range(1, seq_count):
        peer = lax.rem(here + d, seq_count)
        copies.append(remote(x_ref, inbox.at[d - 1], send.at[d - 1], recv.at[d - 1], seq=peer))
    for copy in copies:
        copy.start()
    for copy in copies:
        copy.wait_recv()
    total = x_ref[...]
    for d in range(seq_count - 1):
        total += inbox[d]
    o_ref[...] = total
    for copy in copies:
        copy.wait_send()


def seq_sum(value, seq_count, collective):
    return pl.pallas_call(
        partial(seq_sum_kernel, seq_count),
        out_shape=jax.ShapeDtypeStruct(value.shape, F32),
        in_specs=[pl.BlockSpec(memory_space=pltpu.VMEM)],
        out_specs=pl.BlockSpec(memory_space=pltpu.VMEM),
        scratch_shapes=[
            pltpu.VMEM((seq_count - 1,) + value.shape, F32),
            DMA((seq_count - 1,)),
            DMA((seq_count - 1,)),
        ],
        compiler_params=pltpu.CompilerParams(collective_id=collective, has_side_effects=True),
        name="seq_sum",
    )(value)


def seq_gather_kernel(seq_count, x_ref, o_ref, hold, send, recv, local):
    take = pltpu.make_async_copy(x_ref, hold, local)
    take.start()
    here = greet_seq(seq_count)
    for d in range(1, seq_count):
        peer = lax.rem(here + d, seq_count)
        remote(x_ref, o_ref.at[here], send.at[d - 1], recv.at[d - 1], seq=peer).start()
    take.wait()
    put = pltpu.make_async_copy(hold, o_ref.at[here], local)
    put.start()
    put.wait()
    for d in range(1, seq_count):
        origin = lax.rem(here + seq_count - d, seq_count)
        remote(x_ref, o_ref.at[origin], send.at[d - 1], recv.at[d - 1], seq=origin).wait()


def seq_gather(block, seq_count, collective):
    return pl.pallas_call(
        partial(seq_gather_kernel, seq_count),
        out_shape=jax.ShapeDtypeStruct((seq_count,) + block.shape, block.dtype),
        in_specs=[pl.BlockSpec(memory_space=ANY)],
        out_specs=pl.BlockSpec(memory_space=ANY),
        scratch_shapes=[
            pltpu.VMEM(block.shape, block.dtype),
            DMA((seq_count - 1,)),
            DMA((seq_count - 1,)),
            DMA,
        ],
        compiler_params=pltpu.CompilerParams(collective_id=collective, has_side_effects=True),
        name="seq_gather",
    )(block)


def half_sign(shape):
    lane = lax.broadcasted_iota(jnp.int32, shape, 1)
    return jnp.where(lane < shape[1] // 2, -1.0, 1.0)


def turn(value):
    return pltpu.roll(value, value.shape[1] // 2, 1)


def block_probs(q_rows, keys, doc_col, doc_row, start, scale_by):
    end = keys.shape[0]
    scores = (
        lax.dot_general(q_rows, keys, (((1,), (1,)), ((), ())), preferred_element_type=F32) * scale_by
    )
    shape = scores.shape
    query_pos = start + lax.broadcasted_iota(jnp.int32, shape, 0)
    key_pos = lax.broadcasted_iota(jnp.int32, shape, 1)
    allowed = (doc_col == doc_row) & (key_pos <= query_pos)
    scores = jnp.where(allowed, scores, MASKED_OUT)
    weights = jnp.exp(scores - jnp.max(scores, axis=-1, keepdims=True))
    return weights * (1.0 / jnp.sum(weights, axis=-1, keepdims=True))


def attend_kernel(
    row_block, q_raw, k_raw, v_ref, rq, rk, gq, gk, cos, sin, doc_col, doc_row, o_ref, q_out, k_out
):
    seq_len = q_raw.shape[0]
    sign = half_sign(cos.shape)

    def rotated(raw, scale, gain):
        value = raw[...] * scale[...] * gain[...]
        return (value * cos[...] + turn(value) * (sin[...] * sign)).astype(BF)

    q_out[...] = rotated(q_raw, rq, gq)
    k_out[...] = rotated(k_raw, rk, gk)
    scale_by = HEAD ** (-0.5)
    for start in range(0, seq_len, row_block):
        end = start + row_block
        probs = block_probs(
            q_out[start:end, :], k_out[:end, :], doc_col[start:end, :], doc_row[:, :end], start, scale_by
        )
        o_ref[start:end, :] = jnp.dot(
            probs.astype(BF), v_ref[:end, :], preferred_element_type=F32
        ).astype(BF)


def attend(q_raw, k_raw, values, rq, rk, gq, gk, cos, sin, doc_col, doc_row):
    seq_len, width = q_raw.shape
    head = pl.BlockSpec((seq_len, HEAD), lambda h: (0, h))
    gain = pl.BlockSpec((1, HEAD), lambda h: (0, h))

    def whole(x):
        return pl.BlockSpec(x.shape, lambda h: (0, 0))

    out = jax.ShapeDtypeStruct((seq_len, width), BF)
    return pl.pallas_call(
        partial(attend_kernel, 256),
        grid=(width // HEAD,),
        out_shape=[out, out, out],
        in_specs=[head, head, head, whole(rq), whole(rk), gain, gain, whole(cos), whole(sin)]
        + [whole(doc_col), whole(doc_row)],
        out_specs=[head, head, head],
        compiler_params=pltpu.CompilerParams(vmem_limit_bytes=48 << 20),
        name="attend",
    )(q_raw, k_raw, values, rq, rk, gq, gk, cos, sin, doc_col, doc_row)


def attend_back_kernel(
    row_block,
    q_low,
    k_low,
    v_ref,
    do_ref,
    q_raw,
    k_raw,
    rq,
    rk,
    gq,
    gk,
    cos,
    sin,
    doc_col,
    doc_row,
    uq_ref,
    uk_ref,
    dv_ref,
    dots,
    gain_q,
    gain_k,
    dq_acc,
    dk_acc,
    dv_acc,
):
    seq_len = q_low.shape[0]
    scale_by = HEAD ** (-0.5)
    dk_acc[...] = jnp.zeros_like(dk_acc)
    dv_acc[...] = jnp.zeros_like(dv_acc)
    for start in range(0, seq_len, row_block):
        end = start + row_block
        rows = slice(start, end)
        probs = block_probs(
            q_low[rows, :], k_low[:end, :], doc_col[rows, :], doc_row[:, :end], start, scale_by
        )
        grad_rows = do_ref[rows, :]
        grad_probs = lax.dot_general(
            grad_rows, v_ref[:end, :], (((1,), (1,)), ((), ())), preferred_element_type=F32
        )
        centre = jnp.sum(probs * grad_probs, axis=-1, keepdims=True)
        grad_scores = (probs * (grad_probs - centre)).astype(BF)
        dq_acc[rows, :] = jnp.dot(grad_scores, k_low[:end, :], preferred_element_type=F32)
        over_rows = (((0,), (0,)), ((), ()))
        dk_acc[:end, :] += lax.dot_general(
            grad_scores, q_low[rows, :], over_rows, preferred_element_type=F32
        )
        dv_acc[:end, :] += lax.dot_general(
            probs.astype(BF), grad_rows, over_rows, preferred_element_type=F32
        )
    dv_ref[...] = dv_acc[...].astype(BF)
    sign = half_sign(cos.shape)

    def unrotated(acc, raw, scale, gain, u_ref, gain_ref, lane):
        low = (acc[...] * scale_by).astype(BF).astype(F32)
        back = low * cos[...] - turn(low * sin[...]) * sign
        gain_ref[...] = jnp.sum(back * raw[...] * scale[...], axis=0, keepdims=True)
        u = back * gain[...]
        u_ref[...] = u
        dot = jnp.sum(u * raw[...], axis=1, keepdims=True)

        @pl.when(pl.program_id(0) == 0)
        def _():
            dots[:, lane : lane + 1] = dot

        @pl.when(pl.program_id(0) > 0)
        def _():
            dots[:, lane : lane + 1] += dot

    unrotated(dq_acc, q_raw, rq, gq, uq_ref, gain_q, 0)
    unrotated(dk_acc, k_raw, rk, gk, uk_ref, gain_k, 1)


def attend_back(q_low, k_low, values, d_heads, q_raw, k_raw, rq, rk, gq, gk, cos, sin, doc_col, doc_row):
    seq_len, width = q_raw.shape
    head = pl.BlockSpec((seq_len, HEAD), lambda h: (0, h))
    gain = pl.BlockSpec((1, HEAD), lambda h: (0, h))

    def whole(x):
        return pl.BlockSpec(x.shape, lambda h: (0, 0))

    wide = jax.ShapeDtypeStruct((seq_len, width), F32)
    row = jax.ShapeDtypeStruct((1, width), F32)
    return pl.pallas_call(
        partial(attend_back_kernel, 256),
        grid=(width // HEAD,),
        out_shape=[
            wide,
            wide,
            jax.ShapeDtypeStruct((seq_len, width), BF),
            jax.ShapeDtypeStruct((seq_len, 2), F32),
            row,
            row,
        ],
        in_specs=[head] * 6
        + [whole(rq), whole(rk), gain, gain, whole(cos), whole(sin), whole(doc_col), whole(doc_row)],
        out_specs=[head, head, head, pl.BlockSpec((seq_len, 2), lambda h: (0, 0)), gain, gain],
        scratch_shapes=[pltpu.VMEM((seq_len, HEAD), F32)] * 3,
        compiler_params=pltpu.CompilerParams(vmem_limit_bytes=56 << 20),
        name="attend_back",
    )(q_low, k_low, values, d_heads, q_raw, k_raw, rq, rk, gq, gk, cos, sin, doc_col, doc_row)


def rope_tables(positions, head_dim):
    half_dim = head_dim // 2
    inverse = ROPE_BASE ** (-(jnp.arange(half_dim, dtype=F32) * 2.0 / head_dim))
    angles = positions.astype(F32)[:, None] * inverse[None, :]
    angles = jnp.concatenate([angles, angles], axis=-1)
    return (jnp.cos(angles), jnp.sin(angles))


def dot(left, right, sides=(1, 0), out=F32):
    return lax.dot_general(
        left, right, (((sides[0],), (sides[1],)), ((), ())), preferred_element_type=F32
    ).astype(out)


def inverse_rms(rows):
    return lax.rsqrt(jnp.mean(rows * rows, axis=-1, keepdims=True) + EPSILON)


def on_device(
    inputs,
    out_grad,
    doc_ids,
    routes,
    w_query,
    w_key,
    w_value,
    w_output,
    w_router,
    attn_gain,
    ffn_gain,
    query_gain,
    key_gain,
    w_gate,
    w_up,
    w_down,
):
    seq_count = lax.axis_size("seq")
    shards = lax.axis_size("fsdp")
    tok_rows, model_width = inputs.shape[1:]
    seq_len = tok_rows * seq_count
    rows = w_query.shape[0]
    width = model_width // seq_count
    local_experts = w_gate.shape[0]
    experts = w_router.shape[1]
    top_k = routes.shape[2]
    lanes = 128

    small = jnp.concatenate(
        [
            w_router,
            attn_gain[:, None],
            ffn_gain[:, None],
            jnp.zeros((rows, lanes - experts - 2), BF),
        ],
        axis=1,
    )
    gains = jnp.pad(jnp.stack([query_gain, key_gain]), ((0, 14), (0, lanes - rows)))
    routes_flat = routes.reshape(tok_rows * top_k // lanes, lanes)
    wq, wk, wv, wo, small_all, gains_all, routes_all = gather_start(
        (w_query, w_key, w_value, w_output, small, gains, routes_flat), seq_count, shards, 0
    )
    x_all = lax.all_gather(inputs[0], "seq", axis=0, tiled=True)
    full_gate = lax.all_gather(w_gate, "seq", axis=1, tiled=True)
    full_up = lax.all_gather(w_up, "seq", axis=1, tiled=True)
    full_down = lax.all_gather(w_down, "seq", axis=1, tiled=True)
    dy_all = lax.all_gather(out_grad[0], "fsdp", axis=0, tiled=False)

    wq = wq.reshape(model_width, width)
    wk = wk.reshape(model_width, width)
    wv = wv.reshape(model_width, width)
    wo = wo.reshape(width, model_width)
    small_all = small_all.reshape(model_width, lanes)
    w_r = small_all[:, :experts]
    gain_a = small_all[:, experts].astype(F32)
    gain_f = small_all[:, experts + 1].astype(F32)
    gq = gains_all[:, 0, :rows].reshape(1, width).astype(F32)
    gk = gains_all[:, 1, :rows].reshape(1, width).astype(F32)

    x_float = x_all.astype(F32)
    h1 = (x_float * inverse_rms(x_float) * gain_a).astype(BF)
    q_raw = dot(h1, wq)
    k_raw = dot(h1, wk)
    values = dot(h1, wv, out=BF)
    squares = jnp.stack([jnp.sum(q_raw * q_raw, axis=1), jnp.sum(k_raw * k_raw, axis=1)])
    squares = seq_sum(squares, seq_count, 1)
    scales = lax.rsqrt(squares / model_width + EPSILON)
    rq, rk = scales[0][:, None], scales[1][:, None]
    cos, sin = rope_tables(jnp.arange(seq_len, dtype=jnp.int32), HEAD)
    doc_row = doc_ids
    doc_col = doc_ids.reshape(seq_len, 1)
    attended, q_low, k_low = attend(q_raw, k_raw, values, rq, rk, gq, gk, cos, sin, doc_col, doc_row)
    projected = dot(attended, wo, out=BF).reshape(seq_count, tok_rows, model_width)
    rows_in = inputs[0].astype(F32)
    grad_rows = out_grad[0].astype(F32)
    x_mid = rows_in + seq_scatter(projected, 2)
    scale_f = inverse_rms(x_mid)
    h2 = (x_mid * scale_f * gain_f).astype(BF)

    h2_all = line_gather(h2, shards, 3)
    count = shards * tok_rows
    h2_flat = h2_all.reshape(count, model_width)
    logits = dot(h2_flat, w_r)
    shifted = jnp.exp(logits - jnp.max(logits, axis=-1, keepdims=True))
    gate_probs = shifted / jnp.sum(shifted, axis=-1, keepdims=True)
    routes_all = routes_all.reshape(shards, tok_rows, top_k)
    first_expert = lax.axis_index("fsdp") * local_experts
    expert_ids = jnp.arange(experts, dtype=jnp.int32)
    slots = jnp.arange(CAP, dtype=jnp.int32)

    out_parts = 0.0
    grad_parts = 0.0
    grad_probs = 0.0
    g_gate, g_up, g_down = [], [], []
    for e in range(local_experts):
        expert = first_expert + e
        is_expert = (expert_ids == expert).astype(F32)
        chosen = jnp.any(routes_all == expert, axis=2)
        place = jnp.cumsum(chosen.astype(jnp.int32), axis=1) - 1
        pick = (place[:, None, :] == slots[None, :, None]) & chosen[:, None, :]
        pick_low = pick.astype(BF)
        gate_rows = jnp.sum(gate_probs * is_expert, axis=1).reshape(shards, 1, tok_rows)
        gate_slots = jnp.sum(jnp.where(pick, gate_rows, 0.0), axis=2).reshape(shards * CAP, 1)

        def dispatch(blocks):
            picked = jnp.einsum("jct,jtd->jcd", pick_low, blocks, preferred_element_type=F32)
            return picked.astype(BF).reshape(shards * CAP, model_width)

        def collect(slot_rows):
            blocks = slot_rows.reshape(shards, CAP, model_width)
            return jnp.einsum("jct,jcd->jtd", pick_low, blocks, preferred_element_type=F32)

        expert_in = dispatch(h2_all)
        gate_h = dot(expert_in, full_gate[e])
        up_h = dot(expert_in, full_up[e])
        sigmoid = 1.0 / (1.0 + jnp.exp(-gate_h))
        silu = gate_h * sigmoid
        act = silu * up_h
        act_gated = (act * gate_slots).astype(BF)
        expert_out = dot(act_gated, full_down[e], out=BF)
        out_parts = out_parts + collect(expert_out)

        grad_slots = dispatch(dy_all)
        grad_act = dot(grad_slots, full_down[e], (1, 1))
        g_down.append(dot(act_gated, grad_slots, (0, 0), BF))
        grad_gate_slots = jnp.sum(act * grad_act, axis=1).reshape(shards, CAP, 1)
        grad_act = grad_act * gate_slots
        d_gate = (grad_act * up_h * sigmoid * (1.0 + gate_h * (1.0 - sigmoid))).astype(BF)
        d_up = (grad_act * silu).astype(BF)
        g_gate.append(dot(expert_in, d_gate, (0, 0), BF))
        g_up.append(dot(expert_in, d_up, (0, 0), BF))
        grad_in = (dot(d_gate, full_gate[e], (1, 1)) + dot(d_up, full_up[e], (1, 1))).astype(BF)
        grad_parts = grad_parts + collect(grad_in)
        grad_gates = jnp.sum(jnp.where(pick, grad_gate_slots, 0.0), axis=1).reshape(count, 1)
        grad_probs = grad_probs + grad_gates * is_expert

    grad_logits = gate_probs * (grad_probs - jnp.sum(gate_probs * grad_probs, axis=-1, keepdims=True))
    grad_logits_low = grad_logits.astype(BF)
    router_back = dot(grad_logits_low, w_r, (1, 1)).reshape(shards, tok_rows, model_width)
    router_part = dot(h2_flat, grad_logits_low, (0, 0))
    result = x_mid + lax.psum_scatter(
        out_parts.astype(BF).reshape(count, model_width), "fsdp", scatter_dimension=0, tiled=True
    ).astype(F32)
    grad_h2 = line_scatter((grad_parts + router_back).astype(BF), shards, 4).astype(F32)

    def spread(parts):
        return lax.psum_scatter(jnp.stack(parts), "seq", scatter_dimension=1, tiled=True).astype(F32)

    g_down, g_gate, g_up = spread(g_down), spread(g_gate), spread(g_up)

    u_rows = gain_f * grad_h2
    grad_mid = (
        grad_rows
        + scale_f * u_rows
        - x_mid * scale_f**3 * jnp.mean(u_rows * x_mid, axis=-1, keepdims=True)
    )
    ffn_part = jnp.sum(grad_h2 * x_mid * scale_f, axis=0)

    d_attn = seq_gather(grad_mid.astype(BF), seq_count, 5).reshape(seq_len, model_width)
    d_heads = dot(d_attn, wo, (1, 1), BF)
    u_q, u_k, dv_low, dots, gain_q_part, gain_k_part = attend_back(
        q_low, k_low, values, d_heads, q_raw, k_raw, rq, rk, gq, gk, cos, sin, doc_col, doc_row
    )
    dots = seq_sum(dots.T, seq_count, 6) / model_width

    def norm_back(u, raw, scale, product):
        return (scale * u - raw * (scale**3 * product[:, None])).astype(BF)

    dq_low = norm_back(u_q, q_raw, rq, dots[0])
    dk_low = norm_back(u_k, k_raw, rk, dots[1])
    grad_h1 = dot(dq_low, wq, (1, 1)) + dot(dk_low, wk, (1, 1)) + dot(dv_low, wv, (1, 1))
    grad_h1 = seq_scatter(grad_h1.astype(BF).reshape(seq_count, tok_rows, model_width), 7)

    sheet = (seq_count, shards, rows, width)
    small_part = jnp.concatenate(
        [router_part, ffn_part[:, None], jnp.zeros((model_width, lanes - experts - 1), F32)], axis=1
    ).reshape(seq_count, shards, rows, lanes)
    gains_part = jnp.stack([gain_q_part.reshape(shards, rows), gain_k_part.reshape(shards, rows)], axis=1)
    gains_part = jnp.pad(gains_part, ((0, 0), (0, 6), (0, lanes - rows)))
    g_query, g_key, g_value, g_output, g_small, g_gains = scatter_end(
        (
            dot(h1, dq_low, (0, 0), BF).reshape(sheet),
            dot(h1, dk_low, (0, 0), BF).reshape(sheet),
            dot(h1, dv_low, (0, 0), BF).reshape(sheet),
            dot(attended, d_attn, (0, 0), BF).reshape(shards, rows, model_width),
            small_part,
            gains_part,
        ),
        seq_count,
        shards,
        8,
    )
    g_query, g_key, g_value = (g_query.astype(F32), g_key.astype(F32), g_value.astype(F32))

    scale_a = inverse_rms(rows_in)
    u_rows = gain_a * grad_h1
    input_grad = (
        grad_mid
        + scale_a * u_rows
        - rows_in * scale_a**3 * jnp.mean(u_rows * rows_in, axis=-1, keepdims=True)
    )
    pairs = (
        w_query.astype(F32) * g_query + w_key.astype(F32) * g_key + w_value.astype(F32) * g_value
    )
    g_attn_gain = jnp.sum(pairs, axis=1) / attn_gain.astype(F32)

    return (
        result.astype(BF)[None],
        input_grad[None],
        g_query,
        g_key,
        g_value,
        g_output.astype(F32),
        g_small[:, :experts],
        g_attn_gain,
        g_small[:, experts],
        g_gains[0, :rows],
        g_gains[1, :rows],
        g_gate,
        g_up,
        g_down,
    )


def solution(mesh):
    rows = P("fsdp", "seq", None)
    sheet = P(("seq", "fsdp"), None)
    line = P(("seq", "fsdp"))
    return jax.shard_map(
        on_device,
        mesh=mesh,
        in_specs=(rows, rows, P("fsdp", None), rows) + (sheet,) * 5 + (line,) * 4 + (rows,) * 3,
        out_specs=(rows, rows) + (sheet,) * 5 + (line,) * 4 + (rows,) * 3,
        check_vma=False,
    )
```

time: 2350 us -> 1140 us (0.49)
  waiting for transfers between devices: 1300 us -> 61.7 us
  Pallas kernels: 0 us -> 612 us
  blocking collectives: 334 us -> 0 us
  local copies, waits for them, and re-layouts: 257 us -> 40.7 us
  starting transfers between devices: 48.7 us -> 0.35 us
    all_to_all x11 -> x0, waiting for transfers between devices: 645 us -> none  [the longest x1 204 us: on_device(): lax.all_to_all(grad_send, 'fsdp', split_axis=0, concat_axis=1, tiled=True)]
    pallas_call x0 -> x11, Pallas kernels: none -> 612 us  [the longest x1 121 us: line_gather(): pl.pallas_call(partial(gather_kernel, count), out_shape=jax.ShapeDtypeStr...]
    reduce_scatter x7 -> x4, waiting for transfers between devices: 471 us -> 0.01 us  [the longest x3 0.01 us: spread(): lax.psum_scatter(jnp.stack(parts), 'seq', scatter_dimension=1, tiled=True)]
    all_gather x1 -> x0, blocking collectives: 224 us -> none  [on_device(): lax.all_gather(w_router, ('seq', 'fsdp'), axis=0, tiled=True)]
    all_gather x7 -> x5, waiting for transfers between devices: 179 us -> 58.5 us  [the longest x1 58.5 us: on_device(): full_down = lax.all_gather(w_down, 'seq', axis=1, tiled=True)]
    gather x9 -> x0, local copies, waits for them, and re-layouts: 92.4 us -> none  [the longest x1 21.2 us: on_device(): jnp.take(grad_back, places, axis=0).reshape(tok_rows, top_k, model_width)]
    unnamed x2 -> x0, blocking collectives: 82.2 us -> none
    convert_element_type x12 -> x2, local copies, waits for them, and re-layouts: 61.1 us -> 0.16 us  [the longest x1 0.09 us: on_device(): gq = gains_all[:, 0, :rows].reshape(1, width).astype(F32)]
  transfers between devices with their start and end apart: 26 -> 9, of which waited for: 15 -> 1; matrix products, arithmetic and copies ran while one was open for 21% -> 31% of each run, Pallas kernels for 0% -> 55%
where the time goes in v1:
time: 1140 us; the launch traced here: 1120 us
  Pallas kernels  612 us (54%)
  matrix products  300 us (26%)
  other arithmetic  87.1 us (8%)
  waiting for transfers between devices  61.7 us (5%)
  local copies, waits for them, and re-layouts  40.7 us (4%)
  between operations  15.2 us (1%)
    dot_general x33, matrix products, dot(): lax.dot_general(left, right, (((sides[0],), (sides[1],)), ((), ())), pref...  234 us
    pallas_call x1, Pallas kernels, line_gather(): pl.pallas_call(partial(gather_kernel, count), out_shape=jax.ShapeDtypeStr...  121 us
    pallas_call x2, Pallas kernels, seq_scatter(): pl.pallas_call(partial(seq_scatter_kernel, seq_count), out_shape=jax.Shap...  121 us
    pallas_call x1, Pallas kernels, line_scatter(): pl.pallas_call(partial(scatter_kernel, count), out_shape=jax.ShapeDtypeSt...  105 us
    pallas_call x1, Pallas kernels, gather_start(): pl.pallas_call(partial(start_kernel, count, seq_count), out_shape=shapes,...  84.9 us
    pallas_call x1, Pallas kernels, scatter_end(): pl.pallas_call(partial(end_kernel, count, seq_count), out_shape=shapes, i...  79.9 us
    all_gather x1, waiting for transfers between devices, on_device(): full_down = lax.all_gather(w_down, 'seq', axis=1, tiled=True)  58.5 us
    pallas_call x1, Pallas kernels, seq_gather(): pl.pallas_call(partial(seq_gather_kernel, seq_count), out_shape=jax.Shape...  47.9 us
  transfers between devices with their start and end apart: 9, of which 1 were waited for; matrix products, arithmetic and copies ran while one was open for 31% of the time, Pallas kernels for 55%

profile of v1, /device:TPU:0, one launch (start us, length us, event | category | flops | bytes accessed | tf_op | source)
XLA Modules:
  0.0 1117.1 jit_solution(10864396142004283263)
XLA Ops:
  13.3 84.9 %gather_start.1 = (bf16[4,8,64,512]{3,2,1,0:T(8,128)(2,1)}, bf16[4,8,64,512]{3,2,1,0:T(8,128)(2,1)}, bf16[4,8,64,512]{3,2,1,0:T(8,128)(2,1)}, bf16[8,64,2048]{2,...) custom-call(bf16[64,2048]{1,0:T(8,128)(2,1)} %refs_0_.1, ...), custom_call_target="tpu_custom_call" | custom-call | tf_op jit(solution)/shard_map/gather_start/pallas_call | solution.py:266
  113.6 5.7 multiply_reduce_fusion.3
  123.8 7.7 seq_sum.2
  139.3 6.2 convolution_convert_fusion.12.v_ref
  145.6 16.9 %attend.1 = (bf16[1024,512]{1,0:T(8,128)(2,1)S(1)}, bf16[1024,512]{1,0:T(8,128)(2,1)S(1)}, bf16[1024,512]{1,0:T(8,128)(2,1)S(1)}) custom-call(f32[1024,512]{1,0:T(8,128)} %copy.72.q_raw, f32[1024,512]{1,0:T(8,128)} %copy.73.k_raw, bf16[1024,512]{1,0:T(8,128)(2,1)} %convolution_convert_fusion.12.v_ref, f32[1024,1]{1,0:T(8,128)S(1)} %copy.74.rq, ...), custom_call_target="tpu_custom_call" | custom-call | tf_op jit(solution)/shard_map/attend/pallas_call | solution.py:748
  164.9 70.6 %seq_scatter.2 = f32[256,2048]{1,0:T(8,128)S(1)} custom-call(bf16[4,256,2048]{2,1,0:T(8,128)(2,1)S(1)} %bitcast.191), custom_call_target="tpu_custom_call" | custom-call | tf_op jit(solution)/shard_map/seq_scatter/pallas_call | solution.py:607
  238.4 121.0 %line_gather.1 = bf16[8,256,2048]{2,1,0:T(8,128)(2,1)} custom-call(bf16[256,2048]{1,0:T(8,128)(2,1)} %multiply_convert_fusion.6.x_ref), custom_call_target="tpu_custom_call" | custom-call | tf_op jit(solution)/shard_map/line_gather/pallas_call | solution.py:173
  359.5 6.0 fusion.87
  372.4 10.5 fusion.8
  382.9 10.8 fusion.9
  393.7 6.6 fusion.12
  400.3 6.4 fusion.13
  406.7 6.8 convolution_convert_fusion.3
  413.6 58.5 %all-gather.11.cloned.1.call-done = bf16[2,1024,2048]{2,1,0:T(8,128)(2,1)} async-done(((bf16[2,256,2048]{2,1,0:T(8,128)(2,1)}), bf16[2,1024,2048]{2,1,0:T(8,128)(2,1)}) %all-gather.11.cloned.1.call-update) | async-done | bytes 8388624 | tf_op jit(solution)/shard_map/all_gather | solution.py:927
  472.1 13.3 %multiply_reduce_fusion.1 = (f32[1088]{0:T(1024)S(1)}, f32[1088,1024]{1,0:T(8,128)}) fusion(f32[1088,1024]{1,0:T(8,128)} %fusion.9, f32[1088,1024]{1,0:T(8,128)} %fusion.8, bf16[1088,2048]{1,0:T(8,128)(2,1)} %bitcast.209, bf16[2,1024,2048]{2,1,0:T(8,128)(2,1)} %all-gather.11.cloned.1.call-done), kind=kOutput, calls=%fused_computation.18 | convolution fusion | flops 4571200512 | bytes 22024448 | tf_op jit(solution)/shard_map/dot_general | solution.py:872
  494.5 9.3 multiply_reduce_fusion
  504.8 8.2 multiply_convert_fusion
  513.0 7.3 convert_bitcast_fusion
  520.8 8.1 multiply_convert_fusion.2
  530.3 7.7 convert_bitcast_fusion.1
  538.0 7.5 pad_maximum_fusion.2
  545.6 9.7 convert_bitcast_fusion.2
  555.3 7.2 convert_bitcast_fusion.3
  562.5 7.8 pad_maximum_fusion.1
  570.4 9.9 convert_bitcast_fusion.4
  580.3 7.2 convert_bitcast_fusion.5
  587.5 7.8 pad_maximum_fusion
  595.5 12.7 %copy.86 = bf16[2048,2048]{1,0:T(8,128)(2,1)} copy(bf16[2048,2048]{0,1:T(8,128)(2,1)} %bitcast.194) | data formatting | bytes 16777216 | tf_op jit(solution)/shard_map/dot_general | solution.py:872
  608.2 8.6 fusion.56
  616.8 7.6 convolution_convert_fusion.1
  624.4 8.3 fusion.31
  638.1 12.5 %add_convert_fusion.1 = bf16[8,256,2048]{2,1,0:T(8,128)(2,1)} fusion(f32[8,256,2048]{2,1,0:T(8,128)} %fusion.31, bf16[8,136,2048]{2,1,0:T(8,128)(2,1)S(1)} %bitcast.222, s32[8,256]{1,0:T(8,128)S(1)} %add_bitcast_fusion, pred[8,256]{1,0:T(8,128)(4,1)S(1)} %reduce_or.19), kind=kOutput, calls=%fused_computation.1 | convolution fusion | flops 1149796352 | bytes 29632512 | tf_op jit(solution)/shard_map/jct,jcd->jtd/dot_general | solution.py:992
  650.6 11.5 %fusion.7 = f32[1088,2048]{1,0:T(8,128)} fusion(bf16[1088,1024]{1,0:T(8,128)(2,1)} %get-tuple-element.119, bf16[2,2048,1024]{2,1,0:T(8,128)(2,1)} %all-gather.7.cloned.1.call-done), kind=kOutput, calls=%fused_computation.46 | convolution fusion | flops 4563402752 | bytes 15335424 | tf_op jit(solution)/shard_map/dot_general | solution.py:872
  662.1 9.0 fusion.3
  671.2 8.6 fusion.28
  679.8 7.3 fusion.11
  687.1 10.2 fusion.4
  697.3 17.7 %add_convert_fusion.x_ref = bf16[8,256,2048]{2,1,0:T(8,128)(2,1)} fusion(f32[8,256,2048]{2,1,0:T(8,128)} %bitcast.195, f32[8,256,2048]{2,1,0:T(8,128)} %fusion.28, bf16[8,136,2048]{2,1,0:T(8,128)(2,1)} %bitcast.221, s32[8,256]{1,0:T(8,128)S(1)} %add_bitcast_fusion, pred[8,256]{1,0:T(8,128)(4,1)S(1)} %reduce_or.19), kind=kOutput, calls=%fused_computation | convolution fusion | flops 1153990656 | bytes 46409728 | tf_op jit(solution)/shard_map/jct,jcd->jtd/dot_general | solution.py:992
  715.1 104.8 %line_scatter.1 = bf16[256,2048]{1,0:T(8,128)(2,1)S(1)} custom-call(bf16[8,256,2048]{2,1,0:T(8,128)(2,1)} %add_convert_fusion.x_ref), custom_call_target="tpu_custom_call" | custom-call | tf_op jit(solution)/shard_map/line_scatter/pallas_call | solution.py:449
  822.2 47.9 %seq_gather.1 = bf16[4,256,2048]{2,1,0:T(8,128)(2,1)} custom-call(bf16[256,2048]{1,0:T(8,128)(2,1)} %fusion.76.x_ref), custom_call_target="tpu_custom_call" | custom-call | tf_op jit(solution)/shard_map/seq_gather/pallas_call | solution.py:677
  870.1 6.3 convolution_convert_fusion.11.do_ref
  876.3 22.5 %attend_back.1 = (f32[1024,512]{1,0:T(8,128)}, f32[1024,512]{1,0:T(8,128)}, bf16[1024,512]{1,0:T(8,128)(2,1)}, f32[1024,2]{1,0:T(8,128)}, f32[1,512]{1,0:T(1,128)}, /*index=5*/f32[1,512]{1,0:T(1,128)}) custom-call(bf16[1024,512]{1,0:T(8,128)(2,1)} %copy-done.5, bf16[1024,512]{1,0:T(8,128)(2,1)} %copy-done.6, ...), custom_call_target="tpu_custom_call" | custom-call | tf_op jit(solution)/shard_map/attend_back/pallas_call | solution.py:843
  904.9 5.9 seq_sum.3
  912.2 6.0 fusion.64
  939.1 79.9 %scatter_end.1 = (bf16[64,2048]{1,0:T(8,128)(2,1)}, bf16[64,2048]{1,0:T(8,128)(2,1)}, bf16[64,2048]{1,0:T(8,128)(2,1)}, bf16[64,2048]{1,0:T(8,128)(2,1)}, f32[64,128]{1,0:T(8,128)}, /*index=5*/f32[8,128]{1,0:T(8,128)}) custom-call(bf16[4,8,64,512]{3,2,1,0:T(8,128)(2,1)} %bitcast.229, bf16[4,8,64,512]{3,2,1,0:T(8,128)(2,1)} %bitcast.228, ...), custom_call_target="tpu_custom_call" | custom-call | tf_op jit(solution)/shard_map/scatter_end/pallas_call | solution.py:548
  1026.4 5.6 fusion.88
  1032.0 6.2 add_convert_fusion.2
  1038.3 50.1 %seq_scatter.3 = f32[256,2048]{1,0:T(8,128)S(1)} custom-call(bf16[4,256,2048]{2,1,0:T(8,128)(2,1)S(1)} %bitcast.190), custom_call_target="tpu_custom_call" | custom-call | tf_op jit(solution)/shard_map/seq_scatter/pallas_call | solution.py:607
  (312 shorter events, 123.2 us)
Async XLA Ops:
  7.2 101.8 %all-gather.15.cloned.1.call-start = ((), (), s32[]{:S(2)}) async-start(), calls=%async_computation.12 | async-start | bytes 5242880 | tf_op jit(solution)/shard_map/all_gather | solution.py:924
  8.0 364.4 %all-gather.7.cloned.1.call-start = ((), (), s32[]{:S(2)}) async-start(), calls=%async_computation.4 | async-start | bytes 10485760 | tf_op jit(solution)/shard_map/all_gather | solution.py:925
  8.7 374.1 %all-gather.9.cloned.1.call-start = ((), (), s32[]{:S(2)}) async-start(), calls=%async_computation.5 | async-start | bytes 10485760 | tf_op jit(solution)/shard_map/all_gather | solution.py:926
  9.5 397.3 %all-gather.13.cloned.1.call-start = ((), (), s32[]{:S(2)}) async-start(), calls=%async_computation.8 | async-start | bytes 9437184 | tf_op jit(solution)/shard_map/all_gather | solution.py:928
  10.0 95.7 %copy-start.7 = (s32[1,1024]{1,0:T(1,128)S(1)}, s32[1,1024]{1,0:T(1,128)}, u32[]{:S(2)}) copy-start(s32[1,1024]{1,0:T(1,128)} %doc_row.3) | copy-start | bytes 12292
  10.0 462.0 %all-gather.11.cloned.1.call-start = ((), (), s32[]{:S(2)}) async-start(), calls=%async_computation.6 | async-start | bytes 10485760 | tf_op jit(solution)/shard_map/all_gather | solution.py:927
  10.6 1082.2 %reduce-scatter.11.cloned.1.call-start = ((), (), s32[]{:S(2)}) async-start(), calls=%async_computation.11 | async-start | bytes 10485760 | tf_op jit(solution)/shard_map/reduce_scatter | solution.py:1028
  105.6 33.7 %copy-start.53 = (f32[2048,1]{0,1:T(1,128)}, f32[2048,1]{0,1:T(1,128)S(1)}, u32[]{:S(2)}) copy-start(f32[2048,1]{0,1:T(1,128)S(1)} %copy.96) | copy-start | bytes 24580
  105.7 39.8 %copy-start.8 = (f32[1,512]{1,0:T(1,128)}, f32[1,512]{1,0:T(1,128)S(1)}, u32[]{:S(2)}) copy-start(f32[1,512]{1,0:T(1,128)S(1)} %reshape.361.gq) | copy-start | bytes 6148
  105.8 39.8 %copy-start.9 = (f32[1,512]{1,0:T(1,128)}, f32[1,512]{1,0:T(1,128)S(1)}, u32[]{:S(2)}) copy-start(f32[1,512]{1,0:T(1,128)S(1)} %reshape.362.gk) | copy-start | bytes 6148
  106.0 39.5 %copy-start.2 = (s32[1024,1]{1,0:T(8,128)}, s32[1024,1]{1,0:T(8,128)S(1)}, u32[]{:S(2)}) copy-start(s32[1024,1]{1,0:T(8,128)S(1)} %copy.76.doc_col) | copy-start | bytes 12292
  106.3 130.2 %copy-start.50 = (f32[2048,1]{0,1:T(1,128)}, f32[2048,1]{0,1:T(1,128)S(1)}, u32[]{:S(2)}) copy-start(f32[2048,1]{0,1:T(1,128)S(1)} %copy.97) | copy-start | bytes 24580
  108.9 36.7 %copy-start = (f32[1024,128]{1,0:T(8,128)}, f32[1024,128]{1,0:T(8,128)S(1)}, u32[]{:S(2)}) copy-start(f32[1024,128]{1,0:T(8,128)S(1)} %get-tuple-element.125.sin) | copy-start | bytes 1572868
  108.9 36.7 %copy-start.1 = (f32[1024,128]{1,0:T(8,128)}, f32[1024,128]{1,0:T(8,128)S(1)}, u32[]{:S(2)}) copy-start(f32[1024,128]{1,0:T(8,128)S(1)} %get-tuple-element.126.cos) | copy-start | bytes 1572868
  112.4 26.9 %copy-start.62 = (f32[1024]{0:T(1024)}, f32[1024]{0:T(1024)S(1)}, u32[]{:S(2)}) copy-start(f32[1024]{0:T(1024)S(1)} %add_rsqrt_fusion.1) | copy-start | bytes 12292
  133.1 12.5 %copy-start.3 = (f32[1024,1]{1,0:T(8,128)}, f32[1024,1]{1,0:T(8,128)S(1)}, u32[]{:S(2)}) copy-start(f32[1024,1]{1,0:T(8,128)S(1)} %copy.74.rq) | copy-start | bytes 12292
  133.3 12.3 %copy-start.4 = (f32[1024,1]{1,0:T(8,128)}, f32[1024,1]{1,0:T(8,128)S(1)}, u32[]{:S(2)}) copy-start(f32[1024,1]{1,0:T(8,128)S(1)} %copy.75.rk) | copy-start | bytes 12292
  145.5 17.0 %copy-start.73 = (bf16[8,64,2048]{2,1,0:T(8,128)(2,1)S(1)}, bf16[8,64,2048]{2,1,0:T(8,128)(2,1)}, u32[]{:S(2)}) copy-start(bf16[8,64,2048]{2,1,0:T(8,128)(2,1)} %get-tuple-element.42) | copy-start | bytes 6291460
  164.9 70.6 %copy-start.17 = (bf16[1,256,2048]{2,1,0:T(8,128)(2,1)S(1)}, bf16[1,256,2048]{2,1,0:T(8,128)(2,1)}, u32[]{:S(2)}) copy-start(bf16[1,256,2048]{2,1,0:T(8,128)(2,1)} %param.16) | copy-start | bytes 3145732
  238.4 121.0 %copy-start.23 = (bf16[4,8,64,128]{3,2,1,0:T(8,128)(2,1)S(1)}, bf16[4,8,64,128]{3,2,1,0:T(8,128)(2,1)}, u32[]{:S(2)}) copy-start(bf16[4,8,64,128]{3,2,1,0:T(8,128)(2,1)} %get-tuple-element.36) | copy-start | bytes 1572868
  382.9 10.8 copy-start.69
  382.9 17.4 %slice-start.8 = ((s8[8388608]{0:T(1024)(128)(4,1)}), s8[4194304]{0:T(1024)(128)(4,1)S(1)}, s32[]{:S(2)}) async-start(s8[8388608]{0:T(1024)(128)(4,1)} %bitcast.267), calls=%async_computation.21 | async-start | bytes 8388608
  490.7 13.2 %copy-start.20 = (bf16[8,136,2048]{2,1,0:T(8,128)(2,1)}, bf16[8,136,2048]{2,1,0:T(8,128)(2,1)S(1)}, u32[]{:S(2)}) copy-start(bf16[8,136,2048]{2,1,0:T(8,128)(2,1)S(1)} %convolution_convert_fusion.2) | copy-start | bytes 13369348
  513.0 17.3 %slice-start.4 = ((s8[4456448]{0:T(1024)(128)(4,1)}), s8[262144]{0:T(1024)(128)(4,1)S(1)}, s32[]{:S(2)}) async-start(s8[4456448]{0:T(1024)(128)(4,1)} %bitcast.210), calls=%async_computation.17 | async-start | bytes 524288
  545.5 551.5 %reduce-scatter.9.cloned.1.call-start = ((), (), s32[]{:S(2)}) async-start(), calls=%async_computation.10 | async-start | bytes 10485760 | tf_op jit(solution)/shard_map/reduce_scatter | solution.py:1028
  570.3 530.8 %reduce-scatter.7.cloned.1.call-start = ((), (), s32[]{:S(2)}) async-start(), calls=%async_computation.9 | async-start | bytes 10485760 | tf_op jit(solution)/shard_map/reduce_scatter | solution.py:1028
  595.3 509.8 %reduce-scatter.5.cloned.1.call-start = ((), (), s32[]{:S(2)}) async-start(), calls=%async_computation.7 | async-start | bytes 9437184 | tf_op jit(solution)/shard_map/reduce_scatter | solution.py:1022
  595.5 12.7 %copy-start.24 = (bf16[4,8,64,128]{3,2,1,0:T(8,128)(2,1)S(1)}, bf16[4,8,64,128]{3,2,1,0:T(8,128)(2,1)}, u32[]{:S(2)}) copy-start(bf16[4,8,64,128]{3,2,1,0:T(8,128)(2,1)} %get-tuple-element.36) | copy-start | bytes 1572868
  616.8 15.9 %slice-start.10 = ((s8[8388608]{0:T(1024)(128)(4,1)}), s8[4194304]{0:T(1024)(128)(4,1)S(1)}, s32[]{:S(2)}) async-start(s8[8388608]{0:T(1024)(128)(4,1)} %bitcast.269), calls=%async_computation.23 | async-start | bytes 8388608
  650.6 11.5 %copy-start.34 = (bf16[1088,1024]{1,0:T(8,128)(2,1)S(1)}, bf16[1088,1024]{1,0:T(8,128)(2,1)}, u32[]{:S(2)}) copy-start(bf16[1088,1024]{1,0:T(8,128)(2,1)} %get-tuple-element.118) | copy-start | bytes 6684676
  650.6 29.2 %slice-start.6 = ((s8[8388608]{0:T(1024)(128)(4,1)}), s8[4194304]{0:T(1024)(128)(4,1)S(1)}, s32[]{:S(2)}) async-start(s8[8388608]{0:T(1024)(128)(4,1)} %bitcast.265), calls=%async_computation.19 | async-start | bytes 8388608
  662.1 17.7 %slice-start.7 = ((s8[8388608]{0:T(1024)(128)(4,1)}), s8[4194304]{0:T(1024)(128)(4,1)S(1)}, s32[]{:S(2)}) async-start(s8[8388608]{0:T(1024)(128)(4,1)} %bitcast.265), calls=%async_computation.20 | async-start | bytes 8388608
  715.0 104.8 %copy-start.14 = (f32[256,2048]{1,0:T(8,128)S(1)}, f32[256,2048]{1,0:T(8,128)}, u32[]{:S(2)}) copy-start(f32[256,2048]{1,0:T(8,128)} %copy-done.13) | copy-start | bytes 6291460
  715.0 104.8 %copy-start.51 = (f32[2048,1]{0,1:T(1,128)S(1)}, f32[2048,1]{0,1:T(1,128)}, u32[]{:S(2)}) copy-start(f32[2048,1]{0,1:T(1,128)} %copy-done.50) | copy-start | bytes 24580
  715.0 104.8 %copy-start.58 = (f32[256]{0:T(256)S(1)}, f32[256]{0:T(256)}, u32[]{:S(2)}) copy-start(f32[256]{0:T(256)} %copy-done.57) | copy-start | bytes 3076
  715.0 105.5 %copy-start.22 = (bf16[1,256,2048]{2,1,0:T(8,128)(2,1)S(1)}, bf16[1,256,2048]{2,1,0:T(8,128)(2,1)}, u32[]{:S(2)}) copy-start(bf16[1,256,2048]{2,1,0:T(8,128)(2,1)} %param.17) | copy-start | bytes 3145732
  715.0 105.5 %copy-start.59 = (f32[256]{0:T(256)S(1)}, f32[256]{0:T(256)}, u32[]{:S(2)}) copy-start(f32[256]{0:T(256)} %get-tuple-element.139) | copy-start | bytes 3076
  876.3 35.8 %copy-start.56 = (f32[1,1024]{1,0:T(1,128)S(1)}, f32[1,1024]{1,0:T(1,128)}, u32[]{:S(2)}) copy-start(f32[1,1024]{1,0:T(1,128)} %get-tuple-element.129) | copy-start | bytes 12292
  876.3 35.8 %copy-start.55 = (f32[1,1024]{1,0:T(1,128)S(1)}, f32[1,1024]{1,0:T(1,128)}, u32[]{:S(2)}) copy-start(f32[1,1024]{1,0:T(1,128)} %get-tuple-element.132) | copy-start | bytes 12292
  1038.2 50.3 %copy-start.52 = (f32[64,128]{1,0:T(8,128)S(1)}, f32[64,128]{1,0:T(8,128)}, u32[]{:S(2)}) copy-start(f32[64,128]{1,0:T(8,128)} %get-tuple-element.56) | copy-start | bytes 98308
  1038.2 50.9 %copy-start.44 = (bf16[64,2048]{1,0:T(8,128)(2,1)S(1)}, bf16[64,2048]{1,0:T(8,128)(2,1)}, u32[]{:S(2)}) copy-start(bf16[64,2048]{1,0:T(8,128)(2,1)} %refs_0_.1) | copy-start | bytes 786436
  1038.2 50.9 %copy-start.45 = (bf16[64,2048]{1,0:T(8,128)(2,1)S(1)}, bf16[64,2048]{1,0:T(8,128)(2,1)}, u32[]{:S(2)}) copy-start(bf16[64,2048]{1,0:T(8,128)(2,1)} %refs_1_.1) | copy-start | bytes 786436
  1038.2 50.9 %copy-start.46 = (bf16[64,2048]{1,0:T(8,128)(2,1)S(1)}, bf16[64,2048]{1,0:T(8,128)(2,1)}, u32[]{:S(2)}) copy-start(bf16[64,2048]{1,0:T(8,128)(2,1)} %refs_2_.1) | copy-start | bytes 786436
  1038.2 50.9 %copy-start.47 = (bf16[64,2048]{1,0:T(8,128)(2,1)S(1)}, bf16[64,2048]{1,0:T(8,128)(2,1)}, u32[]{:S(2)}) copy-start(bf16[64,2048]{1,0:T(8,128)(2,1)} %get-tuple-element.52) | copy-start | bytes 786436
  1038.2 50.9 %copy-start.48 = (bf16[64,2048]{1,0:T(8,128)(2,1)S(1)}, bf16[64,2048]{1,0:T(8,128)(2,1)}, u32[]{:S(2)}) copy-start(bf16[64,2048]{1,0:T(8,128)(2,1)} %get-tuple-element.53) | copy-start | bytes 786436
  1038.3 50.9 %copy-start.49 = (bf16[64,2048]{1,0:T(8,128)(2,1)S(1)}, bf16[64,2048]{1,0:T(8,128)(2,1)}, u32[]{:S(2)}) copy-start(bf16[64,2048]{1,0:T(8,128)(2,1)} %get-tuple-element.54) | copy-start | bytes 786436
  1038.3 52.3 %copy-start.68 = (bf16[64]{0:T(256)(128)(2,1)S(1)}, bf16[64]{0:T(256)(128)(2,1)}, u32[]{:S(2)}) copy-start(bf16[64]{0:T(256)(128)(2,1)} %param.25) | copy-start | bytes 388
  1038.3 52.8 %copy-start.18 = (bf16[1,256,2048]{2,1,0:T(8,128)(2,1)S(1)}, bf16[1,256,2048]{2,1,0:T(8,128)(2,1)}, u32[]{:S(2)}) copy-start(bf16[1,256,2048]{2,1,0:T(8,128)(2,1)} %param.16) | copy-start | bytes 3145732
  (47 other events, 270.7 us)
Sparse Core Ops, SparseCore 0:
  9.9 59.4 all-gather.14
  71.3 87.9 all-gather.6
  161.2 124.6 all-gather.8
  287.3 92.7 all-gather.12
  381.7 90.2 all-gather.10
  545.6 86.4 reduce-scatter.10
  635.4 86.4 reduce-scatter.8
  725.0 86.3 reduce-scatter.6
  813.8 121.6 reduce-scatter.4

commit v2 on v1

--- a/solution.py
+++ b/solution.py
@@ -461,17 +461,22 @@
 
 def end_kernel(count, seq_count, *refs):
     sources = refs[:6]
-    outs = refs[6:12]
-    bufs = tuple(refs[12 + 6 * k : 18 + 6 * k] for k in range(4))
-    landing = refs[36]
-    sems = refs[37:44]
-    send_x, recv_x, local = refs[44:]
+    rows_ref = refs[6]
+    outs = refs[7:13]
+    sum_ref = refs[13]
+    bufs = tuple(refs[14 + 6 * k : 20 + 6 * k] for k in range(4))
+    landing = refs[38]
+    sems = refs[39:46]
+    send_x, recv_x, local = refs[46:49]
+    seq = SeqScatter(seq_count, rows_ref, *refs[49:])
     places = where_am_i()
     here = lax.axis_index("seq")
     width = sources[0].shape[3]
     line = LineScatter(count, places, sources, [1, 1, 1, 0, 1, 0], bufs, sems)
     line.begin_loads()
+    seq.take.start()
     greet(count, places, seq_count)
+    seq.begin()
     line.begin()
     own = bufs[0]
 
@@ -504,6 +509,7 @@
             pltpu.make_async_copy(own[a].at[q, here], at_home(a, here), local.at[a]).start()
 
     line.run(after)
+    seq.total(sum_ref)
     for q in range(count):
 
         @pl.when(q == places[1])
@@ -525,9 +531,10 @@
     last.start()
     last.wait()
     line.finish()
-
-
-def scatter_end(arrays, seq_count, shards, collective):
+    seq.finish()
+
+
+def scatter_end(arrays, row_blocks, seq_count, shards, collective):
     count = shards // 2
     gq, gk, gv, go, small, gains = arrays
     rows, width = gq.shape[2:]
@@ -539,6 +546,7 @@
         jax.ShapeDtypeStruct(go.shape[1:], BF),
         jax.ShapeDtypeStruct(small.shape[2:], F32),
         jax.ShapeDtypeStruct(gains.shape[1:], F32),
+        jax.ShapeDtypeStruct(row_blocks.shape[1:], F32),
     ]
     blocks = []
     for a in range(6):
@@ -548,17 +556,18 @@
     return pl.pallas_call(
         partial(end_kernel, count, seq_count),
         out_shape=shapes,
-        in_specs=[pl.BlockSpec(memory_space=ANY)] * 6,
-        out_specs=[pl.BlockSpec(memory_space=ANY)] * 6,
+        in_specs=[pl.BlockSpec(memory_space=ANY)] * 7,
+        out_specs=[pl.BlockSpec(memory_space=ANY)] * 6 + [pl.BlockSpec(memory_space=pltpu.VMEM)],
         scratch_shapes=blocks * 4
         + [pltpu.VMEM((seq_count,) + small.shape[2:], F32)]
         + [DMA((6, count))] * 7
-        + [DMA((4, seq_count - 1)), DMA((4, seq_count - 1)), DMA((6,))],
+        + [DMA((4, seq_count - 1)), DMA((4, seq_count - 1)), DMA((6,))]
+        + seq_scatter_scratch(row_blocks.shape[1:], row_blocks.dtype, seq_count),
         compiler_params=pltpu.CompilerParams(
             collective_id=collective, has_side_effects=True, vmem_limit_bytes=56 << 20
         ),
         name="scatter_end",
-    )(*arrays)
+    )(*arrays, row_blocks)
 
 
 def greet_seq(seq_count):
@@ -571,56 +580,98 @@
     return here
 
 
-def seq_scatter_kernel(seq_count, x_ref, o_ref, own, inbox, send, recv, local):
-    take = pltpu.make_async_copy(x_ref.at[lax.axis_index("seq")], own, local)
+class SeqScatter:
+    def __init__(self, seq_count, x_ref, own, inbox, send, recv, local):
+        here = lax.axis_index("seq")
+        self.own, self.inbox, self.count = own, inbox, seq_count
+        self.take = pltpu.make_async_copy(x_ref.at[here], own, local)
+        self.copies = []
+        for d in range(1, seq_count):
+            peer = lax.rem(here + d, seq_count)
+            self.copies.append(
+                remote(x_ref.at[peer], inbox.at[d - 1], send.at[d - 1], recv.at[d - 1], seq=peer)
+            )
+
+    def begin(self):
+        for copy in self.copies:
+            copy.start()
+
+    def total(self, o_ref):
+        self.take.wait()
+        for copy in self.copies:
+            copy.wait_recv()
+        rows = self.own.shape[0]
+        step = min(32, rows)
+
+        @pl.loop(0, rows // step)
+        def _(k):
+            strip = pl.ds(pl.multiple_of(k * step, step), step)
+            total = self.own[strip, :].astype(F32)
+            for d in range(self.count - 1):
+                total += self.inbox[d, strip, :].astype(F32)
+            o_ref[strip, :] = total
+
+    def finish(self):
+        for copy in self.copies:
+            copy.wait_send()
+
+
+def seq_scatter_scratch(block, dtype, seq_count):
+    return [
+        pltpu.VMEM(block, dtype),
+        pltpu.VMEM((seq_count - 1,) + block, dtype),
+        DMA((seq_count - 1,)),
+        DMA((seq_count - 1,)),
+        DMA,
+    ]
+
+
+def middle_kernel(
+    count, seq_count, x_ref, dy_ref, o_ref, all_ref, own, inbox, xs, xr, xl, hold, s0, s1, s2, recv, local
+):
+    places = where_am_i()
+    i = places[0]
+    seq = SeqScatter(seq_count, x_ref, own, inbox, xs, xr, xl)
+    seq.take.start()
+    take = pltpu.make_async_copy(dy_ref, hold, local.at[0])
     take.start()
-    here = greet_seq(seq_count)
-    copies = []
-    for d in range(1, seq_count):
-        peer = lax.rem(here + d, seq_count)
-        copies.append(
-            remote(x_ref.at[peer], inbox.at[d - 1], send.at[d - 1], recv.at[d - 1], seq=peer)
-        )
-    for copy in copies:
-        copy.start()
+    greet(count, places, seq_count)
+    seq.begin()
     take.wait()
-    for copy in copies:
-        copy.wait_recv()
-    rows = own.shape[0]
-    step = min(32, rows)
-
-    @pl.loop(0, rows // step)
-    def _(k):
-        strip = pl.ds(pl.multiple_of(k * step, step), step)
-        total = own[strip, :].astype(F32)
-        for d in range(seq_count - 1):
-            total += inbox[d, strip, :].astype(F32)
-        o_ref[strip, :] = total
-
-    for copy in copies:
-        copy.wait_send()
-
-
-def seq_scatter(blocks, collective):
+    put = pltpu.make_async_copy(hold, all_ref.at[i], local.at[1])
+    put.start()
+    put.wait()
+    line = LineGather(count, places, [all_ref], [0], s0, s1, s2, recv)
+    line.first(0)
+    for t in range(1, count):
+        line.forward(t)
+        if t == 1:
+            seq.total(o_ref)
+    line.finish()
+    seq.finish()
+
+
+def middle(blocks, dy, shards, collective):
+    count = shards // 2
     seq_count = blocks.shape[0]
     block = blocks.shape[1:]
     return pl.pallas_call(
-        partial(seq_scatter_kernel, seq_count),
-        out_shape=jax.ShapeDtypeStruct(block, F32),
-        in_specs=[pl.BlockSpec(memory_space=ANY)],
-        out_specs=pl.BlockSpec(memory_space=pltpu.VMEM),
-        scratch_shapes=[
-            pltpu.VMEM(block, blocks.dtype),
-            pltpu.VMEM((seq_count - 1,) + block, blocks.dtype),
-            DMA((seq_count - 1,)),
-            DMA((seq_count - 1,)),
-            DMA,
+        partial(middle_kernel, count, seq_count),
+        out_shape=[
+            jax.ShapeDtypeStruct(block, F32),
+            jax.ShapeDtypeStruct((shards,) + dy.shape, dy.dtype),
         ],
+        in_specs=[pl.BlockSpec(memory_space=ANY)] * 2,
+        out_specs=[pl.BlockSpec(memory_space=pltpu.VMEM), pl.BlockSpec(memory_space=ANY)],
+        scratch_shapes=seq_scatter_scratch(block, blocks.dtype, seq_count)
+        + [pltpu.VMEM(dy.shape, dy.dtype)]
+        + line_sems(1, count)
+        + [DMA((2,))],
         compiler_params=pltpu.CompilerParams(
             collective_id=collective, has_side_effects=True, vmem_limit_bytes=32 << 20
         ),
-        name="seq_scatter",
-    )(blocks)
+        name="middle",
+    )(blocks, dy)
 
 
 def seq_sum_kernel(seq_count, x_ref, o_ref, inbox, send, recv):
@@ -657,37 +708,61 @@
     )(value)
 
 
-def seq_gather_kernel(seq_count, x_ref, o_ref, hold, send, recv, local):
-    take = pltpu.make_async_copy(x_ref, hold, local)
+def turn_kernel(
+    count, seq_count, x_ref, parts_ref, o_ref, sum_ref, hold, send, recv, one, own, sib, in_r, in_l, *sems
+):
+    places = where_am_i()
+    here = lax.axis_index("seq")
+    line = LineScatter(count, places, [parts_ref], [0], ([own], [sib], [in_r], [in_l]), sems)
+    line.begin_loads()
+    take = pltpu.make_async_copy(x_ref, hold, one)
     take.start()
-    here = greet_seq(seq_count)
+    greet(count, places, seq_count)
     for d in range(1, seq_count):
         peer = lax.rem(here + d, seq_count)
         remote(x_ref, o_ref.at[here], send.at[d - 1], recv.at[d - 1], seq=peer).start()
+    line.begin()
     take.wait()
-    put = pltpu.make_async_copy(hold, o_ref.at[here], local)
+    put = pltpu.make_async_copy(hold, o_ref.at[here], one)
     put.start()
+
+    def after(a, q):
+        out = pltpu.make_async_copy(own.at[q], sum_ref, sems[6].at[0, q])
+        out.start()
+        out.wait()
+
+    line.run(after)
     put.wait()
     for d in range(1, seq_count):
         origin = lax.rem(here + seq_count - d, seq_count)
         remote(x_ref, o_ref.at[origin], send.at[d - 1], recv.at[d - 1], seq=origin).wait()
-
-
-def seq_gather(block, seq_count, collective):
+    line.finish()
+
+
+def turn_back(block, parts, seq_count, shards, collective):
+    count = shards // 2
+    part = parts.shape[1:]
     return pl.pallas_call(
-        partial(seq_gather_kernel, seq_count),
-        out_shape=jax.ShapeDtypeStruct((seq_count,) + block.shape, block.dtype),
-        in_specs=[pl.BlockSpec(memory_space=ANY)],
-        out_specs=pl.BlockSpec(memory_space=ANY),
+        partial(turn_kernel, count, seq_count),
+        out_shape=[
+            jax.ShapeDtypeStruct((seq_count,) + block.shape, block.dtype),
+            jax.ShapeDtypeStruct(part, parts.dtype),
+        ],
+        in_specs=[pl.BlockSpec(memory_space=ANY)] * 2,
+        out_specs=[pl.BlockSpec(memory_space=ANY)] * 2,
         scratch_shapes=[
             pltpu.VMEM(block.shape, block.dtype),
             DMA((seq_count - 1,)),
             DMA((seq_count - 1,)),
             DMA,
-        ],
-        compiler_params=pltpu.CompilerParams(collective_id=collective, has_side_effects=True),
-        name="seq_gather",
-    )(block)
+        ]
+        + [pltpu.VMEM((count,) + part, parts.dtype)] * 4
+        + [DMA((1, count))] * 7,
+        compiler_params=pltpu.CompilerParams(
+            collective_id=collective, has_side_effects=True, vmem_limit_bytes=48 << 20
+        ),
+        name="turn_back",
+    )(block, parts)
 
 
 def half_sign(shape):
@@ -860,6 +935,373 @@
     )(q_low, k_low, values, d_heads, q_raw, k_raw, rq, rk, gq, gk, cos, sin, doc_col, doc_row)
 
 
+def chunk_order(k, p, count):
+    near = jnp.minimum(p, count - 1 - p)
+    step = (k + 1) // 2
+    both = jnp.where(k % 2 == 1, p - step, p + step)
+    return jnp.where(k <= 2 * near, both, jnp.where(p < count - 1 - p, k, count - 1 - k))
+
+
+def experts_in_kernel(
+    count,
+    cap,
+    h2_ref,
+    dy_ref,
+    targets,
+    router_t,
+    wg_ref,
+    wu_ref,
+    h2_out,
+    x_out,
+    y_out,
+    act_out,
+    by_up_out,
+    by_gate_out,
+    gate_slots,
+    probs_out,
+    h2,
+    wg,
+    wu,
+    dy,
+    xs,
+    ys,
+    acts,
+    by_up,
+    by_gate,
+    s0,
+    s1,
+    s2,
+    recv,
+    w_sem,
+    dy_sem,
+    h_sem,
+    out_sem,
+):
+    places = where_am_i()
+    i, p, sib = places
+    local_experts, model_width, hidden = wg_ref.shape
+    tokens = h2_ref.shape[0]
+    experts = router_t.shape[0]
+    own_in = pltpu.make_async_copy(h2_ref, h2.at[i], h_sem.at[0])
+    own_in.start()
+
+    def fetch(q, buf):
+        src = dy_ref.at[pl.ds(2 * q, 2)]
+        return pltpu.make_async_copy(src, dy.at[buf], dy_sem.at[buf])
+
+    fetch(p, 0).start()
+    for e in range(local_experts):
+        pltpu.make_async_copy(wg_ref.at[e], wg.at[e], w_sem.at[0, e]).start()
+        pltpu.make_async_copy(wu_ref.at[e], wu.at[e], w_sem.at[1, e]).start()
+    greet(count, places)
+    own_in.wait()
+    line = LineGather(count, places, [h2], [0], s0, s1, s2, recv)
+    line.first(0)
+    staged = ((xs, x_out), (ys, y_out), (acts, act_out), (by_up, by_up_out), (by_gate, by_gate_out))
+
+    def store(n, e, q):
+        return pltpu.make_async_copy(staged[n][0].at[e], staged[n][1].at[e, q], out_sem.at[n, e])
+
+    def keep(q):
+        src = h2.at[pl.ds(2 * q, 2)]
+        return pltpu.make_async_copy(src, h2_out.at[pl.ds(2 * q, 2)], h_sem.at[1])
+
+    slot_rows = lax.broadcasted_iota(jnp.int32, (local_experts * cap, tokens), 0)
+    expert_rows = lax.broadcasted_iota(jnp.int32, (experts, tokens), 0)
+
+    @pl.loop(0, count)
+    def _(k):
+        q = chunk_order(k, p, count)
+        buf = k % 2
+
+        @pl.when(k > 0)
+        def _():
+            line.forward(k)
+
+        line.copy(0, 2 * q + lax.rem(sib, 2), 2, 0, sib).wait_recv()
+        fetch(q, buf).wait()
+
+        @pl.when(k + 1 < count)
+        def _():
+            fetch(chunk_order(k + 1, p, count), 1 - buf).start()
+
+        @pl.when(k > 0)
+        def _():
+            for n in range(5):
+                for e in range(local_experts):
+                    store(n, e, q).wait()
+            keep(q).wait()
+
+        keep(q).start()
+        picks = []
+        for j in range(2):
+            slot = 2 * q + j
+            tokens_j = h2[slot]
+            logits = lax.dot_general(
+                router_t[...], tokens_j, (((1,), (1,)), ((), ())), preferred_element_type=F32
+            )
+            shifted = jnp.exp(logits - jnp.max(logits, axis=0, keepdims=True))
+            probs = shifted / jnp.sum(shifted, axis=0, keepdims=True)
+            probs_out[slot] = probs
+            pick = None
+            for e in range(local_experts):
+                mask = slot_rows == targets[slot, e : e + 1, :]
+                gate = jnp.sum(
+                    jnp.where(expert_rows == i * local_experts + e, probs, 0.0), axis=0, keepdims=True
+                )
+                part = slice(e * cap, (e + 1) * cap)
+                gate_slots[e, q, j * cap : (j + 1) * cap, :] = jnp.sum(
+                    jnp.where(mask[part], gate, 0.0), axis=1, keepdims=True
+                )
+                pick = mask if pick is None else pick | mask
+            picks.append(jnp.where(pick, 1.0, 0.0).astype(BF))
+
+        block = 512
+
+        @pl.loop(0, model_width // block)
+        def _(n):
+            cols = pl.ds(pl.multiple_of(n * block, block), block)
+            for source, target in ((0, xs), (1, ys)):
+                got = []
+                for j in range(2):
+                    rows = h2[2 * q + j, :, cols] if source == 0 else dy[buf, j, :, cols]
+                    got.append(jnp.dot(picks[j], rows, preferred_element_type=F32))
+                for e in range(local_experts):
+                    part = slice(e * cap, (e + 1) * cap)
+                    target[e, :, cols] = jnp.concatenate([got[0][part], got[1][part]], axis=0).astype(BF)
+
+        for e in range(local_experts):
+            store(0, e, q).start()
+            store(1, e, q).start()
+
+            @pl.when(k == 0)
+            def _():
+                pltpu.make_async_copy(wg_ref.at[e], wg.at[e], w_sem.at[0, e]).wait()
+                pltpu.make_async_copy(wu_ref.at[e], wu.at[e], w_sem.at[1, e]).wait()
+
+            wide = 256
+
+            @pl.loop(0, hidden // wide)
+            def _(n):
+                cols = pl.ds(pl.multiple_of(n * wide, wide), wide)
+                gate = jnp.dot(xs[e], wg[e, :, cols], preferred_element_type=F32)
+                up = jnp.dot(xs[e], wu[e, :, cols], preferred_element_type=F32)
+                sigmoid = 1.0 / (1.0 + jnp.exp(-gate))
+                silu = gate * sigmoid
+                acts[e, :, cols] = (silu * up).astype(BF)
+                by_up[e, :, cols] = silu.astype(BF)
+                by_gate[e, :, cols] = (up * sigmoid * (1.0 + gate * (1.0 - sigmoid))).astype(BF)
+
+            for n in (2, 3, 4):
+                store(n, e, q).start()
+
+    for n in range(5):
+        for e in range(local_experts):
+            store(n, e, 0).wait()
+    keep(0).wait()
+    sends_done(line)
+
+
+def sends_done(line):
+    i, p, sib = line.places
+    count = line.count
+    line.copy(0, i, 2, 0, sib).wait_send()
+
+    @pl.when(p < count - 1)
+    def _():
+        line.copy(0, i, 0, 0, i + 2).wait_send()
+
+    @pl.when(p > 0)
+    def _():
+        line.copy(0, i, 1, 0, i - 2).wait_send()
+
+    for t in range(1, count):
+
+        @pl.when(p - t >= 0)
+        def _():
+            slot = i - 2 * t
+
+            @pl.when(p < count - 1)
+            def _():
+                line.copy(0, slot, 0, t, i + 2).wait_send()
+
+            line.copy(0, slot, 2, t, sib).wait_send()
+
+        @pl.when(p + t < count)
+        def _():
+            slot = i + 2 * t
+
+            @pl.when(p > 0)
+            def _():
+                line.copy(0, slot, 1, t, i - 2).wait_send()
+
+            line.copy(0, slot, 2, count + t, sib).wait_send()
+
+
+def experts_in(h2, dy_all, targets, router_t, w_gate, w_up, collective):
+    shards, tokens, model_width = dy_all.shape
+    local_experts, _, hidden = w_gate.shape
+    experts = router_t.shape[0]
+    count = shards // 2
+    wide = jax.ShapeDtypeStruct((local_experts, count, 2 * CAP, model_width), BF)
+    thin = jax.ShapeDtypeStruct((local_experts, count, 2 * CAP, hidden), BF)
+    anywhere = pl.BlockSpec(memory_space=ANY)
+    vmem = pl.BlockSpec(memory_space=pltpu.VMEM)
+    return pl.pallas_call(
+        partial(experts_in_kernel, count, CAP),
+        out_shape=[
+            jax.ShapeDtypeStruct((shards, tokens, model_width), BF),
+            wide,
+            wide,
+            thin,
+            thin,
+            thin,
+            jax.ShapeDtypeStruct((local_experts, count, 2 * CAP, 1), F32),
+            jax.ShapeDtypeStruct((shards, experts, tokens), F32),
+        ],
+        in_specs=[anywhere, anywhere, vmem, vmem, anywhere, anywhere],
+        out_specs=[anywhere] * 6 + [vmem, vmem],
+        scratch_shapes=[
+            pltpu.VMEM((shards, tokens, model_width), BF),
+            pltpu.VMEM(w_gate.shape, BF),
+            pltpu.VMEM(w_up.shape, BF),
+            pltpu.VMEM((2, 2, tokens, model_width), BF),
+        ]
+        + [pltpu.VMEM((local_experts, 2 * CAP, model_width), BF)] * 2
+        + [pltpu.VMEM((local_experts, 2 * CAP, hidden), BF)] * 3
+        + line_sems(1, count)
+        + [DMA((2, local_experts)), DMA((2,)), DMA((2,)), DMA((5, local_experts))],
+        compiler_params=pltpu.CompilerParams(
+            collective_id=collective, has_side_effects=True, vmem_limit_bytes=60 << 20
+        ),
+        name="experts_in",
+    )(h2, dy_all, targets, router_t, w_gate, w_up)
+
+
+def experts_out_kernel(
+    cap,
+    y_ref,
+    act_ref,
+    by_up_ref,
+    by_gate_ref,
+    gate_slots,
+    targets,
+    targets_t,
+    probs_ref,
+    router_t,
+    wg,
+    wu,
+    wd,
+    gated_ref,
+    d_gate_ref,
+    d_up_ref,
+    out_ref,
+    back_ref,
+    logit_ref,
+):
+    local_experts, hidden, model_width = wd.shape
+    tokens = targets.shape[2]
+    experts = router_t.shape[0]
+    first = lax.axis_index("fsdp") * local_experts
+    over_lanes = (((1,), (1,)), ((), ()))
+    over_rows = (((0,), (0,)), ((), ()))
+    dots = []
+    for e in range(local_experts):
+        wide = 256
+
+        def step(n, dot):
+            cols = pl.ds(pl.multiple_of(n * wide, wide), wide)
+            grad_act = lax.dot_general(
+                y_ref[e, 0], wd[e, cols, :], over_lanes, preferred_element_type=F32
+            )
+            act = act_ref[e, 0, :, cols].astype(F32)
+            gate = gate_slots[e, 0]
+            dot = dot + jnp.sum(act * grad_act, axis=1, keepdims=True)
+            grad_act = grad_act * gate
+            gated_ref[e, 0, :, cols] = (act * gate).astype(BF)
+            d_up_ref[e, 0, :, cols] = (grad_act * by_up_ref[e, 0, :, cols].astype(F32)).astype(BF)
+            d_gate_ref[e, 0, :, cols] = (grad_act * by_gate_ref[e, 0, :, cols].astype(F32)).astype(BF)
+            return dot
+
+        dots.append(lax.fori_loop(0, hidden // wide, step, jnp.zeros((2 * cap, 1), F32)))
+
+    slot_rows = lax.broadcasted_iota(jnp.int32, (local_experts * cap, tokens), 0)
+    slot_lanes = lax.broadcasted_iota(jnp.int32, (tokens, local_experts * cap), 1)
+    expert_rows = lax.broadcasted_iota(jnp.int32, (experts, tokens), 0)
+    picks, logits_low = [], []
+    for j in range(2):
+        grad_probs = jnp.zeros((experts, tokens), F32)
+        pick = None
+        for e in range(local_experts):
+            part = slice(e * cap, (e + 1) * cap)
+            mask = (slot_rows == targets[j, e : e + 1, :])[part]
+            row = jnp.sum(jnp.where(mask, dots[e][j * cap : (j + 1) * cap], 0.0), axis=0, keepdims=True)
+            grad_probs = jnp.where(expert_rows == first + e, row, grad_probs)
+            hit = slot_lanes == targets_t[j, :, e : e + 1]
+            pick = hit if pick is None else pick | hit
+        probs = probs_ref[j]
+        grad_logits = probs * (grad_probs - jnp.sum(probs * grad_probs, axis=0, keepdims=True))
+        logit_ref[j] = grad_logits.astype(BF)
+        picks.append(jnp.where(pick, 1.0, 0.0).astype(BF))
+        logits_low.append(grad_logits.T.astype(BF))
+
+    block = 512
+
+    @pl.loop(0, model_width // block)
+    def _(n):
+        cols = pl.ds(pl.multiple_of(n * block, block), block)
+        results, grads = [], []
+        for e in range(local_experts):
+            results.append(jnp.dot(gated_ref[e, 0], wd[e, :, cols], preferred_element_type=F32))
+            grads.append(
+                lax.dot_general(d_gate_ref[e, 0], wg[e, cols, :], over_lanes, preferred_element_type=F32)
+                + lax.dot_general(d_up_ref[e, 0], wu[e, cols, :], over_lanes, preferred_element_type=F32)
+            )
+        for j in range(2):
+            part = slice(j * cap, (j + 1) * cap)
+            mine = jnp.concatenate([value[part] for value in results], axis=0).astype(BF)
+            back = jnp.concatenate([value[part] for value in grads], axis=0).astype(BF)
+            out_ref[j, :, cols] = jnp.dot(picks[j], mine, preferred_element_type=F32).astype(BF)
+            back_ref[j, :, cols] = (
+                jnp.dot(picks[j], back, preferred_element_type=F32)
+                + jnp.dot(logits_low[j], router_t[:, cols], preferred_element_type=F32)
+            ).astype(BF)
+
+
+def experts_out(
+    grads, act, by_up, by_gate, gate_slots, targets, targets_t, probs, router_t, w_gate, w_up, w_down
+):
+    local_experts, count, slots, model_width = grads.shape
+    hidden = act.shape[3]
+    shards, experts, tokens = probs.shape
+
+    def chunk(x):
+        return pl.BlockSpec((x.shape[0], 1) + x.shape[2:], lambda q: (0, q, 0, 0))
+
+    def pair(x):
+        return pl.BlockSpec((2,) + x.shape[1:], lambda q: (q, 0, 0))
+
+    def fixed(x):
+        return pl.BlockSpec(
+            x.shape, lambda q: (0,) * len(x.shape), pipeline_mode=pl.Buffered(1)
+        )
+
+    thin = jax.ShapeDtypeStruct(act.shape, BF)
+    full = jax.ShapeDtypeStruct((shards, tokens, model_width), BF)
+    logit = jax.ShapeDtypeStruct(probs.shape, BF)
+    return pl.pallas_call(
+        partial(experts_out_kernel, CAP),
+        grid=(count,),
+        out_shape=[thin, thin, thin, full, full, logit],
+        in_specs=[chunk(grads), chunk(act), chunk(by_up), chunk(by_gate), chunk(gate_slots)]
+        + [pair(targets), pair(targets_t), pair(probs)]
+        + [fixed(router_t), fixed(w_gate), fixed(w_up), fixed(w_down)],
+        out_specs=[chunk(act)] * 3 + [pair(full)] * 2 + [pair(logit)],
+        compiler_params=pltpu.CompilerParams(vmem_limit_bytes=63 << 20),
+        name="experts_out",
+    )(grads, act, by_up, by_gate, gate_slots, targets, targets_t, probs, router_t, w_gate, w_up, w_down)
+
+
 def rope_tables(positions, head_dim):
     half_dim = head_dim // 2
     inverse = ROPE_BASE ** (-(jnp.arange(half_dim, dtype=F32) * 2.0 / head_dim))
@@ -925,7 +1367,6 @@
     full_gate = lax.all_gather(w_gate, "seq", axis=1, tiled=True)
     full_up = lax.all_gather(w_up, "seq", axis=1, tiled=True)
     full_down = lax.all_gather(w_down, "seq", axis=1, tiled=True)
-    dy_all = lax.all_gather(out_grad[0], "fsdp", axis=0, tiled=False)
 
     wq = wq.reshape(model_width, width)
     wk = wk.reshape(model_width, width)
@@ -954,81 +1395,48 @@
     projected = dot(attended, wo, out=BF).reshape(seq_count, tok_rows, model_width)
     rows_in = inputs[0].astype(F32)
     grad_rows = out_grad[0].astype(F32)
-    x_mid = rows_in + seq_scatter(projected, 2)
+    summed, dy_all = middle(projected, out_grad[0], shards, 2)
+    x_mid = rows_in + summed
     scale_f = inverse_rms(x_mid)
     h2 = (x_mid * scale_f * gain_f).astype(BF)
 
-    h2_all = line_gather(h2, shards, 3)
-    count = shards * tok_rows
-    h2_flat = h2_all.reshape(count, model_width)
-    logits = dot(h2_flat, w_r)
-    shifted = jnp.exp(logits - jnp.max(logits, axis=-1, keepdims=True))
-    gate_probs = shifted / jnp.sum(shifted, axis=-1, keepdims=True)
     routes_all = routes_all.reshape(shards, tok_rows, top_k)
-    first_expert = lax.axis_index("fsdp") * local_experts
-    expert_ids = jnp.arange(experts, dtype=jnp.int32)
-    slots = jnp.arange(CAP, dtype=jnp.int32)
-
-    out_parts = 0.0
-    grad_parts = 0.0
-    grad_probs = 0.0
-    g_gate, g_up, g_down = [], [], []
-    for e in range(local_experts):
-        expert = first_expert + e
-        is_expert = (expert_ids == expert).astype(F32)
-        chosen = jnp.any(routes_all == expert, axis=2)
-        place = jnp.cumsum(chosen.astype(jnp.int32), axis=1) - 1
-        pick = (place[:, None, :] == slots[None, :, None]) & chosen[:, None, :]
-        pick_low = pick.astype(BF)
-        gate_rows = jnp.sum(gate_probs * is_expert, axis=1).reshape(shards, 1, tok_rows)
-        gate_slots = jnp.sum(jnp.where(pick, gate_rows, 0.0), axis=2).reshape(shards * CAP, 1)
-
-        def dispatch(blocks):
-            picked = jnp.einsum("jct,jtd->jcd", pick_low, blocks, preferred_element_type=F32)
-            return picked.astype(BF).reshape(shards * CAP, model_width)
-
-        def collect(slot_rows):
-            blocks = slot_rows.reshape(shards, CAP, model_width)
-            return jnp.einsum("jct,jcd->jtd", pick_low, blocks, preferred_element_type=F32)
-
-        expert_in = dispatch(h2_all)
-        gate_h = dot(expert_in, full_gate[e])
-        up_h = dot(expert_in, full_up[e])
-        sigmoid = 1.0 / (1.0 + jnp.exp(-gate_h))
-        silu = gate_h * sigmoid
-        act = silu * up_h
-        act_gated = (act * gate_slots).astype(BF)
-        expert_out = dot(act_gated, full_down[e], out=BF)
-        out_parts = out_parts + collect(expert_out)
-
-        grad_slots = dispatch(dy_all)
-        grad_act = dot(grad_slots, full_down[e], (1, 1))
-        g_down.append(dot(act_gated, grad_slots, (0, 0), BF))
-        grad_gate_slots = jnp.sum(act * grad_act, axis=1).reshape(shards, CAP, 1)
-        grad_act = grad_act * gate_slots
-        d_gate = (grad_act * up_h * sigmoid * (1.0 + gate_h * (1.0 - sigmoid))).astype(BF)
-        d_up = (grad_act * silu).astype(BF)
-        g_gate.append(dot(expert_in, d_gate, (0, 0), BF))
-        g_up.append(dot(expert_in, d_up, (0, 0), BF))
-        grad_in = (dot(d_gate, full_gate[e], (1, 1)) + dot(d_up, full_up[e], (1, 1))).astype(BF)
-        grad_parts = grad_parts + collect(grad_in)
-        grad_gates = jnp.sum(jnp.where(pick, grad_gate_slots, 0.0), axis=1).reshape(count, 1)
-        grad_probs = grad_probs + grad_gates * is_expert
-
-    grad_logits = gate_probs * (grad_probs - jnp.sum(gate_probs * grad_probs, axis=-1, keepdims=True))
-    grad_logits_low = grad_logits.astype(BF)
-    router_back = dot(grad_logits_low, w_r, (1, 1)).reshape(shards, tok_rows, model_width)
-    router_part = dot(h2_flat, grad_logits_low, (0, 0))
-    result = x_mid + lax.psum_scatter(
-        out_parts.astype(BF).reshape(count, model_width), "fsdp", scatter_dimension=0, tiled=True
-    ).astype(F32)
-    grad_h2 = line_scatter((grad_parts + router_back).astype(BF), shards, 4).astype(F32)
-
-    def spread(parts):
-        return lax.psum_scatter(jnp.stack(parts), "seq", scatter_dimension=1, tiled=True).astype(F32)
-
-    g_down, g_gate, g_up = spread(g_down), spread(g_gate), spread(g_up)
-
+    local_ids = lax.axis_index("fsdp") * local_experts + jnp.arange(local_experts, dtype=jnp.int32)
+    chosen = jnp.any(routes_all[:, None] == local_ids[None, :, None, None], axis=3)
+    slot = jnp.cumsum(chosen.astype(jnp.int32), axis=2) - 1
+    slot = slot + CAP * jnp.arange(local_experts, dtype=jnp.int32)[None, :, None]
+    targets = jnp.where(chosen, slot, -1)
+    targets_t = jnp.swapaxes(targets, 1, 2)
+    router_t = w_r.T
+    h2_all, expert_in, grad_slots, act, by_up, by_gate, gate_slots, gate_probs = experts_in(
+        h2, dy_all, targets, router_t, full_gate, full_up, 3
+    )
+    gated, d_gate, d_up, out_parts, grad_parts, grad_logits = experts_out(
+        grad_slots,
+        act,
+        by_up,
+        by_gate,
+        gate_slots,
+        targets,
+        targets_t,
+        gate_probs,
+        router_t,
+        full_gate,
+        full_up,
+        full_down,
+    )
+    router_part = jnp.einsum("jet,jtd->de", grad_logits, h2_all, preferred_element_type=F32)
+
+    def outer(left, right):
+        return jnp.einsum("ejra,ejrb->eab", left, right, preferred_element_type=F32).astype(BF)
+
+    def spread(part):
+        return lax.psum_scatter(part, "seq", scatter_dimension=1, tiled=True).astype(F32)
+
+    g_down = spread(outer(gated, grad_slots))
+    g_gate = spread(outer(expert_in, d_gate))
+    g_up = spread(outer(expert_in, d_up))
+    grad_h2 = line_scatter(grad_parts, shards, 4).astype(F32)
     u_rows = gain_f * grad_h2
     grad_mid = (
         grad_rows
@@ -1037,7 +1445,9 @@
     )
     ffn_part = jnp.sum(grad_h2 * x_mid * scale_f, axis=0)
 
-    d_attn = seq_gather(grad_mid.astype(BF), seq_count, 5).reshape(seq_len, model_width)
+    d_attn, out_sum = turn_back(grad_mid.astype(BF), out_parts, seq_count, shards, 5)
+    d_attn = d_attn.reshape(seq_len, model_width)
+    result = x_mid + out_sum.astype(F32)
     d_heads = dot(d_attn, wo, (1, 1), BF)
     u_q, u_k, dv_low, dots, gain_q_part, gain_k_part = attend_back(
         q_low, k_low, values, d_heads, q_raw, k_raw, rq, rk, gq, gk, cos, sin, doc_col, doc_row
@@ -1050,7 +1460,7 @@
     dq_low = norm_back(u_q, q_raw, rq, dots[0])
     dk_low = norm_back(u_k, k_raw, rk, dots[1])
     grad_h1 = dot(dq_low, wq, (1, 1)) + dot(dk_low, wk, (1, 1)) + dot(dv_low, wv, (1, 1))
-    grad_h1 = seq_scatter(grad_h1.astype(BF).reshape(seq_count, tok_rows, model_width), 7)
+    grad_h1 = grad_h1.astype(BF).reshape(seq_count, tok_rows, model_width)
 
     sheet = (seq_count, shards, rows, width)
     small_part = jnp.concatenate(
@@ -1058,7 +1468,7 @@
     ).reshape(seq_count, shards, rows, lanes)
     gains_part = jnp.stack([gain_q_part.reshape(shards, rows), gain_k_part.reshape(shards, rows)], axis=1)
     gains_part = jnp.pad(gains_part, ((0, 0), (0, 6), (0, lanes - rows)))
-    g_query, g_key, g_value, g_output, g_small, g_gains = scatter_end(
+    g_query, g_key, g_value, g_output, g_small, g_gains, grad_h1 = scatter_end(
         (
             dot(h1, dq_low, (0, 0), BF).reshape(sheet),
             dot(h1, dk_low, (0, 0), BF).reshape(sheet),
@@ -1067,6 +1477,7 @@
             small_part,
             gains_part,
         ),
+        grad_h1,
         seq_count,
         shards,
         8,

time: 1140 us -> 935 us (0.82)
  matrix products: 300 us -> 119 us
  Pallas kernels: 612 us -> 690 us
  other arithmetic: 87.1 us -> 41.3 us
  waiting for transfers between devices: 61.7 us -> 21.9 us
  local copies, waits for them, and re-layouts: 40.7 us -> 28.5 us
    dot_general x33 -> x12, matrix products: 234 us -> 59.2 us  [dot(): lax.dot_general(left, right, (((sides[0],), (sides[1],)), ((), ())), pref...]
    pallas_call x4, Pallas kernels: 290 us -> 367 us  [the longest x1 105 us: turn_back(): pl.pallas_call(partial(turn_kernel, count, seq_count), out_shape=[jax.Sha...]
    all_gather x1, waiting for transfers between devices: 58.5 us -> 0.02 us  [on_device(): full_down = lax.all_gather(w_down, 'seq', axis=1, tiled=True)]
    another operation x7 -> x2, other arithmetic: 24.5 us -> 1.37 us  [the longest x3 23.1 us: spread(): jnp.stack(parts)]
    all_gather x1, waiting for transfers between devices: 0.01 us -> 19.2 us  [on_device(): full_up = lax.all_gather(w_up, 'seq', axis=1, tiled=True)]
    convert_element_type x8 -> x4, other arithmetic: 28.5 us -> 12.3 us  [the longest x3 12.3 us: spread(): lax.psum_scatter(part, 'seq', scatter_dimension=1, tiled=True).astype(F32)]
    dot_general x3 -> x2, local copies, waits for them, and re-layouts: 18.7 us -> 5.76 us  [dot(): lax.dot_general(left, right, (((sides[0],), (sides[1],)), ((), ())), pref...]
    dot_general x8 -> x4, matrix products: 65.6 us -> 59.5 us  [the longest x3 53.2 us: outer(): jnp.einsum('ejra,ejrb->eab', left, right, preferred_element_type=F32)]
  transfers between devices with their start and end apart: 9 -> 7, of which waited for: 1 -> 1; matrix products, arithmetic and copies ran while one was open for 31% -> 17% of each run, Pallas kernels for 55% -> 67%
where the time goes in v2:
time: 935 us; the launch traced here: 916 us
  Pallas kernels  690 us (74%)
  matrix products  119 us (13%)
  other arithmetic  41.3 us (4%)
  local copies, waits for them, and re-layouts  28.5 us (3%)
  waiting for transfers between devices  21.9 us (2%)
  between operations  15.2 us (2%)
    pallas_call x1, Pallas kernels, turn_back(): pl.pallas_call(partial(turn_kernel, count, seq_count), out_shape=[jax.Sha...  105 us
    pallas_call x1, Pallas kernels, line_scatter(): pl.pallas_call(partial(scatter_kernel, count), out_shape=jax.ShapeDtypeSt...  104 us
    pallas_call x1, Pallas kernels, middle(): pl.pallas_call(partial(middle_kernel, count, seq_count), out_shape=[jax.S...  96 us
    pallas_call x1, Pallas kernels, experts_in(): pl.pallas_call(partial(experts_in_kernel, count, CAP), out_shape=[jax.Sha...  91.1 us
    pallas_call x1, Pallas kernels, gather_start(): pl.pallas_call(partial(start_kernel, count, seq_count), out_shape=shapes,...  84.9 us
    pallas_call x1, Pallas kernels, scatter_end(): pl.pallas_call(partial(end_kernel, count, seq_count), out_shape=shapes, i...  82.1 us
    pallas_call x1, Pallas kernels, experts_out(): pl.pallas_call(partial(experts_out_kernel, CAP), grid=(count,), out_shape...  74.9 us
    dot_general x12, matrix products, dot(): lax.dot_general(left, right, (((sides[0],), (sides[1],)), ((), ())), pref...  59.2 us
  transfers between devices with their start and end apart: 7, of which 1 were waited for; matrix products, arithmetic and copies ran while one was open for 17% of the time, Pallas kernels for 67%

profile of v2, /device:TPU:0, one launch (start us, length us, event | category | flops | bytes accessed | tf_op | source)
XLA Modules:
  0.0 916.0 jit_solution(2786551608393498271)
XLA Ops:
  12.7 84.9 %gather_start.1 = (bf16[4,8,64,512]{3,2,1,0:T(8,128)(2,1)}, bf16[4,8,64,512]{3,2,1,0:T(8,128)(2,1)}, bf16[4,8,64,512]{3,2,1,0:T(8,128)(2,1)}, bf16[8,64,2048]{2,...) custom-call(bf16[64,2048]{1,0:T(8,128)(2,1)} %refs_0_.1, ...), custom_call_target="tpu_custom_call" | custom-call | tf_op jit(solution)/shard_map/gather_start/pallas_call | solution.py:266
  97.6 1.4 eq.15
  101.2 1.3 reduce-window.6
  105.4 2.2 fusion.17
  108.4 3.2 fusion
  112.5 5.8 multiply_reduce_fusion.1
  118.3 2.9 copy.109.k_raw
  121.2 6.7 multiply_reduce_fusion.2
  127.8 2.9 copy.108.q_raw
  131.3 7.4 seq_sum.2
  139.9 6.4 convolution_convert_fusion.6.v_ref
  146.4 16.9 %attend.1 = (bf16[1024,512]{1,0:T(8,128)(2,1)S(1)}, bf16[1024,512]{1,0:T(8,128)(2,1)S(1)}, bf16[1024,512]{1,0:T(8,128)(2,1)S(1)}) custom-call(f32[1024,512]{1,0:T(8,128)} %copy.108.q_raw, f32[1024,512]{1,0:T(8,128)} %copy.109.k_raw, bf16[1024,512]{1,0:T(8,128)(2,1)} %convolution_convert_fusion.6.v_ref, f32[1024,1]{1,0:T(8,128)S(1)} %copy.110.rq, ...), custom_call_target="tpu_custom_call" | custom-call | tf_op jit(solution)/shard_map/attend/pallas_call | solution.py:823
  163.4 2.3 convolution_convert_fusion
  165.8 96.0 %middle.1 = (f32[256,2048]{1,0:T(8,128)S(1)}, bf16[8,256,2048]{2,1,0:T(8,128)(2,1)S(1)}) custom-call(bf16[4,256,2048]{2,1,0:T(8,128)(2,1)S(1)} %bitcast.111, bf16[256,2048]{1,0:T(8,128)(2,1)S(1)} %bitcast.110), custom_call_target="tpu_custom_call" | custom-call | tf_op jit(solution)/shard_map/middle/pallas_call | solution.py:658
  261.8 3.3 copy-done.2
  268.0 19.2 %all-gather.8.cloned.1.call-done.wu_ref.wu = bf16[2,2048,1024]{2,1,0:T(8,128)(2,1)} async-done(((bf16[2,512,1024]{2,1,0:T(8,128)(2,1)}), bf16[2,2048,1024]{2,1,0:T(8,128)(2,1)}) %all-gather.8.cloned.1.call-update) | async-done | bytes 8388624 | tf_op jit(solution)/shard_map/all_gather | solution.py:1368
  287.1 91.1 %experts_in.1 = (bf16[8,256,2048]{2,1,0:T(8,128)(2,1)}, bf16[2,4,272,2048]{3,2,1,0:T(8,128)(2,1)}, bf16[2,4,272,2048]{3,2,1,0:T(8,128)(2,1)}, bf16[2,4,272,1024]...) custom-call(bf16[256,2048]{1,0:T(8,128)(2,1)} %multiply_convert_fusi, ...), custom_call_target="tpu_custom_call" | custom-call | tf_op jit(solution)/shard_map/experts_in/pallas_call | solution.py:1150
  378.3 74.9 %experts_out.1 = (bf16[2,4,272,1024]{3,2,1,0:T(8,128)(2,1)}, bf16[2,4,272,1024]{3,2,1,0:T(8,128)(2,1)}, bf16[2,4,272,1024]{3,2,1,0:T(8,128)(2,1)}, bf16[8,256,20...) custom-call(bf16[2,4,272,2048]{3,2,1,0:T(8,128)(2,1)} %get-tuple-element.65.y_ref, ...), custom_call_target="tpu_custom_call" | custom-call | tf_op jit(solution)/shard_map/experts_out/pallas_call | solution.py:1292
  453.2 17.6 %bitcast_convert_fusion.2 = bf16[2,2048,1024]{2,1,0:T(8,128)(2,1)} fusion(bf16[2,4,272,2048]{3,2,1,0:T(8,128)(2,1)} %get-tuple-element.92, bf16[2,4,272,1024]{3,2,1,0:T(8,128)(2,1)} %get-tuple-element.93), kind=kOutput, calls=%fused_computation.2 | convolution fusion | flops 9130999808 | bytes 21757952 | tf_op jit(solution)/shard_map/ejra,ejrb->eab/dot_general | solution.py:1431
  470.9 17.7 %bitcast_convert_fusion.1 = bf16[2,2048,1024]{2,1,0:T(8,128)(2,1)} fusion(bf16[2,4,272,2048]{3,2,1,0:T(8,128)(2,1)} %get-tuple-element.92, bf16[2,4,272,1024]{3,2,1,0:T(8,128)(2,1)} %get-tuple-element.94), kind=kOutput, calls=%fused_computation.1 | convolution fusion | flops 9130999808 | bytes 21757952 | tf_op jit(solution)/shard_map/ejra,ejrb->eab/dot_general | solution.py:1431
  488.8 17.9 %bitcast_convert_fusion = bf16[2,1024,2048]{2,1,0:T(8,128)(2,1)} fusion(bf16[2,4,272,1024]{3,2,1,0:T(8,128)(2,1)} %get-tuple-element.95, bf16[2,4,272,2048]{3,2,1,0:T(8,128)(2,1)} %get-tuple-element.65.y_ref), kind=kOutput, calls=%fused_computation | convolution fusion | flops 9130999808 | bytes 21757952 | tf_op jit(solution)/shard_map/ejra,ejrb->eab/dot_general | solution.py:1431
  506.7 103.5 %line_scatter.1 = bf16[256,2048]{1,0:T(8,128)(2,1)S(1)} custom-call(bf16[8,256,2048]{2,1,0:T(8,128)(2,1)} %get-tuple-element.71.x_ref), custom_call_target="tpu_custom_call" | custom-call | tf_op jit(solution)/shard_map/line_scatter/pallas_call | solution.py:449
  612.2 104.7 %turn_back.1 = (bf16[4,256,2048]{2,1,0:T(8,128)(2,1)}, bf16[256,2048]{1,0:T(8,128)(2,1)S(1)}) custom-call(bf16[256,2048]{1,0:T(8,128)(2,1)S(1)} %fusion.27.x_ref, bf16[8,256,2048]{2,1,0:T(8,128)(2,1)} %get-tuple-element.72.parts_ref), custom_call_target="tpu_custom_call" | custom-call | tf_op jit(solution)/shard_map/turn_back/pallas_call | solution.py:745
  717.0 5.8 convolution_convert_fusion.5.do_ref
  722.7 22.5 %attend_back.1 = (f32[1024,512]{1,0:T(8,128)}, f32[1024,512]{1,0:T(8,128)}, bf16[1024,512]{1,0:T(8,128)(2,1)}, f32[1024,2]{1,0:T(8,128)}, f32[1,512]{1,0:T(1,128)}, /*index=5*/f32[1,512]{1,0:T(1,128)}) custom-call(bf16[1024,512]{1,0:T(8,128)(2,1)} %copy-done.8, bf16[1024,512]{1,0:T(8,128)(2,1)} %copy-done.9, ...), custom_call_target="tpu_custom_call" | custom-call | tf_op jit(solution)/shard_map/attend_back/pallas_call | solution.py:918
  745.3 1.8 copy.127
  747.1 6.0 seq_sum.3
  753.2 1.8 concatenate.19
  755.5 1.3 reduce.20
  756.9 1.3 reduce.21
  759.8 6.2 fusion.38
  766.1 1.3 maximum_maximum_fusion.refs_4_
  769.6 2.4 fusion.39
  772.0 5.6 fusion.40
  777.7 3.7 convolution_convert_fusion.1
  781.4 4.0 convolution_convert_fusion.4
  785.4 4.0 convolution_convert_fusion.3
  789.4 4.2 convolution_convert_fusion.2
  793.7 8.2 add_convert_fusion
  801.9 82.1 %scatter_end.1 = (bf16[64,2048]{1,0:T(8,128)(2,1)}, bf16[64,2048]{1,0:T(8,128)(2,1)}, bf16[64,2048]{1,0:T(8,128)(2,1)}, bf16[64,2048]{1,0:T(8,128)(2,1)}, f32[64...) custom-call(bf16[4,8,64,512]{3,2,1,0:T(8,128)(2,1)} %bitcast.120, bf16[4,8,64,512]{3,2,1,0:T(8,128)(2,1)} %bitcast.121, ...), custom_call_target="tpu_custom_call" | custom-call | tf_op jit(solution)/shard_map/scatter_end/pallas_call | solution.py:556
  883.9 1.8 convert_element_type.182
  885.7 1.4 copy.132
  887.2 1.6 slice_reduce_fusion
  888.8 2.6 add_reduce_fusion
  893.8 2.8 fusion.13
  896.6 4.1 convert_element_type.188
  900.7 4.1 convert_element_type.190
  904.8 4.1 convert_element_type.192
  (174 shorter events, 25.4 us)
Async XLA Ops:
  7.2 101.2 %all-gather.12.cloned.1.call-start = ((), (), s32[]{:S(2)}) async-start(), calls=%async_computation.9 | async-start | bytes 5242880 | tf_op jit(solution)/shard_map/all_gather | solution.py:1366
  7.9 260.0 %all-gather.6.cloned.1.call-start = ((), (), s32[]{:S(2)}) async-start(), calls=%async_computation.3 | async-start | bytes 10485760 | tf_op jit(solution)/shard_map/all_gather | solution.py:1367
  8.7 1.7 copy-start.34
  8.7 1.7 copy-start.33
  8.7 2.7 copy-start.36
  8.7 2.7 copy-start.37
  8.7 278.4 %all-gather.8.cloned.1.call-start = ((), (), s32[]{:S(2)}) async-start(), calls=%async_computation.4 | async-start | bytes 10485760 | tf_op jit(solution)/shard_map/all_gather | solution.py:1368
  9.5 368.9 %all-gather.10.cloned.1.call-start = ((), (), s32[]{:S(2)}) async-start(), calls=%async_computation.5 | async-start | bytes 10485760 | tf_op jit(solution)/shard_map/all_gather | solution.py:1369
  10.0 90.9 %copy-start.10 = (s32[1,1024]{1,0:T(1,128)S(1)}, s32[1,1024]{1,0:T(1,128)}, u32[]{:S(2)}) copy-start(s32[1,1024]{1,0:T(1,128)} %doc_row.3) | copy-start | bytes 12292
  10.1 886.6 %reduce-scatter.4.cloned.1.call-start = ((), (), s32[]{:S(2)}) async-start(), calls=%async_computation.6 | async-start | bytes 10485760 | tf_op jit(solution)/shard_map/reduce_scatter | solution.py:1434
  100.8 45.5 %copy-start.11 = (f32[1,512]{1,0:T(1,128)}, f32[1,512]{1,0:T(1,128)S(1)}, u32[]{:S(2)}) copy-start(f32[1,512]{1,0:T(1,128)S(1)} %reshape.254.gq) | copy-start | bytes 6148
  100.9 45.4 %copy-start.12 = (f32[1,512]{1,0:T(1,128)}, f32[1,512]{1,0:T(1,128)S(1)}, u32[]{:S(2)}) copy-start(f32[1,512]{1,0:T(1,128)S(1)} %reshape.255.gk) | copy-start | bytes 6148
  101.2 45.2 %copy-start.5 = (s32[1024,1]{1,0:T(8,128)}, s32[1024,1]{1,0:T(8,128)S(1)}, u32[]{:S(2)}) copy-start(s32[1024,1]{1,0:T(8,128)S(1)} %copy.112.doc_col) | copy-start | bytes 12292
  103.4 5.0 copy-start.22
  107.6 38.7 %copy-start.3 = (f32[1024,128]{1,0:T(8,128)}, f32[1024,128]{1,0:T(8,128)S(1)}, u32[]{:S(2)}) copy-start(f32[1024,128]{1,0:T(8,128)S(1)} %get-tuple-element.168.sin) | copy-start | bytes 1572868
  107.6 38.7 %copy-start.4 = (f32[1024,128]{1,0:T(8,128)}, f32[1024,128]{1,0:T(8,128)S(1)}, u32[]{:S(2)}) copy-start(f32[1024,128]{1,0:T(8,128)S(1)} %get-tuple-element.169.cos) | copy-start | bytes 1572868
  108.4 4.1 copy-start.25
  139.7 6.7 copy-start.6
  139.9 6.5 copy-start.7
  146.4 17.0 %copy-start.43 = (bf16[8,64,2048]{2,1,0:T(8,128)(2,1)S(1)}, bf16[8,64,2048]{2,1,0:T(8,128)(2,1)}, u32[]{:S(2)}) copy-start(bf16[8,64,2048]{2,1,0:T(8,128)(2,1)} %get-tuple-element.61) | copy-start | bytes 6291460
  163.3 2.4 copy-start.8
  163.3 2.4 copy-start.9
  163.4 2.4 copy-start.13
  163.4 2.4 copy-start
  165.8 99.3 %copy-start.20 = (bf16[1,256,2048]{2,1,0:T(8,128)(2,1)S(1)}, bf16[1,256,2048]{2,1,0:T(8,128)(2,1)}, u32[]{:S(2)}) copy-start(bf16[1,256,2048]{2,1,0:T(8,128)(2,1)} %param.16) | copy-start | bytes 3145732
  261.8 3.3 copy-start.2
  470.9 429.8 %reduce-scatter.6.cloned.1.call-start = ((), (), s32[]{:S(2)}) async-start(), calls=%async_computation.7 | async-start | bytes 10485760 | tf_op jit(solution)/shard_map/reduce_scatter | solution.py:1434
  488.7 416.0 %reduce-scatter.8.cloned.1.call-start = ((), (), s32[]{:S(2)}) async-start(), calls=%async_computation.8 | async-start | bytes 10485760 | tf_op jit(solution)/shard_map/reduce_scatter | solution.py:1434
  506.7 103.6 %copy-start.16 = (f32[256,2048]{1,0:T(8,128)S(1)}, f32[256,2048]{1,0:T(8,128)}, u32[]{:S(2)}) copy-start(f32[256,2048]{1,0:T(8,128)} %copy-done.15) | copy-start | bytes 6291460
  612.2 104.8 %copy-start.44 = (bf16[8,64,2048]{2,1,0:T(8,128)(2,1)S(1)}, bf16[8,64,2048]{2,1,0:T(8,128)(2,1)}, u32[]{:S(2)}) copy-start(bf16[8,64,2048]{2,1,0:T(8,128)(2,1)} %get-tuple-element.61) | copy-start | bytes 6291460
  722.7 37.0 %copy-start.45 = (bf16[8,16,256]{2,1,0:T(8,128)(2,1)S(1)}, bf16[8,16,256]{2,1,0:T(8,128)(2,1)}, u32[]{:S(2)}) copy-start(bf16[8,16,256]{2,1,0:T(8,128)(2,1)} %get-tuple-element.82) | copy-start | bytes 196612
  759.8 6.3 copy-start.27
  759.8 7.6 copy-start.19
  759.8 7.6 copy-start.29
  759.8 7.6 copy-start.30
  766.0 2.0 copy-start.18
  768.0 1.6 copy-start.42
  769.6 2.4 copy-start.41
  772.0 5.7 copy-start.14
  772.0 5.6 copy-start.40
  777.7 3.7 copy-start.26
  785.4 4.0 copy-start.31
  789.4 4.2 copy-start.28
  801.9 86.9 %copy-start.32 = (bf16[64,2048]{1,0:T(8,128)(2,1)S(1)}, bf16[64,2048]{1,0:T(8,128)(2,1)}, u32[]{:S(2)}) copy-start(bf16[64,2048]{1,0:T(8,128)(2,1)} %refs_0_.1) | copy-start | bytes 786436
  883.9 7.4 copy-start.39
  887.2 4.7 copy-start.21
  887.2 4.7 copy-start.23
  891.4 2.4 copy-start.17
  (5 other events, 7.1 us)
Sparse Core Ops, SparseCore 0:
  9.9 58.9 all-gather.11
  70.7 87.9 all-gather.5
  160.6 126.5 all-gather.7
  288.8 87.6 all-gather.9
  471.0 85.4 reduce-scatter.3
  559.7 124.0 reduce-scatter.5
  686.9 85.9 reduce-scatter.7

commit v3 on v2

--- a/solution.py
+++ b/solution.py
@@ -151,41 +151,12 @@
     return i, p, 2 * p + 1 - c
 
 
-def gather_kernel(count, x_ref, o_ref, hold, send_r, send_l, send_s, recv, local):
-    places = where_am_i()
-    i = places[0]
-    take = pltpu.make_async_copy(x_ref, hold, local.at[0])
-    take.start()
-    greet(count, places)
-    take.wait()
-    put = pltpu.make_async_copy(hold, o_ref.at[i], local.at[1])
-    put.start()
-    put.wait()
-    line = LineGather(count, places, [o_ref], [0], send_r, send_l, send_s, recv)
-    line.first(0)
-    for t in range(1, count):
-        line.forward(t)
-    line.finish()
-
-
-def line_gather(block, shards, collective):
-    count = shards // 2
-    return pl.pallas_call(
-        partial(gather_kernel, count),
-        out_shape=jax.ShapeDtypeStruct((shards,) + block.shape, block.dtype),
-        in_specs=[pl.BlockSpec(memory_space=ANY)],
-        out_specs=pl.BlockSpec(memory_space=ANY),
-        scratch_shapes=[pltpu.VMEM(block.shape, block.dtype)] + line_sems(1, count) + [DMA((2,))],
-        compiler_params=pltpu.CompilerParams(collective_id=collective, has_side_effects=True),
-        name="line_gather",
-    )(block)
-
-
 def start_kernel(count, seq_count, *refs):
-    wq, wk, wv, wo, small, gains, routes = refs[:7]
-    outs = refs[7:14]
-    holds = refs[14:21]
-    send_x, recv_x, local, send_r, send_l, send_s, recv = refs[21:]
+    wq, wk, wv, wo, small, gains, routes, rows = refs[:8]
+    outs = refs[8:15]
+    rows_out = refs[15]
+    holds = refs[16:24]
+    send_x, recv_x, local, send_r, send_l, send_s, recv = refs[24:]
     places = where_am_i()
     i = places[0]
     here = lax.axis_index("seq")
@@ -194,8 +165,8 @@
     def columns(ref, peer):
         return ref.at[:, pl.ds(pl.multiple_of(peer * width, width), width)]
 
-    own = [columns(wq, here), columns(wk, here), columns(wv, here), wo, small, gains, routes]
-    for a in range(7):
+    own = [columns(wq, here), columns(wk, here), columns(wv, here), wo, small, gains, routes, rows]
+    for a in range(8):
         pltpu.make_async_copy(own[a], holds[a], local.at[a]).start()
     greet(count, places, seq_count)
 
@@ -221,6 +192,9 @@
     for a in (4, 0, 1, 2):
         for d in range(1, seq_count):
             piece(a, d).start()
+    for d in range(1, seq_count):
+        peer = lax.rem(here + d, seq_count)
+        remote(rows, rows_out.at[here], send_x.at[4, d - 1], recv_x.at[4, d - 1], seq=peer).start()
     axes = [1, 1, 1, 0, 1, 0, 0]
     for a in (3, 5, 6, 4, 0, 1, 2):
         pltpu.make_async_copy(own[a], holds[a], local.at[a]).wait()
@@ -234,9 +208,15 @@
             for d in range(1, seq_count):
                 arrived(a, d).wait_recv()
         line.first(a)
+    pltpu.make_async_copy(rows, holds[7], local.at[7]).wait()
+    pltpu.make_async_copy(holds[7], rows_out.at[here], local.at[7]).start()
     for t in range(1, count):
         line.forward(t)
     line.finish()
+    pltpu.make_async_copy(holds[7], rows_out.at[here], local.at[7]).wait()
+    for d in range(1, seq_count):
+        origin = lax.rem(here + seq_count - d, seq_count)
+        remote(rows, rows_out.at[origin], send_x.at[4, d - 1], recv_x.at[4, d - 1], seq=origin).wait()
     for a in (4, 0, 1, 2):
         for d in range(1, seq_count):
             piece(a, d).wait_send()
@@ -244,7 +224,7 @@
 
 def gather_start(arrays, seq_count, shards, collective):
     count = shards // 2
-    wq, wk, wv, wo, small, gains, routes = arrays
+    wq, wk, wv, wo, small, gains, routes, tokens = arrays
     rows, model_width = wq.shape
     width = model_width // seq_count
     sheet = jax.ShapeDtypeStruct((seq_count, shards, rows, width), BF)
@@ -256,31 +236,40 @@
         jax.ShapeDtypeStruct((seq_count, shards) + small.shape, BF),
         jax.ShapeDtypeStruct((shards,) + gains.shape, BF),
         jax.ShapeDtypeStruct((shards,) + routes.shape, jnp.int32),
+        jax.ShapeDtypeStruct((seq_count,) + tokens.shape, BF),
     ]
     holds = [pltpu.VMEM((rows, width), BF)] * 3 + [
         pltpu.VMEM(wo.shape, BF),
         pltpu.VMEM(small.shape, BF),
         pltpu.VMEM(gains.shape, BF),
         pltpu.VMEM(routes.shape, jnp.int32),
+        pltpu.VMEM(tokens.shape, BF),
     ]
     return pl.pallas_call(
         partial(start_kernel, count, seq_count),
         out_shape=shapes,
-        in_specs=[pl.BlockSpec(memory_space=ANY)] * 7,
-        out_specs=[pl.BlockSpec(memory_space=ANY)] * 7,
+        in_specs=[pl.BlockSpec(memory_space=ANY)] * 8,
+        out_specs=[pl.BlockSpec(memory_space=ANY)] * 8,
         scratch_shapes=holds
-        + [DMA((4, seq_count - 1)), DMA((4, seq_count - 1)), DMA((7,))]
+        + [DMA((5, seq_count - 1)), DMA((5, seq_count - 1)), DMA((8,))]
         + line_sems(7, count),
         compiler_params=pltpu.CompilerParams(collective_id=collective, has_side_effects=True),
         name="gather_start",
     )(*arrays)
 
 
+def chunk_order(k, p, count):
+    near = jnp.minimum(p, count - 1 - p)
+    step = (k + 1) // 2
+    both = jnp.where(k % 2 == 1, p - step, p + step)
+    return jnp.where(k <= 2 * near, both, jnp.where(p < count - 1 - p, k, count - 1 - k))
+
+
 class LineScatter:
     def __init__(self, count, places, sources, axes, bufs, sems):
         self.count, self.places = count, places
         self.sources, self.axes = sources, axes
-        self.own, self.sib, self.in_r, self.in_l = bufs
+        self.own, self.sib, self.inbox = bufs
         self.sems = sems
 
     def load(self, a, q):
@@ -296,31 +285,25 @@
     def right(self, a, q):
         i = self.places[0]
         return remote(
-            self.own[a].at[q], self.in_r[a].at[q], self.sems[0].at[a, q], self.sems[3].at[a, q], fsdp=i + 2
+            self.own[a].at[q], self.inbox[a].at[q], self.sems[0].at[a, q], self.sems[3].at[a, q], fsdp=i + 2
         )
 
     def left(self, a, q):
-        i = self.places[0]
+        i, p, sib = self.places
+        slot = jnp.where(q == p - 1, self.count, q)
         return remote(
-            self.own[a].at[q], self.in_l[a].at[q], self.sems[1].at[a, q], self.sems[4].at[a, q], fsdp=i - 2
+            self.own[a].at[q], self.inbox[a].at[slot], self.sems[1].at[a, q], self.sems[4].at[a, q], fsdp=i - 2
         )
 
-    def order(self):
-        order, low, high = [], 0, self.count - 1
-        while low <= high:
-            order.append(high)
-            if low < high:
-                order.append(low)
-            low, high = low + 1, high - 1
-        return order
-
     def begin_loads(self):
-        for q in self.order():
+        for k in range(self.count):
+            q = chunk_order(self.count - 1 - k, self.places[1], self.count)
             for a in range(len(self.sources)):
                 self.load(a, q).start()
 
     def begin(self):
-        for q in self.order():
+        for k in range(self.count):
+            q = chunk_order(self.count - 1 - k, self.places[1], self.count)
             for a in range(len(self.sources)):
                 self.to_sib(a, q).start()
 
@@ -334,8 +317,8 @@
 
         def strip(index):
             total = own[index].astype(F32) + self.sib[a][index].astype(F32)
-            for other in others:
-                total += other[a][index].astype(F32)
+            for slot in others:
+                total += self.inbox[a][(slot,) + index[1:]].astype(F32)
             own[index] = total.astype(own.dtype)
 
         def rows_of(prefix):
@@ -357,22 +340,23 @@
         self.load(a, q).wait()
         self.to_sib(a, q).wait_recv()
 
-    def run(self, after):
+    def run(self, after, between=None):
         i, p, sib = self.places
         count = self.count
         arrays = range(len(self.sources))
-        for j in range(count - 1):
-            q = count - 1 - j
-
-            @pl.when(q > p)
+
+        @pl.loop(0, count - 1)
+        def _(step):
+            @pl.when(step >= p)
             def _():
+                q = count - 1 - (step - p)
                 for a in arrays:
                     self.ready(a, q)
 
                     @pl.when(p > 0)
                     def _():
                         self.right(a, q).wait_recv()
-                        self.add(a, q, [self.in_r])
+                        self.add(a, q, [q])
 
                     @pl.when(p == 0)
                     def _():
@@ -380,35 +364,50 @@
 
                     self.right(a, q).start()
 
-            @pl.when(j < p)
+            @pl.when(step >= count - 1 - p)
             def _():
+                q = step - (count - 1 - p)
                 for a in arrays:
-                    self.ready(a, j)
+                    self.ready(a, q)
 
                     @pl.when(p < count - 1)
                     def _():
-                        self.left(a, j).wait_recv()
-                        self.add(a, j, [self.in_l])
+                        self.left(a, q).wait_recv()
+                        self.add(a, q, [q])
 
                     @pl.when(p == count - 1)
                     def _():
-                        self.add(a, j, [])
-
-                    self.left(a, j).start()
-
-        for q in range(count):
-
-            @pl.when(q == p)
+                        self.add(a, q, [])
+
+                    self.left(a, q).start()
+
+            if between is not None:
+                between(step)
+
+        for a in arrays:
+            self.ready(a, p)
+
+            @pl.when(p > 0)
             def _():
-                for a in arrays:
-                    self.ready(a, q)
-                    if q > 0:
-                        self.right(a, q).wait_recv()
-                    if q < count - 1:
-                        self.left(a, q).wait_recv()
-                    sides = ([self.in_r] if q > 0 else []) + ([self.in_l] if q < count - 1 else [])
-                    self.add(a, q, sides)
-                    after(a, q)
+                self.right(a, p).wait_recv()
+
+            @pl.when(p < count - 1)
+            def _():
+                self.left(a, p).wait_recv()
+
+            @pl.when(p == 0)
+            def _():
+                self.add(a, p, [count])
+
+            @pl.when(p == count - 1)
+            def _():
+                self.add(a, p, [p])
+
+            @pl.when((p > 0) & (p < count - 1))
+            def _():
+                self.add(a, p, [p, count])
+
+            after(a, p)
 
     def finish(self):
         i, p, sib = self.places
@@ -425,50 +424,16 @@
                     self.left(a, q).wait_send()
 
 
-def scatter_kernel(count, x_ref, o_ref, own, sibling, in_r, in_l, s0, s1, s2, r0, r1, r2, local):
-    places = where_am_i()
-    line = LineScatter(
-        count, places, [x_ref], [0], ([own], [sibling], [in_r], [in_l]), (s0, s1, s2, r0, r1, r2, local)
-    )
-    line.begin_loads()
-    greet(count, places)
-    line.begin()
-
-    def after(a, q):
-        out = pltpu.make_async_copy(own.at[q], o_ref, local.at[0, q])
-        out.start()
-        out.wait()
-
-    line.run(after)
-    line.finish()
-
-
-def line_scatter(blocks, shards, collective):
-    count = shards // 2
-    block = blocks.shape[1:]
-    return pl.pallas_call(
-        partial(scatter_kernel, count),
-        out_shape=jax.ShapeDtypeStruct(block, blocks.dtype),
-        in_specs=[pl.BlockSpec(memory_space=ANY)],
-        out_specs=pl.BlockSpec(memory_space=ANY),
-        scratch_shapes=[pltpu.VMEM((count,) + block, blocks.dtype)] * 4 + [DMA((1, count))] * 7,
-        compiler_params=pltpu.CompilerParams(
-            collective_id=collective, has_side_effects=True, vmem_limit_bytes=48 << 20
-        ),
-        name="line_scatter",
-    )(blocks)
-
-
 def end_kernel(count, seq_count, *refs):
     sources = refs[:6]
     rows_ref = refs[6]
     outs = refs[7:13]
     sum_ref = refs[13]
-    bufs = tuple(refs[14 + 6 * k : 20 + 6 * k] for k in range(4))
-    landing = refs[38]
-    sems = refs[39:46]
-    send_x, recv_x, local = refs[46:49]
-    seq = SeqScatter(seq_count, rows_ref, *refs[49:])
+    bufs = tuple(refs[14 + 6 * k : 20 + 6 * k] for k in range(3))
+    landing = refs[32]
+    sems = refs[33:40]
+    send_x, recv_x, local = refs[40:43]
+    seq = SeqScatter(seq_count, rows_ref, *refs[43:48])
     places = where_am_i()
     here = lax.axis_index("seq")
     width = sources[0].shape[3]
@@ -548,23 +513,25 @@
         jax.ShapeDtypeStruct(gains.shape[1:], F32),
         jax.ShapeDtypeStruct(row_blocks.shape[1:], F32),
     ]
-    blocks = []
+    blocks, inboxes = [], []
     for a in range(6):
         shape = arrays[a].shape
         block = (shape[0],) + shape[2:] if a in (0, 1, 2, 4) else shape[1:]
         blocks.append(pltpu.VMEM((count,) + block, arrays[a].dtype))
+        inboxes.append(pltpu.VMEM((count + 1,) + block, arrays[a].dtype))
     return pl.pallas_call(
         partial(end_kernel, count, seq_count),
         out_shape=shapes,
         in_specs=[pl.BlockSpec(memory_space=ANY)] * 7,
         out_specs=[pl.BlockSpec(memory_space=ANY)] * 6 + [pl.BlockSpec(memory_space=pltpu.VMEM)],
-        scratch_shapes=blocks * 4
+        scratch_shapes=blocks * 2
+        + inboxes
         + [pltpu.VMEM((seq_count,) + small.shape[2:], F32)]
         + [DMA((6, count))] * 7
         + [DMA((4, seq_count - 1)), DMA((4, seq_count - 1)), DMA((6,))]
         + seq_scatter_scratch(row_blocks.shape[1:], row_blocks.dtype, seq_count),
         compiler_params=pltpu.CompilerParams(
-            collective_id=collective, has_side_effects=True, vmem_limit_bytes=56 << 20
+            collective_id=collective, has_side_effects=True, vmem_limit_bytes=62 << 20
         ),
         name="scatter_end",
     )(*arrays, row_blocks)
@@ -645,8 +612,7 @@
     line.first(0)
     for t in range(1, count):
         line.forward(t)
-        if t == 1:
-            seq.total(o_ref)
+    seq.total(o_ref)
     line.finish()
     seq.finish()
 
@@ -708,15 +674,146 @@
     )(value)
 
 
+class GateUpGrads:
+    def __init__(self, ins, outs, scratch, steps):
+        self.ins, self.outs = ins, outs
+        self.held, self.staged, self.in_sem, self.out_sem = scratch
+        self.experts, self.width, self.hidden = outs[0].shape
+        self.tile = self.staged[0].shape[1]
+        self.tiles = self.width // self.tile
+        self.units = self.experts * self.tiles
+        self.share = -(-self.units // steps)
+
+    def fetch(self, n, e):
+        return pltpu.make_async_copy(self.ins[n].at[e], self.held[n].at[e], self.in_sem.at[n, e])
+
+    def begin(self):
+        for e in range(self.experts):
+            for n in range(3):
+                self.fetch(n, e).start()
+        self.logits().start()
+        self.pair(0).start()
+
+    def logits(self):
+        return pltpu.make_async_copy(self.ins[4], self.held[4], self.in_sem.at[3, 0])
+
+    def pair(self, q):
+        buf = lax.rem(q, 2)
+        src = self.ins[3].at[pl.ds(2 * q, 2)]
+        return pltpu.make_async_copy(src, self.held[3].at[buf], self.in_sem.at[4, buf])
+
+    def put(self, n, u, buf):
+        rows = pl.ds(pl.multiple_of(lax.rem(u, self.tiles) * self.tile, self.tile), self.tile)
+        target = self.outs[n].at[u // self.tiles, rows]
+        return pltpu.make_async_copy(self.staged[n].at[buf], target, self.out_sem.at[n, buf])
+
+    def between(self, step):
+        over_rows = (((0,), (0,)), ((), ()))
+        rows, gates, ups, tokens, logits = self.held
+
+        @pl.loop(step * self.share, jnp.minimum((step + 1) * self.share, self.units))
+        def _(u):
+            e = u // self.tiles
+            buf = lax.rem(u, 2)
+
+            @pl.when(lax.rem(u, self.tiles) == 0)
+            def _():
+                for n in range(3):
+                    self.fetch(n, e).wait()
+
+            @pl.when(u >= 2)
+            def _():
+                self.put(0, u - 2, buf).wait()
+                self.put(1, u - 2, buf).wait()
+
+            cols = pl.ds(pl.multiple_of(lax.rem(u, self.tiles) * self.tile, self.tile), self.tile)
+            left = rows[e, :, cols]
+            for n, right in ((0, gates), (1, ups)):
+                self.staged[n][buf] = lax.dot_general(
+                    left, right[e], over_rows, preferred_element_type=F32
+                ).astype(BF)
+                self.put(n, u, buf).start()
+
+        @pl.when(step == 0)
+        def _():
+            self.logits().wait()
+            total_ref = self.outs[2]
+            total_ref[...] = jnp.zeros_like(total_ref)
+            block = 512
+            pairs = self.ins[3].shape[0] // 2
+
+            @pl.loop(0, pairs)
+            def _(q):
+                self.pair(q).wait()
+
+                @pl.when(q + 1 < pairs)
+                def _():
+                    self.pair(q + 1).start()
+
+                buf = lax.rem(q, 2)
+
+                @pl.loop(0, self.width // block)
+                def _(n):
+                    cols = pl.ds(pl.multiple_of(n * block, block), block)
+                    total = total_ref[:, cols]
+                    for j in range(2):
+                        total += jnp.dot(
+                            logits[2 * q + j], tokens[buf, j, :, cols], preferred_element_type=F32
+                        )
+                    total_ref[:, cols] = total
+
+    def finish(self):
+        for u in (self.units - 2, self.units - 1):
+            for n in range(2):
+                self.put(n, u, u % 2).wait()
+
+
 def turn_kernel(
-    count, seq_count, x_ref, parts_ref, o_ref, sum_ref, hold, send, recv, one, own, sib, in_r, in_l, *sems
+    count,
+    seq_count,
+    x_ref,
+    parts_ref,
+    in0,
+    in1,
+    in2,
+    in3,
+    in4,
+    o_ref,
+    sum_ref,
+    out0,
+    out1,
+    out2,
+    hold,
+    send,
+    recv,
+    one,
+    held0,
+    held1,
+    held2,
+    held3,
+    held4,
+    staged0,
+    staged1,
+    in_sem,
+    out_sem,
+    own,
+    sib,
+    inbox,
+    *sems,
 ):
     places = where_am_i()
     here = lax.axis_index("seq")
-    line = LineScatter(count, places, [parts_ref], [0], ([own], [sib], [in_r], [in_l]), sems)
+    line = LineScatter(count, places, [parts_ref], [0], ([own], [sib], [inbox]), sems)
+    grads = GateUpGrads(
+        (in0, in1, in2, in3, in4),
+        (out0, out1, out2),
+        ((held0, held1, held2, held3, held4), (staged0, staged1), in_sem, out_sem),
+        count - 1,
+    )
     line.begin_loads()
     take = pltpu.make_async_copy(x_ref, hold, one)
     take.start()
+    grads.begin()
     greet(count, places, seq_count)
     for d in range(1, seq_count):
         peer = lax.rem(here + d, seq_count)
@@ -731,7 +828,8 @@
         out.start()
         out.wait()
 
-    line.run(after)
+    line.run(after, grads.between)
+    grads.finish()
     put.wait()
     for d in range(1, seq_count):
         origin = lax.rem(here + seq_count - d, seq_count)
@@ -739,30 +837,44 @@
     line.finish()
 
 
-def turn_back(block, parts, seq_count, shards, collective):
+def turn_back(block, parts, expert_in, d_gate, d_up, h2_all, logits, seq_count, shards, collective):
     count = shards // 2
     part = parts.shape[1:]
+    model_width = part[1]
+    local_experts, slots, hidden = d_gate.shape
+    tile = 512
+    grad = jax.ShapeDtypeStruct((local_experts, model_width, hidden), BF)
+    anywhere = pl.BlockSpec(memory_space=ANY)
     return pl.pallas_call(
         partial(turn_kernel, count, seq_count),
         out_shape=[
             jax.ShapeDtypeStruct((seq_count,) + block.shape, block.dtype),
             jax.ShapeDtypeStruct(part, parts.dtype),
+            grad,
+            grad,
+            jax.ShapeDtypeStruct((logits.shape[1], model_width), F32),
         ],
-        in_specs=[pl.BlockSpec(memory_space=ANY)] * 2,
-        out_specs=[pl.BlockSpec(memory_space=ANY)] * 2,
+        in_specs=[anywhere] * 7,
+        out_specs=[anywhere] * 4 + [pl.BlockSpec(memory_space=pltpu.VMEM)],
         scratch_shapes=[
             pltpu.VMEM(block.shape, block.dtype),
             DMA((seq_count - 1,)),
             DMA((seq_count - 1,)),
             DMA,
         ]
-        + [pltpu.VMEM((count,) + part, parts.dtype)] * 4
+        + [pltpu.VMEM(x.shape, BF) for x in (expert_in, d_gate, d_up)]
+        + [pltpu.VMEM((2, 2) + h2_all.shape[1:], BF), pltpu.VMEM(logits.shape, BF)]
+        + [pltpu.VMEM((2, tile, hidden), BF)] * 2
+        + [DMA((5, max(2, local_experts))), DMA((2, 2))]
+        + [pltpu.VMEM((count,) + part, BF)] * 2
+        + [pltpu.VMEM((count + 1,) + part, BF)]
         + [DMA((1, count))] * 7,
         compiler_params=pltpu.CompilerParams(
-            collective_id=collective, has_side_effects=True, vmem_limit_bytes=48 << 20
+            collective_id=collective, has_side_effects=True, vmem_limit_bytes=60 << 20
         ),
+        cost_estimate=pl.CostEstimate(flops=60_000_000_000, bytes_accessed=200_000_000, transcendentals=0),
         name="turn_back",
-    )(block, parts)
+    )(block, parts, expert_in, d_gate, d_up, h2_all, logits)
 
 
 def half_sign(shape):
@@ -935,13 +1047,6 @@
     )(q_low, k_low, values, d_heads, q_raw, k_raw, rq, rk, gq, gk, cos, sin, doc_col, doc_row)
 
 
-def chunk_order(k, p, count):
-    near = jnp.minimum(p, count - 1 - p)
-    step = (k + 1) // 2
-    both = jnp.where(k % 2 == 1, p - step, p + step)
-    return jnp.where(k <= 2 * near, both, jnp.where(p < count - 1 - p, k, count - 1 - k))
-
-
 def experts_in_kernel(
     count,
     cap,
@@ -1000,7 +1105,8 @@
     staged = ((xs, x_out), (ys, y_out), (acts, act_out), (by_up, by_up_out), (by_gate, by_gate_out))
 
     def store(n, e, q):
-        return pltpu.make_async_copy(staged[n][0].at[e], staged[n][1].at[e, q], out_sem.at[n, e])
+        rows = pl.ds(pl.multiple_of(q * 2 * cap, 2 * cap), 2 * cap)
+        return pltpu.make_async_copy(staged[n][0].at[e], staged[n][1].at[e, rows], out_sem.at[n, e])
 
     def keep(q):
         src = h2.at[pl.ds(2 * q, 2)]
@@ -1143,8 +1249,8 @@
     local_experts, _, hidden = w_gate.shape
     experts = router_t.shape[0]
     count = shards // 2
-    wide = jax.ShapeDtypeStruct((local_experts, count, 2 * CAP, model_width), BF)
-    thin = jax.ShapeDtypeStruct((local_experts, count, 2 * CAP, hidden), BF)
+    wide = jax.ShapeDtypeStruct((local_experts, count * 2 * CAP, model_width), BF)
+    thin = jax.ShapeDtypeStruct((local_experts, count * 2 * CAP, hidden), BF)
     anywhere = pl.BlockSpec(memory_space=ANY)
     vmem = pl.BlockSpec(memory_space=pltpu.VMEM)
     return pl.pallas_call(
@@ -1178,126 +1284,345 @@
     )(h2, dy_all, targets, router_t, w_gate, w_up)
 
 
+class StagedScatter(LineScatter):
+    def __init__(self, count, places, stage, bufs, sems):
+        super().__init__(count, places, [None], [0], bufs, sems)
+        self.stage = stage
+
+    def to_sib(self, a, q):
+        sib = self.places[2]
+        return remote(self.stage, self.sib[a].at[q], self.sems[2].at[a, q], self.sems[5].at[a, q], fsdp=sib)
+
+    def ready(self, a, q):
+        self.to_sib(a, q).wait_recv()
+
+    def finish(self):
+        i, p, sib = self.places
+        for q in range(self.count):
+
+            @pl.when(q > p)
+            def _():
+                self.right(0, q).wait_send()
+
+            @pl.when(q < p)
+            def _():
+                self.left(0, q).wait_send()
+
+
 def experts_out_kernel(
+    count,
     cap,
-    y_ref,
-    act_ref,
-    by_up_ref,
-    by_gate_ref,
+    y_in,
+    act_in,
+    by_up_in,
+    by_gate_in,
     gate_slots,
     targets,
     targets_t,
     probs_ref,
     router_t,
+    wg_in,
+    wu_in,
+    wd_in,
+    gated_out,
+    d_gate_out,
+    d_up_out,
+    parts_out,
+    logit_ref,
+    sum_ref,
+    g_down_out,
     wg,
     wu,
     wd,
-    gated_ref,
-    d_gate_ref,
-    d_up_ref,
-    out_ref,
-    back_ref,
-    logit_ref,
+    ys,
+    acts,
+    by_ups,
+    by_gates,
+    gated,
+    d_gate,
+    d_up,
+    parts,
+    stage,
+    own,
+    sibling,
+    inbox,
+    w_sem,
+    in_sem,
+    out_sem,
+    part_sem,
+    down_sem,
+    *rest,
 ):
-    local_experts, hidden, model_width = wd.shape
+    sems = rest[:7]
+    room_gated, room_y = rest[7:] if len(rest) > 7 else (wg, wu)
+    places = where_am_i()
+    i, p, sib = places
+    core = lax.rem(i, 2)
+    local_experts, hidden, model_width = wd_in.shape
     tokens = targets.shape[2]
     experts = router_t.shape[0]
-    first = lax.axis_index("fsdp") * local_experts
+    first = i * local_experts
     over_lanes = (((1,), (1,)), ((), ()))
-    over_rows = (((0,), (0,)), ((), ()))
-    dots = []
-    for e in range(local_experts):
-        wide = 256
-
-        def step(n, dot):
-            cols = pl.ds(pl.multiple_of(n * wide, wide), wide)
-            grad_act = lax.dot_general(
-                y_ref[e, 0], wd[e, cols, :], over_lanes, preferred_element_type=F32
-            )
-            act = act_ref[e, 0, :, cols].astype(F32)
-            gate = gate_slots[e, 0]
-            dot = dot + jnp.sum(act * grad_act, axis=1, keepdims=True)
-            grad_act = grad_act * gate
-            gated_ref[e, 0, :, cols] = (act * gate).astype(BF)
-            d_up_ref[e, 0, :, cols] = (grad_act * by_up_ref[e, 0, :, cols].astype(F32)).astype(BF)
-            d_gate_ref[e, 0, :, cols] = (grad_act * by_gate_ref[e, 0, :, cols].astype(F32)).astype(BF)
-            return dot
-
-        dots.append(lax.fori_loop(0, hidden // wide, step, jnp.zeros((2 * cap, 1), F32)))
-
+    line = StagedScatter(count, places, stage, ([own], [sibling], [inbox]), sems)
+    weights = ((wd_in, wd), (wg_in, wg), (wu_in, wu))
+    inputs = ((y_in, ys), (act_in, acts), (by_up_in, by_ups), (by_gate_in, by_gates))
+    results = ((gated, gated_out), (d_gate, d_gate_out), (d_up, d_up_out))
+
+    def weight(n):
+        return pltpu.make_async_copy(weights[n][0], weights[n][1], w_sem.at[n])
+
+    def rows_of(q):
+        return pl.ds(pl.multiple_of(q * 2 * cap, 2 * cap), 2 * cap)
+
+    def fetch(n, q, buf):
+        src = inputs[n][0].at[:, rows_of(q)]
+        return pltpu.make_async_copy(src, inputs[n][1].at[buf], in_sem.at[n, buf])
+
+    def store(n, q):
+        return pltpu.make_async_copy(results[n][0], results[n][1].at[:, rows_of(q)], out_sem.at[n])
+
+    def put(q):
+        return pltpu.make_async_copy(parts, parts_out.at[pl.ds(2 * q, 2)], part_sem)
+
+    def order(k):
+        return chunk_order(count - 1 - k, p, count)
+
+    weight(0).start()
+    for n in range(4):
+        fetch(n, order(0), 0).start()
+    weight(1).start()
+    weight(2).start()
+    greet(count, places)
     slot_rows = lax.broadcasted_iota(jnp.int32, (local_experts * cap, tokens), 0)
     slot_lanes = lax.broadcasted_iota(jnp.int32, (tokens, local_experts * cap), 1)
     expert_rows = lax.broadcasted_iota(jnp.int32, (experts, tokens), 0)
-    picks, logits_low = [], []
-    for j in range(2):
-        grad_probs = jnp.zeros((experts, tokens), F32)
-        pick = None
+
+    def compute(k):
+        q = order(k)
+        buf = lax.rem(k, 2)
+        for n in range(4):
+            fetch(n, q, buf).wait()
+
+        @pl.when(k + 1 < count)
+        def _():
+            for n in range(4):
+                fetch(n, order(k + 1), 1 - buf).start()
+
+        @pl.when(k > 0)
+        def _():
+            for n in range(3):
+                store(n, q).wait()
+            put(q).wait()
+            line.to_sib(0, order(k - 1)).wait_send()
+
+        @pl.when(k == 0)
+        def _():
+            weight(0).wait()
+
+        dots = []
         for e in range(local_experts):
-            part = slice(e * cap, (e + 1) * cap)
-            mask = (slot_rows == targets[j, e : e + 1, :])[part]
-            row = jnp.sum(jnp.where(mask, dots[e][j * cap : (j + 1) * cap], 0.0), axis=0, keepdims=True)
-            grad_probs = jnp.where(expert_rows == first + e, row, grad_probs)
-            hit = slot_lanes == targets_t[j, :, e : e + 1]
-            pick = hit if pick is None else pick | hit
-        probs = probs_ref[j]
-        grad_logits = probs * (grad_probs - jnp.sum(probs * grad_probs, axis=0, keepdims=True))
-        logit_ref[j] = grad_logits.astype(BF)
-        picks.append(jnp.where(pick, 1.0, 0.0).astype(BF))
-        logits_low.append(grad_logits.T.astype(BF))
-
-    block = 512
-
-    @pl.loop(0, model_width // block)
-    def _(n):
-        cols = pl.ds(pl.multiple_of(n * block, block), block)
-        results, grads = [], []
+            wide = 256
+
+            def step(n, dot):
+                cols = pl.ds(pl.multiple_of(n * wide, wide), wide)
+                grad_act = lax.dot_general(
+                    ys[buf, e], wd[e, cols, :], over_lanes, preferred_element_type=F32
+                )
+                act = acts[buf, e, :, cols].astype(F32)
+                gate = gate_slots[e, q]
+                dot = dot + jnp.sum(act * grad_act, axis=1, keepdims=True)
+                grad_act = grad_act * gate
+                gated[e, :, cols] = (act * gate).astype(BF)
+                d_up[e, :, cols] = (grad_act * by_ups[buf, e, :, cols].astype(F32)).astype(BF)
+                d_gate[e, :, cols] = (grad_act * by_gates[buf, e, :, cols].astype(F32)).astype(BF)
+                return dot
+
+            dots.append(lax.fori_loop(0, hidden // wide, step, jnp.zeros((2 * cap, 1), F32)))
+        for n in range(3):
+            store(n, q).start()
+
+        picks, logits_low = [], []
+        for j in range(2):
+            slot = 2 * q + j
+            grad_probs = jnp.zeros((experts, tokens), F32)
+            pick = None
+            for e in range(local_experts):
+                part = slice(e * cap, (e + 1) * cap)
+                mask = (slot_rows == targets[slot, e : e + 1, :])[part]
+                row = jnp.sum(jnp.where(mask, dots[e][j * cap : (j + 1) * cap], 0.0), axis=0, keepdims=True)
+                grad_probs = jnp.where(expert_rows == first + e, row, grad_probs)
+                hit = slot_lanes == targets_t[slot, :, e : e + 1]
+                pick = hit if pick is None else pick | hit
+            probs = probs_ref[slot]
+            grad_logits = probs * (grad_probs - jnp.sum(probs * grad_probs, axis=0, keepdims=True))
+            logit_ref[slot] = grad_logits.astype(BF)
+            picks.append(jnp.where(pick, 1.0, 0.0).astype(BF))
+            logits_low.append(grad_logits.T.astype(BF))
+
+        @pl.when(k == 0)
+        def _():
+            weight(1).wait()
+            weight(2).wait()
+
+        block = 512
+
+        @pl.loop(0, model_width // block)
+        def _(n):
+            cols = pl.ds(pl.multiple_of(n * block, block), block)
+            outs, grads = [], []
+            for e in range(local_experts):
+                outs.append(jnp.dot(gated[e], wd[e, :, cols], preferred_element_type=F32))
+                grads.append(
+                    lax.dot_general(d_gate[e], wg[e, cols, :], over_lanes, preferred_element_type=F32)
+                    + lax.dot_general(d_up[e], wu[e, cols, :], over_lanes, preferred_element_type=F32)
+                )
+            for j in range(2):
+                part = slice(j * cap, (j + 1) * cap)
+                mine = jnp.concatenate([value[part] for value in outs], axis=0).astype(BF)
+                back = jnp.concatenate([value[part] for value in grads], axis=0).astype(BF)
+                parts[j, :, cols] = jnp.dot(picks[j], mine, preferred_element_type=F32).astype(BF)
+                total = (
+                    jnp.dot(picks[j], back, preferred_element_type=F32)
+                    + jnp.dot(logits_low[j], router_t[:, cols], preferred_element_type=F32)
+                ).astype(BF)
+
+                @pl.when(core == j)
+                def _():
+                    own[q, :, cols] = total
+
+                @pl.when(core != j)
+                def _():
+                    stage[:, cols] = total
+
+        line.to_sib(0, q).start()
+        put(q).start()
+
+    @pl.loop(0, 1)
+    def _(k):
+        compute(k)
+
+    def after(a, q):
+        out = pltpu.make_async_copy(own.at[q], sum_ref, part_sem)
+        out.start()
+        out.wait()
+
+    def down_grads():
+        slots = count * 2 * cap
+        tile = 256
+        tiles = hidden // tile
+        spans = model_width // hidden
+
+        def load_gated(e):
+            return pltpu.make_async_copy(
+                gated_out.at[e], room_gated.at[e, pl.ds(0, slots)], down_sem.at[0, e]
+            )
+
+        def load_y(e, span):
+            src = y_in.at[e, :, pl.ds(span * hidden, hidden)]
+            return pltpu.make_async_copy(src, room_y.at[e, pl.ds(0, slots)], down_sem.at[1, e])
+
+        def put_grad(e, span, n, buf):
+            part = (d_gate, d_up)[buf].at[0, pl.ds(0, tile)]
+            rows = pl.ds(pl.multiple_of(n * tile, tile), tile)
+            target = g_down_out.at[e, rows, pl.ds(span * hidden, hidden)]
+            return pltpu.make_async_copy(part, target, out_sem.at[buf])
+
         for e in range(local_experts):
-            results.append(jnp.dot(gated_ref[e, 0], wd[e, :, cols], preferred_element_type=F32))
-            grads.append(
-                lax.dot_general(d_gate_ref[e, 0], wg[e, cols, :], over_lanes, preferred_element_type=F32)
-                + lax.dot_general(d_up_ref[e, 0], wu[e, cols, :], over_lanes, preferred_element_type=F32)
-            )
-        for j in range(2):
-            part = slice(j * cap, (j + 1) * cap)
-            mine = jnp.concatenate([value[part] for value in results], axis=0).astype(BF)
-            back = jnp.concatenate([value[part] for value in grads], axis=0).astype(BF)
-            out_ref[j, :, cols] = jnp.dot(picks[j], mine, preferred_element_type=F32).astype(BF)
-            back_ref[j, :, cols] = (
-                jnp.dot(picks[j], back, preferred_element_type=F32)
-                + jnp.dot(logits_low[j], router_t[:, cols], preferred_element_type=F32)
-            ).astype(BF)
+            load_gated(e).start()
+            load_y(e, 0).start()
+        for span in range(spans):
+            for e in range(local_experts):
+                if span == 0:
+                    load_gated(e).wait()
+                load_y(e, span).wait()
+
+                @pl.loop(0, tiles // 2)
+                def _(m):
+                    for buf in range(2):
+                        n = 2 * m + buf
+
+                        def wait_last():
+                            put_grad(e, span, n, buf).wait()
+
+                        if span + e > 0:
+                            wait_last()
+                        else:
+                            pl.when(m > 0)(wait_last)
+                        cols = pl.ds(pl.multiple_of(n * tile, tile), tile)
+                        (d_gate, d_up)[buf][0, 0:tile, :] = lax.dot_general(
+                            room_gated[e, 0:slots, cols],
+                            room_y[e, 0:slots, :],
+                            (((0,), (0,)), ((), ())),
+                            preferred_element_type=F32,
+                        ).astype(BF)
+                        put_grad(e, span, n, buf).start()
+
+                if span + 1 < spans:
+                    load_y(e, span + 1).start()
+        for buf in range(2):
+            put_grad(0, 0, 0, buf).wait()
+
+    def between(step):
+        compute(step + 1)
+
+        @pl.when(step == count - 2)
+        def _():
+            for n in range(3):
+                store(n, 0).wait()
+            put(0).wait()
+            line.to_sib(0, order(count - 1)).wait_send()
+            down_grads()
+
+    line.run(lambda a, q: None, between)
+    after(0, p)
+    line.finish()
 
 
 def experts_out(
-    grads, act, by_up, by_gate, gate_slots, targets, targets_t, probs, router_t, w_gate, w_up, w_down
+    grads, act, by_up, by_gate, gate_slots, targets, targets_t, probs, router_t, w_gate, w_up, w_down, collective
 ):
-    local_experts, count, slots, model_width = grads.shape
-    hidden = act.shape[3]
+    local_experts, _, model_width = grads.shape
+    hidden = act.shape[2]
     shards, experts, tokens = probs.shape
-
-    def chunk(x):
-        return pl.BlockSpec((x.shape[0], 1) + x.shape[2:], lambda q: (0, q, 0, 0))
-
-    def pair(x):
-        return pl.BlockSpec((2,) + x.shape[1:], lambda q: (q, 0, 0))
-
-    def fixed(x):
-        return pl.BlockSpec(
-            x.shape, lambda q: (0,) * len(x.shape), pipeline_mode=pl.Buffered(1)
-        )
-
+    count = shards // 2
+    anywhere = pl.BlockSpec(memory_space=ANY)
+    vmem = pl.BlockSpec(memory_space=pltpu.VMEM)
     thin = jax.ShapeDtypeStruct(act.shape, BF)
-    full = jax.ShapeDtypeStruct((shards, tokens, model_width), BF)
-    logit = jax.ShapeDtypeStruct(probs.shape, BF)
+    extra = [] if act.shape[1] <= model_width else [pltpu.VMEM(act.shape, BF)] * 2
     return pl.pallas_call(
-        partial(experts_out_kernel, CAP),
-        grid=(count,),
-        out_shape=[thin, thin, thin, full, full, logit],
-        in_specs=[chunk(grads), chunk(act), chunk(by_up), chunk(by_gate), chunk(gate_slots)]
-        + [pair(targets), pair(targets_t), pair(probs)]
-        + [fixed(router_t), fixed(w_gate), fixed(w_up), fixed(w_down)],
-        out_specs=[chunk(act)] * 3 + [pair(full)] * 2 + [pair(logit)],
-        compiler_params=pltpu.CompilerParams(vmem_limit_bytes=63 << 20),
+        partial(experts_out_kernel, count, CAP),
+        out_shape=[
+            thin,
+            thin,
+            thin,
+            jax.ShapeDtypeStruct((shards, tokens, model_width), BF),
+            jax.ShapeDtypeStruct(probs.shape, BF),
+            jax.ShapeDtypeStruct((tokens, model_width), BF),
+            jax.ShapeDtypeStruct(w_down.shape, BF),
+        ],
+        in_specs=[anywhere] * 4 + [vmem] * 5 + [anywhere] * 3,
+        out_specs=[anywhere] * 4 + [vmem, anywhere, anywhere],
+        scratch_shapes=[pltpu.VMEM(x.shape, BF) for x in (w_gate, w_up, w_down)]
+        + [pltpu.VMEM((2, local_experts, 2 * CAP, model_width), BF)]
+        + [pltpu.VMEM((2, local_experts, 2 * CAP, hidden), BF)] * 3
+        + [pltpu.VMEM((local_experts, 2 * CAP, hidden), BF)] * 3
+        + [
+            pltpu.VMEM((2, tokens, model_width), BF),
+            pltpu.VMEM((tokens, model_width), BF),
+            pltpu.VMEM((count, tokens, model_width), BF),
+            pltpu.VMEM((count, tokens, model_width), BF),
+            pltpu.VMEM((count + 1, tokens, model_width), BF),
+            DMA((3,)),
+            DMA((4, 2)),
+            DMA((3,)),
+            DMA,
+            DMA((2, local_experts)),
+        ]
+        + [DMA((1, count))] * 7
+        + extra,
+        compiler_params=pltpu.CompilerParams(
+            collective_id=collective, has_side_effects=True, vmem_limit_bytes=63 << 20
+        ),
         name="experts_out",
     )(grads, act, by_up, by_gate, gate_slots, targets, targets_t, probs, router_t, w_gate, w_up, w_down)
 
@@ -1360,10 +1685,10 @@
     )
     gains = jnp.pad(jnp.stack([query_gain, key_gain]), ((0, 14), (0, lanes - rows)))
     routes_flat = routes.reshape(tok_rows * top_k // lanes, lanes)
-    wq, wk, wv, wo, small_all, gains_all, routes_all = gather_start(
-        (w_query, w_key, w_value, w_output, small, gains, routes_flat), seq_count, shards, 0
+    wq, wk, wv, wo, small_all, gains_all, routes_all, x_all = gather_start(
+        (w_query, w_key, w_value, w_output, small, gains, routes_flat, inputs[0]), seq_count, shards, 0
     )
-    x_all = lax.all_gather(inputs[0], "seq", axis=0, tiled=True)
+    x_all = x_all.reshape(seq_len, model_width)
     full_gate = lax.all_gather(w_gate, "seq", axis=1, tiled=True)
     full_up = lax.all_gather(w_up, "seq", axis=1, tiled=True)
     full_down = lax.all_gather(w_down, "seq", axis=1, tiled=True)
@@ -1411,7 +1736,7 @@
     h2_all, expert_in, grad_slots, act, by_up, by_gate, gate_slots, gate_probs = experts_in(
         h2, dy_all, targets, router_t, full_gate, full_up, 3
     )
-    gated, d_gate, d_up, out_parts, grad_parts, grad_logits = experts_out(
+    gated, d_gate, d_up, out_parts, grad_logits, grad_h2, g_down = experts_out(
         grad_slots,
         act,
         by_up,
@@ -1424,19 +1749,15 @@
         full_gate,
         full_up,
         full_down,
+        4,
     )
-    router_part = jnp.einsum("jet,jtd->de", grad_logits, h2_all, preferred_element_type=F32)
-
-    def outer(left, right):
-        return jnp.einsum("ejra,ejrb->eab", left, right, preferred_element_type=F32).astype(BF)
 
     def spread(part):
-        return lax.psum_scatter(part, "seq", scatter_dimension=1, tiled=True).astype(F32)
-
-    g_down = spread(outer(gated, grad_slots))
-    g_gate = spread(outer(expert_in, d_gate))
-    g_up = spread(outer(expert_in, d_up))
-    grad_h2 = line_scatter(grad_parts, shards, 4).astype(F32)
+        return lax.psum_scatter(part, "seq", scatter_dimension=1, tiled=True)
+
+    g_down = spread(g_down)
+    grad_h2 = grad_h2.astype(F32)
+
     u_rows = gain_f * grad_h2
     grad_mid = (
         grad_rows
@@ -1445,13 +1766,27 @@
     )
     ffn_part = jnp.sum(grad_h2 * x_mid * scale_f, axis=0)
 
-    d_attn, out_sum = turn_back(grad_mid.astype(BF), out_parts, seq_count, shards, 5)
+    d_attn, out_sum, g_gate, g_up, router_part = turn_back(
+        grad_mid.astype(BF),
+        out_parts,
+        expert_in,
+        d_gate,
+        d_up,
+        h2_all,
+        grad_logits,
+        seq_count,
+        shards,
+        5,
+    )
+    g_gate = spread(g_gate)
+    g_up = spread(g_up)
     d_attn = d_attn.reshape(seq_len, model_width)
     result = x_mid + out_sum.astype(F32)
     d_heads = dot(d_attn, wo, (1, 1), BF)
     u_q, u_k, dv_low, dots, gain_q_part, gain_k_part = attend_back(
         q_low, k_low, values, d_heads, q_raw, k_raw, rq, rk, gq, gk, cos, sin, doc_col, doc_row
     )
+    dots, g_down = lax.optimization_barrier((dots, g_down))
     dots = seq_sum(dots.T, seq_count, 6) / model_width
 
     def norm_back(u, raw, scale, product):
@@ -1464,7 +1799,7 @@
 
     sheet = (seq_count, shards, rows, width)
     small_part = jnp.concatenate(
-        [router_part, ffn_part[:, None], jnp.zeros((model_width, lanes - experts - 1), F32)], axis=1
+        [router_part.T, ffn_part[:, None], jnp.zeros((model_width, lanes - experts - 1), F32)], axis=1
     ).reshape(seq_count, shards, rows, lanes)
     gains_part = jnp.stack([gain_q_part.reshape(shards, rows), gain_k_part.reshape(shards, rows)], axis=1)
     gains_part = jnp.pad(gains_part, ((0, 0), (0, 6), (0, lanes - rows)))
@@ -1508,9 +1843,9 @@
         g_small[:, experts],
         g_gains[0, :rows],
         g_gains[1, :rows],
-        g_gate,
-        g_up,
-        g_down,
+        g_gate.astype(F32),
+        g_up.astype(F32),
+        g_down.astype(F32),
     )
 
 

time: 935 us -> 858 us (0.918); the launches traced: 916 us -> 850 us
  Pallas kernels: 690 us -> 602 us
  waiting for transfers between devices: 21.9 us -> 101 us
  matrix products: 119 us -> 50.4 us
  other arithmetic: 41.3 us -> 55.4 us
    pallas_call x2 -> x1, Pallas kernels: 178 us -> 109 us  [experts_out(): pl.pallas_call(partial(experts_out_kernel, count, CAP), out_shape=[thin,...]
    reduce_scatter x3, waiting for transfers between devices: 0.01 us -> 62.1 us  [spread(): return lax.psum_scatter(part, 'seq', scatter_dimension=1, tiled=True)]
    dot_general x4 -> x0, matrix products: 59.5 us -> none  [the longest x3 53.2 us: outer(): jnp.einsum('ejra,ejrb->eab', left, right, preferred_element_type=F32)]
    pallas_call x1, Pallas kernels: 96 us -> 73.4 us  [middle(): pl.pallas_call(partial(middle_kernel, count, seq_count), out_shape=[jax.S...]
    all_gather x1, waiting for transfers between devices: 19.2 us -> 36.1 us  [on_device(): full_up = lax.all_gather(w_up, 'seq', axis=1, tiled=True)]
    convert_element_type x3 -> x5, other arithmetic: 12.3 us -> 18.8 us  [the longest x2 6.36 us: on_device(): h1 = (x_float * inverse_rms(x_float) * gain_a).astype(BF)]
  transfers between devices with their start and end apart: 7 -> 6, of which waited for: 1 -> 2; matrix products, arithmetic and copies ran while one was open for 17% -> 14% of each run, Pallas kernels for 67% -> 58%
where the time goes in v3:
time: 858 us; the launch traced here: 850 us
  Pallas kernels  602 us (70%)
  waiting for transfers between devices  101 us (12%)
  other arithmetic  55.4 us (6%)
  matrix products  50.4 us (6%)
  local copies, waits for them, and re-layouts  26.3 us (3%)
  between operations  15.5 us (2%)
    pallas_call x1, Pallas kernels, experts_out(): pl.pallas_call(partial(experts_out_kernel, count, CAP), out_shape=[thin,...  109 us
    pallas_call x1, Pallas kernels, turn_back(): pl.pallas_call(partial(turn_kernel, count, seq_count), out_shape=[jax.Sha...  101 us
    pallas_call x1, Pallas kernels, experts_in(): pl.pallas_call(partial(experts_in_kernel, count, CAP), out_shape=[jax.Sha...  91.1 us
    pallas_call x1, Pallas kernels, scatter_end(): pl.pallas_call(partial(end_kernel, count, seq_count), out_shape=shapes, i...  89.4 us
    pallas_call x1, Pallas kernels, gather_start(): pl.pallas_call(partial(start_kernel, count, seq_count), out_shape=shapes,...  85 us
    pallas_call x1, Pallas kernels, middle(): pl.pallas_call(partial(middle_kernel, count, seq_count), out_shape=[jax.S...  73.4 us
    reduce_scatter x3, waiting for transfers between devices, spread(): return lax.psum_scatter(part, 'seq', scatter_dimension=1, tiled=True)  62.1 us
    dot_general x12, matrix products, dot(): lax.dot_general(left, right, (((sides[0],), (sides[1],)), ((), ())), pref...  50.4 us
  transfers between devices with their start and end apart: 6, of which 2 were waited for; matrix products, arithmetic and copies ran while one was open for 14% of the time, Pallas kernels for 58%

profile of v3, /device:TPU:0, one launch (start us, length us, event | category | flops | bytes accessed | tf_op | source)
XLA Modules:
  0.0 850.4 jit_solution(2849075439365790459)
XLA Ops:
  12.1 85.0 %gather_start.1 = (bf16[4,8,64,512]{3,2,1,0:T(8,128)(2,1)}, bf16[4,8,64,512]{3,2,1,0:T(8,128)(2,1)}, bf16[4,8,64,512]{3,2,1,0:T(8,128)(2,1)}, bf16[8,64,2048]{2,...) custom-call(bf16[64,2048]{1,0:T(8,128)(2,1)} %refs_0_.1, ...), custom_call_target="tpu_custom_call" | custom-call | tf_op jit(solution)/shard_map/gather_start/pallas_call | solution.py:248
  97.1 1.5 eq.15
  100.2 3.2 multiply_reduce_fusion
  105.3 2.4 multiply_reduce_fusion.2
  107.7 2.0 copy.109.k_raw
  109.7 5.2 multiply_reduce_fusion.3
  115.0 1.8 copy.108.q_raw
  117.4 7.2 seq_sum.2
  128.6 1.4 copy.117
  129.9 1.4 fusion.15
  133.3 2.2 fusion.16
  135.6 5.9 convolution_convert_fusion.6.v_ref
  141.5 16.5 %attend.1 = (bf16[1024,512]{1,0:T(8,128)(2,1)S(1)}, bf16[1024,512]{1,0:T(8,128)(2,1)S(1)}, bf16[1024,512]{1,0:T(8,128)(2,1)S(1)}) custom-call(f32[1024,512]{1,0:T(8,128)} %copy.108.q_raw, f32[1024,512]{1,0:T(8,128)} %copy.109.k_raw, bf16[1024,512]{1,0:T(8,128)(2,1)} %convolution_convert_fusion.6.v_ref, f32[1024,1]{1,0:T(8,128)S(1)} %copy.110.rq, ...), custom_call_target="tpu_custom_call" | custom-call | tf_op jit(solution)/shard_map/attend/pallas_call | solution.py:935
  158.0 2.3 convolution_convert_fusion
  160.4 73.4 %middle.1 = (f32[256,2048]{1,0:T(8,128)S(1)}, bf16[8,256,2048]{2,1,0:T(8,128)(2,1)S(1)}) custom-call(bf16[4,256,2048]{2,1,0:T(8,128)(2,1)S(1)} %bitcast.94, bf16[256,2048]{1,0:T(8,128)(2,1)S(1)} %bitcast.93), custom_call_target="tpu_custom_call" | custom-call | tf_op jit(solution)/shard_map/middle/pallas_call | solution.py:624
  233.8 3.3 copy-done.2
  240.0 36.1 %all-gather.6.cloned.1.call-done.wu_ref.wu_in = bf16[2,2048,1024]{2,1,0:T(8,128)(2,1)} async-done(((bf16[2,512,1024]{2,1,0:T(8,128)(2,1)}), bf16[2,2048,1024]{2,1,0:T(8,128)(2,1)}) %all-gather.6.cloned.1.call-update) | async-done | bytes 8388624 | tf_op jit(solution)/shard_map/all_gather | solution.py:1693
  276.2 91.1 %experts_in.1 = (bf16[8,256,2048]{2,1,0:T(8,128)(2,1)}, bf16[2,1088,2048]{2,1,0:T(8,128)(2,1)}, bf16[2,1088,2048]{2,1,0:T(8,128)(2,1)}, bf16[2,1088,1024]{2,1,0:...) custom-call(bf16[256,2048]{1,0:T(8,128)(2,1)} %multiply_convert_fusi, ...), custom_call_target="tpu_custom_call" | custom-call | tf_op jit(solution)/shard_map/experts_in/pallas_call | solution.py:1256
  367.3 108.9 %experts_out.1 = (bf16[2,1088,1024]{2,1,0:T(8,128)(2,1)}, bf16[2,1088,1024]{2,1,0:T(8,128)(2,1)}, bf16[2,1088,1024]{2,1,0:T(8,128)(2,1)}, bf16[8,256,2048]{2,1,0...) custom-call(bf16[2,1088,2048]{2,1,0:T(8,128)(2,1)} %get-tuple-element.72.y_in, ...), custom_call_target="tpu_custom_call" | custom-call | tf_op jit(solution)/shard_map/experts_out/pallas_call | solution.py:1592
  477.5 2.3 fusion.8
  479.8 1.7 fusion.27.x_ref
  481.5 101.3 %turn_back.1 = (bf16[4,256,2048]{2,1,0:T(8,128)(2,1)}, bf16[256,2048]{1,0:T(8,128)(2,1)}, bf16[2,2048,1024]{2,1,0:T(8,128)(2,1)}, bf16[2,2048,1024]{2,1,0:T(8,128)(2,1)}, f32[16,2048]{1,0:T(8,128)}) custom-call(bf16[256,2048]{1,0:T(8,128)(2,1)} %fusion.27.x_ref, bf16[8,256,2048]{2,1,0:T(8,128)(2,1)} %get-tuple-element.79.parts_ref, ...), custom_call_target="tpu_custom_call" | custom-call | flops 60000002048 | bytes 200000000 | tf_op jit(solution)/shard_map/turn_back/pallas_call | solution.py:848
  583.5 5.4 fusion.1
  588.8 1.9 concatenate.19
  590.7 1.3 copy.130
  592.0 6.3 convolution_convert_fusion.5.do_ref
  598.3 22.7 %attend_back.1 = (f32[1024,512]{1,0:T(8,128)}, f32[1024,512]{1,0:T(8,128)}, bf16[1024,512]{1,0:T(8,128)(2,1)}, f32[1024,2]{1,0:T(8,128)}, f32[1,512]{1,0:T(1,128)}, /*index=5*/f32[1,512]{1,0:T(1,128)}) custom-call(bf16[1024,512]{1,0:T(8,128)(2,1)} %copy-done.8, bf16[1024,512]{1,0:T(8,128)(2,1)} %copy-done.9, ...), custom_call_target="tpu_custom_call" | custom-call | tf_op jit(solution)/shard_map/attend_back/pallas_call | solution.py:1030
  621.6 1.3 reduce.21
  623.0 1.3 reduce.22
  625.1 2.9 maximum_maximum_fusion.refs_4_
  628.0 6.0 convolution_convert_fusion.1
  634.0 3.8 convolution_convert_fusion.2
  638.5 6.1 seq_sum.3
  645.4 4.5 subtract_convert_fusion
  649.9 2.4 fusion.30
  652.3 2.4 fusion.31
  654.7 3.7 convolution_convert_fusion.4
  658.4 3.7 convolution_convert_fusion.3
  662.1 6.3 add_convert_fusion
  668.4 89.4 %scatter_end.1 = (bf16[64,2048]{1,0:T(8,128)(2,1)}, bf16[64,2048]{1,0:T(8,128)(2,1)}, bf16[64,2048]{1,0:T(8,128)(2,1)}, bf16[64,2048]{1,0:T(8,128)(2,1)}, f32[64...) custom-call(bf16[4,8,64,512]{3,2,1,0:T(8,128)(2,1)} %bitcast.109, bf16[4,8,64,512]{3,2,1,0:T(8,128)(2,1)} %bitcast.110, ...), custom_call_target="tpu_custom_call" | custom-call | tf_op jit(solution)/shard_map/scatter_end/pallas_call | solution.py:522
  757.9 1.8 convert_element_type.193
  759.6 1.4 copy.132
  761.1 4.1 convert_element_type.200
  765.3 4.3 convert_element_type.198
  770.3 1.3 add_reduce_fusion
  774.1 2.9 fusion.12
  776.9 62.1 %reduce-scatter.8.cloned.1.call-done = bf16[2,512,1024]{2,1,0:T(8,128)(2,1)} async-done(((bf16[2,2048,1024]{2,1,0:T(8,128)(2,1)}), bf16[2,512,1024]{2,1,0:T(8,128)(2,1)}) %reduce-scatter.8.cloned.1.call-update) | async-done | bytes 2097168 | tf_op jit(solution)/shard_map/reduce_scatter | solution.py:1756
  839.0 4.1 convert_element_type.199
  (182 shorter events, 25.5 us)
Async XLA Ops:
  7.2 232.8 %all-gather.4.cloned.1.call-start = ((), (), s32[]{:S(2)}) async-start(), calls=%async_computation.3 | async-start | bytes 10485760 | tf_op jit(solution)/shard_map/all_gather | solution.py:1692
  8.0 2.8 copy-start.44
  8.0 2.8 copy-start.45
  8.0 268.2 %all-gather.6.cloned.1.call-start = ((), (), s32[]{:S(2)}) async-start(), calls=%async_computation.4 | async-start | bytes 10485760 | tf_op jit(solution)/shard_map/all_gather | solution.py:1693
  8.7 358.6 %all-gather.8.cloned.1.call-start = ((), (), s32[]{:S(2)}) async-start(), calls=%async_computation.5 | async-start | bytes 10485760 | tf_op jit(solution)/shard_map/all_gather | solution.py:1694
  9.5 628.3 %reduce-scatter.4.cloned.1.call-start = ((), (), s32[]{:S(2)}) async-start(), calls=%async_computation.6 | async-start | bytes 10485760 | tf_op jit(solution)/shard_map/reduce_scatter | solution.py:1756
  97.1 2.5 copy-start.25
  100.2 3.5 copy-start.18
  104.7 3.0 copy-start.28
  115.0 11.8 %copy-start.10 = (s32[1,1024]{1,0:T(1,128)S(1)}, s32[1,1024]{1,0:T(1,128)}, u32[]{:S(2)}) copy-start(s32[1,1024]{1,0:T(1,128)} %doc_row.3) | copy-start | bytes 12292
  125.6 15.8 %copy-start.5 = (f32[1024,1]{1,0:T(8,128)}, f32[1024,1]{1,0:T(8,128)S(1)}, u32[]{:S(2)}) copy-start(f32[1024,1]{1,0:T(8,128)S(1)} %copy.110.rq) | copy-start | bytes 12292
  125.8 15.6 %copy-start.6 = (f32[1024,1]{1,0:T(8,128)}, f32[1024,1]{1,0:T(8,128)S(1)}, u32[]{:S(2)}) copy-start(f32[1024,1]{1,0:T(8,128)S(1)} %copy.111.rk) | copy-start | bytes 12292
  126.8 14.7 %copy-start.11 = (f32[1,512]{1,0:T(1,128)}, f32[1,512]{1,0:T(1,128)S(1)}, u32[]{:S(2)}) copy-start(f32[1,512]{1,0:T(1,128)S(1)} %reshape.299.gq) | copy-start | bytes 6148
  126.8 14.6 %copy-start.12 = (f32[1,512]{1,0:T(1,128)}, f32[1,512]{1,0:T(1,128)S(1)}, u32[]{:S(2)}) copy-start(f32[1,512]{1,0:T(1,128)S(1)} %reshape.300.gk) | copy-start | bytes 6148
  127.1 14.4 %copy-start.7 = (s32[1024,1]{1,0:T(8,128)}, s32[1024,1]{1,0:T(8,128)S(1)}, u32[]{:S(2)}) copy-start(s32[1024,1]{1,0:T(8,128)S(1)} %copy.112.doc_col) | copy-start | bytes 12292
  131.3 10.1 %copy-start.21 = (s32[8,2,256]{1,2,0:T(8,128)}, s32[8,2,256]{1,2,0:T(8,128)S(1)}, u32[]{:S(2)}) copy-start(s32[8,2,256]{1,2,0:T(8,128)S(1)} %fusion.15) | copy-start | bytes 49156
  133.1 2.5 copy-start.29
  135.5 5.9 copy-start.3
  135.5 5.9 copy-start.4
  141.5 16.5 %copy-start.51 = (bf16[8,64,2048]{2,1,0:T(8,128)(2,1)S(1)}, bf16[8,64,2048]{2,1,0:T(8,128)(2,1)}, u32[]{:S(2)}) copy-start(bf16[8,64,2048]{2,1,0:T(8,128)(2,1)} %get-tuple-element.68) | copy-start | bytes 6291460
  158.0 2.4 copy-start.8
  158.0 2.4 copy-start.9
  158.0 2.4 copy-start.13
  160.4 76.7 %copy-start.19 = (bf16[1,256,2048]{2,1,0:T(8,128)(2,1)S(1)}, bf16[1,256,2048]{2,1,0:T(8,128)(2,1)}, u32[]{:S(2)}) copy-start(bf16[1,256,2048]{2,1,0:T(8,128)(2,1)} %param.16) | copy-start | bytes 3145732
  233.8 3.3 copy-start.2
  476.3 3.5 copy-start.1
  476.3 288.9 %reduce-scatter.6.cloned.1.call-start = ((), (), s32[]{:S(2)}) async-start(), calls=%async_computation.7 | async-start | bytes 10485760 | tf_op jit(solution)/shard_map/reduce_scatter | solution.py:1756
  476.5 3.2 copy-start.16
  582.8 256.2 %reduce-scatter.8.cloned.1.call-start = ((), (), s32[]{:S(2)}) async-start(), calls=%async_computation.8 | async-start | bytes 10485760 | tf_op jit(solution)/shard_map/reduce_scatter | solution.py:1756
  583.5 7.2 copy-start.39
  621.1 6.9 copy-start.14
  628.0 6.0 copy-start.26
  628.0 6.0 copy-start.31
  634.0 3.8 copy-start.35
  645.3 4.5 copy-start.50
  652.3 2.5 copy-start.27
  765.2 4.4 copy-start.40
  765.2 5.1 copy-start.32
  765.2 5.1 copy-start.33
  765.2 5.1 copy-start.34
  765.2 5.1 copy-start.36
  765.2 5.1 copy-start.37
  765.2 5.1 copy-start.38
  765.3 8.8 %copy-start.30 = (bf16[256,2048]{1,0:T(8,128)(2,1)S(1)}, bf16[256,2048]{1,0:T(8,128)(2,1)}, u32[]{:S(2)}) copy-start(bf16[256,2048]{1,0:T(8,128)(2,1)} %get-tuple-element.85) | copy-start | bytes 3145732
  769.6 2.6 copy-start.20
  769.6 2.6 copy-start.24
  771.6 2.4 copy-start.17
  771.6 2.4 copy-start.23
  (10 other events, 18.0 us)
Sparse Core Ops, SparseCore 0:
  9.9 135.5 all-gather.3
  147.3 128.8 all-gather.5
  278.0 87.6 all-gather.7
  476.4 137.6 reduce-scatter.3
  617.4 128.9 reduce-scatter.5
  749.3 89.6 reduce-scatter.7

commit v4 on v3

--- a/solution.py
+++ b/solution.py
@@ -156,7 +156,7 @@
     outs = refs[8:15]
     rows_out = refs[15]
     holds = refs[16:24]
-    send_x, recv_x, local, send_r, send_l, send_s, recv = refs[24:]
+    send_x, recv_x, local, send_r, send_l, send_s, recv, send_y, recv_y = refs[24:]
     places = where_am_i()
     i = places[0]
     here = lax.axis_index("seq")
@@ -192,9 +192,8 @@
     for a in (4, 0, 1, 2):
         for d in range(1, seq_count):
             piece(a, d).start()
-    for d in range(1, seq_count):
-        peer = lax.rem(here + d, seq_count)
-        remote(rows, rows_out.at[here], send_x.at[4, d - 1], recv_x.at[4, d - 1], seq=peer).start()
+    gather = SeqGather(seq_count, rows, rows_out, send_y, recv_y)
+    gather.begin()
     axes = [1, 1, 1, 0, 1, 0, 0]
     for a in (3, 5, 6, 4, 0, 1, 2):
         pltpu.make_async_copy(own[a], holds[a], local.at[a]).wait()
@@ -212,11 +211,11 @@
     pltpu.make_async_copy(holds[7], rows_out.at[here], local.at[7]).start()
     for t in range(1, count):
         line.forward(t)
+        if t == 1:
+            gather.relay()
     line.finish()
     pltpu.make_async_copy(holds[7], rows_out.at[here], local.at[7]).wait()
-    for d in range(1, seq_count):
-        origin = lax.rem(here + seq_count - d, seq_count)
-        remote(rows, rows_out.at[origin], send_x.at[4, d - 1], recv_x.at[4, d - 1], seq=origin).wait()
+    gather.finish()
     for a in (4, 0, 1, 2):
         for d in range(1, seq_count):
             piece(a, d).wait_send()
@@ -251,8 +250,9 @@
         in_specs=[pl.BlockSpec(memory_space=ANY)] * 8,
         out_specs=[pl.BlockSpec(memory_space=ANY)] * 8,
         scratch_shapes=holds
-        + [DMA((5, seq_count - 1)), DMA((5, seq_count - 1)), DMA((8,))]
-        + line_sems(7, count),
+        + [DMA((4, seq_count - 1)), DMA((4, seq_count - 1)), DMA((8,))]
+        + line_sems(7, count)
+        + seq_gather_sems(seq_count),
         compiler_params=pltpu.CompilerParams(collective_id=collective, has_side_effects=True),
         name="gather_start",
     )(*arrays)
@@ -439,7 +439,7 @@
     width = sources[0].shape[3]
     line = LineScatter(count, places, sources, [1, 1, 1, 0, 1, 0], bufs, sems)
     line.begin_loads()
-    seq.take.start()
+    seq.begin_loads()
     greet(count, places, seq_count)
     seq.begin()
     line.begin()
@@ -473,7 +473,12 @@
                 piece(a, q, d).start()
             pltpu.make_async_copy(own[a].at[q, here], at_home(a, here), local.at[a]).start()
 
-    line.run(after)
+    def between(step):
+        @pl.when(step == 0)
+        def _():
+            seq.relay()
+
+    line.run(after, between)
     seq.total(sum_ref)
     for q in range(count):
 
@@ -550,33 +555,84 @@
 class SeqScatter:
     def __init__(self, seq_count, x_ref, own, inbox, send, recv, local):
         here = lax.axis_index("seq")
-        self.own, self.inbox, self.count = own, inbox, seq_count
-        self.take = pltpu.make_async_copy(x_ref.at[here], own, local)
-        self.copies = []
-        for d in range(1, seq_count):
-            peer = lax.rem(here + d, seq_count)
-            self.copies.append(
-                remote(x_ref.at[peer], inbox.at[d - 1], send.at[d - 1], recv.at[d - 1], seq=peer)
-            )
+        self.own, self.inbox, self.local, self.count = own, inbox, local, seq_count
+        self.take = pltpu.make_async_copy(x_ref.at[here], own, local.at[0])
+        rows = own.shape[0]
+        self.half = rows // 2
+        low, high = pl.ds(0, self.half), pl.ds(self.half, self.half)
+        if seq_count != 4:
+            self.copies = []
+            for d in range(1, seq_count):
+                peer = lax.rem(here + d, seq_count)
+                self.copies.append(
+                    remote(x_ref.at[peer], inbox.at[d - 1], send.at[d - 1], recv.at[d - 1], seq=peer)
+                )
+            return
+        beside = here + 1 - 2 * lax.rem(here, 2)
+        across = lax.rem(here + 2, 4)
+        corner = 3 - here
+        self.loads = [
+            pltpu.make_async_copy(x_ref.at[across, low], inbox.at[3, low], local.at[1]),
+            pltpu.make_async_copy(x_ref.at[beside, high], inbox.at[3, high], local.at[2]),
+        ]
+        plans = (
+            (x_ref.at[corner, low], inbox.at[2, low], beside),
+            (x_ref.at[corner, high], inbox.at[2, high], across),
+            (x_ref.at[beside, low], inbox.at[0, low], beside),
+            (x_ref.at[across, high], inbox.at[1, high], across),
+            (inbox.at[3, low], inbox.at[1, low], across),
+            (inbox.at[3, high], inbox.at[0, high], beside),
+        )
+        self.copies = [
+            remote(src, dst, send.at[n], recv.at[n], seq=peer) for n, (src, dst, peer) in enumerate(plans)
+        ]
+
+    def begin_loads(self):
+        self.take.start()
+        if self.count == 4:
+            for load in self.loads:
+                load.start()
 
     def begin(self):
-        for copy in self.copies:
+        for copy in self.copies[:4] if self.count == 4 else self.copies:
             copy.start()
+
+    def strips(self, start, rows, body):
+        step = min(32, rows)
+
+        @pl.loop(0, rows // step)
+        def _(k):
+            body(pl.ds(pl.multiple_of(start + k * step, step), step))
+
+    def relay(self):
+        if self.count != 4:
+            return
+        inbox = self.inbox
+
+        def add(strip):
+            inbox[3, strip, :] = (
+                inbox[3, strip, :].astype(F32) + inbox[2, strip, :].astype(F32)
+            ).astype(inbox.dtype)
+
+        for n, start in ((0, 0), (1, self.half)):
+            self.loads[n].wait()
+            self.copies[n].wait_recv()
+            self.strips(start, self.half, add)
+            self.copies[4 + n].start()
 
     def total(self, o_ref):
         self.take.wait()
-        for copy in self.copies:
+        for copy in self.copies[2:] if self.count == 4 else self.copies:
             copy.wait_recv()
-        rows = self.own.shape[0]
-        step = min(32, rows)
-
-        @pl.loop(0, rows // step)
-        def _(k):
-            strip = pl.ds(pl.multiple_of(k * step, step), step)
+        parts = 2 if self.count == 4 else self.count - 1
+
+        def add(strip):
             total = self.own[strip, :].astype(F32)
-            for d in range(self.count - 1):
+            for d in range(parts):
                 total += self.inbox[d, strip, :].astype(F32)
             o_ref[strip, :] = total
+
+        self.strips(0, self.own.shape[0], add)
 
     def finish(self):
         for copy in self.copies:
@@ -584,13 +640,68 @@
 
 
 def seq_scatter_scratch(block, dtype, seq_count):
+    boxes = 4 if seq_count == 4 else seq_count - 1
+    copies = 6 if seq_count == 4 else seq_count - 1
     return [
         pltpu.VMEM(block, dtype),
-        pltpu.VMEM((seq_count - 1,) + block, dtype),
-        DMA((seq_count - 1,)),
-        DMA((seq_count - 1,)),
-        DMA,
+        pltpu.VMEM((boxes,) + block, dtype),
+        DMA((copies,)),
+        DMA((copies,)),
+        DMA((3,)),
     ]
+
+
+class SeqGather:
+    def __init__(self, seq_count, x_ref, o_ref, send, recv):
+        here = lax.axis_index("seq")
+        self.count = seq_count
+        rows = x_ref.shape[0]
+        low, high = pl.ds(0, rows // 2), pl.ds(rows // 2, rows // 2)
+        if seq_count != 4:
+            peers = [lax.rem(here + d, seq_count) for d in range(1, seq_count)]
+            origins = [lax.rem(here + seq_count - d, seq_count) for d in range(1, seq_count)]
+            out = [(x_ref, o_ref.at[here], peer) for peer in peers]
+            landed = [o_ref.at[origin] for origin in origins]
+        else:
+            beside = here + 1 - 2 * lax.rem(here, 2)
+            across = lax.rem(here + 2, 4)
+            corner = 3 - here
+            out = [
+                (x_ref, o_ref.at[here], beside),
+                (x_ref, o_ref.at[here], across),
+                (o_ref.at[across, low], o_ref.at[across, low], beside),
+                (o_ref.at[beside, high], o_ref.at[beside, high], across),
+            ]
+            landed = [o_ref.at[beside], o_ref.at[across], o_ref.at[corner, low], o_ref.at[corner, high]]
+        self.sends = [
+            remote(src, dst, send.at[n], recv.at[n], seq=peer) for n, (src, dst, peer) in enumerate(out)
+        ]
+        self.lands = [
+            remote(ref, ref, send.at[n], recv.at[n], seq=out[n][2]) for n, ref in enumerate(landed)
+        ]
+
+    def begin(self):
+        for copy in self.sends[:2] if self.count == 4 else self.sends:
+            copy.start()
+
+    def relay(self):
+        if self.count == 4:
+            for n in (0, 1):
+                self.lands[n].wait_recv()
+            for n in (2, 3):
+                self.sends[n].start()
+
+    def finish(self):
+        for n, copy in enumerate(self.lands):
+            if self.count != 4 or n > 1:
+                copy.wait_recv()
+        for copy in self.sends:
+            copy.wait_send()
+
+
+def seq_gather_sems(seq_count):
+    copies = 4 if seq_count == 4 else seq_count - 1
+    return [DMA((copies,)), DMA((copies,))]
 
 
 def middle_kernel(
@@ -599,7 +710,7 @@
     places = where_am_i()
     i = places[0]
     seq = SeqScatter(seq_count, x_ref, own, inbox, xs, xr, xl)
-    seq.take.start()
+    seq.begin_loads()
     take = pltpu.make_async_copy(dy_ref, hold, local.at[0])
     take.start()
     greet(count, places, seq_count)
@@ -612,6 +723,8 @@
     line.first(0)
     for t in range(1, count):
         line.forward(t)
+        if t == 1:
+            seq.relay()
     seq.total(o_ref)
     line.finish()
     seq.finish()
@@ -674,98 +787,49 @@
     )(value)
 
 
-class GateUpGrads:
-    def __init__(self, ins, outs, scratch, steps):
-        self.ins, self.outs = ins, outs
-        self.held, self.staged, self.in_sem, self.out_sem = scratch
-        self.experts, self.width, self.hidden = outs[0].shape
-        self.tile = self.staged[0].shape[1]
-        self.tiles = self.width // self.tile
-        self.units = self.experts * self.tiles
-        self.share = -(-self.units // steps)
-
-    def fetch(self, n, e):
-        return pltpu.make_async_copy(self.ins[n].at[e], self.held[n].at[e], self.in_sem.at[n, e])
-
-    def begin(self):
-        for e in range(self.experts):
-            for n in range(3):
-                self.fetch(n, e).start()
-        self.logits().start()
-        self.pair(0).start()
-
-    def logits(self):
-        return pltpu.make_async_copy(self.ins[4], self.held[4], self.in_sem.at[3, 0])
+class RouterGrad:
+    def __init__(self, tokens_in, logits_in, out, tokens, logits, sems):
+        self.tokens_in, self.logits_in, self.out = tokens_in, logits_in, out
+        self.tokens, self.logits, self.sems = tokens, logits, sems
+
+    def take(self):
+        return pltpu.make_async_copy(self.logits_in, self.logits, self.sems.at[2])
 
     def pair(self, q):
         buf = lax.rem(q, 2)
-        src = self.ins[3].at[pl.ds(2 * q, 2)]
-        return pltpu.make_async_copy(src, self.held[3].at[buf], self.in_sem.at[4, buf])
-
-    def put(self, n, u, buf):
-        rows = pl.ds(pl.multiple_of(lax.rem(u, self.tiles) * self.tile, self.tile), self.tile)
-        target = self.outs[n].at[u // self.tiles, rows]
-        return pltpu.make_async_copy(self.staged[n].at[buf], target, self.out_sem.at[n, buf])
-
-    def between(self, step):
-        over_rows = (((0,), (0,)), ((), ()))
-        rows, gates, ups, tokens, logits = self.held
-
-        @pl.loop(step * self.share, jnp.minimum((step + 1) * self.share, self.units))
-        def _(u):
-            e = u // self.tiles
-            buf = lax.rem(u, 2)
-
-            @pl.when(lax.rem(u, self.tiles) == 0)
+        src = self.tokens_in.at[pl.ds(2 * q, 2)]
+        return pltpu.make_async_copy(src, self.tokens.at[buf], self.sems.at[buf])
+
+    def begin(self):
+        self.take().start()
+        self.pair(0).start()
+
+    def run(self):
+        self.take().wait()
+        self.out[...] = jnp.zeros_like(self.out)
+        width = self.out.shape[1]
+        block = 512
+        pairs = self.tokens_in.shape[0] // 2
+
+        @pl.loop(0, pairs)
+        def _(q):
+            self.pair(q).wait()
+
+            @pl.when(q + 1 < pairs)
             def _():
-                for n in range(3):
-                    self.fetch(n, e).wait()
-
-            @pl.when(u >= 2)
-            def _():
-                self.put(0, u - 2, buf).wait()
-                self.put(1, u - 2, buf).wait()
-
-            cols = pl.ds(pl.multiple_of(lax.rem(u, self.tiles) * self.tile, self.tile), self.tile)
-            left = rows[e, :, cols]
-            for n, right in ((0, gates), (1, ups)):
-                self.staged[n][buf] = lax.dot_general(
-                    left, right[e], over_rows, preferred_element_type=F32
-                ).astype(BF)
-                self.put(n, u, buf).start()
-
-        @pl.when(step == 0)
-        def _():
-            self.logits().wait()
-            total_ref = self.outs[2]
-            total_ref[...] = jnp.zeros_like(total_ref)
-            block = 512
-            pairs = self.ins[3].shape[0] // 2
-
-            @pl.loop(0, pairs)
-            def _(q):
-                self.pair(q).wait()
-
-                @pl.when(q + 1 < pairs)
-                def _():
-                    self.pair(q + 1).start()
-
-                buf = lax.rem(q, 2)
-
-                @pl.loop(0, self.width // block)
-                def _(n):
-                    cols = pl.ds(pl.multiple_of(n * block, block), block)
-                    total = total_ref[:, cols]
-                    for j in range(2):
-                        total += jnp.dot(
-                            logits[2 * q + j], tokens[buf, j, :, cols], preferred_element_type=F32
-                        )
-                    total_ref[:, cols] = total
-
-    def finish(self):
-        for u in (self.units - 2, self.units - 1):
-            for n in range(2):
-                self.put(n, u, u % 2).wait()
+                self.pair(q + 1).start()
+
+            buf = lax.rem(q, 2)
+
+            @pl.loop(0, width // block)
+            def _(n):
+                cols = pl.ds(pl.multiple_of(n * block, block), block)
+                total = self.out[:, cols]
+                for j in range(2):
+                    total += jnp.dot(
+                        self.logits[2 * q + j], self.tokens[buf, j, :, cols], preferred_element_type=F32
+                    )
+                self.out[:, cols] = total
 
 
 def turn_kernel(
@@ -773,29 +837,25 @@
     seq_count,
     x_ref,
     parts_ref,
-    in0,
-    in1,
-    in2,
-    in3,
-    in4,
+    left_ref,
+    right_ref,
+    h2_ref,
+    logits_ref,
     o_ref,
     sum_ref,
-    out0,
-    out1,
-    out2,
+    grad_ref,
+    router_ref,
     hold,
     send,
     recv,
     one,
-    held0,
-    held1,
-    held2,
-    held3,
-    held4,
-    staged0,
-    staged1,
-    in_sem,
-    out_sem,
+    tiles_in,
+    held,
+    staged,
+    outer_sem,
+    tokens,
+    logits,
+    router_sem,
     own,
     sib,
     inbox,
@@ -804,20 +864,16 @@
     places = where_am_i()
     here = lax.axis_index("seq")
     line = LineScatter(count, places, [parts_ref], [0], ([own], [sib], [inbox]), sems)
-    grads = GateUpGrads(
-        (in0, in1, in2, in3, in4),
-        (out0, out1, out2),
-        ((held0, held1, held2, held3, held4), (staged0, staged1), in_sem, out_sem),
-        count - 1,
-    )
+    grads = OuterGrads(left_ref, right_ref, grad_ref, (tiles_in, held, staged, outer_sem), count - 1)
+    router = RouterGrad(h2_ref, logits_ref, router_ref, tokens, logits, router_sem)
     line.begin_loads()
     take = pltpu.make_async_copy(x_ref, hold, one)
     take.start()
     grads.begin()
+    router.begin()
     greet(count, places, seq_count)
-    for d in range(1, seq_count):
-        peer = lax.rem(here + d, seq_count)
-        remote(x_ref, o_ref.at[here], send.at[d - 1], recv.at[d - 1], seq=peer).start()
+    rows = SeqGather(seq_count, x_ref, o_ref, send, recv)
+    rows.begin()
     line.begin()
     take.wait()
     put = pltpu.make_async_copy(hold, o_ref.at[here], one)
@@ -828,44 +884,49 @@
         out.start()
         out.wait()
 
-    line.run(after, grads.between)
+    def between(step):
+        @pl.when(step == 1)
+        def _():
+            rows.relay()
+
+        grads.between(step)
+
+        @pl.when(step == 0)
+        def _():
+            router.run()
+
+    line.run(after, between)
     grads.finish()
     put.wait()
-    for d in range(1, seq_count):
-        origin = lax.rem(here + seq_count - d, seq_count)
-        remote(x_ref, o_ref.at[origin], send.at[d - 1], recv.at[d - 1], seq=origin).wait()
+    rows.finish()
     line.finish()
 
 
-def turn_back(block, parts, expert_in, d_gate, d_up, h2_all, logits, seq_count, shards, collective):
+def turn_back(block, parts, expert_in, d_up, h2_all, logits, seq_count, shards, collective):
     count = shards // 2
     part = parts.shape[1:]
     model_width = part[1]
-    local_experts, slots, hidden = d_gate.shape
-    tile = 512
-    grad = jax.ShapeDtypeStruct((local_experts, model_width, hidden), BF)
+    local_experts, slots, hidden = d_up.shape
     anywhere = pl.BlockSpec(memory_space=ANY)
     return pl.pallas_call(
         partial(turn_kernel, count, seq_count),
         out_shape=[
             jax.ShapeDtypeStruct((seq_count,) + block.shape, block.dtype),
             jax.ShapeDtypeStruct(part, parts.dtype),
-            grad,
-            grad,
+            jax.ShapeDtypeStruct((local_experts, model_width, hidden), BF),
             jax.ShapeDtypeStruct((logits.shape[1], model_width), F32),
         ],
-        in_specs=[anywhere] * 7,
-        out_specs=[anywhere] * 4 + [pl.BlockSpec(memory_space=pltpu.VMEM)],
-        scratch_shapes=[
-            pltpu.VMEM(block.shape, block.dtype),
-            DMA((seq_count - 1,)),
-            DMA((seq_count - 1,)),
-            DMA,
+        in_specs=[anywhere] * 6,
+        out_specs=[anywhere] * 3 + [pl.BlockSpec(memory_space=pltpu.VMEM)],
+        scratch_shapes=[pltpu.VMEM(block.shape, block.dtype)]
+        + seq_gather_sems(seq_count)
+        + [DMA]
+        + outer_scratch(d_up, 512)
+        + [
+            pltpu.VMEM((2, 2) + h2_all.shape[1:], BF),
+            pltpu.VMEM(logits.shape, BF),
+            DMA((3,)),
         ]
-        + [pltpu.VMEM(x.shape, BF) for x in (expert_in, d_gate, d_up)]
-        + [pltpu.VMEM((2, 2) + h2_all.shape[1:], BF), pltpu.VMEM(logits.shape, BF)]
-        + [pltpu.VMEM((2, tile, hidden), BF)] * 2
-        + [DMA((5, max(2, local_experts))), DMA((2, 2))]
         + [pltpu.VMEM((count,) + part, BF)] * 2
         + [pltpu.VMEM((count + 1,) + part, BF)]
         + [DMA((1, count))] * 7,
@@ -874,7 +935,7 @@
         ),
         cost_estimate=pl.CostEstimate(flops=60_000_000_000, bytes_accessed=200_000_000, transcendentals=0),
         name="turn_back",
-    )(block, parts, expert_in, d_gate, d_up, h2_all, logits)
+    )(block, parts, expert_in, d_up, h2_all, logits)
 
 
 def half_sign(shape):
@@ -1284,39 +1345,236 @@
     )(h2, dy_all, targets, router_t, w_gate, w_up)
 
 
-class StagedScatter(LineScatter):
-    def __init__(self, count, places, stage, bufs, sems):
-        super().__init__(count, places, [None], [0], bufs, sems)
-        self.stage = stage
-
-    def to_sib(self, a, q):
-        sib = self.places[2]
-        return remote(self.stage, self.sib[a].at[q], self.sems[2].at[a, q], self.sems[5].at[a, q], fsdp=sib)
-
-    def ready(self, a, q):
-        self.to_sib(a, q).wait_recv()
-
-    def finish(self):
-        i, p, sib = self.places
-        for q in range(self.count):
-
-            @pl.when(q > p)
-            def _():
-                self.right(0, q).wait_send()
-
-            @pl.when(q < p)
-            def _():
-                self.left(0, q).wait_send()
-
-
-def experts_out_kernel(
-    count,
+def experts_mid_kernel(
     cap,
     y_in,
     act_in,
     by_up_in,
     by_gate_in,
     gate_slots,
+    wd_in,
+    gated_out,
+    d_gate_out,
+    d_up_out,
+    dots_ref,
+    g_down_out,
+    wd,
+    ys,
+    acts,
+    by_ups,
+    by_gates,
+    gated,
+    d_gate,
+    d_up,
+    staged,
+    in_sem,
+    out_sem,
+    grad_sem,
+):
+    local_experts, hidden, model_width = wd_in.shape
+    count = gate_slots.shape[1]
+    slots = ys.shape[1]
+    over_lanes = (((1,), (1,)), ((), ()))
+    over_rows = (((0,), (0,)), ((), ()))
+    inputs = ((wd_in, wd), (y_in, ys), (act_in, acts), (by_up_in, by_ups), (by_gate_in, by_gates))
+    results = ((gated, gated_out), (d_gate, d_gate_out), (d_up, d_up_out))
+    wide = 256
+    tile = staged.shape[1]
+
+    def fetch(n, e):
+        return pltpu.make_async_copy(inputs[n][0].at[e], inputs[n][1].at[e], in_sem.at[n, e])
+
+    def store(n, e):
+        return pltpu.make_async_copy(results[n][0].at[e], results[n][1].at[e], out_sem.at[n, e])
+
+    def put_grad(e, n, buf):
+        rows = pl.ds(pl.multiple_of(n * tile, tile), tile)
+        return pltpu.make_async_copy(staged.at[buf], g_down_out.at[e, rows], grad_sem.at[buf])
+
+    for e in range(local_experts):
+        for n in range(5):
+            fetch(n, e).start()
+    for e in range(local_experts):
+        for n in range(5):
+            fetch(n, e).wait()
+        gate = jnp.concatenate([gate_slots[e, q] for q in range(count)], axis=0)
+
+        def step(n, dot):
+            cols = pl.ds(pl.multiple_of(n * wide, wide), wide)
+            grad_act = lax.dot_general(ys[e], wd[e, cols, :], over_lanes, preferred_element_type=F32)
+            act = acts[e, :, cols].astype(F32)
+            dot = dot + jnp.sum(act * grad_act, axis=1, keepdims=True)
+            grad_act = grad_act * gate
+            gated[e, :, cols] = (act * gate).astype(BF)
+            d_up[e, :, cols] = (grad_act * by_ups[e, :, cols].astype(F32)).astype(BF)
+            d_gate[e, :, cols] = (grad_act * by_gates[e, :, cols].astype(F32)).astype(BF)
+            return dot
+
+        dot = lax.fori_loop(0, hidden // wide, step, jnp.zeros((slots, 1), F32))
+        for q in range(count):
+            dots_ref[e, q] = dot[2 * cap * q : 2 * cap * (q + 1)]
+        for n in range(3):
+            store(n, e).start()
+
+        @pl.loop(0, hidden // tile // 2)
+        def _(m):
+            for buf in range(2):
+                n = 2 * m + buf
+
+                def wait_last():
+                    put_grad(e, n, buf).wait()
+
+                if e > 0:
+                    wait_last()
+                else:
+                    pl.when(m > 0)(wait_last)
+                cols = pl.ds(pl.multiple_of(n * tile, tile), tile)
+                staged[buf] = lax.dot_general(
+                    gated[e, :, cols], ys[e], over_rows, preferred_element_type=F32
+                ).astype(BF)
+                put_grad(e, n, buf).start()
+
+    for buf in range(2):
+        put_grad(0, 0, buf).wait()
+    for e in range(local_experts):
+        for n in range(3):
+            store(n, e).wait()
+
+
+def experts_mid(grads, act, by_up, by_gate, gate_slots, w_down):
+    local_experts, slots, model_width = grads.shape
+    anywhere = pl.BlockSpec(memory_space=ANY)
+    vmem = pl.BlockSpec(memory_space=pltpu.VMEM)
+    thin = jax.ShapeDtypeStruct(act.shape, BF)
+    return pl.pallas_call(
+        partial(experts_mid_kernel, CAP),
+        out_shape=[
+            thin,
+            thin,
+            thin,
+            jax.ShapeDtypeStruct(gate_slots.shape, F32),
+            jax.ShapeDtypeStruct(w_down.shape, BF),
+        ],
+        in_specs=[anywhere] * 4 + [vmem, anywhere],
+        out_specs=[anywhere] * 3 + [vmem, anywhere],
+        scratch_shapes=[pltpu.VMEM(w_down.shape, BF), pltpu.VMEM(grads.shape, BF)]
+        + [pltpu.VMEM(act.shape, BF)] * 6
+        + [
+            pltpu.VMEM((2, 256, model_width), BF),
+            DMA((5, local_experts)),
+            DMA((3, local_experts)),
+            DMA((2,)),
+        ],
+        compiler_params=pltpu.CompilerParams(vmem_limit_bytes=60 << 20),
+        cost_estimate=pl.CostEstimate(flops=18_000_000_000, bytes_accessed=60_000_000, transcendentals=0),
+        name="experts_mid",
+    )(grads, act, by_up, by_gate, gate_slots, w_down)
+
+
+class StagedScatter(LineScatter):
+    def __init__(self, count, places, stage, bufs, sems):
+        super().__init__(count, places, [None], [0], bufs, sems)
+        self.stage = stage
+
+    def to_sib(self, a, q):
+        sib = self.places[2]
+        return remote(self.stage, self.sib[a].at[q], self.sems[2].at[a, q], self.sems[5].at[a, q], fsdp=sib)
+
+    def ready(self, a, q):
+        self.to_sib(a, q).wait_recv()
+
+    def finish(self):
+        i, p, sib = self.places
+        for q in range(self.count):
+
+            @pl.when(q > p)
+            def _():
+                self.right(0, q).wait_send()
+
+            @pl.when(q < p)
+            def _():
+                self.left(0, q).wait_send()
+
+
+class OuterGrads:
+    def __init__(self, left, right, out, scratch, steps):
+        self.left, self.right, self.out = left, right, out
+        self.tiles_in, self.held, self.staged, self.sems = scratch
+        self.experts, self.width, self.hidden = out.shape
+        self.tile = self.staged.shape[1]
+        self.tiles = self.width // self.tile
+        self.units = self.experts * self.tiles
+        self.share = -(-self.units // steps)
+
+    def span(self, u):
+        start = lax.rem(u, self.tiles) * self.tile
+        return pl.ds(pl.multiple_of(start, self.tile), self.tile)
+
+    def fetch(self, u):
+        src = self.left.at[u // self.tiles, :, self.span(u)]
+        return pltpu.make_async_copy(src, self.tiles_in.at[lax.rem(u, 2)], self.sems.at[0, lax.rem(u, 2)])
+
+    def put(self, u):
+        buf = lax.rem(u, 2)
+        target = self.out.at[u // self.tiles, self.span(u)]
+        return pltpu.make_async_copy(self.staged.at[buf], target, self.sems.at[1, buf])
+
+    def hold(self):
+        return pltpu.make_async_copy(self.right, self.held, self.sems.at[2, 0])
+
+    def begin(self):
+        self.hold().start()
+        self.fetch(0).start()
+
+    def between(self, step):
+        @pl.loop(step * self.share, jnp.minimum((step + 1) * self.share, self.units))
+        def _(u):
+            @pl.when(u == 0)
+            def _():
+                self.hold().wait()
+
+            self.fetch(u).wait()
+
+            @pl.when(u + 1 < self.units)
+            def _():
+                self.fetch(u + 1).start()
+
+            @pl.when(u >= 2)
+            def _():
+                self.put(u - 2).wait()
+
+            buf = lax.rem(u, 2)
+            self.staged[buf] = lax.dot_general(
+                self.tiles_in[buf],
+                self.held[u // self.tiles],
+                (((0,), (0,)), ((), ())),
+                preferred_element_type=F32,
+            ).astype(BF)
+            self.put(u).start()
+
+    def finish(self):
+        self.put(self.units - 2).wait()
+        self.put(self.units - 1).wait()
+
+
+def outer_scratch(right, tile):
+    slots, hidden = right.shape[1:]
+    return [
+        pltpu.VMEM((2, slots, tile), BF),
+        pltpu.VMEM(right.shape, BF),
+        pltpu.VMEM((2, tile, hidden), BF),
+        DMA((3, 2)),
+    ]
+
+
+def experts_out_kernel(
+    count,
+    cap,
+    x_in,
+    gated_in,
+    d_gate_in,
+    d_up_in,
+    dots,
     targets,
     targets_t,
     probs_ref,
@@ -1324,20 +1582,13 @@
     wg_in,
     wu_in,
     wd_in,
-    gated_out,
-    d_gate_out,
-    d_up_out,
     parts_out,
     logit_ref,
     sum_ref,
-    g_down_out,
+    g_gate_out,
     wg,
     wu,
     wd,
-    ys,
-    acts,
-    by_ups,
-    by_gates,
     gated,
     d_gate,
     d_up,
@@ -1348,13 +1599,13 @@
     inbox,
     w_sem,
     in_sem,
-    out_sem,
     part_sem,
-    down_sem,
-    *rest,
+    tiles_in,
+    held,
+    staged,
+    outer_sem,
+    *sems,
 ):
-    sems = rest[:7]
-    room_gated, room_y = rest[7:] if len(rest) > 7 else (wg, wu)
     places = where_am_i()
     i, p, sib = places
     core = lax.rem(i, 2)
@@ -1364,22 +1615,16 @@
     first = i * local_experts
     over_lanes = (((1,), (1,)), ((), ()))
     line = StagedScatter(count, places, stage, ([own], [sibling], [inbox]), sems)
+    grads_of = OuterGrads(x_in, d_gate_in, g_gate_out, (tiles_in, held, staged, outer_sem), count - 1)
     weights = ((wd_in, wd), (wg_in, wg), (wu_in, wu))
-    inputs = ((y_in, ys), (act_in, acts), (by_up_in, by_ups), (by_gate_in, by_gates))
-    results = ((gated, gated_out), (d_gate, d_gate_out), (d_up, d_up_out))
+    inputs = ((gated_in, gated), (d_gate_in, d_gate), (d_up_in, d_up))
 
     def weight(n):
         return pltpu.make_async_copy(weights[n][0], weights[n][1], w_sem.at[n])
 
-    def rows_of(q):
-        return pl.ds(pl.multiple_of(q * 2 * cap, 2 * cap), 2 * cap)
-
     def fetch(n, q, buf):
-        src = inputs[n][0].at[:, rows_of(q)]
-        return pltpu.make_async_copy(src, inputs[n][1].at[buf], in_sem.at[n, buf])
-
-    def store(n, q):
-        return pltpu.make_async_copy(results[n][0], results[n][1].at[:, rows_of(q)], out_sem.at[n])
+        rows = pl.ds(pl.multiple_of(q * 2 * cap, 2 * cap), 2 * cap)
+        return pltpu.make_async_copy(inputs[n][0].at[:, rows], inputs[n][1].at[buf], in_sem.at[n, buf])
 
     def put(q):
         return pltpu.make_async_copy(parts, parts_out.at[pl.ds(2 * q, 2)], part_sem)
@@ -1387,11 +1632,11 @@
     def order(k):
         return chunk_order(count - 1 - k, p, count)
 
-    weight(0).start()
-    for n in range(4):
+    for n in range(3):
         fetch(n, order(0), 0).start()
-    weight(1).start()
-    weight(2).start()
+    for n in range(3):
+        weight(n).start()
+    grads_of.begin()
     greet(count, places)
     slot_rows = lax.broadcasted_iota(jnp.int32, (local_experts * cap, tokens), 0)
     slot_lanes = lax.broadcasted_iota(jnp.int32, (tokens, local_experts * cap), 1)
@@ -1400,47 +1645,6 @@
     def compute(k):
         q = order(k)
         buf = lax.rem(k, 2)
-        for n in range(4):
-            fetch(n, q, buf).wait()
-
-        @pl.when(k + 1 < count)
-        def _():
-            for n in range(4):
-                fetch(n, order(k + 1), 1 - buf).start()
-
-        @pl.when(k > 0)
-        def _():
-            for n in range(3):
-                store(n, q).wait()
-            put(q).wait()
-            line.to_sib(0, order(k - 1)).wait_send()
-
-        @pl.when(k == 0)
-        def _():
-            weight(0).wait()
-
-        dots = []
-        for e in range(local_experts):
-            wide = 256
-
-            def step(n, dot):
-                cols = pl.ds(pl.multiple_of(n * wide, wide), wide)
-                grad_act = lax.dot_general(
-                    ys[buf, e], wd[e, cols, :], over_lanes, preferred_element_type=F32
-                )
-                act = acts[buf, e, :, cols].astype(F32)
-                gate = gate_slots[e, q]
-                dot = dot + jnp.sum(act * grad_act, axis=1, keepdims=True)
-                grad_act = grad_act * gate
-                gated[e, :, cols] = (act * gate).astype(BF)
-                d_up[e, :, cols] = (grad_act * by_ups[buf, e, :, cols].astype(F32)).astype(BF)
-                d_gate[e, :, cols] = (grad_act * by_gates[buf, e, :, cols].astype(F32)).astype(BF)
-                return dot
-
-            dots.append(lax.fori_loop(0, hidden // wide, step, jnp.zeros((2 * cap, 1), F32)))
-        for n in range(3):
-            store(n, q).start()
-
         picks, logits_low = [], []
         for j in range(2):
             slot = 2 * q + j
@@ -1449,7 +1653,8 @@
             for e in range(local_experts):
                 part = slice(e * cap, (e + 1) * cap)
                 mask = (slot_rows == targets[slot, e : e + 1, :])[part]
-                row = jnp.sum(jnp.where(mask, dots[e][j * cap : (j + 1) * cap], 0.0), axis=0, keepdims=True)
+                dot = dots[e, q, j * cap : (j + 1) * cap, :]
+                row = jnp.sum(jnp.where(mask, dot, 0.0), axis=0, keepdims=True)
                 grad_probs = jnp.where(expert_rows == first + e, row, grad_probs)
                 hit = slot_lanes == targets_t[slot, :, e : e + 1]
                 pick = hit if pick is None else pick | hit
@@ -1458,11 +1663,23 @@
             logit_ref[slot] = grad_logits.astype(BF)
             picks.append(jnp.where(pick, 1.0, 0.0).astype(BF))
             logits_low.append(grad_logits.T.astype(BF))
+        for n in range(3):
+            fetch(n, q, buf).wait()
+
+        @pl.when(k + 1 < count)
+        def _():
+            for n in range(3):
+                fetch(n, order(k + 1), 1 - buf).start()
+
+        @pl.when(k > 0)
+        def _():
+            put(q).wait()
+            line.to_sib(0, order(k - 1)).wait_send()
 
         @pl.when(k == 0)
         def _():
-            weight(1).wait()
-            weight(2).wait()
+            for n in range(3):
+                weight(n).wait()
 
         block = 512
 
@@ -1471,10 +1688,10 @@
             cols = pl.ds(pl.multiple_of(n * block, block), block)
             outs, grads = [], []
             for e in range(local_experts):
-                outs.append(jnp.dot(gated[e], wd[e, :, cols], preferred_element_type=F32))
+                outs.append(jnp.dot(gated[buf, e], wd[e, :, cols], preferred_element_type=F32))
                 grads.append(
-                    lax.dot_general(d_gate[e], wg[e, cols, :], over_lanes, preferred_element_type=F32)
-                    + lax.dot_general(d_up[e], wu[e, cols, :], over_lanes, preferred_element_type=F32)
+                    lax.dot_general(d_gate[buf, e], wg[e, cols, :], over_lanes, preferred_element_type=F32)
+                    + lax.dot_general(d_up[buf, e], wu[e, cols, :], over_lanes, preferred_element_type=F32)
                 )
             for j in range(2):
                 part = slice(j * cap, (j + 1) * cap)
@@ -1501,111 +1718,41 @@
     def _(k):
         compute(k)
 
-    def after(a, q):
-        out = pltpu.make_async_copy(own.at[q], sum_ref, part_sem)
-        out.start()
-        out.wait()
-
-    def down_grads():
-        slots = count * 2 * cap
-        tile = 256
-        tiles = hidden // tile
-        spans = model_width // hidden
-
-        def load_gated(e):
-            return pltpu.make_async_copy(
-                gated_out.at[e], room_gated.at[e, pl.ds(0, slots)], down_sem.at[0, e]
-            )
-
-        def load_y(e, span):
-            src = y_in.at[e, :, pl.ds(span * hidden, hidden)]
-            return pltpu.make_async_copy(src, room_y.at[e, pl.ds(0, slots)], down_sem.at[1, e])
-
-        def put_grad(e, span, n, buf):
-            part = (d_gate, d_up)[buf].at[0, pl.ds(0, tile)]
-            rows = pl.ds(pl.multiple_of(n * tile, tile), tile)
-            target = g_down_out.at[e, rows, pl.ds(span * hidden, hidden)]
-            return pltpu.make_async_copy(part, target, out_sem.at[buf])
-
-        for e in range(local_experts):
-            load_gated(e).start()
-            load_y(e, 0).start()
-        for span in range(spans):
-            for e in range(local_experts):
-                if span == 0:
-                    load_gated(e).wait()
-                load_y(e, span).wait()
-
-                @pl.loop(0, tiles // 2)
-                def _(m):
-                    for buf in range(2):
-                        n = 2 * m + buf
-
-                        def wait_last():
-                            put_grad(e, span, n, buf).wait()
-
-                        if span + e > 0:
-                            wait_last()
-                        else:
-                            pl.when(m > 0)(wait_last)
-                        cols = pl.ds(pl.multiple_of(n * tile, tile), tile)
-                        (d_gate, d_up)[buf][0, 0:tile, :] = lax.dot_general(
-                            room_gated[e, 0:slots, cols],
-                            room_y[e, 0:slots, :],
-                            (((0,), (0,)), ((), ())),
-                            preferred_element_type=F32,
-                        ).astype(BF)
-                        put_grad(e, span, n, buf).start()
-
-                if span + 1 < spans:
-                    load_y(e, span + 1).start()
-        for buf in range(2):
-            put_grad(0, 0, 0, buf).wait()
-
     def between(step):
         compute(step + 1)
-
-        @pl.when(step == count - 2)
-        def _():
-            for n in range(3):
-                store(n, 0).wait()
-            put(0).wait()
-            line.to_sib(0, order(count - 1)).wait_send()
-            down_grads()
+        grads_of.between(step)
 
     line.run(lambda a, q: None, between)
-    after(0, p)
+    grads_of.finish()
+    put(0).wait()
+    line.to_sib(0, order(count - 1)).wait_send()
+    out = pltpu.make_async_copy(own.at[p], sum_ref, part_sem)
+    out.start()
+    out.wait()
     line.finish()
 
 
 def experts_out(
-    grads, act, by_up, by_gate, gate_slots, targets, targets_t, probs, router_t, w_gate, w_up, w_down, collective
+    expert_in, gated, d_gate, d_up, dots, targets, targets_t, probs, router_t, w_gate, w_up, w_down, collective
 ):
-    local_experts, _, model_width = grads.shape
-    hidden = act.shape[2]
+    local_experts, slots, model_width = expert_in.shape
+    hidden = gated.shape[2]
     shards, experts, tokens = probs.shape
     count = shards // 2
     anywhere = pl.BlockSpec(memory_space=ANY)
     vmem = pl.BlockSpec(memory_space=pltpu.VMEM)
-    thin = jax.ShapeDtypeStruct(act.shape, BF)
-    extra = [] if act.shape[1] <= model_width else [pltpu.VMEM(act.shape, BF)] * 2
     return pl.pallas_call(
         partial(experts_out_kernel, count, CAP),
         out_shape=[
-            thin,
-            thin,
-            thin,
             jax.ShapeDtypeStruct((shards, tokens, model_width), BF),
             jax.ShapeDtypeStruct(probs.shape, BF),
             jax.ShapeDtypeStruct((tokens, model_width), BF),
-            jax.ShapeDtypeStruct(w_down.shape, BF),
+            jax.ShapeDtypeStruct(w_gate.shape, BF),
         ],
         in_specs=[anywhere] * 4 + [vmem] * 5 + [anywhere] * 3,
-        out_specs=[anywhere] * 4 + [vmem, anywhere, anywhere],
+        out_specs=[anywhere, vmem, anywhere, anywhere],
         scratch_shapes=[pltpu.VMEM(x.shape, BF) for x in (w_gate, w_up, w_down)]
-        + [pltpu.VMEM((2, local_experts, 2 * CAP, model_width), BF)]
         + [pltpu.VMEM((2, local_experts, 2 * CAP, hidden), BF)] * 3
-        + [pltpu.VMEM((local_experts, 2 * CAP, hidden), BF)] * 3
         + [
             pltpu.VMEM((2, tokens, model_width), BF),
             pltpu.VMEM((tokens, model_width), BF),
@@ -1613,18 +1760,17 @@
             pltpu.VMEM((count, tokens, model_width), BF),
             pltpu.VMEM((count + 1, tokens, model_width), BF),
             DMA((3,)),
-            DMA((4, 2)),
-            DMA((3,)),
+            DMA((3, 2)),
             DMA,
-            DMA((2, local_experts)),
         ]
-        + [DMA((1, count))] * 7
-        + extra,
+        + outer_scratch(d_gate, 256)
+        + [DMA((1, count))] * 7,
         compiler_params=pltpu.CompilerParams(
             collective_id=collective, has_side_effects=True, vmem_limit_bytes=63 << 20
         ),
+        cost_estimate=pl.CostEstimate(flops=60_000_000_000, bytes_accessed=200_000_000, transcendentals=0),
         name="experts_out",
-    )(grads, act, by_up, by_gate, gate_slots, targets, targets_t, probs, router_t, w_gate, w_up, w_down)
+    )(expert_in, gated, d_gate, d_up, dots, targets, targets_t, probs, router_t, w_gate, w_up, w_down)
 
 
 def rope_tables(positions, head_dim):
@@ -1736,12 +1882,15 @@
     h2_all, expert_in, grad_slots, act, by_up, by_gate, gate_slots, gate_probs = experts_in(
         h2, dy_all, targets, router_t, full_gate, full_up, 3
     )
-    gated, d_gate, d_up, out_parts, grad_logits, grad_h2, g_down = experts_out(
-        grad_slots,
-        act,
-        by_up,
-        by_gate,
-        gate_slots,
+    gated, d_gate, d_up, dots_slots, g_down = experts_mid(
+        grad_slots, act, by_up, by_gate, gate_slots, full_down
+    )
+    out_parts, grad_logits, grad_h2, g_gate = experts_out(
+        expert_in,
+        gated,
+        d_gate,
+        d_up,
+        dots_slots,
         targets,
         targets_t,
         gate_probs,
@@ -1756,6 +1905,7 @@
         return lax.psum_scatter(part, "seq", scatter_dimension=1, tiled=True)
 
     g_down = spread(g_down)
+    g_gate = spread(g_gate)
     grad_h2 = grad_h2.astype(F32)
 
     u_rows = gain_f * grad_h2
@@ -1766,19 +1916,9 @@
     )
     ffn_part = jnp.sum(grad_h2 * x_mid * scale_f, axis=0)
 
-    d_attn, out_sum, g_gate, g_up, router_part = turn_back(
-        grad_mid.astype(BF),
-        out_parts,
-        expert_in,
-        d_gate,
-        d_up,
-        h2_all,
-        grad_logits,
-        seq_count,
-        shards,
-        5,
+    d_attn, out_sum, g_up, router_part = turn_back(
+        grad_mid.astype(BF), out_parts, expert_in, d_up, h2_all, grad_logits, seq_count, shards, 5
     )
-    g_gate = spread(g_gate)
     g_up = spread(g_up)
     d_attn = d_attn.reshape(seq_len, model_width)
     result = x_mid + out_sum.astype(F32)
@@ -1786,7 +1926,7 @@
     u_q, u_k, dv_low, dots, gain_q_part, gain_k_part = attend_back(
         q_low, k_low, values, d_heads, q_raw, k_raw, rq, rk, gq, gk, cos, sin, doc_col, doc_row
     )
-    dots, g_down = lax.optimization_barrier((dots, g_down))
+    dots, g_down, g_gate = lax.optimization_barrier((dots, g_down, g_gate))
     dots = seq_sum(dots.T, seq_count, 6) / model_width
 
     def norm_back(u, raw, scale, product):

time: 858 us -> 771 us (0.90)
  waiting for transfers between devices: 101 us -> 3.73 us
  Pallas kernels: 602 us -> 611 us
    reduce_scatter x3, waiting for transfers between devices: 62.1 us -> 0.01 us  [spread(): return lax.psum_scatter(part, 'seq', scatter_dimension=1, tiled=True)]
    all_gather x1, waiting for transfers between devices: 36.1 us -> 1.59 us  [on_device(): full_up = lax.all_gather(w_up, 'seq', axis=1, tiled=True)]
    pallas_call x1 -> x2, Pallas kernels: 109 us -> 135 us  [the longest x1 99.6 us: experts_out(): pl.pallas_call(partial(experts_out_kernel, count, CAP), out_shape=[jax.Sh...]
    pallas_call x1, Pallas kernels: 101 us -> 79.2 us  [turn_back(): pl.pallas_call(partial(turn_kernel, count, seq_count), out_shape=[jax.Sha...]
  transfers between devices with their start and end apart: 6 -> 6, of which waited for: 2 -> 1; matrix products, arithmetic and copies ran while one was open for 14% -> 16% of each run, Pallas kernels for 58% -> 75%
where the time goes in v4:
time: 771 us; the launch traced here: 763 us
  Pallas kernels  611 us (79%)
  other arithmetic  54.4 us (7%)
  matrix products  51.2 us (7%)
  local copies, waits for them, and re-layouts  27.4 us (4%)
  between operations  15.3 us (2%)
    pallas_call x1, Pallas kernels, experts_out(): pl.pallas_call(partial(experts_out_kernel, count, CAP), out_shape=[jax.Sh...  99.6 us
    pallas_call x1, Pallas kernels, experts_in(): pl.pallas_call(partial(experts_in_kernel, count, CAP), out_shape=[jax.Sha...  91.5 us
    pallas_call x1, Pallas kernels, scatter_end(): pl.pallas_call(partial(end_kernel, count, seq_count), out_shape=shapes, i...  90.4 us
    pallas_call x1, Pallas kernels, gather_start(): pl.pallas_call(partial(start_kernel, count, seq_count), out_shape=shapes,...  88.3 us
    pallas_call x1, Pallas kernels, turn_back(): pl.pallas_call(partial(turn_kernel, count, seq_count), out_shape=[jax.Sha...  79.2 us
    pallas_call x1, Pallas kernels, middle(): pl.pallas_call(partial(middle_kernel, count, seq_count), out_shape=[jax.S...  74 us
    dot_general x12, matrix products, dot(): lax.dot_general(left, right, (((sides[0],), (sides[1],)), ((), ())), pref...  51.2 us
    pallas_call x1, Pallas kernels, experts_mid(): pl.pallas_call(partial(experts_mid_kernel, CAP), out_shape=[thin, thin, t...  35.1 us
  transfers between devices with their start and end apart: 6, of which 1 were waited for; matrix products, arithmetic and copies ran while one was open for 16% of the time, Pallas kernels for 75%

profile of v4, /device:TPU:0, one launch (start us, length us, event | category | flops | bytes accessed | tf_op | source)
XLA Modules:
  0.0 762.9 jit_solution(14506701045410908277)
XLA Ops:
  12.1 88.3 %gather_start.1 = (bf16[4,8,64,512]{3,2,1,0:T(8,128)(2,1)}, bf16[4,8,64,512]{3,2,1,0:T(8,128)(2,1)}, bf16[4,8,64,512]{3,2,1,0:T(8,128)(2,1)}, bf16[8,64,2048]{2,...) custom-call(bf16[64,2048]{1,0:T(8,128)(2,1)} %refs_0_.1, ...), custom_call_target="tpu_custom_call" | custom-call | tf_op jit(solution)/shard_map/gather_start/pallas_call | solution.py:247
  100.4 1.5 eq.15
  103.5 3.2 multiply_reduce_fusion
  108.9 2.4 multiply_reduce_fusion.2
  111.4 2.0 copy.109.k_raw
  113.4 5.2 multiply_reduce_fusion.3
  118.6 1.8 copy.108.q_raw
  121.0 7.1 seq_sum.2
  132.7 1.4 copy.117
  134.1 1.4 fusion.15
  137.4 2.2 fusion.16
  139.7 6.5 convolution_convert_fusion.6.v_ref
  146.3 16.5 %attend.1 = (bf16[1024,512]{1,0:T(8,128)(2,1)S(1)}, bf16[1024,512]{1,0:T(8,128)(2,1)S(1)}, bf16[1024,512]{1,0:T(8,128)(2,1)S(1)}) custom-call(f32[1024,512]{1,0:T(8,128)} %copy.108.q_raw, f32[1024,512]{1,0:T(8,128)} %copy.109.k_raw, bf16[1024,512]{1,0:T(8,128)(2,1)} %convolution_convert_fusion.6.v_ref, f32[1024,1]{1,0:T(8,128)S(1)} %copy.110.rq, ...), custom_call_target="tpu_custom_call" | custom-call | tf_op jit(solution)/shard_map/attend/pallas_call | solution.py:996
  162.8 2.3 convolution_convert_fusion
  165.2 74.0 %middle.1 = (f32[256,2048]{1,0:T(8,128)S(1)}, bf16[8,256,2048]{2,1,0:T(8,128)(2,1)S(1)}) custom-call(bf16[4,256,2048]{2,1,0:T(8,128)(2,1)S(1)} %bitcast.94, bf16[256,2048]{1,0:T(8,128)(2,1)S(1)} %bitcast.93), custom_call_target="tpu_custom_call" | custom-call | tf_op jit(solution)/shard_map/middle/pallas_call | solution.py:737
  239.2 3.3 copy-done.2
  245.5 1.6 all-gather.6.cloned.1.call-done.wu_ref.wu_in
  247.1 91.5 %experts_in.1 = (bf16[8,256,2048]{2,1,0:T(8,128)(2,1)}, bf16[2,1088,2048]{2,1,0:T(8,128)(2,1)}, bf16[2,1088,2048]{2,1,0:T(8,128)(2,1)}, bf16[2,1088,1024]{2,1,0:...) custom-call(bf16[256,2048]{1,0:T(8,128)(2,1)} %multiply_convert_fusi, ...), custom_call_target="tpu_custom_call" | custom-call | tf_op jit(solution)/shard_map/experts_in/pallas_call | solution.py:1317
  338.6 35.1 %experts_mid.1 = (bf16[2,1088,1024]{2,1,0:T(8,128)(2,1)}, bf16[2,1088,1024]{2,1,0:T(8,128)(2,1)}, bf16[2,1088,1024]{2,1,0:T(8,128)(2,1)}, f32[2,4,272,1]{3,2,1,0:T(8,128)}, bf16[2,1024,2048]{2,1,0:T(8,128)(2,1)}) custom-call(bf16[2,1088,2048]{2,1,0:T(8,128)(2,1)} %get-tuple-element.76.y_in, bf16[2,1088,1024]{2,1,0:T(8,128)(2,1)} %get-tuple-element.77.act_in, ...), custom_call_target="tpu_custom_call" | custom-call | flops 17999998976 | bytes 60000000 | tf_op jit(solution)/shard_map/experts_mid/pallas_call | solution.py:1449
  373.9 99.6 %experts_out.1 = (bf16[8,256,2048]{2,1,0:T(8,128)(2,1)}, bf16[8,16,256]{2,1,0:T(8,128)(2,1)}, bf16[256,2048]{1,0:T(8,128)(2,1)}, bf16[2,2048,1024]{2,1,0:T(8,128)(2,1)}) custom-call(bf16[2,1088,2048]{2,1,0:T(8,128)(2,1)} %get-tuple-element.75.x_in.left_ref, bf16[2,1088,1024]{2,1,0:T(8,128)(2,1)} %get-tuple-element.81.gated_in, ...), custom_call_target="tpu_custom_call" | custom-call | flops 60000002048 | bytes 200000000 | tf_op jit(solution)/shard_map/experts_out/pallas_call | solution.py:1744
  474.7 2.3 fusion.8
  477.0 1.7 fusion.27.x_ref
  478.6 79.2 %turn_back.1 = (bf16[4,256,2048]{2,1,0:T(8,128)(2,1)}, bf16[256,2048]{1,0:T(8,128)(2,1)}, bf16[2,2048,1024]{2,1,0:T(8,128)(2,1)}, f32[16,2048]{1,0:T(8,128)}) custom-call(bf16[256,2048]{1,0:T(8,128)(2,1)} %fusion.27.x_ref, bf16[8,256,2048]{2,1,0:T(8,128)(2,1)} %get-tuple-element.87.parts_ref, bf16[2,1088,2048]{2,1,0:T(8,128)(2,1)} %get-tuple-element.75.x_in.left_ref, ...), custom_call_target="tpu_custom_call" | custom-call | flops 60000002048 | bytes 200000000 | tf_op jit(solution)/shard_map/turn_back/pallas_call | solution.py:911
  558.6 5.3 fusion.1
  564.0 1.9 concatenate.19
  565.9 1.3 copy.130
  567.2 6.3 convolution_convert_fusion.5.do_ref
  573.5 22.5 %attend_back.1 = (f32[1024,512]{1,0:T(8,128)}, f32[1024,512]{1,0:T(8,128)}, bf16[1024,512]{1,0:T(8,128)(2,1)}, f32[1024,2]{1,0:T(8,128)}, f32[1,512]{1,0:T(1,128)}, /*index=5*/f32[1,512]{1,0:T(1,128)}) custom-call(bf16[1024,512]{1,0:T(8,128)(2,1)} %copy-done.8, bf16[1024,512]{1,0:T(8,128)(2,1)} %copy-done.9, ...), custom_call_target="tpu_custom_call" | custom-call | tf_op jit(solution)/shard_map/attend_back/pallas_call | solution.py:1091
  596.5 1.3 reduce.21
  597.9 1.3 reduce.22
  600.0 2.9 maximum_maximum_fusion.refs_4_
  602.9 6.1 convolution_convert_fusion.1
  609.0 3.8 convolution_convert_fusion.2
  613.6 6.5 seq_sum.3
  620.9 4.5 subtract_convert_fusion
  625.4 2.4 fusion.30
  627.8 2.4 fusion.31
  630.2 3.7 convolution_convert_fusion.4
  633.9 3.7 convolution_convert_fusion.3
  637.6 6.4 add_convert_fusion
  643.9 90.4 %scatter_end.1 = (bf16[64,2048]{1,0:T(8,128)(2,1)}, bf16[64,2048]{1,0:T(8,128)(2,1)}, bf16[64,2048]{1,0:T(8,128)(2,1)}, bf16[64,2048]{1,0:T(8,128)(2,1)}, f32[64...) custom-call(bf16[4,8,64,512]{3,2,1,0:T(8,128)(2,1)} %bitcast.109, bf16[4,8,64,512]{3,2,1,0:T(8,128)(2,1)} %bitcast.110, ...), custom_call_target="tpu_custom_call" | custom-call | tf_op jit(solution)/shard_map/scatter_end/pallas_call | solution.py:527
  734.3 1.8 convert_element_type.193
  736.1 1.4 copy.132
  737.5 4.2 convert_element_type.198
  741.8 2.5 convert_element_type.200
  745.1 1.3 add_reduce_fusion
  748.9 2.9 fusion.12
  751.7 4.1 convert_element_type.199
  (195 shorter events, 26.6 us)
Async XLA Ops:
  7.2 238.3 %all-gather.4.cloned.1.call-start = ((), (), s32[]{:S(2)}) async-start(), calls=%async_computation.3 | async-start | bytes 10485760 | tf_op jit(solution)/shard_map/all_gather | solution.py:1838
  8.0 2.8 copy-start.50
  8.0 2.8 copy-start.51
  8.0 239.1 %all-gather.6.cloned.1.call-start = ((), (), s32[]{:S(2)}) async-start(), calls=%async_computation.4 | async-start | bytes 10485760 | tf_op jit(solution)/shard_map/all_gather | solution.py:1839
  8.7 329.9 %all-gather.8.cloned.1.call-start = ((), (), s32[]{:S(2)}) async-start(), calls=%async_computation.5 | async-start | bytes 10485760 | tf_op jit(solution)/shard_map/all_gather | solution.py:1840
  9.5 603.4 %reduce-scatter.4.cloned.1.call-start = ((), (), s32[]{:S(2)}) async-start(), calls=%async_computation.6 | async-start | bytes 10485760 | tf_op jit(solution)/shard_map/reduce_scatter | solution.py:1905
  100.3 2.4 copy-start.24
  103.5 3.9 copy-start.40
  103.5 3.8 copy-start.18
  108.4 3.0 copy-start.28
  118.6 12.4 %copy-start.10 = (s32[1,1024]{1,0:T(1,128)S(1)}, s32[1,1024]{1,0:T(1,128)}, u32[]{:S(2)}) copy-start(s32[1,1024]{1,0:T(1,128)} %doc_row.3) | copy-start | bytes 12292
  129.7 16.5 %copy-start.5 = (f32[1024,1]{1,0:T(8,128)}, f32[1024,1]{1,0:T(8,128)S(1)}, u32[]{:S(2)}) copy-start(f32[1024,1]{1,0:T(8,128)S(1)} %copy.110.rq) | copy-start | bytes 12292
  130.0 16.2 %copy-start.6 = (f32[1024,1]{1,0:T(8,128)}, f32[1024,1]{1,0:T(8,128)S(1)}, u32[]{:S(2)}) copy-start(f32[1024,1]{1,0:T(8,128)S(1)} %copy.111.rk) | copy-start | bytes 12292
  130.9 15.3 %copy-start.11 = (f32[1,512]{1,0:T(1,128)}, f32[1,512]{1,0:T(1,128)S(1)}, u32[]{:S(2)}) copy-start(f32[1,512]{1,0:T(1,128)S(1)} %reshape.299.gq) | copy-start | bytes 6148
  131.0 15.2 %copy-start.12 = (f32[1,512]{1,0:T(1,128)}, f32[1,512]{1,0:T(1,128)S(1)}, u32[]{:S(2)}) copy-start(f32[1,512]{1,0:T(1,128)S(1)} %reshape.300.gk) | copy-start | bytes 6148
  131.2 15.0 %copy-start.7 = (s32[1024,1]{1,0:T(8,128)}, s32[1024,1]{1,0:T(8,128)S(1)}, u32[]{:S(2)}) copy-start(s32[1024,1]{1,0:T(8,128)S(1)} %copy.112.doc_col) | copy-start | bytes 12292
  135.4 10.7 %copy-start.25 = (s32[8,2,256]{1,2,0:T(8,128)}, s32[8,2,256]{1,2,0:T(8,128)S(1)}, u32[]{:S(2)}) copy-start(s32[8,2,256]{1,2,0:T(8,128)S(1)} %fusion.15) | copy-start | bytes 49156
  137.2 2.5 copy-start.29
  139.7 6.6 copy-start.3
  139.7 6.6 copy-start.4
  146.2 16.5 %copy-start.57 = (bf16[8,64,2048]{2,1,0:T(8,128)(2,1)S(1)}, bf16[8,64,2048]{2,1,0:T(8,128)(2,1)}, u32[]{:S(2)}) copy-start(bf16[8,64,2048]{2,1,0:T(8,128)(2,1)} %get-tuple-element.71) | copy-start | bytes 6291460
  165.2 77.4 %copy-start.19 = (bf16[1,256,2048]{2,1,0:T(8,128)(2,1)S(1)}, bf16[1,256,2048]{2,1,0:T(8,128)(2,1)}, u32[]{:S(2)}) copy-start(bf16[1,256,2048]{2,1,0:T(8,128)(2,1)} %param.16) | copy-start | bytes 3145732
  239.2 3.3 copy-start.2
  373.8 239.0 %reduce-scatter.6.cloned.1.call-start = ((), (), s32[]{:S(2)}) async-start(), calls=%async_computation.7 | async-start | bytes 10485760 | tf_op jit(solution)/shard_map/reduce_scatter | solution.py:1905
  473.5 3.5 copy-start.1
  473.5 278.3 %reduce-scatter.8.cloned.1.call-start = ((), (), s32[]{:S(2)}) async-start(), calls=%async_computation.8 | async-start | bytes 10485760 | tf_op jit(solution)/shard_map/reduce_scatter | solution.py:1905
  473.5 3.4 copy-start.16
  558.6 7.2 copy-start.42
  596.0 6.9 copy-start.14
  602.9 6.1 copy-start.26
  602.9 6.1 copy-start.32
  609.0 3.8 copy-start.36
  609.0 11.9 %copy-start.44 = (f32[1,1024]{1,0:T(1,128)S(1)}, f32[1,1024]{1,0:T(1,128)}, u32[]{:S(2)}) copy-start(f32[1,1024]{1,0:T(1,128)} %get-tuple-element.188) | copy-start | bytes 12292
  609.0 11.9 %copy-start.45 = (f32[1,1024]{1,0:T(1,128)S(1)}, f32[1,1024]{1,0:T(1,128)}, u32[]{:S(2)}) copy-start(f32[1,1024]{1,0:T(1,128)} %get-tuple-element.191) | copy-start | bytes 12292
  620.9 4.5 copy-start.56
  737.5 4.2 copy-start.30
  741.7 2.6 copy-start.43
  741.7 3.3 copy-start.33
  741.8 3.3 copy-start.34
  741.8 3.3 copy-start.35
  741.8 3.3 copy-start.37
  741.8 3.3 copy-start.38
  741.8 3.3 copy-start.39
  741.8 7.1 copy-start.31
  744.4 2.6 copy-start.20
  744.4 2.6 copy-start.23
  746.4 2.4 copy-start.17
  746.4 2.4 copy-start.22
  (16 other events, 29.1 us)
Sparse Core Ops, SparseCore 0:
  9.9 120.7 all-gather.3
  132.5 114.5 all-gather.5
  248.9 86.9 all-gather.7
  373.9 85.8 reduce-scatter.3
  473.6 116.8 reduce-scatter.5
  593.5 109.8 reduce-scatter.7

commit v5 on v4

--- a/solution.py
+++ b/solution.py
@@ -2,6 +2,7 @@
 
 import jax
 import jax.numpy as jnp
+import numpy as np
 from jax import lax
 from jax.experimental import pallas as pl
 from jax.experimental.pallas import tpu as pltpu
@@ -152,7 +153,7 @@
 
 
 def start_kernel(count, seq_count, *refs):
-    wq, wk, wv, wo, small, gains, routes, rows = refs[:8]
+    wq, wk, wv, small, gains, routes, wo, rows = refs[:8]
     outs = refs[8:15]
     rows_out = refs[15]
     holds = refs[16:24]
@@ -165,44 +166,37 @@
     def columns(ref, peer):
         return ref.at[:, pl.ds(pl.multiple_of(peer * width, width), width)]
 
-    own = [columns(wq, here), columns(wk, here), columns(wv, here), wo, small, gains, routes, rows]
+    own = [columns(wq, here), columns(wk, here), columns(wv, here), small, gains, routes, wo, rows]
     for a in range(8):
         pltpu.make_async_copy(own[a], holds[a], local.at[a]).start()
     greet(count, places, seq_count)
 
     def piece(a, d):
         peer = lax.rem(here + d, seq_count)
-        src = small if a == 4 else columns((wq, wk, wv)[a], peer)
-        slot = 3 if a == 4 else a
-        return remote(
-            src, outs[a].at[here, i], send_x.at[slot, d - 1], recv_x.at[slot, d - 1], seq=peer
-        )
+        src = small if a == 3 else columns((wq, wk, wv)[a], peer)
+        return remote(src, outs[a].at[here, i], send_x.at[a, d - 1], recv_x.at[a, d - 1], seq=peer)
 
     def arrived(a, d):
         origin = lax.rem(here + seq_count - d, seq_count)
-        slot = 3 if a == 4 else a
-        return remote(
-            outs[a].at[origin, i],
-            outs[a].at[origin, i],
-            send_x.at[slot, d - 1],
-            recv_x.at[slot, d - 1],
-            seq=origin,
-        )
-
-    for a in (4, 0, 1, 2):
+        ref = outs[a].at[origin, i]
+        return remote(ref, ref, send_x.at[a, d - 1], recv_x.at[a, d - 1], seq=origin)
+
+    for a in (3, 0, 1, 2):
         for d in range(1, seq_count):
             piece(a, d).start()
     gather = SeqGather(seq_count, rows, rows_out, send_y, recv_y)
     gather.begin()
-    axes = [1, 1, 1, 0, 1, 0, 0]
-    for a in (3, 5, 6, 4, 0, 1, 2):
+    axes = [1, 1, 1, 1, 0, 0, 0]
+
+    def target(a):
+        return outs[a].at[here, i] if axes[a] == 1 else outs[a].at[i]
+
+    for a in (4, 5, 6, 3, 0, 1, 2):
         pltpu.make_async_copy(own[a], holds[a], local.at[a]).wait()
-        target = outs[a].at[here, i] if axes[a] == 1 else outs[a].at[i]
-        pltpu.make_async_copy(holds[a], target, local.at[a]).start()
+        pltpu.make_async_copy(holds[a], target(a), local.at[a]).start()
     line = LineGather(count, places, outs, axes, send_r, send_l, send_s, recv)
-    for a in (5, 6, 4, 0, 1, 2, 3):
-        target = outs[a].at[here, i] if axes[a] == 1 else outs[a].at[i]
-        pltpu.make_async_copy(holds[a], target, local.at[a]).wait()
+    for a in (4, 5, 6, 3, 0, 1, 2):
+        pltpu.make_async_copy(holds[a], target(a), local.at[a]).wait()
         if axes[a] == 1:
             for d in range(1, seq_count):
                 arrived(a, d).wait_recv()
@@ -216,14 +210,14 @@
     line.finish()
     pltpu.make_async_copy(holds[7], rows_out.at[here], local.at[7]).wait()
     gather.finish()
-    for a in (4, 0, 1, 2):
+    for a in (3, 0, 1, 2):
         for d in range(1, seq_count):
             piece(a, d).wait_send()
 
 
 def gather_start(arrays, seq_count, shards, collective):
     count = shards // 2
-    wq, wk, wv, wo, small, gains, routes, tokens = arrays
+    wq, wk, wv, small, gains, routes, wo, tokens = arrays
     rows, model_width = wq.shape
     width = model_width // seq_count
     sheet = jax.ShapeDtypeStruct((seq_count, shards, rows, width), BF)
@@ -231,17 +225,17 @@
         sheet,
         sheet,
         sheet,
-        jax.ShapeDtypeStruct((shards,) + wo.shape, BF),
         jax.ShapeDtypeStruct((seq_count, shards) + small.shape, BF),
         jax.ShapeDtypeStruct((shards,) + gains.shape, BF),
         jax.ShapeDtypeStruct((shards,) + routes.shape, jnp.int32),
+        jax.ShapeDtypeStruct((shards,) + wo.shape, BF),
         jax.ShapeDtypeStruct((seq_count,) + tokens.shape, BF),
     ]
     holds = [pltpu.VMEM((rows, width), BF)] * 3 + [
-        pltpu.VMEM(wo.shape, BF),
         pltpu.VMEM(small.shape, BF),
         pltpu.VMEM(gains.shape, BF),
         pltpu.VMEM(routes.shape, jnp.int32),
+        pltpu.VMEM(wo.shape, BF),
         pltpu.VMEM(tokens.shape, BF),
     ]
     return pl.pallas_call(
@@ -340,51 +334,49 @@
         self.load(a, q).wait()
         self.to_sib(a, q).wait_recv()
 
-    def run(self, after, between=None):
+    def event(self, step):
         i, p, sib = self.places
         count = self.count
         arrays = range(len(self.sources))
 
-        @pl.loop(0, count - 1)
-        def _(step):
-            @pl.when(step >= p)
-            def _():
-                q = count - 1 - (step - p)
-                for a in arrays:
-                    self.ready(a, q)
-
-                    @pl.when(p > 0)
-                    def _():
-                        self.right(a, q).wait_recv()
-                        self.add(a, q, [q])
-
-                    @pl.when(p == 0)
-                    def _():
-                        self.add(a, q, [])
-
-                    self.right(a, q).start()
-
-            @pl.when(step >= count - 1 - p)
-            def _():
-                q = step - (count - 1 - p)
-                for a in arrays:
-                    self.ready(a, q)
-
-                    @pl.when(p < count - 1)
-                    def _():
-                        self.left(a, q).wait_recv()
-                        self.add(a, q, [q])
-
-                    @pl.when(p == count - 1)
-                    def _():
-                        self.add(a, q, [])
-
-                    self.left(a, q).start()
-
-            if between is not None:
-                between(step)
-
-        for a in arrays:
+        @pl.when(step >= p)
+        def _():
+            q = count - 1 - (step - p)
+            for a in arrays:
+                self.ready(a, q)
+
+                @pl.when(p > 0)
+                def _():
+                    self.right(a, q).wait_recv()
+                    self.add(a, q, [q])
+
+                @pl.when(p == 0)
+                def _():
+                    self.add(a, q, [])
+
+                self.right(a, q).start()
+
+        @pl.when(step >= count - 1 - p)
+        def _():
+            q = step - (count - 1 - p)
+            for a in arrays:
+                self.ready(a, q)
+
+                @pl.when(p < count - 1)
+                def _():
+                    self.left(a, q).wait_recv()
+                    self.add(a, q, [q])
+
+                @pl.when(p == count - 1)
+                def _():
+                    self.add(a, q, [])
+
+                self.left(a, q).start()
+
+    def final(self, after):
+        i, p, sib = self.places
+        count = self.count
+        for a in range(len(self.sources)):
             self.ready(a, p)
 
             @pl.when(p > 0)
@@ -408,6 +400,15 @@
                 self.add(a, p, [p, count])
 
             after(a, p)
+
+    def run(self, after, between=None):
+        @pl.loop(0, self.count - 1)
+        def _(step):
+            self.event(step)
+            if between is not None:
+                between(step)
+
+        self.final(after)
 
     def finish(self):
         i, p, sib = self.places
@@ -426,22 +427,24 @@
 
 def end_kernel(count, seq_count, *refs):
     sources = refs[:6]
-    rows_ref = refs[6]
-    outs = refs[7:13]
-    sum_ref = refs[13]
-    bufs = tuple(refs[14 + 6 * k : 20 + 6 * k] for k in range(3))
-    landing = refs[32]
-    sems = refs[33:40]
-    send_x, recv_x, local = refs[40:43]
-    seq = SeqScatter(seq_count, rows_ref, *refs[43:48])
+    factors = refs[6:12]
+    outs = refs[12:18]
+    sum_ref = refs[18]
+    bufs = tuple(refs[19 + 6 * k : 25 + 6 * k] for k in range(3))
+    landing = refs[37]
+    sems = refs[38:45]
+    send_x, recv_x, local = refs[45:48]
+    held = refs[48:54]
+    rows_ref, factor_sem = refs[54:56]
+    seq = SeqScatter(seq_count, rows_ref, *refs[56:61])
     places = where_am_i()
     here = lax.axis_index("seq")
     width = sources[0].shape[3]
     line = LineScatter(count, places, sources, [1, 1, 1, 0, 1, 0], bufs, sems)
     line.begin_loads()
-    seq.begin_loads()
+    for n in range(6):
+        pltpu.make_async_copy(factors[n], held[n], factor_sem.at[n]).start()
     greet(count, places, seq_count)
-    seq.begin()
     line.begin()
     own = bufs[0]
 
@@ -473,8 +476,32 @@
                 piece(a, q, d).start()
             pltpu.make_async_copy(own[a].at[q, here], at_home(a, here), local.at[a]).start()
 
+    def back_rows():
+        for n in range(6):
+            pltpu.make_async_copy(factors[n], held[n], factor_sem.at[n]).wait()
+        tokens, model_width = rows_ref.shape[1:]
+        tile = 512
+        tiles = model_width // tile
+
+        @pl.loop(0, seq_count * tiles)
+        def _(u):
+            block = u // tiles
+            strip = pl.ds(pl.multiple_of(block * tokens, tokens), tokens)
+            cols = pl.ds(pl.multiple_of(lax.rem(u, tiles) * tile, tile), tile)
+            total = jnp.zeros((tokens, tile), F32)
+            for n in range(3):
+                total += lax.dot_general(
+                    held[n][strip, :], held[3 + n][cols, :], (((1,), (1,)), ((), ())), preferred_element_type=F32
+                )
+            rows_ref[block, :, cols] = total.astype(BF)
+
+        seq.begin_loads()
+        seq.begin()
+
     def between(step):
-        @pl.when(step == 0)
+        pl.when(step == 0)(back_rows)
+
+        @pl.when(step == 1)
         def _():
             seq.relay()
 
@@ -504,10 +531,11 @@
     seq.finish()
 
 
-def scatter_end(arrays, row_blocks, seq_count, shards, collective):
+def scatter_end(arrays, factors, seq_count, shards, collective):
     count = shards // 2
     gq, gk, gv, go, small, gains = arrays
     rows, width = gq.shape[2:]
+    tokens, model_width = factors[0].shape[0] // seq_count, factors[3].shape[0]
     home = jax.ShapeDtypeStruct((rows, width * seq_count), BF)
     shapes = [
         home,
@@ -516,7 +544,7 @@
         jax.ShapeDtypeStruct(go.shape[1:], BF),
         jax.ShapeDtypeStruct(small.shape[2:], F32),
         jax.ShapeDtypeStruct(gains.shape[1:], F32),
-        jax.ShapeDtypeStruct(row_blocks.shape[1:], F32),
+        jax.ShapeDtypeStruct((tokens, model_width), F32),
     ]
     blocks, inboxes = [], []
     for a in range(6):
@@ -527,19 +555,21 @@
     return pl.pallas_call(
         partial(end_kernel, count, seq_count),
         out_shape=shapes,
-        in_specs=[pl.BlockSpec(memory_space=ANY)] * 7,
+        in_specs=[pl.BlockSpec(memory_space=ANY)] * 12,
         out_specs=[pl.BlockSpec(memory_space=ANY)] * 6 + [pl.BlockSpec(memory_space=pltpu.VMEM)],
         scratch_shapes=blocks * 2
         + inboxes
         + [pltpu.VMEM((seq_count,) + small.shape[2:], F32)]
         + [DMA((6, count))] * 7
         + [DMA((4, seq_count - 1)), DMA((4, seq_count - 1)), DMA((6,))]
-        + seq_scatter_scratch(row_blocks.shape[1:], row_blocks.dtype, seq_count),
+        + [pltpu.VMEM(x.shape, BF) for x in factors]
+        + [pltpu.VMEM((seq_count, tokens, model_width), BF), DMA((6,))]
+        + seq_scatter_scratch((tokens, model_width), BF, seq_count),
         compiler_params=pltpu.CompilerParams(
             collective_id=collective, has_side_effects=True, vmem_limit_bytes=62 << 20
         ),
         name="scatter_end",
-    )(*arrays, row_blocks)
+    )(*arrays, *factors)
 
 
 def greet_seq(seq_count):
@@ -704,8 +734,46 @@
     return [DMA((copies,)), DMA((copies,))]
 
 
+def slot_targets(first, local_experts, cap, routes, targets, targets_t):
+    shards, top_k, tokens = routes.shape
+    earlier = lax.broadcasted_iota(jnp.int32, (tokens, tokens), 0)
+    later = lax.broadcasted_iota(jnp.int32, (tokens, tokens), 1)
+    upto = jnp.where(earlier <= later, 1.0, 0.0).astype(BF)
+    row = lax.broadcasted_iota(jnp.int32, (8, tokens), 0)
+    for j in range(shards):
+        named = routes[j]
+        chosen = jnp.zeros((8, tokens), F32)
+        for e in range(local_experts):
+            hit = jnp.max(jnp.where(named == first + e, 1.0, 0.0), axis=0, keepdims=True)
+            chosen = jnp.where(row == e, hit, chosen)
+        place = jnp.dot(chosen.astype(BF), upto, preferred_element_type=F32) - 1.0
+        slot = jnp.where(chosen > 0.5, place + (cap * row).astype(F32), -1.0)
+        targets[j] = slot[0:local_experts].astype(jnp.int32)
+        targets_t[j] = slot.T[:, 0:local_experts].astype(jnp.int32)
+
+
 def middle_kernel(
-    count, seq_count, x_ref, dy_ref, o_ref, all_ref, own, inbox, xs, xr, xl, hold, s0, s1, s2, recv, local
+    count,
+    seq_count,
+    cap,
+    x_ref,
+    dy_ref,
+    routes,
+    o_ref,
+    all_ref,
+    targets,
+    targets_t,
+    own,
+    inbox,
+    xs,
+    xr,
+    xl,
+    hold,
+    s0,
+    s1,
+    s2,
+    recv,
+    local,
 ):
     places = where_am_i()
     i = places[0]
@@ -721,6 +789,8 @@
     put.wait()
     line = LineGather(count, places, [all_ref], [0], s0, s1, s2, recv)
     line.first(0)
+    local_experts = targets.shape[1]
+    slot_targets(i * local_experts, local_experts, cap, routes, targets, targets_t)
     for t in range(1, count):
         line.forward(t)
         if t == 1:
@@ -730,18 +800,23 @@
     seq.finish()
 
 
-def middle(blocks, dy, shards, collective):
+def middle(blocks, dy, routes, local_experts, collective):
+    shards, _, tokens = routes.shape
     count = shards // 2
     seq_count = blocks.shape[0]
     block = blocks.shape[1:]
+    anywhere = pl.BlockSpec(memory_space=ANY)
+    vmem = pl.BlockSpec(memory_space=pltpu.VMEM)
     return pl.pallas_call(
-        partial(middle_kernel, count, seq_count),
+        partial(middle_kernel, count, seq_count, CAP),
         out_shape=[
             jax.ShapeDtypeStruct(block, F32),
             jax.ShapeDtypeStruct((shards,) + dy.shape, dy.dtype),
+            jax.ShapeDtypeStruct((shards, local_experts, tokens), jnp.int32),
+            jax.ShapeDtypeStruct((shards, tokens, local_experts), jnp.int32),
         ],
-        in_specs=[pl.BlockSpec(memory_space=ANY)] * 2,
-        out_specs=[pl.BlockSpec(memory_space=pltpu.VMEM), pl.BlockSpec(memory_space=ANY)],
+        in_specs=[anywhere, anywhere, vmem],
+        out_specs=[vmem, anywhere, vmem, vmem],
         scratch_shapes=seq_scatter_scratch(block, blocks.dtype, seq_count)
         + [pltpu.VMEM(dy.shape, dy.dtype)]
         + line_sems(1, count)
@@ -750,47 +825,14 @@
             collective_id=collective, has_side_effects=True, vmem_limit_bytes=32 << 20
         ),
         name="middle",
-    )(blocks, dy)
-
-
-def seq_sum_kernel(seq_count, x_ref, o_ref, inbox, send, recv):
-    here = greet_seq(seq_count)
-    copies = []
-    for d in range(1, seq_count):
-        peer = lax.rem(here + d, seq_count)
-        copies.append(remote(x_ref, inbox.at[d - 1], send.at[d - 1], recv.at[d - 1], seq=peer))
-    for copy in copies:
-        copy.start()
-    for copy in copies:
-        copy.wait_recv()
-    total = x_ref[...]
-    for d in range(seq_count - 1):
-        total += inbox[d]
-    o_ref[...] = total
-    for copy in copies:
-        copy.wait_send()
-
-
-def seq_sum(value, seq_count, collective):
-    return pl.pallas_call(
-        partial(seq_sum_kernel, seq_count),
-        out_shape=jax.ShapeDtypeStruct(value.shape, F32),
-        in_specs=[pl.BlockSpec(memory_space=pltpu.VMEM)],
-        out_specs=pl.BlockSpec(memory_space=pltpu.VMEM),
-        scratch_shapes=[
-            pltpu.VMEM((seq_count - 1,) + value.shape, F32),
-            DMA((seq_count - 1,)),
-            DMA((seq_count - 1,)),
-        ],
-        compiler_params=pltpu.CompilerParams(collective_id=collective, has_side_effects=True),
-        name="seq_sum",
-    )(value)
+    )(blocks, dy, routes)
 
 
 class RouterGrad:
-    def __init__(self, tokens_in, logits_in, out, tokens, logits, sems):
+    def __init__(self, tokens_in, logits_in, gain_row, out, tokens, logits, total, sems):
         self.tokens_in, self.logits_in, self.out = tokens_in, logits_in, out
         self.tokens, self.logits, self.sems = tokens, logits, sems
+        self.gain_row, self.total = gain_row, total
 
     def take(self):
         return pltpu.make_async_copy(self.logits_in, self.logits, self.sems.at[2])
@@ -806,8 +848,8 @@
 
     def run(self):
         self.take().wait()
-        self.out[...] = jnp.zeros_like(self.out)
-        width = self.out.shape[1]
+        self.total[...] = jnp.zeros_like(self.total)
+        experts, width = self.total.shape
         block = 512
         pairs = self.tokens_in.shape[0] // 2
 
@@ -824,12 +866,21 @@
             @pl.loop(0, width // block)
             def _(n):
                 cols = pl.ds(pl.multiple_of(n * block, block), block)
-                total = self.out[:, cols]
+                total = self.total[:, cols]
                 for j in range(2):
                     total += jnp.dot(
                         self.logits[2 * q + j], self.tokens[buf, j, :, cols], preferred_element_type=F32
                     )
-                self.out[:, cols] = total
+                self.total[:, cols] = total
+
+        lanes = self.out.shape[1]
+
+        @pl.loop(0, width // block)
+        def _(n):
+            cols = pl.ds(pl.multiple_of(n * block, block), block)
+            gain = jnp.broadcast_to(self.gain_row[:, cols], (8, block))
+            rest = jnp.zeros((lanes - experts - 8, block), F32)
+            self.out[cols, :] = jnp.concatenate([self.total[:, cols], gain, rest], axis=0).T
 
 
 def turn_kernel(
@@ -838,9 +889,11 @@
     x_ref,
     parts_ref,
     left_ref,
-    right_ref,
+    right0,
+    right1,
     h2_ref,
     logits_ref,
+    gain_row,
     o_ref,
     sum_ref,
     grad_ref,
@@ -855,6 +908,7 @@
     outer_sem,
     tokens,
     logits,
+    router_sum,
     router_sem,
     own,
     sib,
@@ -864,8 +918,8 @@
     places = where_am_i()
     here = lax.axis_index("seq")
     line = LineScatter(count, places, [parts_ref], [0], ([own], [sib], [inbox]), sems)
-    grads = OuterGrads(left_ref, right_ref, grad_ref, (tiles_in, held, staged, outer_sem), count - 1)
-    router = RouterGrad(h2_ref, logits_ref, router_ref, tokens, logits, router_sem)
+    grads = OuterGrads(left_ref, (right0, right1), grad_ref, (tiles_in, held, staged, outer_sem), count - 1)
+    router = RouterGrad(h2_ref, logits_ref, gain_row, router_ref, tokens, logits, router_sum, router_sem)
     line.begin_loads()
     take = pltpu.make_async_copy(x_ref, hold, one)
     take.start()
@@ -890,10 +944,7 @@
             rows.relay()
 
         grads.between(step)
-
-        @pl.when(step == 0)
-        def _():
-            router.run()
+        pl.when(step == 0)(router.run)
 
     line.run(after, between)
     grads.finish()
@@ -902,29 +953,29 @@
     line.finish()
 
 
-def turn_back(block, parts, expert_in, d_up, h2_all, logits, seq_count, shards, collective):
+def turn_back(block, parts, expert_in, d_gate, d_up, h2_all, logits, gain_row, seq_count, shards, collective):
     count = shards // 2
     part = parts.shape[1:]
-    model_width = part[1]
-    local_experts, slots, hidden = d_up.shape
+    model_width = block.shape[1]
     anywhere = pl.BlockSpec(memory_space=ANY)
     return pl.pallas_call(
         partial(turn_kernel, count, seq_count),
         out_shape=[
             jax.ShapeDtypeStruct((seq_count,) + block.shape, block.dtype),
             jax.ShapeDtypeStruct(part, parts.dtype),
-            jax.ShapeDtypeStruct((local_experts, model_width, hidden), BF),
-            jax.ShapeDtypeStruct((logits.shape[1], model_width), F32),
+            jax.ShapeDtypeStruct((d_gate.shape[0], model_width, 2 * d_gate.shape[2]), BF),
+            jax.ShapeDtypeStruct((model_width, 128), F32),
         ],
-        in_specs=[anywhere] * 6,
+        in_specs=[anywhere] * 7 + [pl.BlockSpec(memory_space=pltpu.VMEM)],
         out_specs=[anywhere] * 3 + [pl.BlockSpec(memory_space=pltpu.VMEM)],
         scratch_shapes=[pltpu.VMEM(block.shape, block.dtype)]
         + seq_gather_sems(seq_count)
         + [DMA]
-        + outer_scratch(d_up, 512)
+        + outer_scratch(d_up, 512, 2)
         + [
             pltpu.VMEM((2, 2) + h2_all.shape[1:], BF),
             pltpu.VMEM(logits.shape, BF),
+            pltpu.VMEM((logits.shape[1], model_width), F32),
             DMA((3,)),
         ]
         + [pltpu.VMEM((count,) + part, BF)] * 2
@@ -935,7 +986,7 @@
         ),
         cost_estimate=pl.CostEstimate(flops=60_000_000_000, bytes_accessed=200_000_000, transcendentals=0),
         name="turn_back",
-    )(block, parts, expert_in, d_up, h2_all, logits)
+    )(block, parts, expert_in, d_gate, d_up, h2_all, logits, gain_row)
 
 
 def half_sign(shape):
@@ -961,18 +1012,69 @@
     return weights * (1.0 / jnp.sum(weights, axis=-1, keepdims=True))
 
 
+class SeqSum:
+    def __init__(self, seq_count, sheet, inbox, send, recv):
+        here = lax.axis_index("seq")
+        self.sheet, self.inbox = sheet, inbox
+        self.copies = []
+        for d in range(1, seq_count):
+            peer = lax.rem(here + d, seq_count)
+            self.copies.append(remote(sheet, inbox.at[d - 1], send.at[d - 1], recv.at[d - 1], seq=peer))
+
+    def begin(self):
+        for copy in self.copies:
+            copy.start()
+
+    def total(self):
+        for copy in self.copies:
+            copy.wait_recv()
+        total = self.sheet[...]
+        for d in range(len(self.copies)):
+            total += self.inbox[d]
+        for copy in self.copies:
+            copy.wait_send()
+        return total
+
+
 def attend_kernel(
-    row_block, q_raw, k_raw, v_ref, rq, rk, gq, gk, cos, sin, doc_col, doc_row, o_ref, q_out, k_out
+    seq_count,
+    row_block,
+    model_width,
+    q_raw,
+    k_raw,
+    v_ref,
+    squares,
+    gq,
+    gk,
+    cos,
+    sin,
+    doc_col,
+    doc_row,
+    o_ref,
+    q_out,
+    k_out,
+    scales,
+    inbox,
+    send,
+    recv,
 ):
     seq_len = q_raw.shape[0]
+
+    @pl.when(pl.program_id(0) == 0)
+    def _():
+        greet_seq(seq_count)
+        sums = SeqSum(seq_count, squares, inbox, send, recv)
+        sums.begin()
+        scales[...] = lax.rsqrt(sums.total() / model_width + EPSILON).T
+
     sign = half_sign(cos.shape)
 
-    def rotated(raw, scale, gain):
-        value = raw[...] * scale[...] * gain[...]
+    def rotated(raw, lane, gain):
+        value = raw[...] * scales[:, lane : lane + 1] * gain[...]
         return (value * cos[...] + turn(value) * (sin[...] * sign)).astype(BF)
 
-    q_out[...] = rotated(q_raw, rq, gq)
-    k_out[...] = rotated(k_raw, rk, gk)
+    q_out[...] = rotated(q_raw, 0, gq)
+    k_out[...] = rotated(k_raw, 1, gk)
     scale_by = HEAD ** (-0.5)
     for start in range(0, seq_len, row_block):
         end = start + row_block
@@ -984,55 +1086,92 @@
         ).astype(BF)
 
 
-def attend(q_raw, k_raw, values, rq, rk, gq, gk, cos, sin, doc_col, doc_row):
+def attend(q_raw, k_raw, values, squares, gq, gk, cos, sin, doc_col, doc_row, model_width, seq_count, collective):
     seq_len, width = q_raw.shape
     head = pl.BlockSpec((seq_len, HEAD), lambda h: (0, h))
     gain = pl.BlockSpec((1, HEAD), lambda h: (0, h))
 
-    def whole(x):
-        return pl.BlockSpec(x.shape, lambda h: (0, 0))
+    def whole(shape):
+        return pl.BlockSpec(shape, lambda h: (0, 0))
 
     out = jax.ShapeDtypeStruct((seq_len, width), BF)
     return pl.pallas_call(
-        partial(attend_kernel, 256),
+        partial(attend_kernel, seq_count, 256, model_width),
         grid=(width // HEAD,),
-        out_shape=[out, out, out],
-        in_specs=[head, head, head, whole(rq), whole(rk), gain, gain, whole(cos), whole(sin)]
-        + [whole(doc_col), whole(doc_row)],
-        out_specs=[head, head, head],
-        compiler_params=pltpu.CompilerParams(vmem_limit_bytes=48 << 20),
+        out_shape=[
+            out,
+            out,
+            out,
+            jax.ShapeDtypeStruct((seq_len, 8), F32),
+        ],
+        in_specs=[head, head, head, whole(squares.shape), gain, gain, whole(cos.shape), whole(sin.shape)]
+        + [whole(doc_col.shape), whole(doc_row.shape)],
+        out_specs=[head, head, head, whole((seq_len, 8))],
+        scratch_shapes=[
+            pltpu.VMEM((seq_count - 1,) + squares.shape, F32),
+            DMA((seq_count - 1,)),
+            DMA((seq_count - 1,)),
+        ],
+        compiler_params=pltpu.CompilerParams(
+            collective_id=collective, has_side_effects=True, vmem_limit_bytes=48 << 20
+        ),
         name="attend",
-    )(q_raw, k_raw, values, rq, rk, gq, gk, cos, sin, doc_col, doc_row)
+    )(q_raw, k_raw, values, squares, gq, gk, cos, sin, doc_col, doc_row)
 
 
 def attend_back_kernel(
+    count,
+    seq_count,
+    heads,
     row_block,
+    model_width,
     q_low,
     k_low,
     v_ref,
     do_ref,
     q_raw,
     k_raw,
-    rq,
-    rk,
+    scales,
     gq,
     gk,
     cos,
     sin,
     doc_col,
     doc_row,
-    uq_ref,
-    uk_ref,
+    parts_ref,
+    dq_ref,
+    dk_ref,
     dv_ref,
-    dots,
-    gain_q,
-    gain_k,
+    gain_ref,
+    sum_ref,
     dq_acc,
     dk_acc,
     dv_acc,
+    uq,
+    uk,
+    dots,
+    sheet,
+    inbox,
+    send,
+    recv,
+    own,
+    sib,
+    landed,
+    *sems,
 ):
     seq_len = q_low.shape[0]
+    head = pl.program_id(0)
     scale_by = HEAD ** (-0.5)
+    places = where_am_i()
+    line = LineScatter(count, places, [parts_ref], [0], ([own], [sib], [landed]), sems)
+
+    @pl.when(head == 0)
+    def _():
+        line.begin_loads()
+        greet(count, places, seq_count)
+        line.begin()
+        dots[...] = jnp.zeros_like(dots)
+
     dk_acc[...] = jnp.zeros_like(dk_acc)
     dv_acc[...] = jnp.zeros_like(dv_acc)
     for start in range(0, seq_len, row_block):
@@ -1055,57 +1194,140 @@
         dv_acc[:end, :] += lax.dot_general(
             probs.astype(BF), grad_rows, over_rows, preferred_element_type=F32
         )
+        if start == row_block:
+
+            @pl.when(head == 0)
+            def _():
+                line.event(0)
+
     dv_ref[...] = dv_acc[...].astype(BF)
     sign = half_sign(cos.shape)
-
-    def unrotated(acc, raw, scale, gain, u_ref, gain_ref, lane):
+    cols = pl.ds(pl.multiple_of(head * HEAD, HEAD), HEAD)
+    blocks, _, lanes = gain_ref.shape
+    rows = HEAD // blocks
+
+    def unrotated(acc, raw, gain, u_ref, lane):
         low = (acc[...] * scale_by).astype(BF).astype(F32)
         back = low * cos[...] - turn(low * sin[...]) * sign
-        gain_ref[...] = jnp.sum(back * raw[...] * scale[...], axis=0, keepdims=True)
+        value = raw[:, cols]
+        grad_gain = jnp.sum(back * value * scales[:, lane : lane + 1], axis=0, keepdims=True)
         u = back * gain[...]
-        u_ref[...] = u
-        dot = jnp.sum(u * raw[...], axis=1, keepdims=True)
-
-        @pl.when(pl.program_id(0) == 0)
+        u_ref[:, cols] = u
+        dots[:, lane : lane + 1] += jnp.sum(u * value, axis=1, keepdims=True)
+        return grad_gain
+
+    grads = (unrotated(dq_acc, q_raw, gq, uq, 0), unrotated(dk_acc, k_raw, gk, uk, 1))
+    which = lax.broadcasted_iota(jnp.int32, (8, lanes), 0)
+    both = jnp.where(which == 0, grads[0], jnp.where(which == 1, grads[1], 0.0))
+    for block in range(blocks):
+        gain_ref[block] = both if block == 0 else pltpu.roll(both, lanes - block * rows, 1)
+
+    for step in range(1, count - 1):
+
+        @pl.when(head == min(step, heads - 1))
         def _():
-            dots[:, lane : lane + 1] = dot
-
-        @pl.when(pl.program_id(0) > 0)
-        def _():
-            dots[:, lane : lane + 1] += dot
-
-    unrotated(dq_acc, q_raw, rq, gq, uq_ref, gain_q, 0)
-    unrotated(dk_acc, k_raw, rk, gk, uk_ref, gain_k, 1)
-
-
-def attend_back(q_low, k_low, values, d_heads, q_raw, k_raw, rq, rk, gq, gk, cos, sin, doc_col, doc_row):
+            line.event(step)
+
+    @pl.when(head == heads - 1)
+    def _():
+        sheet[...] = dots[...].T
+        sums = SeqSum(seq_count, sheet, inbox, send, recv)
+        sums.begin()
+        dots[...] = sums.total().T / model_width
+        strip = 128
+
+        @pl.loop(0, seq_len // strip)
+        def _(n):
+            part = pl.ds(pl.multiple_of(n * strip, strip), strip)
+            for lane, u_ref, raw, out in ((0, uq, q_raw, dq_ref), (1, uk, k_raw, dk_ref)):
+                scale = scales[part, lane : lane + 1]
+                product = dots[part, lane : lane + 1]
+                out[part, :] = (
+                    scale * u_ref[part, :] - raw[part, :] * (scale * scale * scale * product)
+                ).astype(BF)
+
+        def after(a, q):
+            out = pltpu.make_async_copy(own.at[q], sum_ref, sems[6].at[0, q])
+            out.start()
+            out.wait()
+
+        line.final(after)
+        line.finish()
+
+
+def attend_back(
+    q_low,
+    k_low,
+    values,
+    d_heads,
+    q_raw,
+    k_raw,
+    scales,
+    gq,
+    gk,
+    cos,
+    sin,
+    doc_col,
+    doc_row,
+    parts,
+    rows,
+    model_width,
+    seq_count,
+    collective,
+):
     seq_len, width = q_raw.shape
+    heads = width // HEAD
+    blocks = HEAD // rows
+    shards = parts.shape[0]
+    count = shards // 2
+    part = parts.shape[1:]
     head = pl.BlockSpec((seq_len, HEAD), lambda h: (0, h))
     gain = pl.BlockSpec((1, HEAD), lambda h: (0, h))
 
-    def whole(x):
-        return pl.BlockSpec(x.shape, lambda h: (0, 0))
-
-    wide = jax.ShapeDtypeStruct((seq_len, width), F32)
-    row = jax.ShapeDtypeStruct((1, width), F32)
+    def whole(shape):
+        return pl.BlockSpec(shape, lambda h: (0, 0))
+
+    def once(x):
+        return pl.BlockSpec(x.shape, lambda h: (0, 0), pipeline_mode=pl.Buffered(1))
+
+    out = jax.ShapeDtypeStruct((seq_len, width), BF)
     return pl.pallas_call(
-        partial(attend_back_kernel, 256),
-        grid=(width // HEAD,),
+        partial(attend_back_kernel, count, seq_count, heads, 256, model_width),
+        grid=(heads,),
         out_shape=[
-            wide,
-            wide,
-            jax.ShapeDtypeStruct((seq_len, width), BF),
-            jax.ShapeDtypeStruct((seq_len, 2), F32),
-            row,
-            row,
+            out,
+            out,
+            out,
+            jax.ShapeDtypeStruct((width // rows, 8, HEAD), F32),
+            jax.ShapeDtypeStruct(part, BF),
         ],
-        in_specs=[head] * 6
-        + [whole(rq), whole(rk), gain, gain, whole(cos), whole(sin), whole(doc_col), whole(doc_row)],
-        out_specs=[head, head, head, pl.BlockSpec((seq_len, 2), lambda h: (0, 0)), gain, gain],
-        scratch_shapes=[pltpu.VMEM((seq_len, HEAD), F32)] * 3,
-        compiler_params=pltpu.CompilerParams(vmem_limit_bytes=56 << 20),
+        in_specs=[head] * 4
+        + [once(q_raw), once(k_raw), once(scales), gain, gain, once(cos), once(sin)]
+        + [once(doc_col), once(doc_row), pl.BlockSpec(memory_space=ANY)],
+        out_specs=[
+            whole((seq_len, width)),
+            whole((seq_len, width)),
+            head,
+            pl.BlockSpec((blocks, 8, HEAD), lambda h: (h, 0, 0)),
+            pl.BlockSpec(memory_space=ANY),
+        ],
+        scratch_shapes=[pltpu.VMEM((seq_len, HEAD), F32)] * 3
+        + [pltpu.VMEM((seq_len, width), F32)] * 2
+        + [
+            pltpu.VMEM((seq_len, 8), F32),
+            pltpu.VMEM((8, seq_len), F32),
+            pltpu.VMEM((seq_count - 1, 8, seq_len), F32),
+            DMA((seq_count - 1,)),
+            DMA((seq_count - 1,)),
+        ]
+        + [pltpu.VMEM((count,) + part, BF)] * 2
+        + [pltpu.VMEM((count + 1,) + part, BF)]
+        + [DMA((1, count))] * 7,
+        compiler_params=pltpu.CompilerParams(
+            collective_id=collective, has_side_effects=True, vmem_limit_bytes=60 << 20
+        ),
         name="attend_back",
-    )(q_low, k_low, values, d_heads, q_raw, k_raw, rq, rk, gq, gk, cos, sin, doc_col, doc_row)
+    )(q_low, k_low, values, d_heads, q_raw, k_raw, scales, gq, gk, cos, sin, doc_col, doc_row, parts)
 
 
 def experts_in_kernel(
@@ -1115,8 +1337,7 @@
     dy_ref,
     targets,
     router_t,
-    wg_ref,
-    wu_ref,
+    wgu_ref,
     h2_out,
     x_out,
     y_out,
@@ -1126,8 +1347,7 @@
     gate_slots,
     probs_out,
     h2,
-    wg,
-    wu,
+    wgu,
     dy,
     xs,
     ys,
@@ -1145,7 +1365,8 @@
 ):
     places = where_am_i()
     i, p, sib = places
-    local_experts, model_width, hidden = wg_ref.shape
+    local_experts, model_width, hidden = wgu_ref.shape
+    hidden = hidden // 2
     tokens = h2_ref.shape[0]
     experts = router_t.shape[0]
     own_in = pltpu.make_async_copy(h2_ref, h2.at[i], h_sem.at[0])
@@ -1157,8 +1378,7 @@
 
     fetch(p, 0).start()
     for e in range(local_experts):
-        pltpu.make_async_copy(wg_ref.at[e], wg.at[e], w_sem.at[0, e]).start()
-        pltpu.make_async_copy(wu_ref.at[e], wu.at[e], w_sem.at[1, e]).start()
+        pltpu.make_async_copy(wgu_ref.at[e], wgu.at[e], w_sem.at[e]).start()
     greet(count, places)
     own_in.wait()
     line = LineGather(count, places, [h2], [0], s0, s1, s2, recv)
@@ -1243,16 +1463,16 @@
 
             @pl.when(k == 0)
             def _():
-                pltpu.make_async_copy(wg_ref.at[e], wg.at[e], w_sem.at[0, e]).wait()
-                pltpu.make_async_copy(wu_ref.at[e], wu.at[e], w_sem.at[1, e]).wait()
+                pltpu.make_async_copy(wgu_ref.at[e], wgu.at[e], w_sem.at[e]).wait()
 
             wide = 256
 
             @pl.loop(0, hidden // wide)
             def _(n):
                 cols = pl.ds(pl.multiple_of(n * wide, wide), wide)
-                gate = jnp.dot(xs[e], wg[e, :, cols], preferred_element_type=F32)
-                up = jnp.dot(xs[e], wu[e, :, cols], preferred_element_type=F32)
+                beyond = pl.ds(pl.multiple_of(hidden + n * wide, wide), wide)
+                gate = jnp.dot(xs[e], wgu[e, :, cols], preferred_element_type=F32)
+                up = jnp.dot(xs[e], wgu[e, :, beyond], preferred_element_type=F32)
                 sigmoid = 1.0 / (1.0 + jnp.exp(-gate))
                 silu = gate * sigmoid
                 acts[e, :, cols] = (silu * up).astype(BF)
@@ -1305,9 +1525,10 @@
             line.copy(0, slot, 2, count + t, sib).wait_send()
 
 
-def experts_in(h2, dy_all, targets, router_t, w_gate, w_up, collective):
+def experts_in(h2, dy_all, targets, router_t, w_gate_up, collective):
     shards, tokens, model_width = dy_all.shape
-    local_experts, _, hidden = w_gate.shape
+    local_experts, _, hidden = w_gate_up.shape
+    hidden = hidden // 2
     experts = router_t.shape[0]
     count = shards // 2
     wide = jax.ShapeDtypeStruct((local_experts, count * 2 * CAP, model_width), BF)
@@ -1326,23 +1547,22 @@
             jax.ShapeDtypeStruct((local_experts, count, 2 * CAP, 1), F32),
             jax.ShapeDtypeStruct((shards, experts, tokens), F32),
         ],
-        in_specs=[anywhere, anywhere, vmem, vmem, anywhere, anywhere],
+        in_specs=[anywhere, anywhere, vmem, vmem, anywhere],
         out_specs=[anywhere] * 6 + [vmem, vmem],
         scratch_shapes=[
             pltpu.VMEM((shards, tokens, model_width), BF),
-            pltpu.VMEM(w_gate.shape, BF),
-            pltpu.VMEM(w_up.shape, BF),
+            pltpu.VMEM(w_gate_up.shape, BF),
             pltpu.VMEM((2, 2, tokens, model_width), BF),
         ]
         + [pltpu.VMEM((local_experts, 2 * CAP, model_width), BF)] * 2
         + [pltpu.VMEM((local_experts, 2 * CAP, hidden), BF)] * 3
         + line_sems(1, count)
-        + [DMA((2, local_experts)), DMA((2,)), DMA((2,)), DMA((5, local_experts))],
+        + [DMA((local_experts,)), DMA((2,)), DMA((2,)), DMA((5, local_experts))],
         compiler_params=pltpu.CompilerParams(
             collective_id=collective, has_side_effects=True, vmem_limit_bytes=60 << 20
         ),
         name="experts_in",
-    )(h2, dy_all, targets, router_t, w_gate, w_up)
+    )(h2, dy_all, targets, router_t, w_gate_up)
 
 
 def experts_mid_kernel(
@@ -1497,10 +1717,11 @@
 
 
 class OuterGrads:
-    def __init__(self, left, right, out, scratch, steps):
-        self.left, self.right, self.out = left, right, out
+    def __init__(self, left, rights, out, scratch, steps):
+        self.left, self.rights, self.out = left, rights, out
         self.tiles_in, self.held, self.staged, self.sems = scratch
-        self.experts, self.width, self.hidden = out.shape
+        self.experts, self.width, _ = out.shape
+        self.hidden = rights[0].shape[2]
         self.tile = self.staged.shape[1]
         self.tiles = self.width // self.tile
         self.units = self.experts * self.tiles
@@ -1519,11 +1740,12 @@
         target = self.out.at[u // self.tiles, self.span(u)]
         return pltpu.make_async_copy(self.staged.at[buf], target, self.sems.at[1, buf])
 
-    def hold(self):
-        return pltpu.make_async_copy(self.right, self.held, self.sems.at[2, 0])
+    def hold(self, n):
+        return pltpu.make_async_copy(self.rights[n], self.held.at[n], self.sems.at[2, n])
 
     def begin(self):
-        self.hold().start()
+        for n in range(len(self.rights)):
+            self.hold(n).start()
         self.fetch(0).start()
 
     def between(self, step):
@@ -1531,7 +1753,8 @@
         def _(u):
             @pl.when(u == 0)
             def _():
-                self.hold().wait()
+                for n in range(len(self.rights)):
+                    self.hold(n).wait()
 
             self.fetch(u).wait()
 
@@ -1544,12 +1767,13 @@
                 self.put(u - 2).wait()
 
             buf = lax.rem(u, 2)
-            self.staged[buf] = lax.dot_general(
-                self.tiles_in[buf],
-                self.held[u // self.tiles],
-                (((0,), (0,)), ((), ())),
-                preferred_element_type=F32,
-            ).astype(BF)
+            for n in range(len(self.rights)):
+                self.staged[buf, :, n * self.hidden : (n + 1) * self.hidden] = lax.dot_general(
+                    self.tiles_in[buf],
+                    self.held[n, u // self.tiles],
+                    (((0,), (0,)), ((), ())),
+                    preferred_element_type=F32,
+                ).astype(BF)
             self.put(u).start()
 
     def finish(self):
@@ -1557,12 +1781,12 @@
         self.put(self.units - 1).wait()
 
 
-def outer_scratch(right, tile):
+def outer_scratch(right, tile, factors):
     slots, hidden = right.shape[1:]
     return [
         pltpu.VMEM((2, slots, tile), BF),
-        pltpu.VMEM(right.shape, BF),
-        pltpu.VMEM((2, tile, hidden), BF),
+        pltpu.VMEM((factors,) + right.shape, BF),
+        pltpu.VMEM((2, tile, factors * hidden), BF),
         DMA((3, 2)),
     ]
 
@@ -1570,7 +1794,6 @@
 def experts_out_kernel(
     count,
     cap,
-    x_in,
     gated_in,
     d_gate_in,
     d_up_in,
@@ -1579,15 +1802,13 @@
     targets_t,
     probs_ref,
     router_t,
-    wg_in,
-    wu_in,
+    wgu_in,
     wd_in,
-    parts_out,
+    parts_a,
+    parts_b,
     logit_ref,
     sum_ref,
-    g_gate_out,
-    wg,
-    wu,
+    wgu,
     wd,
     gated,
     d_gate,
@@ -1600,10 +1821,6 @@
     w_sem,
     in_sem,
     part_sem,
-    tiles_in,
-    held,
-    staged,
-    outer_sem,
     *sems,
 ):
     places = where_am_i()
@@ -1615,8 +1832,7 @@
     first = i * local_experts
     over_lanes = (((1,), (1,)), ((), ()))
     line = StagedScatter(count, places, stage, ([own], [sibling], [inbox]), sems)
-    grads_of = OuterGrads(x_in, d_gate_in, g_gate_out, (tiles_in, held, staged, outer_sem), count - 1)
-    weights = ((wd_in, wd), (wg_in, wg), (wu_in, wu))
+    weights = ((wgu_in, wgu), (wd_in, wd))
     inputs = ((gated_in, gated), (d_gate_in, d_gate), (d_up_in, d_up))
 
     def weight(n):
@@ -1626,17 +1842,19 @@
         rows = pl.ds(pl.multiple_of(q * 2 * cap, 2 * cap), 2 * cap)
         return pltpu.make_async_copy(inputs[n][0].at[:, rows], inputs[n][1].at[buf], in_sem.at[n, buf])
 
-    def put(q):
-        return pltpu.make_async_copy(parts, parts_out.at[pl.ds(2 * q, 2)], part_sem)
+    first_part = parts_a.shape[2]
+
+    def put(n, q):
+        src = parts.at[:, :, pl.ds(n * first_part, (parts_a, parts_b)[n].shape[2])]
+        return pltpu.make_async_copy(src, (parts_a, parts_b)[n].at[pl.ds(2 * q, 2)], part_sem.at[n])
 
     def order(k):
         return chunk_order(count - 1 - k, p, count)
 
     for n in range(3):
         fetch(n, order(0), 0).start()
-    for n in range(3):
+    for n in range(2):
         weight(n).start()
-    grads_of.begin()
     greet(count, places)
     slot_rows = lax.broadcasted_iota(jnp.int32, (local_experts * cap, tokens), 0)
     slot_lanes = lax.broadcasted_iota(jnp.int32, (tokens, local_experts * cap), 1)
@@ -1673,31 +1891,30 @@
 
         @pl.when(k > 0)
         def _():
-            put(q).wait()
             line.to_sib(0, order(k - 1)).wait_send()
 
         @pl.when(k == 0)
         def _():
-            for n in range(3):
-                weight(n).wait()
+            weight(0).wait()
 
         block = 512
 
         @pl.loop(0, model_width // block)
         def _(n):
             cols = pl.ds(pl.multiple_of(n * block, block), block)
-            outs, grads = [], []
+            grads = []
             for e in range(local_experts):
-                outs.append(jnp.dot(gated[buf, e], wd[e, :, cols], preferred_element_type=F32))
                 grads.append(
-                    lax.dot_general(d_gate[buf, e], wg[e, cols, :], over_lanes, preferred_element_type=F32)
-                    + lax.dot_general(d_up[buf, e], wu[e, cols, :], over_lanes, preferred_element_type=F32)
+                    lax.dot_general(
+                        d_gate[buf, e], wgu[e, cols, 0:hidden], over_lanes, preferred_element_type=F32
+                    )
+                    + lax.dot_general(
+                        d_up[buf, e], wgu[e, cols, hidden:], over_lanes, preferred_element_type=F32
+                    )
                 )
             for j in range(2):
                 part = slice(j * cap, (j + 1) * cap)
-                mine = jnp.concatenate([value[part] for value in outs], axis=0).astype(BF)
                 back = jnp.concatenate([value[part] for value in grads], axis=0).astype(BF)
-                parts[j, :, cols] = jnp.dot(picks[j], mine, preferred_element_type=F32).astype(BF)
                 total = (
                     jnp.dot(picks[j], back, preferred_element_type=F32)
                     + jnp.dot(logits_low[j], router_t[:, cols], preferred_element_type=F32)
@@ -1712,31 +1929,49 @@
                     stage[:, cols] = total
 
         line.to_sib(0, q).start()
-        put(q).start()
+
+        @pl.when(k > 0)
+        def _():
+            put(0, q).wait()
+            put(1, q).wait()
+
+        @pl.when(k == 0)
+        def _():
+            weight(1).wait()
+
+        @pl.loop(0, model_width // block)
+        def _(n):
+            cols = pl.ds(pl.multiple_of(n * block, block), block)
+            outs = []
+            for e in range(local_experts):
+                outs.append(jnp.dot(gated[buf, e], wd[e, :, cols], preferred_element_type=F32))
+            for j in range(2):
+                part = slice(j * cap, (j + 1) * cap)
+                mine = jnp.concatenate([value[part] for value in outs], axis=0).astype(BF)
+                parts[j, :, cols] = jnp.dot(picks[j], mine, preferred_element_type=F32).astype(BF)
+
+        put(0, q).start()
+        put(1, q).start()
 
     @pl.loop(0, 1)
     def _(k):
         compute(k)
 
-    def between(step):
-        compute(step + 1)
-        grads_of.between(step)
-
-    line.run(lambda a, q: None, between)
-    grads_of.finish()
-    put(0).wait()
+    line.run(lambda a, q: None, lambda step: compute(step + 1))
+    put(0, 0).wait()
+    put(1, 0).wait()
     line.to_sib(0, order(count - 1)).wait_send()
-    out = pltpu.make_async_copy(own.at[p], sum_ref, part_sem)
+    out = pltpu.make_async_copy(own.at[p], sum_ref, part_sem.at[0])
     out.start()
     out.wait()
     line.finish()
 
 
 def experts_out(
-    expert_in, gated, d_gate, d_up, dots, targets, targets_t, probs, router_t, w_gate, w_up, w_down, collective
+    gated, d_gate, d_up, dots, targets, targets_t, probs, router_t, w_gate_up, w_down, collective
 ):
-    local_experts, slots, model_width = expert_in.shape
-    hidden = gated.shape[2]
+    local_experts, slots, hidden = gated.shape
+    model_width = router_t.shape[1]
     shards, experts, tokens = probs.shape
     count = shards // 2
     anywhere = pl.BlockSpec(memory_space=ANY)
@@ -1744,14 +1979,14 @@
     return pl.pallas_call(
         partial(experts_out_kernel, count, CAP),
         out_shape=[
-            jax.ShapeDtypeStruct((shards, tokens, model_width), BF),
+            jax.ShapeDtypeStruct((shards, tokens, model_width // 8 * 5), BF),
+            jax.ShapeDtypeStruct((shards, tokens, model_width // 8 * 3), BF),
             jax.ShapeDtypeStruct(probs.shape, BF),
             jax.ShapeDtypeStruct((tokens, model_width), BF),
-            jax.ShapeDtypeStruct(w_gate.shape, BF),
         ],
-        in_specs=[anywhere] * 4 + [vmem] * 5 + [anywhere] * 3,
-        out_specs=[anywhere, vmem, anywhere, anywhere],
-        scratch_shapes=[pltpu.VMEM(x.shape, BF) for x in (w_gate, w_up, w_down)]
+        in_specs=[anywhere] * 3 + [vmem] * 5 + [anywhere] * 2,
+        out_specs=[anywhere, anywhere, vmem, anywhere],
+        scratch_shapes=[pltpu.VMEM(x.shape, BF) for x in (w_gate_up, w_down)]
         + [pltpu.VMEM((2, local_experts, 2 * CAP, hidden), BF)] * 3
         + [
             pltpu.VMEM((2, tokens, model_width), BF),
@@ -1759,26 +1994,25 @@
             pltpu.VMEM((count, tokens, model_width), BF),
             pltpu.VMEM((count, tokens, model_width), BF),
             pltpu.VMEM((count + 1, tokens, model_width), BF),
-            DMA((3,)),
+            DMA((2,)),
             DMA((3, 2)),
-            DMA,
+            DMA((2,)),
         ]
-        + outer_scratch(d_gate, 256)
         + [DMA((1, count))] * 7,
         compiler_params=pltpu.CompilerParams(
-            collective_id=collective, has_side_effects=True, vmem_limit_bytes=63 << 20
+            collective_id=collective, has_side_effects=True, vmem_limit_bytes=67_043_328
         ),
         cost_estimate=pl.CostEstimate(flops=60_000_000_000, bytes_accessed=200_000_000, transcendentals=0),
         name="experts_out",
-    )(expert_in, gated, d_gate, d_up, dots, targets, targets_t, probs, router_t, w_gate, w_up, w_down)
-
-
-def rope_tables(positions, head_dim):
+    )(gated, d_gate, d_up, dots, targets, targets_t, probs, router_t, w_gate_up, w_down)
+
+
+def rope_tables(seq_len, head_dim):
     half_dim = head_dim // 2
-    inverse = ROPE_BASE ** (-(jnp.arange(half_dim, dtype=F32) * 2.0 / head_dim))
-    angles = positions.astype(F32)[:, None] * inverse[None, :]
-    angles = jnp.concatenate([angles, angles], axis=-1)
-    return (jnp.cos(angles), jnp.sin(angles))
+    inverse = np.float32(ROPE_BASE) ** (-(np.arange(half_dim, dtype=np.float32) * 2.0 / head_dim))
+    angles = np.arange(seq_len, dtype=np.float32)[:, None] * inverse.astype(np.float32)[None, :]
+    angles = np.concatenate([angles, angles], axis=-1).astype(np.float64)
+    return (np.cos(angles).astype(np.float32), np.sin(angles).astype(np.float32))
 
 
 def dot(left, right, sides=(1, 0), out=F32):
@@ -1830,19 +2064,17 @@
         axis=1,
     )
     gains = jnp.pad(jnp.stack([query_gain, key_gain]), ((0, 14), (0, lanes - rows)))
-    routes_flat = routes.reshape(tok_rows * top_k // lanes, lanes)
-    wq, wk, wv, wo, small_all, gains_all, routes_all, x_all = gather_start(
-        (w_query, w_key, w_value, w_output, small, gains, routes_flat, inputs[0]), seq_count, shards, 0
+    wq, wk, wv, small_all, gains_all, routes_all, wo, x_all = gather_start(
+        (w_query, w_key, w_value, small, gains, routes[0].T, w_output, inputs[0]), seq_count, shards, 0
     )
     x_all = x_all.reshape(seq_len, model_width)
-    full_gate = lax.all_gather(w_gate, "seq", axis=1, tiled=True)
-    full_up = lax.all_gather(w_up, "seq", axis=1, tiled=True)
+    gate_up = jnp.concatenate([w_gate, w_up], axis=2)
+    full_gate_up = lax.all_gather(gate_up, "seq", axis=1, tiled=True)
     full_down = lax.all_gather(w_down, "seq", axis=1, tiled=True)
 
     wq = wq.reshape(model_width, width)
     wk = wk.reshape(model_width, width)
     wv = wv.reshape(model_width, width)
-    wo = wo.reshape(width, model_width)
     small_all = small_all.reshape(model_width, lanes)
     w_r = small_all[:, :experts]
     gain_a = small_all[:, experts].astype(F32)
@@ -1855,38 +2087,33 @@
     q_raw = dot(h1, wq)
     k_raw = dot(h1, wk)
     values = dot(h1, wv, out=BF)
-    squares = jnp.stack([jnp.sum(q_raw * q_raw, axis=1), jnp.sum(k_raw * k_raw, axis=1)])
-    squares = seq_sum(squares, seq_count, 1)
-    scales = lax.rsqrt(squares / model_width + EPSILON)
-    rq, rk = scales[0][:, None], scales[1][:, None]
-    cos, sin = rope_tables(jnp.arange(seq_len, dtype=jnp.int32), HEAD)
+    squares = jnp.stack(
+        [jnp.sum(q_raw * q_raw, axis=1), jnp.sum(k_raw * k_raw, axis=1)]
+        + [jnp.ones((seq_len,), F32)] * 6
+    )
+    cos, sin = rope_tables(seq_len, HEAD)
     doc_row = doc_ids
     doc_col = doc_ids.reshape(seq_len, 1)
-    attended, q_low, k_low = attend(q_raw, k_raw, values, rq, rk, gq, gk, cos, sin, doc_col, doc_row)
+    attended, q_low, k_low, scales = attend(
+        q_raw, k_raw, values, squares, gq, gk, cos, sin, doc_col, doc_row, model_width, seq_count, 1
+    )
+    wo = wo.reshape(width, model_width)
     projected = dot(attended, wo, out=BF).reshape(seq_count, tok_rows, model_width)
     rows_in = inputs[0].astype(F32)
     grad_rows = out_grad[0].astype(F32)
-    summed, dy_all = middle(projected, out_grad[0], shards, 2)
+    summed, dy_all, targets, targets_t = middle(projected, out_grad[0], routes_all, local_experts, 2)
     x_mid = rows_in + summed
     scale_f = inverse_rms(x_mid)
     h2 = (x_mid * scale_f * gain_f).astype(BF)
 
-    routes_all = routes_all.reshape(shards, tok_rows, top_k)
-    local_ids = lax.axis_index("fsdp") * local_experts + jnp.arange(local_experts, dtype=jnp.int32)
-    chosen = jnp.any(routes_all[:, None] == local_ids[None, :, None, None], axis=3)
-    slot = jnp.cumsum(chosen.astype(jnp.int32), axis=2) - 1
-    slot = slot + CAP * jnp.arange(local_experts, dtype=jnp.int32)[None, :, None]
-    targets = jnp.where(chosen, slot, -1)
-    targets_t = jnp.swapaxes(targets, 1, 2)
     router_t = w_r.T
     h2_all, expert_in, grad_slots, act, by_up, by_gate, gate_slots, gate_probs = experts_in(
-        h2, dy_all, targets, router_t, full_gate, full_up, 3
+        h2, dy_all, targets, router_t, full_gate_up, 3
     )
     gated, d_gate, d_up, dots_slots, g_down = experts_mid(
         grad_slots, act, by_up, by_gate, gate_slots, full_down
     )
-    out_parts, grad_logits, grad_h2, g_gate = experts_out(
-        expert_in,
+    parts_a, parts_b, grad_logits, grad_h2 = experts_out(
         gated,
         d_gate,
         d_up,
@@ -1895,8 +2122,7 @@
         targets_t,
         gate_probs,
         router_t,
-        full_gate,
-        full_up,
+        full_gate_up,
         full_down,
         4,
     )
@@ -1905,7 +2131,7 @@
         return lax.psum_scatter(part, "seq", scatter_dimension=1, tiled=True)
 
     g_down = spread(g_down)
-    g_gate = spread(g_gate)
+    grad_h2, g_down = lax.optimization_barrier((grad_h2, g_down))
     grad_h2 = grad_h2.astype(F32)
 
     u_rows = gain_f * grad_h2
@@ -1916,46 +2142,58 @@
     )
     ffn_part = jnp.sum(grad_h2 * x_mid * scale_f, axis=0)
 
-    d_attn, out_sum, g_up, router_part = turn_back(
-        grad_mid.astype(BF), out_parts, expert_in, d_up, h2_all, grad_logits, seq_count, shards, 5
+    d_attn, sum_a, g_gate_up, small_part = turn_back(
+        grad_mid.astype(BF),
+        parts_a,
+        expert_in,
+        d_gate,
+        d_up,
+        h2_all,
+        grad_logits,
+        ffn_part[None],
+        seq_count,
+        shards,
+        5,
     )
-    g_up = spread(g_up)
+    g_gate_up = spread(g_gate_up)
     d_attn = d_attn.reshape(seq_len, model_width)
-    result = x_mid + out_sum.astype(F32)
     d_heads = dot(d_attn, wo, (1, 1), BF)
-    u_q, u_k, dv_low, dots, gain_q_part, gain_k_part = attend_back(
-        q_low, k_low, values, d_heads, q_raw, k_raw, rq, rk, gq, gk, cos, sin, doc_col, doc_row
+    dq_low, dk_low, dv_low, gains_part, sum_b = attend_back(
+        q_low,
+        k_low,
+        values,
+        d_heads,
+        q_raw,
+        k_raw,
+        scales,
+        gq,
+        gk,
+        cos,
+        sin,
+        doc_col,
+        doc_row,
+        parts_b,
+        rows,
+        model_width,
+        seq_count,
+        6,
     )
-    dots, g_down, g_gate = lax.optimization_barrier((dots, g_down, g_gate))
-    dots = seq_sum(dots.T, seq_count, 6) / model_width
-
-    def norm_back(u, raw, scale, product):
-        return (scale * u - raw * (scale**3 * product[:, None])).astype(BF)
-
-    dq_low = norm_back(u_q, q_raw, rq, dots[0])
-    dk_low = norm_back(u_k, k_raw, rk, dots[1])
-    grad_h1 = dot(dq_low, wq, (1, 1)) + dot(dk_low, wk, (1, 1)) + dot(dv_low, wv, (1, 1))
-    grad_h1 = grad_h1.astype(BF).reshape(seq_count, tok_rows, model_width)
+    result = x_mid + jnp.concatenate([sum_a, sum_b], axis=1).astype(F32)
 
     sheet = (seq_count, shards, rows, width)
-    small_part = jnp.concatenate(
-        [router_part.T, ffn_part[:, None], jnp.zeros((model_width, lanes - experts - 1), F32)], axis=1
-    ).reshape(seq_count, shards, rows, lanes)
-    gains_part = jnp.stack([gain_q_part.reshape(shards, rows), gain_k_part.reshape(shards, rows)], axis=1)
-    gains_part = jnp.pad(gains_part, ((0, 0), (0, 6), (0, lanes - rows)))
     g_query, g_key, g_value, g_output, g_small, g_gains, grad_h1 = scatter_end(
         (
             dot(h1, dq_low, (0, 0), BF).reshape(sheet),
             dot(h1, dk_low, (0, 0), BF).reshape(sheet),
             dot(h1, dv_low, (0, 0), BF).reshape(sheet),
             dot(attended, d_attn, (0, 0), BF).reshape(shards, rows, model_width),
-            small_part,
+            small_part.reshape(seq_count, shards, rows, lanes),
             gains_part,
         ),
-        grad_h1,
+        (dq_low, dk_low, dv_low, wq, wk, wv),
         seq_count,
         shards,
-        8,
+        7,
     )
     g_query, g_key, g_value = (g_query.astype(F32), g_key.astype(F32), g_value.astype(F32))
 
@@ -1983,8 +2221,8 @@
         g_small[:, experts],
         g_gains[0, :rows],
         g_gains[1, :rows],
-        g_gate.astype(F32),
-        g_up.astype(F32),
+        g_gate_up[:, :, : g_gate_up.shape[2] // 2].astype(F32),
+        g_gate_up[:, :, g_gate_up.shape[2] // 2 :].astype(F32),
         g_down.astype(F32),
     )
 

time: 771 us -> 742 us (0.962)
  matrix products: 51.2 us -> 38.5 us
  other arithmetic: 54.4 us -> 46 us
  local copies, waits for them, and re-layouts: 27.4 us -> 19.3 us
    pallas_call x1, Pallas kernels: 79.2 us -> 56.9 us  [turn_back(): pl.pallas_call(partial(turn_kernel, count, seq_count), out_shape=[jax.Sha...]
    pallas_call x5 -> x3, Pallas kernels: 127 us -> 140 us  [the longest x1 74 us: middle(): pl.pallas_call(partial(middle_kernel, count, seq_count, CAP), out_shape=[...]
    dot_general x12 -> x9, matrix products: 51.2 us -> 38.5 us  [dot(): lax.dot_general(left, right, (((sides[0],), (sides[1],)), ((), ())), pref...]
  transfers between devices with their start and end apart: 6 -> 4, of which waited for: 1 -> 1; matrix products, arithmetic and copies ran while one was open for 16% -> 11% of each run, Pallas kernels for 75% -> 70%
where the time goes in v5:
time: 742 us; the launch traced here: 735 us
  Pallas kernels  609 us (82%)
  other arithmetic  46 us (6%)
  matrix products  38.5 us (5%)
  local copies, waits for them, and re-layouts  19.3 us (3%)
  between operations  14.9 us (2%)
    pallas_call x1, Pallas kernels, experts_out(): pl.pallas_call(partial(experts_out_kernel, count, CAP), out_shape=[jax.Sh...  99.5 us
    pallas_call x1, Pallas kernels, scatter_end(): pl.pallas_call(partial(end_kernel, count, seq_count), out_shape=shapes, i...  97.6 us
    pallas_call x1, Pallas kernels, experts_in(): pl.pallas_call(partial(experts_in_kernel, count, CAP), out_shape=[jax.Sha...  90.9 us
    pallas_call x1, Pallas kernels, gather_start(): pl.pallas_call(partial(start_kernel, count, seq_count), out_shape=shapes,...  88.5 us
    pallas_call x1, Pallas kernels, middle(): pl.pallas_call(partial(middle_kernel, count, seq_count, CAP), out_shape=[...  74 us
    pallas_call x1, Pallas kernels, turn_back(): pl.pallas_call(partial(turn_kernel, count, seq_count), out_shape=[jax.Sha...  56.9 us
    pallas_call x1, Pallas kernels, attend_back(): pl.pallas_call(partial(attend_back_kernel, count, seq_count, heads, 256,...  42.5 us
    dot_general x9, matrix products, dot(): lax.dot_general(left, right, (((sides[0],), (sides[1],)), ((), ())), pref...  38.5 us
  transfers between devices with their start and end apart: 4, of which 1 were waited for; matrix products, arithmetic and copies ran while one was open for 11% of the time, Pallas kernels for 70%

profile of v5, /device:TPU:0, one launch (start us, length us, event | category | flops | bytes accessed | tf_op | source)
XLA Modules:
  0.0 734.7 jit_solution(13966855202478541456)
XLA Ops:
  7.2 4.8 pad_maximum_fusion
  12.1 0.7 all-gather.5.cloned.1.call-update
  13.7 0.7 fusion.20.refs_4_
  14.4 0.7 maximum_maximum_fusion.1.refs_3_
  15.1 88.5 %gather_start.1 = (bf16[4,8,64,512]{3,2,1,0:T(8,128)(2,1)}, bf16[4,8,64,512]{3,2,1,0:T(8,128)(2,1)}, bf16[4,8,64,512]{3,2,1,0:T(8,128)(2,1)}, bf16[4,8,64,128]{3...) custom-call(bf16[64,2048]{1,0:T(8,128)(2,1)} %refs_0_.1, ...), custom_call_target="tpu_custom_call" | custom-call | tf_op jit(solution)/shard_map/gather_start/pallas_call | solution.py:241
  103.6 0.8 convert_reduce_fusion.2
  104.6 1.9 copy.63
  106.4 2.0 convert_reduce_fusion
  108.4 3.2 multiply_reduce_fusion
  111.7 0.6 fusion.21
  112.3 1.0 multiply_convert_fusion
  113.9 3.8 multiply_reduce_fusion.3
  117.7 3.6 copy.55.q_raw
  121.4 5.9 multiply_reduce_fusion.2
  127.3 3.0 copy.56.k_raw
  130.4 5.6 convolution_convert_fusion.6.v_ref
  136.1 23.9 %attend.1 = (bf16[1024,512]{1,0:T(8,128)(2,1)S(1)}, bf16[1024,512]{1,0:T(8,128)(2,1)S(1)}, bf16[1024,512]{1,0:T(8,128)(2,1)S(1)}, f32[1024,8]{1,0:T(8,128)S(1)}) custom-call(f32[1024,512]{1,0:T(8,128)} %copy.55.q_raw, f32[1024,512]{1,0:T(8,128)} %copy.56.k_raw, bf16[1024,512]{1,0:T(8,128)(2,1)} %convolution_convert_fusion.6.v_ref, ...), custom_call_target="tpu_custom_call" | custom-call | tf_op jit(solution)/shard_map/attend/pallas_call | solution.py:1098
  160.1 2.4 convolution_convert_fusion
  162.5 74.0 %middle.1 = (f32[256,2048]{1,0:T(8,128)S(1)}, bf16[8,256,2048]{2,1,0:T(8,128)(2,1)S(1)}, s32[8,2,256]{2,1,0:T(2,128)S(1)}, s32[8,256,2]{2,1,0:T(8,128)S(1)}) custom-call(bf16[4,256,2048]{2,1,0:T(8,128)(2,1)S(1)} %bitcast.75, bf16[256,2048]{1,0:T(8,128)(2,1)S(1)} %bitcast.74, s32[8,8,256]{2,1,0:T(8,128)S(1)} %copy-done.9), custom_call_target="tpu_custom_call" | custom-call | tf_op jit(solution)/shard_map/middle/pallas_call | solution.py:810
  236.5 3.3 copy-done.2
  240.8 0.6 multiply_multiply_fusion.1
  241.4 0.7 copy-done.17
  242.1 1.2 multiply_convert_fusion.1.h2_ref
  243.3 90.9 %experts_in.1 = (bf16[8,256,2048]{2,1,0:T(8,128)(2,1)}, bf16[2,1088,2048]{2,1,0:T(8,128)(2,1)}, bf16[2,1088,2048]{2,1,0:T(8,128)(2,1)}, bf16[2,1088,1024]{2,1,0:...) custom-call(bf16[256,2048]{1,0:T(8,128)(2,1)} %multiply_convert_fusi, ...), custom_call_target="tpu_custom_call" | custom-call | tf_op jit(solution)/shard_map/experts_in/pallas_call | solution.py:1538
  334.3 35.1 %experts_mid.1 = (bf16[2,1088,1024]{2,1,0:T(8,128)(2,1)}, bf16[2,1088,1024]{2,1,0:T(8,128)(2,1)}, bf16[2,1088,1024]{2,1,0:T(8,128)(2,1)}, f32[2,4,272,1]{3,2,1,0:T(8,128)}, bf16[2,1024,2048]{2,1,0:T(8,128)(2,1)}) custom-call(bf16[2,1088,2048]{2,1,0:T(8,128)(2,1)} %get-tuple-element.77.y_in, bf16[2,1088,1024]{2,1,0:T(8,128)(2,1)} %get-tuple-element.78.act_in, ...), custom_call_target="tpu_custom_call" | custom-call | flops 17999998976 | bytes 60000000 | tf_op jit(solution)/shard_map/experts_mid/pallas_call | solution.py:1669
  369.5 99.5 %experts_out.1 = (bf16[8,256,1280]{2,1,0:T(8,128)(2,1)}, bf16[8,256,768]{2,1,0:T(8,128)(2,1)}, bf16[8,16,256]{2,1,0:T(8,128)(2,1)}, bf16[256,2048]{1,0:T(8,128)(2,1)}) custom-call(bf16[2,1088,1024]{2,1,0:T(8,128)(2,1)} %get-tuple-element.82.gated_in, bf16[2,1088,1024]{2,1,0:T(8,128)(2,1)} %get-tuple-element.83.d_gate_in.right0, ...), custom_call_target="tpu_custom_call" | custom-call | flops 60000002048 | bytes 200000000 | tf_op jit(solution)/shard_map/experts_out/pallas_call | solution.py:1979
  469.1 3.3 fusion.8
  472.4 2.9 fusion.22.x_ref
  475.3 56.9 %turn_back.1 = (bf16[4,256,2048]{2,1,0:T(8,128)(2,1)}, bf16[256,1280]{1,0:T(8,128)(2,1)}, bf16[2,2048,2048]{2,1,0:T(8,128)(2,1)}, f32[2048,128]{1,0:T(8,128)}) custom-call(bf16[256,2048]{1,0:T(8,128)(2,1)} %fusion.22.x_ref, bf16[8,256,1280]{2,1,0:T(8,128)(2,1)} %get-tuple-element.91.parts_ref, bf16[2,1088,2048]{2,1,0:T(8,128)(2,1)} %get-tuple-element.92.left_ref, ...), custom_call_target="tpu_custom_call" | custom-call | flops 60000002048 | bytes 200000000 | tf_op jit(solution)/shard_map/turn_back/pallas_call | solution.py:961
  532.3 0.6 copy-done.48
  532.9 5.5 fusion.1
  538.4 3.3 convolution_convert_fusion.5.do_ref
  541.7 42.5 %attend_back.1 = (bf16[1024,512]{1,0:T(8,128)(2,1)}, bf16[1024,512]{1,0:T(8,128)(2,1)}, bf16[1024,512]{1,0:T(8,128)(2,1)}, f32[8,8,128]{2,1,0:T(8,128)}, bf16[256,768]{1,0:T(8,128)(2,1)}) custom-call(bf16[1024,512]{1,0:T(8,128)(2,1)} %copy-done.6, bf16[1024,512]{1,0:T(8,128)(2,1)} %copy-done.7, bf16[1024,512]{1,0:T(8,128)(2,1)} %convolution_convert_fusion.6.v_ref, ...), custom_call_target="tpu_custom_call" | custom-call | tf_op jit(solution)/shard_map/attend_back/pallas_call | solution.py:1294
  584.3 6.2 convolution_convert_fusion.1
  590.5 3.8 convolution_convert_fusion.4
  594.3 3.8 convolution_convert_fusion.3
  598.0 3.8 convolution_convert_fusion.2
  601.8 97.6 %scatter_end.1 = (bf16[64,2048]{1,0:T(8,128)(2,1)}, bf16[64,2048]{1,0:T(8,128)(2,1)}, bf16[64,2048]{1,0:T(8,128)(2,1)}, bf16[64,2048]{1,0:T(8,128)(2,1)}, f32[64...) custom-call(bf16[4,8,64,512]{3,2,1,0:T(8,128)(2,1)} %bitcast.90, bf16[4,8,64,512]{3,2,1,0:T(8,128)(2,1)} %bitcast.91, ...), custom_call_target="tpu_custom_call" | custom-call | tf_op jit(solution)/shard_map/scatter_end/pallas_call | solution.py:555
  699.4 1.4 copy.62
  700.8 1.8 convert_element_type.160
  702.7 4.4 convert_element_type.167
  707.1 0.7 slice_reduce_fusion
  707.8 1.3 add_reduce_fusion
  709.7 1.6 slice_bitcast_fusion
  711.3 0.6 fusion.9
  711.9 3.1 fusion.12
  715.0 6.0 reduce-scatter.5.cloned.1.call-done
  721.0 6.7 slice_convert_fusion
  (143 shorter events, 3.6 us)
Async XLA Ops:
  7.2 236.1 %all-gather.3.cloned.1.call-start = ((), (), s32[]{:S(2)}) async-start(), calls=%async_computation.2 | async-start | bytes 20971520 | tf_op jit(solution)/shard_map/all_gather | solution.py:2072
  12.1 322.2 %all-gather.5.cloned.1.call-start = ((), (), s32[]{:S(2)}) async-start(), calls=%async_computation.3 | async-start | bytes 10485760 | tf_op jit(solution)/shard_map/all_gather | solution.py:2073
  12.8 456.3 %reduce-scatter.3.cloned.1.call-start = ((), (), s32[]{:S(2)}) async-start(), calls=%async_computation.4 | async-start | bytes 10485760 | tf_op jit(solution)/shard_map/reduce_scatter | solution.py:2131
  13.6 122.4 %copy-start.3 = (s32[1024,1]{1,0:T(8,128)}, s32[1024,1]{1,0:T(8,128)S(1)}, u32[]{:S(2)}) copy-start(s32[1024,1]{1,0:T(8,128)S(1)} %copy.57.doc_col) | copy-start | bytes 12292
  104.5 31.5 %copy-start.11 = (f32[1,512]{1,0:T(1,128)}, f32[1,512]{1,0:T(1,128)S(1)}, u32[]{:S(2)}) copy-start(f32[1,512]{1,0:T(1,128)S(1)} %reshape.213.gk) | copy-start | bytes 6148
  104.6 31.4 %copy-start.12 = (f32[1,512]{1,0:T(1,128)}, f32[1,512]{1,0:T(1,128)S(1)}, u32[]{:S(2)}) copy-start(f32[1,512]{1,0:T(1,128)S(1)} %reshape.212.gq) | copy-start | bytes 6148
  108.4 3.9 copy-start.43
  108.4 133.0 %copy-start.41 = (f32[2048]{0:T(1024)}, f32[2048]{0:T(1024)S(1)}, u32[]{:S(2)}) copy-start(f32[2048]{0:T(1024)S(1)} %get-tuple-element.162) | copy-start | bytes 24580
  108.4 3.8 copy-start.20
  113.3 4.4 copy-start.26
  117.7 3.7 copy-start.28
  127.3 3.1 copy-start.29
  130.4 5.6 copy-start.4
  130.4 5.6 copy-start.5
  136.0 24.0 %copy-start.56 = (bf16[8,64,2048]{2,1,0:T(8,128)(2,1)S(1)}, bf16[8,64,2048]{2,1,0:T(8,128)(2,1)}, u32[]{:S(2)}) copy-start(bf16[8,64,2048]{2,1,0:T(8,128)(2,1)} %get-tuple-element.72) | copy-start | bytes 6291460
  160.0 2.5 copy-start.6
  160.0 2.5 copy-start.7
  160.0 2.5 copy-start.8
  160.0 2.4 copy-start.14
  160.0 2.4 copy-start
  162.5 77.3 %copy-start.21 = (bf16[1,256,2048]{2,1,0:T(8,128)(2,1)S(1)}, bf16[1,256,2048]{2,1,0:T(8,128)(2,1)}, u32[]{:S(2)}) copy-start(bf16[1,256,2048]{2,1,0:T(8,128)(2,1)} %param.18) | copy-start | bytes 3145732
  236.5 3.3 copy-start.2
  369.4 351.6 %reduce-scatter.5.cloned.1.call-start = ((), (), s32[]{:S(2)}) async-start(), calls=%async_computation.5 | async-start | bytes 20971520 | tf_op jit(solution)/shard_map/reduce_scatter | solution.py:2131
  469.0 3.4 copy-start.1
  469.0 3.4 copy-start.42
  469.0 3.4 copy-start.47
  469.1 3.4 copy-start.49
  469.1 3.3 copy-start.18
  532.9 5.5 copy-start.57
  532.9 5.5 copy-start.58
  541.7 42.5 %copy-start.15 = (bf16[1024,512]{1,0:T(8,128)(2,1)S(1)}, bf16[1024,512]{1,0:T(8,128)(2,1)}, u32[]{:S(2)}) copy-start(bf16[1024,512]{1,0:T(8,128)(2,1)} %copy-done.14) | copy-start | bytes 3145732
  584.3 6.2 copy-start.25
  584.3 6.2 copy-start.30
  590.5 3.8 copy-start.31
  594.3 3.8 copy-start.32
  702.6 4.4 copy-start.45
  702.6 5.2 copy-start.33
  702.6 5.2 copy-start.34
  702.6 5.2 copy-start.35
  702.6 5.1 copy-start.38
  702.6 5.1 copy-start.39
  702.6 5.1 copy-start.40
  702.6 9.3 %copy-start.36 = (bf16[256,1280]{1,0:T(8,128)(2,1)S(1)}, bf16[256,1280]{1,0:T(8,128)(2,1)}, u32[]{:S(2)}) copy-start(bf16[256,1280]{1,0:T(8,128)(2,1)} %get-tuple-element.95) | copy-start | bytes 1966084
  702.7 9.3 %copy-start.37 = (bf16[256,768]{1,0:T(8,128)(2,1)S(1)}, bf16[256,768]{1,0:T(8,128)(2,1)}, u32[]{:S(2)}) copy-start(bf16[256,768]{1,0:T(8,128)(2,1)} %get-tuple-element.101) | copy-start | bytes 1179652
  707.1 4.3 copy-start.22
  707.1 4.3 copy-start.24
  709.1 2.8 copy-start.19
  709.1 2.8 copy-start.23
  (15 other events, 19.2 us)
Sparse Core Ops, SparseCore 0:
  12.1 229.0 all-gather.2
  243.0 87.7 all-gather.4
  369.6 86.1 reduce-scatter.2
  532.4 188.5 reduce-scatter.4

commit v6 on v5

--- a/solution.py
+++ b/solution.py
@@ -266,28 +266,30 @@
         self.own, self.sib, self.inbox = bufs
         self.sems = sems
 
+    def view(self, a, ref):
+        return ref
+
     def load(self, a, q):
         i = self.places[0]
         src = slot_of(self.sources[a], self.axes[a], 2 * q + lax.rem(i, 2))
-        return pltpu.make_async_copy(src, self.own[a].at[q], self.sems[6].at[a, q])
+        return pltpu.make_async_copy(self.view(a, src), self.view(a, self.own[a].at[q]), self.sems[6].at[a, q])
 
     def to_sib(self, a, q):
         sib = self.places[2]
         src = slot_of(self.sources[a], self.axes[a], 2 * q + lax.rem(sib, 2))
-        return remote(src, self.sib[a].at[q], self.sems[2].at[a, q], self.sems[5].at[a, q], fsdp=sib)
+        dst = self.view(a, self.sib[a].at[q])
+        return remote(self.view(a, src), dst, self.sems[2].at[a, q], self.sems[5].at[a, q], fsdp=sib)
 
     def right(self, a, q):
         i = self.places[0]
-        return remote(
-            self.own[a].at[q], self.inbox[a].at[q], self.sems[0].at[a, q], self.sems[3].at[a, q], fsdp=i + 2
-        )
+        src, dst = self.view(a, self.own[a].at[q]), self.view(a, self.inbox[a].at[q])
+        return remote(src, dst, self.sems[0].at[a, q], self.sems[3].at[a, q], fsdp=i + 2)
 
     def left(self, a, q):
         i, p, sib = self.places
         slot = jnp.where(q == p - 1, self.count, q)
-        return remote(
-            self.own[a].at[q], self.inbox[a].at[slot], self.sems[1].at[a, q], self.sems[4].at[a, q], fsdp=i - 2
-        )
+        src, dst = self.view(a, self.own[a].at[q]), self.view(a, self.inbox[a].at[slot])
+        return remote(src, dst, self.sems[1].at[a, q], self.sems[4].at[a, q], fsdp=i - 2)
 
     def begin_loads(self):
         for k in range(self.count):
@@ -423,6 +425,33 @@
                 @pl.when(q < p)
                 def _():
                     self.left(a, q).wait_send()
+
+
+class SplitScatter(LineScatter):
+    def __init__(self, count, places, source, bufs, sems):
+        super().__init__(count, places, [source] * 2, [0] * 2, tuple([buf] * 2 for buf in bufs), sems)
+        self.half = bufs[0].shape[-1] // 2
+
+    def cols(self, a):
+        return pl.ds(a * self.half, self.half)
+
+    def view(self, a, ref):
+        return ref.at[:, self.cols(a)]
+
+    def add(self, a, q, others):
+        own = self.own[a]
+        rows = own.shape[1]
+        step = rows
+        while step * self.half > 65536 and step % 16 == 0:
+            step //= 2
+
+        @pl.loop(0, rows // step)
+        def _(k):
+            index = (pl.ds(pl.multiple_of(k * step, step), step), self.cols(a))
+            total = own[(q,) + index].astype(F32) + self.sib[a][(q,) + index].astype(F32)
+            for slot in others:
+                total += self.inbox[a][(slot,) + index].astype(F32)
+            own[(q,) + index] = total.astype(own.dtype)
 
 
 def end_kernel(count, seq_count, *refs):
@@ -816,7 +845,7 @@
             jax.ShapeDtypeStruct((shards, tokens, local_experts), jnp.int32),
         ],
         in_specs=[anywhere, anywhere, vmem],
-        out_specs=[vmem, anywhere, vmem, vmem],
+        out_specs=[vmem, pl.BlockSpec(memory_space=pltpu.HBM), vmem, vmem],
         scratch_shapes=seq_scatter_scratch(block, blocks.dtype, seq_count)
         + [pltpu.VMEM(dy.shape, dy.dtype)]
         + line_sems(1, count)
@@ -828,61 +857,6 @@
     )(blocks, dy, routes)
 
 
-class RouterGrad:
-    def __init__(self, tokens_in, logits_in, gain_row, out, tokens, logits, total, sems):
-        self.tokens_in, self.logits_in, self.out = tokens_in, logits_in, out
-        self.tokens, self.logits, self.sems = tokens, logits, sems
-        self.gain_row, self.total = gain_row, total
-
-    def take(self):
-        return pltpu.make_async_copy(self.logits_in, self.logits, self.sems.at[2])
-
-    def pair(self, q):
-        buf = lax.rem(q, 2)
-        src = self.tokens_in.at[pl.ds(2 * q, 2)]
-        return pltpu.make_async_copy(src, self.tokens.at[buf], self.sems.at[buf])
-
-    def begin(self):
-        self.take().start()
-        self.pair(0).start()
-
-    def run(self):
-        self.take().wait()
-        self.total[...] = jnp.zeros_like(self.total)
-        experts, width = self.total.shape
-        block = 512
-        pairs = self.tokens_in.shape[0] // 2
-
-        @pl.loop(0, pairs)
-        def _(q):
-            self.pair(q).wait()
-
-            @pl.when(q + 1 < pairs)
-            def _():
-                self.pair(q + 1).start()
-
-            buf = lax.rem(q, 2)
-
-            @pl.loop(0, width // block)
-            def _(n):
-                cols = pl.ds(pl.multiple_of(n * block, block), block)
-                total = self.total[:, cols]
-                for j in range(2):
-                    total += jnp.dot(
-                        self.logits[2 * q + j], self.tokens[buf, j, :, cols], preferred_element_type=F32
-                    )
-                self.total[:, cols] = total
-
-        lanes = self.out.shape[1]
-
-        @pl.loop(0, width // block)
-        def _(n):
-            cols = pl.ds(pl.multiple_of(n * block, block), block)
-            gain = jnp.broadcast_to(self.gain_row[:, cols], (8, block))
-            rest = jnp.zeros((lanes - experts - 8, block), F32)
-            self.out[cols, :] = jnp.concatenate([self.total[:, cols], gain, rest], axis=0).T
-
-
 def turn_kernel(
     count,
     seq_count,
@@ -891,13 +865,9 @@
     left_ref,
     right0,
     right1,
-    h2_ref,
-    logits_ref,
-    gain_row,
     o_ref,
     sum_ref,
     grad_ref,
-    router_ref,
     hold,
     send,
     recv,
@@ -906,10 +876,6 @@
     held,
     staged,
     outer_sem,
-    tokens,
-    logits,
-    router_sum,
-    router_sem,
     own,
     sib,
     inbox,
@@ -917,14 +883,12 @@
 ):
     places = where_am_i()
     here = lax.axis_index("seq")
-    line = LineScatter(count, places, [parts_ref], [0], ([own], [sib], [inbox]), sems)
+    line = SplitScatter(count, places, parts_ref, (own, sib, inbox), sems)
     grads = OuterGrads(left_ref, (right0, right1), grad_ref, (tiles_in, held, staged, outer_sem), count - 1)
-    router = RouterGrad(h2_ref, logits_ref, gain_row, router_ref, tokens, logits, router_sum, router_sem)
     line.begin_loads()
     take = pltpu.make_async_copy(x_ref, hold, one)
     take.start()
     grads.begin()
-    router.begin()
     greet(count, places, seq_count)
     rows = SeqGather(seq_count, x_ref, o_ref, send, recv)
     rows.begin()
@@ -934,7 +898,7 @@
     put.start()
 
     def after(a, q):
-        out = pltpu.make_async_copy(own.at[q], sum_ref, sems[6].at[0, q])
+        out = pltpu.make_async_copy(line.view(a, own.at[q]), line.view(a, sum_ref), sems[6].at[a, q])
         out.start()
         out.wait()
 
@@ -944,7 +908,6 @@
             rows.relay()
 
         grads.between(step)
-        pl.when(step == 0)(router.run)
 
     line.run(after, between)
     grads.finish()
@@ -953,7 +916,7 @@
     line.finish()
 
 
-def turn_back(block, parts, expert_in, d_gate, d_up, h2_all, logits, gain_row, seq_count, shards, collective):
+def turn_back(block, parts, expert_in, d_gate, d_up, seq_count, shards, collective):
     count = shards // 2
     part = parts.shape[1:]
     model_width = block.shape[1]
@@ -964,29 +927,22 @@
             jax.ShapeDtypeStruct((seq_count,) + block.shape, block.dtype),
             jax.ShapeDtypeStruct(part, parts.dtype),
             jax.ShapeDtypeStruct((d_gate.shape[0], model_width, 2 * d_gate.shape[2]), BF),
-            jax.ShapeDtypeStruct((model_width, 128), F32),
         ],
-        in_specs=[anywhere] * 7 + [pl.BlockSpec(memory_space=pltpu.VMEM)],
-        out_specs=[anywhere] * 3 + [pl.BlockSpec(memory_space=pltpu.VMEM)],
+        in_specs=[anywhere] * 5,
+        out_specs=[anywhere] * 3,
         scratch_shapes=[pltpu.VMEM(block.shape, block.dtype)]
         + seq_gather_sems(seq_count)
         + [DMA]
         + outer_scratch(d_up, 512, 2)
-        + [
-            pltpu.VMEM((2, 2) + h2_all.shape[1:], BF),
-            pltpu.VMEM(logits.shape, BF),
-            pltpu.VMEM((logits.shape[1], model_width), F32),
-            DMA((3,)),
-        ]
         + [pltpu.VMEM((count,) + part, BF)] * 2
         + [pltpu.VMEM((count + 1,) + part, BF)]
-        + [DMA((1, count))] * 7,
+        + [DMA((2, count))] * 7,
         compiler_params=pltpu.CompilerParams(
             collective_id=collective, has_side_effects=True, vmem_limit_bytes=60 << 20
         ),
         cost_estimate=pl.CostEstimate(flops=60_000_000_000, bytes_accessed=200_000_000, transcendentals=0),
         name="turn_back",
-    )(block, parts, expert_in, d_gate, d_up, h2_all, logits, gain_row)
+    )(block, parts, expert_in, d_gate, d_up)
 
 
 def half_sign(shape):
@@ -1596,7 +1552,7 @@
     slots = ys.shape[1]
     over_lanes = (((1,), (1,)), ((), ()))
     over_rows = (((0,), (0,)), ((), ()))
-    inputs = ((wd_in, wd), (y_in, ys), (act_in, acts), (by_up_in, by_ups), (by_gate_in, by_gates))
+    inputs = ((y_in, ys), (wd_in, wd), (act_in, acts), (by_up_in, by_ups), (by_gate_in, by_gates))
     results = ((gated, gated_out), (d_gate, d_gate_out), (d_up, d_up_out))
     wide = 256
     tile = staged.shape[1]
@@ -1615,13 +1571,19 @@
         for n in range(5):
             fetch(n, e).start()
     for e in range(local_experts):
-        for n in range(5):
+        for n in range(2):
             fetch(n, e).wait()
         gate = jnp.concatenate([gate_slots[e, q] for q in range(count)], axis=0)
 
         def step(n, dot):
             cols = pl.ds(pl.multiple_of(n * wide, wide), wide)
             grad_act = lax.dot_general(ys[e], wd[e, cols, :], over_lanes, preferred_element_type=F32)
+
+            @pl.when(n == 0)
+            def _():
+                for kind in range(2, 5):
+                    fetch(kind, e).wait()
+
             act = acts[e, :, cols].astype(F32)
             dot = dot + jnp.sum(act * grad_act, axis=1, keepdims=True)
             grad_act = grad_act * gate
@@ -1691,29 +1653,31 @@
     )(grads, act, by_up, by_gate, gate_slots, w_down)
 
 
-class StagedScatter(LineScatter):
+class StagedScatter(SplitScatter):
     def __init__(self, count, places, stage, bufs, sems):
-        super().__init__(count, places, [None], [0], bufs, sems)
+        super().__init__(count, places, None, bufs, sems)
         self.stage = stage
 
     def to_sib(self, a, q):
         sib = self.places[2]
-        return remote(self.stage, self.sib[a].at[q], self.sems[2].at[a, q], self.sems[5].at[a, q], fsdp=sib)
+        src, dst = self.view(a, self.stage), self.view(a, self.sib[a].at[q])
+        return remote(src, dst, self.sems[2].at[a, q], self.sems[5].at[a, q], fsdp=sib)
 
     def ready(self, a, q):
         self.to_sib(a, q).wait_recv()
 
     def finish(self):
         i, p, sib = self.places
-        for q in range(self.count):
-
-            @pl.when(q > p)
-            def _():
-                self.right(0, q).wait_send()
-
-            @pl.when(q < p)
-            def _():
-                self.left(0, q).wait_send()
+        for a in range(2):
+            for q in range(self.count):
+
+                @pl.when(q > p)
+                def _():
+                    self.right(a, q).wait_send()
+
+                @pl.when(q < p)
+                def _():
+                    self.left(a, q).wait_send()
 
 
 class OuterGrads:
@@ -1804,10 +1768,15 @@
     router_t,
     wgu_in,
     wd_in,
+    tokens_in,
+    x_in,
+    dy_in,
+    gain_row,
     parts_a,
     parts_b,
-    logit_ref,
-    sum_ref,
+    grad_ref,
+    low_ref,
+    small_ref,
     wgu,
     wd,
     gated,
@@ -1821,6 +1790,11 @@
     w_sem,
     in_sem,
     part_sem,
+    held_tokens,
+    x_mid,
+    dy,
+    router_sum,
+    row_sem,
     *sems,
 ):
     places = where_am_i()
@@ -1831,7 +1805,7 @@
     experts = router_t.shape[0]
     first = i * local_experts
     over_lanes = (((1,), (1,)), ((), ()))
-    line = StagedScatter(count, places, stage, ([own], [sibling], [inbox]), sems)
+    line = StagedScatter(count, places, stage, (own, sibling, inbox), sems)
     weights = ((wgu_in, wgu), (wd_in, wd))
     inputs = ((gated_in, gated), (d_gate_in, d_gate), (d_up_in, d_up))
 
@@ -1855,15 +1829,24 @@
         fetch(n, order(0), 0).start()
     for n in range(2):
         weight(n).start()
+    take_x = pltpu.make_async_copy(x_in, x_mid, row_sem.at[0])
+    take_dy = pltpu.make_async_copy(dy_in, dy, row_sem.at[1])
+    take_x.start()
+    take_dy.start()
+    router_sum[...] = jnp.zeros_like(router_sum)
     greet(count, places)
     slot_rows = lax.broadcasted_iota(jnp.int32, (local_experts * cap, tokens), 0)
     slot_lanes = lax.broadcasted_iota(jnp.int32, (tokens, local_experts * cap), 1)
     expert_rows = lax.broadcasted_iota(jnp.int32, (experts, tokens), 0)
 
+    def take_tokens(q):
+        return pltpu.make_async_copy(tokens_in.at[pl.ds(2 * q, 2)], held_tokens, row_sem.at[2])
+
     def compute(k):
         q = order(k)
         buf = lax.rem(k, 2)
-        picks, logits_low = [], []
+        take_tokens(q).start()
+        picks, logits_low, logits_row = [], [], []
         for j in range(2):
             slot = 2 * q + j
             grad_probs = jnp.zeros((experts, tokens), F32)
@@ -1878,7 +1861,7 @@
                 pick = hit if pick is None else pick | hit
             probs = probs_ref[slot]
             grad_logits = probs * (grad_probs - jnp.sum(probs * grad_probs, axis=0, keepdims=True))
-            logit_ref[slot] = grad_logits.astype(BF)
+            logits_row.append(grad_logits.astype(BF))
             picks.append(jnp.where(pick, 1.0, 0.0).astype(BF))
             logits_low.append(grad_logits.T.astype(BF))
         for n in range(3):
@@ -1892,6 +1875,7 @@
         @pl.when(k > 0)
         def _():
             line.to_sib(0, order(k - 1)).wait_send()
+            line.to_sib(1, order(k - 1)).wait_send()
 
         @pl.when(k == 0)
         def _():
@@ -1928,7 +1912,11 @@
                 def _():
                     stage[:, cols] = total
 
-        line.to_sib(0, q).start()
+            @pl.when(n == model_width // block // 2 - 1)
+            def _():
+                line.to_sib(0, q).start()
+
+        line.to_sib(1, q).start()
 
         @pl.when(k > 0)
         def _():
@@ -1938,6 +1926,8 @@
         @pl.when(k == 0)
         def _():
             weight(1).wait()
+
+        take_tokens(q).wait()
 
         @pl.loop(0, model_width // block)
         def _(n):
@@ -1949,6 +1939,10 @@
                 part = slice(j * cap, (j + 1) * cap)
                 mine = jnp.concatenate([value[part] for value in outs], axis=0).astype(BF)
                 parts[j, :, cols] = jnp.dot(picks[j], mine, preferred_element_type=F32).astype(BF)
+            total = router_sum[:, cols]
+            for j in range(2):
+                total += jnp.dot(logits_row[j], held_tokens[j, :, cols], preferred_element_type=F32)
+            router_sum[:, cols] = total
 
         put(0, q).start()
         put(1, q).start()
@@ -1961,14 +1955,51 @@
     put(0, 0).wait()
     put(1, 0).wait()
     line.to_sib(0, order(count - 1)).wait_send()
-    out = pltpu.make_async_copy(own.at[p], sum_ref, part_sem.at[0])
-    out.start()
-    out.wait()
+    line.to_sib(1, order(count - 1)).wait_send()
+    take_x.wait()
+    take_dy.wait()
+    strip = 16
+
+    def norm_back(n, total):
+        rows = pl.ds(pl.multiple_of(n * strip, strip), strip)
+        back = own[p, rows, :].astype(F32)
+        x = x_mid[rows, :]
+        scale = lax.rsqrt(jnp.mean(x * x, axis=1, keepdims=True) + EPSILON)
+        u = gain_row[...] * back
+        product = jnp.mean(u * x, axis=1, keepdims=True)
+        grad = dy[rows, :].astype(F32) + scale * u - x * (scale * scale * scale * product)
+        grad_ref[rows, :] = grad
+        low_ref[rows, :] = grad.astype(BF)
+        return total + jnp.sum(back * x * scale, axis=0, keepdims=True)
+
+    norm_part = lax.fori_loop(0, tokens // strip, norm_back, jnp.zeros((1, model_width), F32))
+    lanes = small_ref.shape[1]
+    piece = 512
+    for n in range(model_width // piece):
+        cols = slice(n * piece, (n + 1) * piece)
+        norm = jnp.broadcast_to(norm_part[:, cols], (8, piece))
+        rest = jnp.zeros((lanes - experts - 8, piece), F32)
+        small_ref[cols, :] = jnp.concatenate([router_sum[:, cols], norm, rest], axis=0).T
+
     line.finish()
 
 
 def experts_out(
-    gated, d_gate, d_up, dots, targets, targets_t, probs, router_t, w_gate_up, w_down, collective
+    gated,
+    d_gate,
+    d_up,
+    dots,
+    targets,
+    targets_t,
+    probs,
+    router_t,
+    w_gate_up,
+    w_down,
+    h2_all,
+    x_mid,
+    dy,
+    gain_row,
+    collective,
 ):
     local_experts, slots, hidden = gated.shape
     model_width = router_t.shape[1]
@@ -1979,13 +2010,14 @@
     return pl.pallas_call(
         partial(experts_out_kernel, count, CAP),
         out_shape=[
-            jax.ShapeDtypeStruct((shards, tokens, model_width // 8 * 5), BF),
-            jax.ShapeDtypeStruct((shards, tokens, model_width // 8 * 3), BF),
-            jax.ShapeDtypeStruct(probs.shape, BF),
+            jax.ShapeDtypeStruct((shards, tokens, model_width // 2), BF),
+            jax.ShapeDtypeStruct((shards, tokens, model_width // 2), BF),
+            jax.ShapeDtypeStruct((tokens, model_width), F32),
             jax.ShapeDtypeStruct((tokens, model_width), BF),
+            jax.ShapeDtypeStruct((model_width, 128), F32),
         ],
-        in_specs=[anywhere] * 3 + [vmem] * 5 + [anywhere] * 2,
-        out_specs=[anywhere, anywhere, vmem, anywhere],
+        in_specs=[anywhere] * 3 + [vmem] * 5 + [anywhere] * 5 + [vmem],
+        out_specs=[anywhere, anywhere, vmem, vmem, vmem],
         scratch_shapes=[pltpu.VMEM(x.shape, BF) for x in (w_gate_up, w_down)]
         + [pltpu.VMEM((2, local_experts, 2 * CAP, hidden), BF)] * 3
         + [
@@ -1997,14 +2029,34 @@
             DMA((2,)),
             DMA((3, 2)),
             DMA((2,)),
+            pltpu.VMEM((2, tokens, model_width), BF),
+            pltpu.VMEM((tokens, model_width), F32),
+            pltpu.VMEM((tokens, model_width), BF),
+            pltpu.VMEM((experts, model_width), F32),
+            DMA((3,)),
         ]
-        + [DMA((1, count))] * 7,
+        + [DMA((2, count))] * 7,
         compiler_params=pltpu.CompilerParams(
             collective_id=collective, has_side_effects=True, vmem_limit_bytes=67_043_328
         ),
         cost_estimate=pl.CostEstimate(flops=60_000_000_000, bytes_accessed=200_000_000, transcendentals=0),
         name="experts_out",
-    )(gated, d_gate, d_up, dots, targets, targets_t, probs, router_t, w_gate_up, w_down)
+    )(
+        gated,
+        d_gate,
+        d_up,
+        dots,
+        targets,
+        targets_t,
+        probs,
+        router_t,
+        w_gate_up,
+        w_down,
+        h2_all,
+        x_mid,
+        dy,
+        gain_row,
+    )
 
 
 def rope_tables(seq_len, head_dim):
@@ -2084,8 +2136,8 @@
 
     x_float = x_all.astype(F32)
     h1 = (x_float * inverse_rms(x_float) * gain_a).astype(BF)
-    q_raw = dot(h1, wq)
-    k_raw = dot(h1, wk)
+    h1 = lax.optimization_barrier(h1)
+    q_raw, k_raw = lax.optimization_barrier((dot(h1, wq), dot(h1, wk)))
     values = dot(h1, wv, out=BF)
     squares = jnp.stack(
         [jnp.sum(q_raw * q_raw, axis=1), jnp.sum(k_raw * k_raw, axis=1)]
@@ -2113,7 +2165,7 @@
     gated, d_gate, d_up, dots_slots, g_down = experts_mid(
         grad_slots, act, by_up, by_gate, gate_slots, full_down
     )
-    parts_a, parts_b, grad_logits, grad_h2 = experts_out(
+    parts_a, parts_b, grad_mid, grad_low, small_part = experts_out(
         gated,
         d_gate,
         d_up,
@@ -2124,6 +2176,10 @@
         router_t,
         full_gate_up,
         full_down,
+        h2_all,
+        x_mid,
+        out_grad[0],
+        gain_f[None],
         4,
     )
 
@@ -2131,30 +2187,9 @@
         return lax.psum_scatter(part, "seq", scatter_dimension=1, tiled=True)
 
     g_down = spread(g_down)
-    grad_h2, g_down = lax.optimization_barrier((grad_h2, g_down))
-    grad_h2 = grad_h2.astype(F32)
-
-    u_rows = gain_f * grad_h2
-    grad_mid = (
-        grad_rows
-        + scale_f * u_rows
-        - x_mid * scale_f**3 * jnp.mean(u_rows * x_mid, axis=-1, keepdims=True)
-    )
-    ffn_part = jnp.sum(grad_h2 * x_mid * scale_f, axis=0)
-
-    d_attn, sum_a, g_gate_up, small_part = turn_back(
-        grad_mid.astype(BF),
-        parts_a,
-        expert_in,
-        d_gate,
-        d_up,
-        h2_all,
-        grad_logits,
-        ffn_part[None],
-        seq_count,
-        shards,
-        5,
-    )
+    grad_low, g_down = lax.optimization_barrier((grad_low, g_down))
+
+    d_attn, sum_a, g_gate_up = turn_back(grad_low, parts_a, expert_in, d_gate, d_up, seq_count, shards, 5)
     g_gate_up = spread(g_gate_up)
     d_attn = d_attn.reshape(seq_len, model_width)
     d_heads = dot(d_attn, wo, (1, 1), BF)

time: 742 us -> 727 us (0.980)
  other arithmetic: 46 us -> 36.6 us
  transfers between devices with their start and end apart: 4 -> 4, of which waited for: 1 -> 1; matrix products, arithmetic and copies ran while one was open for 11% -> 9% of each run, Pallas kernels for 70% -> 72%
where the time goes in v6:
time: 727 us; the launch traced here: 718 us
  Pallas kernels  609 us (84%)
  matrix products  36.9 us (5%)
  other arithmetic  36.6 us (5%)
  local copies, waits for them, and re-layouts  14.9 us (2%)
  between operations  14.8 us (2%)
    pallas_call x1, Pallas kernels, scatter_end(): pl.pallas_call(partial(end_kernel, count, seq_count), out_shape=shapes, i...  98 us
    pallas_call x1, Pallas kernels, experts_out(): pl.pallas_call(partial(experts_out_kernel, count, CAP), out_shape=[jax.Sh...  96.8 us
    pallas_call x1, Pallas kernels, experts_in(): pl.pallas_call(partial(experts_in_kernel, count, CAP), out_shape=[jax.Sha...  89.9 us
    pallas_call x1, Pallas kernels, gather_start(): pl.pallas_call(partial(start_kernel, count, seq_count), out_shape=shapes,...  88.5 us
    pallas_call x1, Pallas kernels, middle(): pl.pallas_call(partial(middle_kernel, count, seq_count, CAP), out_shape=[...  74 us
    pallas_call x1, Pallas kernels, turn_back(): pl.pallas_call(partial(turn_kernel, count, seq_count), out_shape=[jax.Sha...  52.1 us
    pallas_call x1, Pallas kernels, attend_back(): pl.pallas_call(partial(attend_back_kernel, count, seq_count, heads, 256,...  49.4 us
    dot_general x9, matrix products, dot(): lax.dot_general(left, right, (((sides[0],), (sides[1],)), ((), ())), pref...  36.9 us
  transfers between devices with their start and end apart: 4, of which 1 were waited for; matrix products, arithmetic and copies ran while one was open for 9% of the time, Pallas kernels for 72%

profile of v6, /device:TPU:0, one launch (start us, length us, event | category | flops | bytes accessed | tf_op | source)
XLA Modules:
  0.0 718.2 jit_solution(16071348469513055836)
XLA Ops:
  7.2 4.8 pad_maximum_fusion
  12.1 0.7 all-gather.5.cloned.1.call-update
  13.7 0.7 fusion.13.refs_4_
  14.4 0.7 maximum_maximum_fusion.1.refs_3_
  15.1 88.5 %gather_start.1 = (bf16[4,8,64,512]{3,2,1,0:T(8,128)(2,1)}, bf16[4,8,64,512]{3,2,1,0:T(8,128)(2,1)}, bf16[4,8,64,512]{3,2,1,0:T(8,128)(2,1)}, bf16[4,8,64,128]{3...) custom-call(bf16[64,2048]{1,0:T(8,128)(2,1)} %refs_0_.1, ...), custom_call_target="tpu_custom_call" | custom-call | tf_op jit(solution)/shard_map/gather_start/pallas_call | solution.py:241
  103.6 3.1 multiply_reduce_fusion
  106.8 0.8 convert_reduce_fusion.2
  107.8 0.7 convert_reduce_fusion
  108.5 5.4 fusion.1
  113.9 0.8 copy.51
  114.7 5.9 fusion.15.k_raw
  120.8 2.3 fusion.14.q_raw
  123.1 0.3 multiply_reduce_fusion.2
  123.5 0.9 copy-done.19
  124.5 1.0 copy-done.28
  125.5 3.3 convolution_convert_fusion.6.v_ref
  128.8 24.1 %attend.1 = (bf16[1024,512]{1,0:T(8,128)(2,1)S(1)}, bf16[1024,512]{1,0:T(8,128)(2,1)S(1)}, bf16[1024,512]{1,0:T(8,128)(2,1)S(1)}, f32[1024,8]{1,0:T(8,128)S(1)}) custom-call(f32[1024,512]{1,0:T(8,128)} %copy-done.19, f32[1024,512]{1,0:T(8,128)} %copy-done.18, bf16[1024,512]{1,0:T(8,128)(2,1)} %convolution_convert_fusion.6.v_ref, ...), custom_call_target="tpu_custom_call" | custom-call | tf_op jit(solution)/shard_map/attend/pallas_call | solution.py:1054
  153.0 2.3 convolution_convert_fusion
  155.5 74.0 %middle.1 = (f32[256,2048]{1,0:T(8,128)S(1)}, bf16[8,256,2048]{2,1,0:T(8,128)(2,1)S(1)}, s32[8,2,256]{2,1,0:T(2,128)S(1)}, s32[8,256,2]{2,1,0:T(8,128)S(1)}) custom-call(bf16[4,256,2048]{2,1,0:T(8,128)(2,1)S(1)} %bitcast.68, bf16[256,2048]{1,0:T(8,128)(2,1)S(1)} %bitcast.70, s32[8,8,256]{2,1,0:T(8,128)S(1)} %copy-done.8), custom_call_target="tpu_custom_call" | custom-call | tf_op jit(solution)/shard_map/middle/pallas_call | solution.py:839
  229.4 3.3 copy-done
  232.7 0.4 multiply_reduce_fusion.1
  233.7 1.3 copy-done.16
  235.0 1.2 multiply_convert_fusion.h2_ref
  236.2 5.0 all-gather.3.cloned.1.call-done.wgu_ref.wgu_in
  241.2 89.9 %experts_in.1 = (bf16[8,256,2048]{2,1,0:T(8,128)(2,1)}, bf16[2,1088,2048]{2,1,0:T(8,128)(2,1)}, bf16[2,1088,2048]{2,1,0:T(8,128)(2,1)}, bf16[2,1088,1024]{2,1,0:...) custom-call(bf16[256,2048]{1,0:T(8,128)(2,1)} %multiply_convert_fusi, ...), custom_call_target="tpu_custom_call" | custom-call | tf_op jit(solution)/shard_map/experts_in/pallas_call | solution.py:1494
  331.1 36.2 %experts_mid.1 = (bf16[2,1088,1024]{2,1,0:T(8,128)(2,1)}, bf16[2,1088,1024]{2,1,0:T(8,128)(2,1)}, bf16[2,1088,1024]{2,1,0:T(8,128)(2,1)}, f32[2,4,272,1]{3,2,1,0:T(8,128)}, bf16[2,1024,2048]{2,1,0:T(8,128)(2,1)}) custom-call(bf16[2,1088,2048]{2,1,0:T(8,128)(2,1)} %get-tuple-element.81.y_in, bf16[2,1088,1024]{2,1,0:T(8,128)(2,1)} %get-tuple-element.82.act_in, ...), custom_call_target="tpu_custom_call" | custom-call | flops 17999998976 | bytes 60000000 | tf_op jit(solution)/shard_map/experts_mid/pallas_call | solution.py:1631
  367.4 96.8 %experts_out.1 = (bf16[8,256,1024]{2,1,0:T(8,128)(2,1)}, bf16[8,256,1024]{2,1,0:T(8,128)(2,1)}, f32[256,2048]{1,0:T(8,128)}, bf16[256,2048]{1,0:T(8,128)(2,1)}, f32[2048,128]{1,0:T(8,128)}) custom-call(bf16[2,1088,1024]{2,1,0:T(8,128)(2,1)} %get-tuple-element.86.gated_in, bf16[2,1088,1024]{2,1,0:T(8,128)(2,1)} %get-tuple-element.87.d_gate_in.right0, ...), custom_call_target="tpu_custom_call" | custom-call | flops 60000002048 | bytes 200000000 | tf_op jit(solution)/shard_map/experts_out/pallas_call | solution.py:2010
  464.3 52.1 %turn_back.1 = (bf16[4,256,2048]{2,1,0:T(8,128)(2,1)}, bf16[256,1024]{1,0:T(8,128)(2,1)}, bf16[2,2048,2048]{2,1,0:T(8,128)(2,1)}) custom-call(bf16[256,2048]{1,0:T(8,128)(2,1)} %get-tuple-element.95.x_ref, bf16[8,256,1024]{2,1,0:T(8,128)(2,1)} %get-tuple-element.96.parts_ref, bf16[2,1088,2048]{2,1,0:T(8,128)(2,1)} %get-tuple-element.97.left_ref, ...), custom_call_target="tpu_custom_call" | custom-call | flops 60000002048 | bytes 200000000 | tf_op jit(solution)/shard_map/turn_back/pallas_call | solution.py:924
  516.4 1.6 copy-done.52
  518.0 5.5 convolution_convert_fusion.5.do_ref
  523.5 49.4 %attend_back.1 = (bf16[1024,512]{1,0:T(8,128)(2,1)}, bf16[1024,512]{1,0:T(8,128)(2,1)}, bf16[1024,512]{1,0:T(8,128)(2,1)}, f32[8,8,128]{2,1,0:T(8,128)}, bf16[256,1024]{1,0:T(8,128)(2,1)}) custom-call(bf16[1024,512]{1,0:T(8,128)(2,1)} %copy-done.4, bf16[1024,512]{1,0:T(8,128)(2,1)} %copy-done.5, bf16[1024,512]{1,0:T(8,128)(2,1)} %convolution_convert_fusion.6.v_ref, ...), custom_call_target="tpu_custom_call" | custom-call | tf_op jit(solution)/shard_map/attend_back/pallas_call | solution.py:1250
  572.9 6.3 convolution_convert_fusion.1
  579.2 3.8 convolution_convert_fusion.4
  583.0 3.8 convolution_convert_fusion.3
  586.7 3.8 convolution_convert_fusion.2
  590.5 98.0 %scatter_end.1 = (bf16[64,2048]{1,0:T(8,128)(2,1)}, bf16[64,2048]{1,0:T(8,128)(2,1)}, bf16[64,2048]{1,0:T(8,128)(2,1)}, bf16[64,2048]{1,0:T(8,128)(2,1)}, f32[64...) custom-call(bf16[4,8,64,512]{3,2,1,0:T(8,128)(2,1)} %bitcast.82, bf16[4,8,64,512]{3,2,1,0:T(8,128)(2,1)} %bitcast.83, ...), custom_call_target="tpu_custom_call" | custom-call | tf_op jit(solution)/shard_map/scatter_end/pallas_call | solution.py:584
  688.5 1.4 copy.50
  689.9 1.8 convert_element_type.147
  691.7 4.4 convert_element_type.154
  696.1 0.7 slice_reduce_fusion
  696.9 1.3 add_reduce_fusion
  698.3 0.5 convert_divide_fusion
  698.8 0.6 fusion.2
  699.4 1.3 slice_bitcast_fusion
  700.7 1.3 fusion.7
  701.9 0.7 copy-done.29
  702.7 1.9 fusion.5
  704.6 6.7 slice_convert_fusion
  (128 shorter events, 2.3 us)
Async XLA Ops:
  7.2 234.0 %all-gather.3.cloned.1.call-start = ((), (), s32[]{:S(2)}) async-start(), calls=%async_computation.2 | async-start | bytes 20971520 | tf_op jit(solution)/shard_map/all_gather | solution.py:2124
  12.1 1.7 copy-start.47
  12.1 1.7 copy-start.48
  12.1 319.0 %all-gather.5.cloned.1.call-start = ((), (), s32[]{:S(2)}) async-start(), calls=%async_computation.3 | async-start | bytes 10485760 | tf_op jit(solution)/shard_map/all_gather | solution.py:2125
  12.8 451.4 %reduce-scatter.3.cloned.1.call-start = ((), (), s32[]{:S(2)}) async-start(), calls=%async_computation.4 | async-start | bytes 10485760 | tf_op jit(solution)/shard_map/reduce_scatter | solution.py:2187
  13.6 115.2 %copy-start.1 = (s32[1024,1]{1,0:T(8,128)}, s32[1024,1]{1,0:T(8,128)S(1)}, u32[]{:S(2)}) copy-start(s32[1024,1]{1,0:T(8,128)S(1)} %copy.47.doc_col) | copy-start | bytes 12292
  103.6 4.2 copy-start.23
  107.7 21.1 %copy-start.10 = (f32[1,512]{1,0:T(1,128)}, f32[1,512]{1,0:T(1,128)S(1)}, u32[]{:S(2)}) copy-start(f32[1,512]{1,0:T(1,128)S(1)} %reshape.179.gk) | copy-start | bytes 6148
  107.7 21.0 %copy-start.11 = (f32[1,512]{1,0:T(1,128)}, f32[1,512]{1,0:T(1,128)S(1)}, u32[]{:S(2)}) copy-start(f32[1,512]{1,0:T(1,128)S(1)} %reshape.178.gq) | copy-start | bytes 6148
  108.4 5.4 copy-start.41
  108.5 125.2 %copy-start.44 = (f32[2048]{0:T(1024)}, f32[2048]{0:T(1024)S(1)}, u32[]{:S(2)}) copy-start(f32[2048]{0:T(1024)S(1)} %get-tuple-element.164) | copy-start | bytes 24580
  108.5 6.2 copy-start.27
  114.7 5.9 copy-start.24
  114.7 6.1 copy-start.26
  120.6 2.5 copy-start.18
  123.1 2.3 copy-start.28
  125.5 3.3 copy-start.2
  125.5 3.3 copy-start.3
  128.8 24.2 %copy-start.51 = (bf16[8,64,2048]{2,1,0:T(8,128)(2,1)S(1)}, bf16[8,64,2048]{2,1,0:T(8,128)(2,1)}, u32[]{:S(2)}) copy-start(bf16[8,64,2048]{2,1,0:T(8,128)(2,1)} %get-tuple-element.76) | copy-start | bytes 6291460
  153.0 2.4 copy-start.4
  153.0 2.4 copy-start.5
  153.0 2.4 copy-start.7
  153.0 2.4 copy-start.13
  153.0 2.4 copy-start.6
  153.0 2.4 copy-start.8
  155.4 77.3 %copy-start.20 = (bf16[1,256,2048]{2,1,0:T(8,128)(2,1)S(1)}, bf16[1,256,2048]{2,1,0:T(8,128)(2,1)}, u32[]{:S(2)}) copy-start(bf16[1,256,2048]{2,1,0:T(8,128)(2,1)} %param.18) | copy-start | bytes 3145732
  229.4 3.3 copy-start
  367.4 337.3 %reduce-scatter.5.cloned.1.call-start = ((), (), s32[]{:S(2)}) async-start(), calls=%async_computation.5 | async-start | bytes 20971520 | tf_op jit(solution)/shard_map/reduce_scatter | solution.py:2187
  523.5 49.4 %copy-start.14 = (bf16[1024,512]{1,0:T(8,128)(2,1)S(1)}, bf16[1024,512]{1,0:T(8,128)(2,1)}, u32[]{:S(2)}) copy-start(bf16[1024,512]{1,0:T(8,128)(2,1)} %copy-done.13) | copy-start | bytes 3145732
  572.9 6.3 copy-start.25
  572.9 6.3 copy-start.30
  579.2 3.8 copy-start.31
  583.0 3.8 copy-start.32
  691.7 4.4 copy-start.43
  691.7 5.1 copy-start.33
  691.7 5.2 copy-start.34
  691.7 5.2 copy-start.35
  691.7 5.1 copy-start.38
  691.7 5.1 copy-start.39
  691.7 5.1 copy-start.40
  696.1 2.1 copy-start.50
  696.1 2.7 copy-start.21
  696.1 2.7 copy-start.22
  696.1 2.7 copy-start.42
  698.2 2.4 copy-start.17
  698.2 2.4 copy-start.36
  698.2 2.4 copy-start.37
  700.7 2.0 copy-start.29
  (9 other events, 10.5 us)
Sparse Core Ops, SparseCore 0:
  12.1 229.0 all-gather.2
  243.0 87.5 all-gather.4
  367.5 85.9 reduce-scatter.2
  516.5 187.7 reduce-scatter.4

commit v7 on v6

--- a/solution.py
+++ b/solution.py
@@ -528,12 +528,11 @@
         seq.begin()
 
     def between(step):
-        pl.when(step == 0)(back_rows)
-
         @pl.when(step == 1)
         def _():
             seq.relay()
 
+    back_rows()
     line.run(after, between)
     seq.total(sum_ref)
     for q in range(count):
@@ -903,11 +902,11 @@
         out.wait()
 
     def between(step):
+        grads.between(step)
+
         @pl.when(step == 1)
         def _():
             rows.relay()
-
-        grads.between(step)
 
     line.run(after, between)
     grads.finish()
@@ -1570,7 +1569,8 @@
     for e in range(local_experts):
         for n in range(5):
             fetch(n, e).start()
-    for e in range(local_experts):
+    @pl.loop(0, local_experts)
+    def _(e):
         for n in range(2):
             fetch(n, e).wait()
         gate = jnp.concatenate([gate_slots[e, q] for q in range(count)], axis=0)
@@ -1603,13 +1603,10 @@
             for buf in range(2):
                 n = 2 * m + buf
 
-                def wait_last():
+                @pl.when((m > 0) | (e > 0))
+                def _():
                     put_grad(e, n, buf).wait()
 
-                if e > 0:
-                    wait_last()
-                else:
-                    pl.when(m > 0)(wait_last)
                 cols = pl.ds(pl.multiple_of(n * tile, tile), tile)
                 staged[buf] = lax.dot_general(
                     gated[e, :, cols], ys[e], over_rows, preferred_element_type=F32
@@ -1806,11 +1803,13 @@
     first = i * local_experts
     over_lanes = (((1,), (1,)), ((), ()))
     line = StagedScatter(count, places, stage, (own, sibling, inbox), sems)
-    weights = ((wgu_in, wgu), (wd_in, wd))
+    block = 512
+    take_down = pltpu.make_async_copy(wd_in, wd, w_sem.at[model_width // block])
     inputs = ((gated_in, gated), (d_gate_in, d_gate), (d_up_in, d_up))
 
     def weight(n):
-        return pltpu.make_async_copy(weights[n][0], weights[n][1], w_sem.at[n])
+        rows = pl.ds(pl.multiple_of(n * block, block), block)
+        return pltpu.make_async_copy(wgu_in.at[:, rows], wgu.at[:, rows], w_sem.at[n])
 
     def fetch(n, q, buf):
         rows = pl.ds(pl.multiple_of(q * 2 * cap, 2 * cap), 2 * cap)
@@ -1827,8 +1826,9 @@
 
     for n in range(3):
         fetch(n, order(0), 0).start()
-    for n in range(2):
+    for n in range(model_width // block):
         weight(n).start()
+    take_down.start()
     take_x = pltpu.make_async_copy(x_in, x_mid, row_sem.at[0])
     take_dy = pltpu.make_async_copy(dy_in, dy, row_sem.at[1])
     take_x.start()
@@ -1877,15 +1877,14 @@
             line.to_sib(0, order(k - 1)).wait_send()
             line.to_sib(1, order(k - 1)).wait_send()
 
-        @pl.when(k == 0)
-        def _():
-            weight(0).wait()
-
-        block = 512
-
         @pl.loop(0, model_width // block)
         def _(n):
             cols = pl.ds(pl.multiple_of(n * block, block), block)
+
+            @pl.when(k == 0)
+            def _():
+                weight(n).wait()
+
             grads = []
             for e in range(local_experts):
                 grads.append(
@@ -1925,7 +1924,7 @@
 
         @pl.when(k == 0)
         def _():
-            weight(1).wait()
+            take_down.wait()
 
         take_tokens(q).wait()
 
@@ -1947,11 +1946,15 @@
         put(0, q).start()
         put(1, q).start()
 
-    @pl.loop(0, 1)
+    @pl.loop(0, count)
     def _(k):
         compute(k)
 
-    line.run(lambda a, q: None, lambda step: compute(step + 1))
+        @pl.when(k < count - 1)
+        def _():
+            line.event(k)
+
+    line.final(lambda a, q: None)
     put(0, 0).wait()
     put(1, 0).wait()
     line.to_sib(0, order(count - 1)).wait_send()
@@ -2026,7 +2029,7 @@
             pltpu.VMEM((count, tokens, model_width), BF),
             pltpu.VMEM((count, tokens, model_width), BF),
             pltpu.VMEM((count + 1, tokens, model_width), BF),
-            DMA((2,)),
+            DMA((model_width // 512 + 1,)),
             DMA((3, 2)),
             DMA((2,)),
             pltpu.VMEM((2, tokens, model_width), BF),

time: 727 us -> 721 us (level)
    pallas_call x1, Pallas kernels: 52.1 us -> 43.1 us  [turn_back(): pl.pallas_call(partial(turn_kernel, count, seq_count), out_shape=[jax.Sha...]
  transfers between devices with their start and end apart: 4 -> 4, of which waited for: 1 -> 1; matrix products, arithmetic and copies ran while one was open for 9% -> 9% of each run, Pallas kernels for 72% -> 74%
where the time goes in v7:
time: 721 us; the launch traced here: 713 us
  Pallas kernels  604 us (84%)
  matrix products  37 us (5%)
  other arithmetic  36.5 us (5%)
  local copies, waits for them, and re-layouts  14.9 us (2%)
  between operations  14.8 us (2%)
    pallas_call x1, Pallas kernels, scatter_end(): pl.pallas_call(partial(end_kernel, count, seq_count), out_shape=shapes, i...  102 us
    pallas_call x1, Pallas kernels, experts_out(): pl.pallas_call(partial(experts_out_kernel, count, CAP), out_shape=[jax.Sh...  96.8 us
    pallas_call x1, Pallas kernels, experts_in(): pl.pallas_call(partial(experts_in_kernel, count, CAP), out_shape=[jax.Sha...  89.9 us
    pallas_call x1, Pallas kernels, gather_start(): pl.pallas_call(partial(start_kernel, count, seq_count), out_shape=shapes,...  88.5 us
    pallas_call x1, Pallas kernels, middle(): pl.pallas_call(partial(middle_kernel, count, seq_count, CAP), out_shape=[...  74 us
    pallas_call x1, Pallas kernels, attend_back(): pl.pallas_call(partial(attend_back_kernel, count, seq_count, heads, 256,...  49 us
    pallas_call x1, Pallas kernels, turn_back(): pl.pallas_call(partial(turn_kernel, count, seq_count), out_shape=[jax.Sha...  43.1 us
    dot_general x9, matrix products, dot(): lax.dot_general(left, right, (((sides[0],), (sides[1],)), ((), ())), pref...  37 us
  transfers between devices with their start and end apart: 4, of which 1 were waited for; matrix products, arithmetic and copies ran while one was open for 9% of the time, Pallas kernels for 74%

profile of v7, /device:TPU:0, one launch (start us, length us, event | category | flops | bytes accessed | tf_op | source)
XLA Modules:
  0.0 713.0 jit_solution(2152959164337432588)
XLA Ops:
  7.2 4.8 pad_maximum_fusion
  12.1 0.7 all-gather.5.cloned.1.call-update
  13.7 0.7 fusion.13.refs_4_
  14.4 0.7 maximum_maximum_fusion.1.refs_3_
  15.1 88.5 %gather_start.1 = (bf16[4,8,64,512]{3,2,1,0:T(8,128)(2,1)}, bf16[4,8,64,512]{3,2,1,0:T(8,128)(2,1)}, bf16[4,8,64,512]{3,2,1,0:T(8,128)(2,1)}, bf16[4,8,64,128]{3...) custom-call(bf16[64,2048]{1,0:T(8,128)(2,1)} %refs_0_.1, ...), custom_call_target="tpu_custom_call" | custom-call | tf_op jit(solution)/shard_map/gather_start/pallas_call | solution.py:241
  103.6 3.1 multiply_reduce_fusion
  106.8 0.8 convert_reduce_fusion.2
  107.8 0.7 convert_reduce_fusion
  108.5 5.4 fusion.1
  113.9 0.8 copy.51
  114.7 5.9 fusion.15.k_raw
  120.8 2.3 fusion.14.q_raw
  123.1 0.3 multiply_reduce_fusion.2
  123.5 0.9 copy-done.19
  124.5 1.0 copy-done.28
  125.5 3.3 convolution_convert_fusion.6.v_ref
  128.8 24.1 %attend.1 = (bf16[1024,512]{1,0:T(8,128)(2,1)S(1)}, bf16[1024,512]{1,0:T(8,128)(2,1)S(1)}, bf16[1024,512]{1,0:T(8,128)(2,1)S(1)}, f32[1024,8]{1,0:T(8,128)S(1)}) custom-call(f32[1024,512]{1,0:T(8,128)} %copy-done.19, f32[1024,512]{1,0:T(8,128)} %copy-done.18, bf16[1024,512]{1,0:T(8,128)(2,1)} %convolution_convert_fusion.6.v_ref, ...), custom_call_target="tpu_custom_call" | custom-call | tf_op jit(solution)/shard_map/attend/pallas_call | solution.py:1053
  153.0 2.3 convolution_convert_fusion
  155.5 74.0 %middle.1 = (f32[256,2048]{1,0:T(8,128)S(1)}, bf16[8,256,2048]{2,1,0:T(8,128)(2,1)S(1)}, s32[8,2,256]{2,1,0:T(2,128)S(1)}, s32[8,256,2]{2,1,0:T(8,128)S(1)}) custom-call(bf16[4,256,2048]{2,1,0:T(8,128)(2,1)S(1)} %bitcast.68, bf16[256,2048]{1,0:T(8,128)(2,1)S(1)} %bitcast.70, s32[8,8,256]{2,1,0:T(8,128)S(1)} %copy-done.8), custom_call_target="tpu_custom_call" | custom-call | tf_op jit(solution)/shard_map/middle/pallas_call | solution.py:838
  229.4 3.3 copy-done
  232.7 0.4 multiply_reduce_fusion.1
  233.7 1.3 copy-done.16
  235.0 1.2 multiply_convert_fusion.h2_ref
  236.2 5.0 all-gather.3.cloned.1.call-done.wgu_ref.wgu_in
  241.2 89.9 %experts_in.1 = (bf16[8,256,2048]{2,1,0:T(8,128)(2,1)}, bf16[2,1088,2048]{2,1,0:T(8,128)(2,1)}, bf16[2,1088,2048]{2,1,0:T(8,128)(2,1)}, bf16[2,1088,1024]{2,1,0:...) custom-call(bf16[256,2048]{1,0:T(8,128)(2,1)} %multiply_convert_fusi, ...), custom_call_target="tpu_custom_call" | custom-call | tf_op jit(solution)/shard_map/experts_in/pallas_call | solution.py:1493
  331.1 36.2 %experts_mid.1 = (bf16[2,1088,1024]{2,1,0:T(8,128)(2,1)}, bf16[2,1088,1024]{2,1,0:T(8,128)(2,1)}, bf16[2,1088,1024]{2,1,0:T(8,128)(2,1)}, f32[2,4,272,1]{3,2,1,0:T(8,128)}, bf16[2,1024,2048]{2,1,0:T(8,128)(2,1)}) custom-call(bf16[2,1088,2048]{2,1,0:T(8,128)(2,1)} %get-tuple-element.81.y_in, bf16[2,1088,1024]{2,1,0:T(8,128)(2,1)} %get-tuple-element.82.act_in, ...), custom_call_target="tpu_custom_call" | custom-call | flops 17999998976 | bytes 60000000 | tf_op jit(solution)/shard_map/experts_mid/pallas_call | solution.py:1628
  367.4 96.8 %experts_out.1 = (bf16[8,256,1024]{2,1,0:T(8,128)(2,1)}, bf16[8,256,1024]{2,1,0:T(8,128)(2,1)}, f32[256,2048]{1,0:T(8,128)}, bf16[256,2048]{1,0:T(8,128)(2,1)}, f32[2048,128]{1,0:T(8,128)}) custom-call(bf16[2,1088,1024]{2,1,0:T(8,128)(2,1)} %get-tuple-element.86.gated_in, bf16[2,1088,1024]{2,1,0:T(8,128)(2,1)} %get-tuple-element.87.d_gate_in.right0, ...), custom_call_target="tpu_custom_call" | custom-call | flops 60000002048 | bytes 200000000 | tf_op jit(solution)/shard_map/experts_out/pallas_call | solution.py:2013
  464.2 43.1 %turn_back.1 = (bf16[4,256,2048]{2,1,0:T(8,128)(2,1)}, bf16[256,1024]{1,0:T(8,128)(2,1)}, bf16[2,2048,2048]{2,1,0:T(8,128)(2,1)}) custom-call(bf16[256,2048]{1,0:T(8,128)(2,1)} %get-tuple-element.95.x_ref, bf16[8,256,1024]{2,1,0:T(8,128)(2,1)} %get-tuple-element.96.parts_ref, bf16[2,1088,2048]{2,1,0:T(8,128)(2,1)} %get-tuple-element.97.left_ref, ...), custom_call_target="tpu_custom_call" | custom-call | flops 60000002048 | bytes 200000000 | tf_op jit(solution)/shard_map/turn_back/pallas_call | solution.py:923
  507.4 1.6 copy-done.52
  508.9 5.5 convolution_convert_fusion.5.do_ref
  514.5 49.0 %attend_back.1 = (bf16[1024,512]{1,0:T(8,128)(2,1)}, bf16[1024,512]{1,0:T(8,128)(2,1)}, bf16[1024,512]{1,0:T(8,128)(2,1)}, f32[8,8,128]{2,1,0:T(8,128)}, bf16[256,1024]{1,0:T(8,128)(2,1)}) custom-call(bf16[1024,512]{1,0:T(8,128)(2,1)} %copy-done.4, bf16[1024,512]{1,0:T(8,128)(2,1)} %copy-done.5, bf16[1024,512]{1,0:T(8,128)(2,1)} %convolution_convert_fusion.6.v_ref, ...), custom_call_target="tpu_custom_call" | custom-call | tf_op jit(solution)/shard_map/attend_back/pallas_call | solution.py:1249
  563.5 6.3 convolution_convert_fusion.1
  569.8 3.8 convolution_convert_fusion.4
  573.5 3.8 convolution_convert_fusion.3
  577.3 3.8 convolution_convert_fusion.2
  581.1 102.3 %scatter_end.1 = (bf16[64,2048]{1,0:T(8,128)(2,1)}, bf16[64,2048]{1,0:T(8,128)(2,1)}, bf16[64,2048]{1,0:T(8,128)(2,1)}, bf16[64,2048]{1,0:T(8,128)(2,1)}, f32[64...) custom-call(bf16[4,8,64,512]{3,2,1,0:T(8,128)(2,1)} %bitcast.82, bf16[4,8,64,512]{3,2,1,0:T(8,128)(2,1)} %bitcast.83, ...), custom_call_target="tpu_custom_call" | custom-call | tf_op jit(solution)/shard_map/scatter_end/pallas_call | solution.py:583
  683.4 1.4 copy.50
  684.8 1.8 convert_element_type.147
  686.7 4.3 convert_element_type.154
  690.9 0.7 slice_reduce_fusion
  691.7 1.3 add_reduce_fusion
  693.1 0.5 convert_divide_fusion
  693.6 0.6 fusion.2
  694.2 1.3 slice_bitcast_fusion
  695.5 1.3 fusion.7
  696.7 0.7 copy-done.29
  697.4 1.9 fusion.5
  699.4 6.7 slice_convert_fusion
  (128 shorter events, 2.3 us)
Async XLA Ops:
  7.2 234.0 %all-gather.3.cloned.1.call-start = ((), (), s32[]{:S(2)}) async-start(), calls=%async_computation.2 | async-start | bytes 20971520 | tf_op jit(solution)/shard_map/all_gather | solution.py:2127
  12.1 1.7 copy-start.47
  12.1 1.7 copy-start.48
  12.1 319.0 %all-gather.5.cloned.1.call-start = ((), (), s32[]{:S(2)}) async-start(), calls=%async_computation.3 | async-start | bytes 10485760 | tf_op jit(solution)/shard_map/all_gather | solution.py:2128
  12.8 451.4 %reduce-scatter.3.cloned.1.call-start = ((), (), s32[]{:S(2)}) async-start(), calls=%async_computation.4 | async-start | bytes 10485760 | tf_op jit(solution)/shard_map/reduce_scatter | solution.py:2190
  13.6 115.2 %copy-start.1 = (s32[1024,1]{1,0:T(8,128)}, s32[1024,1]{1,0:T(8,128)S(1)}, u32[]{:S(2)}) copy-start(s32[1024,1]{1,0:T(8,128)S(1)} %copy.47.doc_col) | copy-start | bytes 12292
  103.6 4.2 copy-start.23
  107.7 21.1 %copy-start.10 = (f32[1,512]{1,0:T(1,128)}, f32[1,512]{1,0:T(1,128)S(1)}, u32[]{:S(2)}) copy-start(f32[1,512]{1,0:T(1,128)S(1)} %reshape.179.gk) | copy-start | bytes 6148
  107.7 21.0 %copy-start.11 = (f32[1,512]{1,0:T(1,128)}, f32[1,512]{1,0:T(1,128)S(1)}, u32[]{:S(2)}) copy-start(f32[1,512]{1,0:T(1,128)S(1)} %reshape.178.gq) | copy-start | bytes 6148
  108.4 5.4 copy-start.41
  108.5 125.2 %copy-start.44 = (f32[2048]{0:T(1024)}, f32[2048]{0:T(1024)S(1)}, u32[]{:S(2)}) copy-start(f32[2048]{0:T(1024)S(1)} %get-tuple-element.164) | copy-start | bytes 24580
  108.5 6.2 copy-start.27
  114.7 5.9 copy-start.24
  114.7 6.1 copy-start.26
  120.6 2.5 copy-start.18
  123.1 2.3 copy-start.28
  125.5 3.3 copy-start.2
  125.5 3.3 copy-start.3
  128.8 24.2 %copy-start.51 = (bf16[8,64,2048]{2,1,0:T(8,128)(2,1)S(1)}, bf16[8,64,2048]{2,1,0:T(8,128)(2,1)}, u32[]{:S(2)}) copy-start(bf16[8,64,2048]{2,1,0:T(8,128)(2,1)} %get-tuple-element.76) | copy-start | bytes 6291460
  153.0 2.4 copy-start.4
  153.0 2.4 copy-start.5
  153.0 2.4 copy-start.7
  153.0 2.4 copy-start.13
  153.0 2.4 copy-start.6
  153.0 2.4 copy-start.8
  155.4 77.3 %copy-start.20 = (bf16[1,256,2048]{2,1,0:T(8,128)(2,1)S(1)}, bf16[1,256,2048]{2,1,0:T(8,128)(2,1)}, u32[]{:S(2)}) copy-start(bf16[1,256,2048]{2,1,0:T(8,128)(2,1)} %param.18) | copy-start | bytes 3145732
  229.4 3.3 copy-start
  367.3 332.0 %reduce-scatter.5.cloned.1.call-start = ((), (), s32[]{:S(2)}) async-start(), calls=%async_computation.5 | async-start | bytes 20971520 | tf_op jit(solution)/shard_map/reduce_scatter | solution.py:2190
  514.5 49.0 %copy-start.14 = (bf16[1024,512]{1,0:T(8,128)(2,1)S(1)}, bf16[1024,512]{1,0:T(8,128)(2,1)}, u32[]{:S(2)}) copy-start(bf16[1024,512]{1,0:T(8,128)(2,1)} %copy-done.13) | copy-start | bytes 3145732
  563.4 6.3 copy-start.25
  563.5 6.3 copy-start.30
  569.8 3.8 copy-start.31
  573.5 3.8 copy-start.32
  686.6 4.3 copy-start.43
  686.6 5.0 copy-start.33
  686.6 5.0 copy-start.34
  686.6 5.0 copy-start.35
  686.6 5.0 copy-start.38
  686.6 5.0 copy-start.39
  686.7 5.0 copy-start.40
  690.9 2.1 copy-start.50
  690.9 2.7 copy-start.21
  690.9 2.7 copy-start.22
  690.9 2.7 copy-start.42
  693.0 2.4 copy-start.17
  693.0 2.4 copy-start.36
  693.0 2.4 copy-start.37
  695.4 2.0 copy-start.29
  (9 other events, 10.5 us)
Sparse Core Ops, SparseCore 0:
  12.1 229.0 all-gather.2
  243.0 87.5 all-gather.4
  367.5 85.9 reduce-scatter.2
  507.5 187.9 reduce-scatter.4

commit v8 on v7

--- a/solution.py
+++ b/solution.py
@@ -528,11 +528,12 @@
         seq.begin()
 
     def between(step):
+        pl.when(step == 0)(back_rows)
+
         @pl.when(step == 1)
         def _():
             seq.relay()
 
-    back_rows()
     line.run(after, between)
     seq.total(sum_ref)
     for q in range(count):

time: 721 us -> 717 us (level)
  transfers between devices with their start and end apart: 4 -> 4, of which waited for: 1 -> 2; matrix products, arithmetic and copies ran while one was open for 9% -> 9% of each run, Pallas kernels for 74% -> 73%
where the time goes in v8:
time: 717 us; the launch traced here: 709 us
  Pallas kernels  599 us (84%)
  matrix products  37 us (5%)
  other arithmetic  36.5 us (5%)
  local copies, waits for them, and re-layouts  14.9 us (2%)
  between operations  14.8 us (2%)
    pallas_call x1, Pallas kernels, scatter_end(): pl.pallas_call(partial(end_kernel, count, seq_count), out_shape=shapes, i...  97.4 us
    pallas_call x1, Pallas kernels, experts_out(): pl.pallas_call(partial(experts_out_kernel, count, CAP), out_shape=[jax.Sh...  96.8 us
    pallas_call x1, Pallas kernels, experts_in(): pl.pallas_call(partial(experts_in_kernel, count, CAP), out_shape=[jax.Sha...  89.9 us
    pallas_call x1, Pallas kernels, gather_start(): pl.pallas_call(partial(start_kernel, count, seq_count), out_shape=shapes,...  88.5 us
    pallas_call x1, Pallas kernels, middle(): pl.pallas_call(partial(middle_kernel, count, seq_count, CAP), out_shape=[...  74 us
    pallas_call x1, Pallas kernels, attend_back(): pl.pallas_call(partial(attend_back_kernel, count, seq_count, heads, 256,...  49 us
    pallas_call x1, Pallas kernels, turn_back(): pl.pallas_call(partial(turn_kernel, count, seq_count), out_shape=[jax.Sha...  43.1 us
    dot_general x9, matrix products, dot(): lax.dot_general(left, right, (((sides[0],), (sides[1],)), ((), ())), pref...  37 us
  transfers between devices with their start and end apart: 4, of which 2 were waited for; matrix products, arithmetic and copies ran while one was open for 9% of the time, Pallas kernels for 73%

profile of v8, /device:TPU:0, one launch (start us, length us, event | category | flops | bytes accessed | tf_op | source)
XLA Modules:
  0.0 709.1 jit_solution(8899211599944036644)
XLA Ops:
  7.2 4.8 pad_maximum_fusion
  12.1 0.7 all-gather.5.cloned.1.call-update
  13.7 0.7 fusion.13.refs_4_
  14.4 0.7 maximum_maximum_fusion.1.refs_3_
  15.1 88.5 %gather_start.1 = (bf16[4,8,64,512]{3,2,1,0:T(8,128)(2,1)}, bf16[4,8,64,512]{3,2,1,0:T(8,128)(2,1)}, bf16[4,8,64,512]{3,2,1,0:T(8,128)(2,1)}, bf16[4,8,64,128]{3...) custom-call(bf16[64,2048]{1,0:T(8,128)(2,1)} %refs_0_.1, ...), custom_call_target="tpu_custom_call" | custom-call | tf_op jit(solution)/shard_map/gather_start/pallas_call | solution.py:241
  103.6 3.1 multiply_reduce_fusion
  106.8 0.8 convert_reduce_fusion.2
  107.8 0.7 convert_reduce_fusion
  108.5 5.4 fusion.1
  113.9 0.8 copy.51
  114.7 5.9 fusion.15.k_raw
  120.8 2.3 fusion.14.q_raw
  123.5 0.9 copy-done.19
  124.5 1.0 copy-done.28
  125.5 3.3 convolution_convert_fusion.6.v_ref
  128.8 24.1 %attend.1 = (bf16[1024,512]{1,0:T(8,128)(2,1)S(1)}, bf16[1024,512]{1,0:T(8,128)(2,1)S(1)}, bf16[1024,512]{1,0:T(8,128)(2,1)S(1)}, f32[1024,8]{1,0:T(8,128)S(1)}) custom-call(f32[1024,512]{1,0:T(8,128)} %copy-done.19, f32[1024,512]{1,0:T(8,128)} %copy-done.18, bf16[1024,512]{1,0:T(8,128)(2,1)} %convolution_convert_fusion.6.v_ref, ...), custom_call_target="tpu_custom_call" | custom-call | tf_op jit(solution)/shard_map/attend/pallas_call | solution.py:1054
  153.0 2.3 convolution_convert_fusion
  155.5 74.0 %middle.1 = (f32[256,2048]{1,0:T(8,128)S(1)}, bf16[8,256,2048]{2,1,0:T(8,128)(2,1)S(1)}, s32[8,2,256]{2,1,0:T(2,128)S(1)}, s32[8,256,2]{2,1,0:T(8,128)S(1)}) custom-call(bf16[4,256,2048]{2,1,0:T(8,128)(2,1)S(1)} %bitcast.68, bf16[256,2048]{1,0:T(8,128)(2,1)S(1)} %bitcast.70, s32[8,8,256]{2,1,0:T(8,128)S(1)} %copy-done.8), custom_call_target="tpu_custom_call" | custom-call | tf_op jit(solution)/shard_map/middle/pallas_call | solution.py:839
  229.4 3.3 copy-done
  232.7 0.4 multiply_reduce_fusion.1
  233.7 1.3 copy-done.16
  235.0 1.2 multiply_convert_fusion.h2_ref
  236.2 5.0 all-gather.3.cloned.1.call-done.wgu_ref.wgu_in
  241.2 89.9 %experts_in.1 = (bf16[8,256,2048]{2,1,0:T(8,128)(2,1)}, bf16[2,1088,2048]{2,1,0:T(8,128)(2,1)}, bf16[2,1088,2048]{2,1,0:T(8,128)(2,1)}, bf16[2,1088,1024]{2,1,0:...) custom-call(bf16[256,2048]{1,0:T(8,128)(2,1)} %multiply_convert_fusi, ...), custom_call_target="tpu_custom_call" | custom-call | tf_op jit(solution)/shard_map/experts_in/pallas_call | solution.py:1494
  331.1 36.2 %experts_mid.1 = (bf16[2,1088,1024]{2,1,0:T(8,128)(2,1)}, bf16[2,1088,1024]{2,1,0:T(8,128)(2,1)}, bf16[2,1088,1024]{2,1,0:T(8,128)(2,1)}, f32[2,4,272,1]{3,2,1,0:T(8,128)}, bf16[2,1024,2048]{2,1,0:T(8,128)(2,1)}) custom-call(bf16[2,1088,2048]{2,1,0:T(8,128)(2,1)} %get-tuple-element.81.y_in, bf16[2,1088,1024]{2,1,0:T(8,128)(2,1)} %get-tuple-element.82.act_in, ...), custom_call_target="tpu_custom_call" | custom-call | flops 17999998976 | bytes 60000000 | tf_op jit(solution)/shard_map/experts_mid/pallas_call | solution.py:1629
  367.4 96.8 %experts_out.1 = (bf16[8,256,1024]{2,1,0:T(8,128)(2,1)}, bf16[8,256,1024]{2,1,0:T(8,128)(2,1)}, f32[256,2048]{1,0:T(8,128)}, bf16[256,2048]{1,0:T(8,128)(2,1)}, f32[2048,128]{1,0:T(8,128)}) custom-call(bf16[2,1088,1024]{2,1,0:T(8,128)(2,1)} %get-tuple-element.86.gated_in, bf16[2,1088,1024]{2,1,0:T(8,128)(2,1)} %get-tuple-element.87.d_gate_in.right0, ...), custom_call_target="tpu_custom_call" | custom-call | flops 60000002048 | bytes 200000000 | tf_op jit(solution)/shard_map/experts_out/pallas_call | solution.py:2014
  464.2 43.1 %turn_back.1 = (bf16[4,256,2048]{2,1,0:T(8,128)(2,1)}, bf16[256,1024]{1,0:T(8,128)(2,1)}, bf16[2,2048,2048]{2,1,0:T(8,128)(2,1)}) custom-call(bf16[256,2048]{1,0:T(8,128)(2,1)} %get-tuple-element.95.x_ref, bf16[8,256,1024]{2,1,0:T(8,128)(2,1)} %get-tuple-element.96.parts_ref, bf16[2,1088,2048]{2,1,0:T(8,128)(2,1)} %get-tuple-element.97.left_ref, ...), custom_call_target="tpu_custom_call" | custom-call | flops 60000002048 | bytes 200000000 | tf_op jit(solution)/shard_map/turn_back/pallas_call | solution.py:924
  507.4 1.6 copy-done.52
  508.9 5.5 convolution_convert_fusion.5.do_ref
  514.5 49.0 %attend_back.1 = (bf16[1024,512]{1,0:T(8,128)(2,1)}, bf16[1024,512]{1,0:T(8,128)(2,1)}, bf16[1024,512]{1,0:T(8,128)(2,1)}, f32[8,8,128]{2,1,0:T(8,128)}, bf16[256,1024]{1,0:T(8,128)(2,1)}) custom-call(bf16[1024,512]{1,0:T(8,128)(2,1)} %copy-done.4, bf16[1024,512]{1,0:T(8,128)(2,1)} %copy-done.5, bf16[1024,512]{1,0:T(8,128)(2,1)} %convolution_convert_fusion.6.v_ref, ...), custom_call_target="tpu_custom_call" | custom-call | tf_op jit(solution)/shard_map/attend_back/pallas_call | solution.py:1250
  563.5 6.3 convolution_convert_fusion.1
  569.8 3.8 convolution_convert_fusion.4
  573.5 3.8 convolution_convert_fusion.3
  577.3 3.8 convolution_convert_fusion.2
  581.1 97.4 %scatter_end.1 = (bf16[64,2048]{1,0:T(8,128)(2,1)}, bf16[64,2048]{1,0:T(8,128)(2,1)}, bf16[64,2048]{1,0:T(8,128)(2,1)}, bf16[64,2048]{1,0:T(8,128)(2,1)}, f32[64...) custom-call(bf16[4,8,64,512]{3,2,1,0:T(8,128)(2,1)} %bitcast.82, bf16[4,8,64,512]{3,2,1,0:T(8,128)(2,1)} %bitcast.83, ...), custom_call_target="tpu_custom_call" | custom-call | tf_op jit(solution)/shard_map/scatter_end/pallas_call | solution.py:584
  678.4 1.4 copy.50
  679.9 1.8 convert_element_type.147
  681.7 4.2 convert_element_type.154
  685.9 0.7 slice_reduce_fusion
  686.7 1.3 add_reduce_fusion
  688.1 0.5 convert_divide_fusion
  688.6 0.6 fusion.2
  689.2 1.3 slice_bitcast_fusion
  690.5 1.3 fusion.7
  691.7 0.7 copy-done.29
  692.4 1.9 fusion.5
  694.4 1.1 reduce-scatter.5.cloned.1.call-done
  695.5 6.7 slice_convert_fusion
  (128 shorter events, 2.6 us)
Async XLA Ops:
  7.2 234.0 %all-gather.3.cloned.1.call-start = ((), (), s32[]{:S(2)}) async-start(), calls=%async_computation.2 | async-start | bytes 20971520 | tf_op jit(solution)/shard_map/all_gather | solution.py:2128
  12.1 1.7 copy-start.47
  12.1 1.7 copy-start.48
  12.1 319.0 %all-gather.5.cloned.1.call-start = ((), (), s32[]{:S(2)}) async-start(), calls=%async_computation.3 | async-start | bytes 10485760 | tf_op jit(solution)/shard_map/all_gather | solution.py:2129
  12.8 451.4 %reduce-scatter.3.cloned.1.call-start = ((), (), s32[]{:S(2)}) async-start(), calls=%async_computation.4 | async-start | bytes 10485760 | tf_op jit(solution)/shard_map/reduce_scatter | solution.py:2191
  13.6 115.2 %copy-start.1 = (s32[1024,1]{1,0:T(8,128)}, s32[1024,1]{1,0:T(8,128)S(1)}, u32[]{:S(2)}) copy-start(s32[1024,1]{1,0:T(8,128)S(1)} %copy.47.doc_col) | copy-start | bytes 12292
  103.6 4.2 copy-start.23
  107.7 21.1 %copy-start.10 = (f32[1,512]{1,0:T(1,128)}, f32[1,512]{1,0:T(1,128)S(1)}, u32[]{:S(2)}) copy-start(f32[1,512]{1,0:T(1,128)S(1)} %reshape.179.gk) | copy-start | bytes 6148
  107.7 21.0 %copy-start.11 = (f32[1,512]{1,0:T(1,128)}, f32[1,512]{1,0:T(1,128)S(1)}, u32[]{:S(2)}) copy-start(f32[1,512]{1,0:T(1,128)S(1)} %reshape.178.gq) | copy-start | bytes 6148
  108.4 5.4 copy-start.41
  108.5 125.2 %copy-start.44 = (f32[2048]{0:T(1024)}, f32[2048]{0:T(1024)S(1)}, u32[]{:S(2)}) copy-start(f32[2048]{0:T(1024)S(1)} %get-tuple-element.164) | copy-start | bytes 24580
  108.5 6.2 copy-start.27
  114.7 5.9 copy-start.24
  114.7 6.1 copy-start.26
  120.6 2.5 copy-start.18
  123.1 2.3 copy-start.28
  125.5 3.3 copy-start.2
  125.5 3.3 copy-start.3
  128.8 24.2 %copy-start.51 = (bf16[8,64,2048]{2,1,0:T(8,128)(2,1)S(1)}, bf16[8,64,2048]{2,1,0:T(8,128)(2,1)}, u32[]{:S(2)}) copy-start(bf16[8,64,2048]{2,1,0:T(8,128)(2,1)} %get-tuple-element.76) | copy-start | bytes 6291460
  153.0 2.4 copy-start.4
  153.0 2.4 copy-start.5
  153.0 2.4 copy-start.7
  153.0 2.4 copy-start.13
  153.0 2.4 copy-start.6
  153.0 2.4 copy-start.8
  155.4 77.3 %copy-start.20 = (bf16[1,256,2048]{2,1,0:T(8,128)(2,1)S(1)}, bf16[1,256,2048]{2,1,0:T(8,128)(2,1)}, u32[]{:S(2)}) copy-start(bf16[1,256,2048]{2,1,0:T(8,128)(2,1)} %param.18) | copy-start | bytes 3145732
  229.4 3.3 copy-start
  367.3 328.2 %reduce-scatter.5.cloned.1.call-start = ((), (), s32[]{:S(2)}) async-start(), calls=%async_computation.5 | async-start | bytes 20971520 | tf_op jit(solution)/shard_map/reduce_scatter | solution.py:2191
  514.5 49.0 %copy-start.14 = (bf16[1024,512]{1,0:T(8,128)(2,1)S(1)}, bf16[1024,512]{1,0:T(8,128)(2,1)}, u32[]{:S(2)}) copy-start(bf16[1024,512]{1,0:T(8,128)(2,1)} %copy-done.13) | copy-start | bytes 3145732
  563.4 6.3 copy-start.25
  563.5 6.3 copy-start.30
  569.8 3.8 copy-start.31
  573.5 3.8 copy-start.32
  681.6 4.3 copy-start.43
  681.6 5.0 copy-start.33
  681.6 5.0 copy-start.34
  681.6 5.0 copy-start.35
  681.6 5.0 copy-start.38
  681.7 5.0 copy-start.39
  681.7 5.0 copy-start.40
  685.9 2.1 copy-start.50
  685.9 2.7 copy-start.21
  685.9 2.7 copy-start.22
  685.9 2.7 copy-start.42
  688.0 2.4 copy-start.17
  688.0 2.4 copy-start.36
  688.0 2.4 copy-start.37
  690.5 2.0 copy-start.29
  (9 other events, 10.5 us)
Sparse Core Ops, SparseCore 0:
  12.1 229.0 all-gather.2
  243.0 87.5 all-gather.4
  367.5 85.9 reduce-scatter.2
  507.5 187.9 reduce-scatter.4
